TPU v7x, 32 devices: a whole 2x2x4 slice. The times are simulated.
32 devices in a mesh: member: 2 (over y), lon: 8 (over z, x), lat: 2 (over core).
Axes of the slice: x: 2, y: 2, z: 4, core: 2. Of those that a mesh axis runs over, the one named last changes fastest.
Arguments:
- state_field: bfloat16 [928, 32768], P('lat', ('member', 'lon')), parts along dimension 1, may hold values from -20 to 20
- skip_gain: float32 [4, 3, 64], replicated, may hold values from 0.25 to 2
- embed_weight: bfloat16 [64, 256], replicated, may hold values from -0.75 to 0.75
- qkv_weight: bfloat16 [256, 768], replicated, may hold values from -0.375 to 0.375
- head_scale: float32 [8], replicated, may hold values from 0.5 to 4
- out_weight: bfloat16 [256, 256], replicated, may hold values from -0.375 to 0.375
- norm_gain: float32 [256], replicated, may hold values from 0.1 to 1.9
- back_weight: bfloat16 [256, 64], replicated, may hold values from -0.375 to 0.375
Outputs:
- forecast: bfloat16 [928, 32768], P('lat', ('member', 'lon')), parts along dimension 1
There are 2 independent parts, one for each index of `member`. A program takes and returns all parts, laid end to end along the dimension named above; an argument that names none is the same for every part. Nothing has to cross between parts.
All inputs are finite; a program needn't handle non-finite values.
Results may differ from a plain program's by a relative error of at most 0.0022.
Values may be sent and summed in bfloat16 or wider, within the bound.
No kernel may reach another device: no remote copies, remote signals or barrier semaphores. Data moves between devices by JAX's collectives and lax.ppermute only.
A program may use at most 128 MiB of HBM per device.

v0:
```python
import functools
import math

import jax
import jax.numpy as jnp
import numpy as np
from jax import lax
from jax.experimental import pallas as pl
from jax.experimental.pallas import tpu as pltpu
from jax.sharding import PartitionSpec as P

C = 64
HEADS = 8
HEAD_DIM = 32
E = 256
LANES = 128
HALO = 96
LEAD = 16

LOW = np.array(
    [
        -0.010597401784997278,
        0.032883011666982945,
        0.030841381835986965,
        -0.18703481171888114,
        -0.02798376941698385,
        0.6308807679295904,
        0.7148465705525415,
        0.23037781330885523,
    ]
)
HIGH = np.array([(-1.0) ** j * LOW[7 - j] for j in range(8)])
F32 = jnp.float32
BF16 = jnp.bfloat16


def analysis_matrix(taps, out_start, out_rows, in_start, in_rows):
    m = np.zeros((out_rows, in_rows), np.float32)
    for j in range(out_rows):
        for t in range(8):
            r = 2 * (out_start + j) - 3 + t - in_start
            if 0 <= r < in_rows:
                m[j, r] = taps[t]
    return m


def synthesis_matrix(taps, out_start, out_rows, in_start, in_rows):
    m = np.zeros((out_rows, in_rows), np.float32)
    for j in range(out_rows):
        for r in range(in_rows):
            t = out_start + j - 2 * (in_start + r) + 3
            if 0 <= t < 8:
                m[j, r] = taps[t]
    return m


def two_terms(value):
    top = value.astype(BF16)
    return top, (value - top.astype(F32)).astype(BF16)


def masked_rows(matrix, start, count, lat, lats):
    row = lax.broadcasted_iota(jnp.int32, matrix.shape, 0) + (start + lat * count)
    return jnp.where((row >= 0) & (row < count * lats), matrix, 0.0)


def mxu(a, b):
    return jnp.dot(a, b, preferred_element_type=F32)


def dot3(matrix, value):
    mh, ml = two_terms(matrix)
    vh, vl = two_terms(value)
    return mxu(mh, vh) + mxu(mh, vl) + mxu(ml, vh)


def lane_pair(rows, even, odd):
    lane = lax.broadcasted_iota(jnp.int32, (rows, LANES), 1)
    return jnp.where(lane < C, F32(even), F32(odd))


def split_weights(rows, taps):
    def tap(j):
        return float(taps[j]) if 0 <= j < 8 else 0.0

    return [lane_pair(rows, tap(2 * d + 3), tap(2 * d + 4)) for d in range(-2, 3)]


def first_half(rows):
    return lax.broadcasted_iota(jnp.int32, (rows, LANES), 1) < C


def half_turn(value):
    return pltpu.roll(value, C, 1)


def split_pair(cols, start, k, weights, left):
    def one(cell):
        total = None
        for d in range(-2, 3):
            p = cell + d - start
            if 0 <= p < len(cols):
                term = weights[d + 2] * cols[p]
                total = term if total is None else total + term
        return total

    a, b = one(k), one(k + 1)
    zero = jnp.zeros(cols[0].shape, F32)
    a = zero if a is None else a
    b = zero if b is None else b
    return jnp.where(left, a, b) + half_turn(jnp.where(left, b, a))


def both_halves(cols, left):
    cells = []
    for col in cols:
        turned = half_turn(col)
        cells.append(jnp.where(left, col, turned))
        cells.append(jnp.where(left, turned, col))
    return cells


def join_weights(rows, taps, odd_first):
    def tap(t):
        return float(taps[t]) if 0 <= t < 8 else 0.0

    if odd_first:
        return [lane_pair(rows, tap(6 - 2 * i), tap(7 - 2 * i)) for i in range(4)]
    return [lane_pair(rows, tap(7 - 2 * i), tap(8 - 2 * i)) for i in range(5)]


def join_pair(low_cells, high_cells, index, weights_low, weights_high):
    total = None
    for i in range(len(weights_low)):
        term = weights_low[i] * low_cells[index + i] + weights_high[i] * high_cells[index + i]
        total = term if total is None else total + term
    return total


def columns(ref, row, rows, lead=()):
    count = ref.shape[-1] // LANES
    return [ref[lead + (pl.ds(row, rows), pl.ds(LANES * p, LANES))] for p in range(count)]


def put(ref, row, rows, p, value, lead=()):
    ref[lead + (pl.ds(row, rows), pl.ds(LANES * p, LANES))] = value


class Geometry:
    def __init__(self, rows, cells):
        self.rows = [rows >> level for level in range(5)]
        self.cells = [cells >> level for level in range(5)]
        up = lambda value, step: -(-value // step) * step
        self.band = [None, (-4, up(self.rows[1] + 4, 16))]
        self.low = [None, (-52, up(self.rows[1] + 97, 112))]
        self.band.append((-8, up(self.rows[2] + 11, 16)))
        self.low.append((-24, up(self.rows[2] + 45, 8)))
        self.band.append((-3, up(self.rows[3] + 6, 8)))
        self.low.append((-11, up(self.rows[3] + 20, 8)))
        self.band.append((-3, up(self.rows[4] + 6, 8)))
        self.low.append((-3, up(self.rows[4] + 6, 8)))
        self.band_cells = [None, (-2, self.cells[1] // 2 + 2)]
        self.low_cells = [None, (-2, self.cells[1] // 2 + 2)]
        for level in (2, 3, 4):
            self.band_cells.append((-3, self.cells[level] // 2 + 3))
            self.low_cells.append((-4, self.cells[level] // 2 + 4))
        self.extended = LEAD + HALO + rows + HALO
        blocks = self.low[1][1] // 112
        self.extended = max(self.extended, 224 * (blocks - 1) + 256)


STEP = 8


def first_level_kernel(geo, lats, place, x, edge, tl, th, gain, g1, d1, send_e, send_o, ext, la, ha):
    lat, parity = place[0], place[1]
    rows = geo.rows[0]
    low_start, low_rows = geo.low[1]
    band_start, band_rows = geo.band[1]
    width = x.shape[1]
    top = slice(LEAD, LEAD + HALO)
    bottom = slice(LEAD + HALO + rows, LEAD + 2 * HALO + rows)
    ext[0:LEAD, :] = jnp.zeros((LEAD, width), BF16)
    tail = geo.extended - (LEAD + 2 * HALO + rows)
    if tail:
        ext[geo.extended - tail :, :] = jnp.zeros((tail, width), BF16)
    ext[LEAD + HALO : LEAD + HALO + rows, :] = x[...]

    @pl.when(lat == 0)
    def _():
        ext[top, :] = jnp.zeros((HALO, width), BF16)
        ext[bottom, :] = edge[...]

    @pl.when(lat != 0)
    def _():
        ext[top, :] = edge[...]
        ext[bottom, :] = jnp.zeros((HALO, width), BF16)

    for b in range(low_rows // 112):
        mh, ml = two_terms(masked_rows(tl[...], low_start + 112 * b, geo.rows[1], lat, lats))
        data = ext[224 * b : 224 * b + 256, :]
        la[112 * b : 112 * b + 112, :] = mxu(mh, data) + mxu(ml, data)
    for b in range(band_rows // 120):
        mh, ml = two_terms(masked_rows(th[...], band_start + 120 * b, geo.rows[1], lat, lats))
        data = ext[96 + 240 * b : 352 + 240 * b, :]
        ha[120 * b : 120 * b + 120, :] = mxu(mh, data) + mxu(ml, data)

    wl, wh = split_weights(STEP, LOW), split_weights(STEP, HIGH)
    left = first_half(STEP)
    first, pairs = geo.low_cells[1]

    def lows(c, carry):
        row = pl.multiple_of(c * STEP, STEP)
        cols = columns(la, row, STEP)
        for q in range(pairs):
            put(g1, row, STEP, q, split_pair(cols, 0, first + 2 * q, wl, left))
        return carry

    lax.fori_loop(0, low_rows // STEP, lows, 0)
    bfirst, bpairs = geo.band_cells[1]
    skip = band_start - low_start

    def details(c, carry):
        row = pl.multiple_of(c * STEP, STEP)
        cols = columns(la, row + skip, STEP)
        g = [jnp.broadcast_to(gain[b : b + 1, :], (STEP, LANES)) for b in range(3)]
        for q in range(bpairs):
            put(d1, row, STEP, q, split_pair(cols, 0, bfirst + 2 * q, wh, left) * g[0], (0,))
        cols = columns(ha, row, STEP)
        for q in range(bpairs):
            put(d1, row, STEP, q, split_pair(cols, 0, bfirst + 2 * q, wl, left) * g[1], (1,))
            put(d1, row, STEP, q, split_pair(cols, 0, bfirst + 2 * q, wh, left) * g[2], (2,))
        return carry

    lax.fori_loop(0, band_rows // STEP, details, 0)
    edge_lanes = 2 * LANES
    shift = (geo.cells[1] // 2) * LANES

    def fill(to_left, to_right):
        for b in range(3):
            at = slice(b * edge_lanes, (b + 1) * edge_lanes)
            to_left[:, at] = d1[b, :, 0:edge_lanes].astype(BF16)
            to_right[:, at] = d1[b, :, shift : shift + edge_lanes].astype(BF16)

    @pl.when(parity == 0)
    def _():
        fill(send_o, send_e)

    @pl.when(parity != 0)
    def _():
        fill(send_e, send_o)


def deep_kernel(geo, lats, place, g1, *refs):
    lat, parity = place[0], place[1]
    mats, refs = refs[:6], refs[6:]
    gain, refs = refs[0], refs[1:]
    d = {2: refs[0], 3: refs[1], 4: refs[2]}
    ll4, send_e, send_o, p2, m2, p3, m3 = refs[3:10]
    scratch = refs[10:]
    grids = {1: g1, 2: scratch[0], 3: scratch[1], 4: ll4}
    lo = {2: scratch[2], 3: scratch[4], 4: scratch[6]}
    hi = {2: scratch[3], 3: scratch[5], 4: scratch[7]}
    wl, wh = split_weights(STEP, LOW), split_weights(STEP, HIGH)
    left = first_half(STEP)
    for level in (2, 3, 4):
        n = geo.rows[level]
        low_start, low_rows = geo.low[level]
        band_start, band_rows = geo.band[level]
        source = grids[level - 1]
        vh, vl = two_terms(source[...])
        for matrix, start, out in (
            (mats[2 * (level - 2)], low_start, lo[level]),
            (mats[2 * (level - 2) + 1], band_start, hi[level]),
        ):
            mh, ml = two_terms(masked_rows(matrix[...], start, n, lat, lats))
            out[...] = mxu(mh, vh) + mxu(mh, vl) + mxu(ml, vh)
        in_start = geo.low_cells[level - 1][0] // 2
        first, pairs = geo.low_cells[level]
        bfirst, bpairs = geo.band_cells[level]
        skip = band_start - low_start
        target = grids[level]
        bands = d[level]

        def lows(c, carry):
            row = pl.multiple_of(c * STEP, STEP)
            cols = columns(lo[level], row, STEP)
            for q in range(pairs):
                put(target, row, STEP, q, split_pair(cols, in_start, first + 2 * q, wl, left))
            return carry

        lax.fori_loop(0, low_rows // STEP, lows, 0)

        def details(c, carry):
            row = pl.multiple_of(c * STEP, STEP)
            g = [
                jnp.broadcast_to(gain[3 * (level - 2) + b : 3 * (level - 2) + b + 1, :], (STEP, LANES))
                for b in range(3)
            ]
            cols = columns(lo[level], row + skip, STEP)
            for q in range(bpairs):
                out = split_pair(cols, in_start, bfirst + 2 * q, wh, left) * g[0]
                put(bands, row, STEP, q, out, (0,))
            cols = columns(hi[level], row, STEP)
            for q in range(bpairs):
                out = split_pair(cols, in_start, bfirst + 2 * q, wl, left) * g[1]
                put(bands, row, STEP, q, out, (1,))
                out = split_pair(cols, in_start, bfirst + 2 * q, wh, left) * g[2]
                put(bands, row, STEP, q, out, (2,))
            return carry

        lax.fori_loop(0, band_rows // STEP, details, 0)

    def fill(distance, to_left, to_right):
        for at, level, count, row in exchange_plan(geo)[distance]:
            n = geo.band[level][1]
            move = distance * geo.cells[level] // 2
            for b in range(3):
                lanes = slice(b * count * LANES, (b + 1) * count * LANES)
                to_left[row : row + n, lanes] = d[level][b, :, 0 : count * LANES].astype(BF16)
                to_right[row : row + n, lanes] = d[level][
                    b, :, move * LANES : (move + count) * LANES
                ].astype(BF16)

    @pl.when(parity == 0)
    def _():
        fill(1, send_o, send_e)

    @pl.when(parity != 0)
    def _():
        fill(1, send_e, send_o)

    fill(2, m2, p2)
    fill(3, m3, p3)


def exchange_plan(geo):
    plan = {}
    for distance in (1, 2, 3):
        entries, row = [], 0
        for level in (2, 3, 4):
            count = geo.band_cells[level][1] - distance * geo.cells[level] // 2
            if count > 0:
                entries.append((len(entries), level, count, row))
                row += -(-geo.band[level][1] // 16) * 16
        plan[distance] = entries
    return plan


def plan_shape(geo, distance):
    entries = exchange_plan(geo)[distance]
    rows = sum(-(-geo.band[level][1] // 16) * 16 for _, level, _, _ in entries)
    return (rows, max(count for _, _, count, _ in entries) * 3 * LANES)


def attention_kernel(geo, lats, blocks, place, keys, grid, we, wqkv, scale, wo, gain, wb, out):
    lat = place[0]
    rows, width = grid.shape
    cells = width // C
    field = grid[...]
    own = jnp.concatenate([field[:, C * c : C * (c + 1)] for c in range(cells)], 0)
    count = own.shape[0]
    embedded = mxu(own.astype(BF16), we[...])
    queries = mxu(embedded.astype(BF16), wqkv[:, 0:E]).astype(BF16)
    lane = lax.broadcasted_iota(jnp.int32, (1, E), 1)
    block = keys.shape[0] // blocks
    factor = [scale[h] * (1.0 / math.sqrt(HEAD_DIM)) for h in range(HEADS)]

    def keyvals(start):
        spread = mxu(keys[pl.ds(start, block), :], we[...]).astype(BF16)
        both = mxu(spread, wqkv[:, E : 3 * E]).astype(BF16)
        return both[:, 0:E], both[:, E : 2 * E]

    def scores_of(h, k):
        mine = (lane >= h * HEAD_DIM) & (lane < (h + 1) * HEAD_DIM)
        q = jnp.where(mine, queries, jnp.zeros_like(queries))
        s = lax.dot_general(q, k, (((1,), (1,)), ((), ())), preferred_element_type=F32)
        return s * factor[h]

    def masked(h, value):
        mine = (lane >= h * HEAD_DIM) & (lane < (h + 1) * HEAD_DIM)
        return jnp.where(mine, value, jnp.zeros_like(value))

    if blocks == 1:
        k, v = keyvals(0)
        attended = jnp.zeros((count, E), F32)
        for h in range(HEADS):
            s = scores_of(h, k)
            w = jnp.exp(s - jnp.max(s, -1, keepdims=True))
            total = jnp.sum(w, -1, keepdims=True)
            attended = attended + masked(h, mxu(w.astype(BF16), v) / total)
    else:

        def one_block(b, carry):
            peaks, totals, sums = carry
            k, v = keyvals(pl.multiple_of(b * block, 16))
            new_peaks, new_totals = [], []
            shrunk = jnp.zeros((count, E), F32)
            for h in range(HEADS):
                s = scores_of(h, k)
                peak = jnp.maximum(peaks[h], jnp.max(s, -1, keepdims=True))
                shrink = jnp.exp(peaks[h] - peak)
                w = jnp.exp(s - peak)
                new_peaks.append(peak)
                new_totals.append(totals[h] * shrink + jnp.sum(w, -1, keepdims=True))
                shrunk = shrunk + masked(h, sums * shrink + mxu(w.astype(BF16), v))
            return tuple(new_peaks), tuple(new_totals), shrunk

        start = (
            tuple(jnp.full((count, 1), -1e30, F32) for _ in range(HEADS)),
            tuple(jnp.zeros((count, 1), F32) for _ in range(HEADS)),
            jnp.zeros((count, E), F32),
        )
        _, totals, sums = lax.fori_loop(0, blocks, one_block, start)
        attended = jnp.zeros((count, E), F32)
        for h in range(HEADS):
            attended = attended + masked(h, sums / totals[h])
    hidden = embedded + mxu(attended.astype(BF16), wo[...])
    square = jnp.mean(hidden * hidden, -1, keepdims=True)
    normed = (hidden * lax.rsqrt(square + 1e-06) * gain[...]).astype(BF16)
    update = mxu(normed, wb[...])
    back = [
        jnp.concatenate(
            [update[rows * c : rows * (c + 1), :], update[rows * (c + 1) : rows * (c + 2), :]], 1
        )
        for c in range(0, cells, 2)
    ]
    start = geo.band[4][0]
    for q, value in enumerate(back):
        at = slice(q * LANES, (q + 1) * LANES)
        out[:, at] = masked_rows(field[:, at] + value, start, geo.rows[4], lat, lats)


def synthesis_kernel(geo, lats, place, coarse, d1, d2, d3, d4, *refs):
    lat, parity = place[0], place[1]
    e1, o1, e2, o2, from_m2, from_p2, from_m3, from_p3 = refs[:8]
    mats, refs = refs[8:16], refs[16:]
    out, up3, up2, up1, sides, xh, xl, ylow, yhigh = refs
    bands = {2: d2, 3: d3, 4: d4}
    plan = exchange_plan(geo)
    left = first_half(STEP)

    def from_sides(level, b):
        n = geo.band[level][1]
        pairs = geo.band_cells[level][1]
        cols = [bands[level][b, :, LANES * p : LANES * (p + 1)] for p in range(pairs)]
        for distance in (1, 2, 3):
            for at, which, count, row in plan[distance]:
                if which != level:
                    continue
                move = distance * geo.cells[level] // 2
                for p in range(count):
                    lanes = slice((b * count + p) * LANES, (b * count + p + 1) * LANES)
                    if distance == 1:
                        even, odd = e2[row : row + n, lanes], o2[row : row + n, lanes]
                        low = jnp.where(parity == 0, odd.astype(F32), even.astype(F32))
                        high = jnp.where(parity == 0, even.astype(F32), odd.astype(F32))
                    else:
                        lows, highs = {2: (from_m2, from_p2), 3: (from_m3, from_p3)}[distance]
                        low = lows[row : row + n, lanes].astype(F32)
                        high = highs[row : row + n, lanes].astype(F32)
                    cols[p] = cols[p] + low
                    cols[p + move] = cols[p + move] + high
        return cols

    uppers = {4: coarse, 3: up3, 2: up2, 1: up1}
    for level in (4, 3, 2):
        pairs = geo.band_cells[level][1]
        m_low, m_high = mats[2 * (4 - level)], mats[2 * (4 - level) + 1]
        below = level - 1
        start, rows = geo.band[below]
        s_low = masked_rows(m_low[...], start, geo.rows[below], lat, lats)
        s_high = masked_rows(m_high[...], start, geo.rows[below], lat, lats)
        source = uppers[level][...]
        lonlow = dot3(s_low, source) + dot3(s_high, jnp.concatenate(from_sides(level, 1), 1))
        lonhigh = dot3(s_low, jnp.concatenate(from_sides(level, 0), 1)) + dot3(
            s_high, jnp.concatenate(from_sides(level, 2), 1)
        )
        width = pairs * LANES
        ylow[0:rows, 0:width] = lonlow
        yhigh[0:rows, 0:width] = lonhigh
        odd = below > 1
        wl, wh = join_weights(STEP, LOW, odd), join_weights(STEP, HIGH, odd)
        target = uppers[below]
        first, out_pairs = geo.band_cells[below]
        begin = geo.band_cells[level][0]

        def joined(c, carry):
            row = pl.multiple_of(c * STEP, STEP)
            lo = both_halves([ylow[pl.ds(row, STEP), pl.ds(LANES * p, LANES)] for p in range(pairs)], left)
            hi = both_halves([yhigh[pl.ds(row, STEP), pl.ds(LANES * p, LANES)] for p in range(pairs)], left)
            for q in range(out_pairs):
                m = first + 2 * q
                a = (m - 1) // 2 if odd else m // 2
                index = (a - 1 if odd else a - 2) - begin
                put(target, row, STEP, q, join_pair(lo, hi, index, wl, wh))
            return carry

        lax.fori_loop(0, rows // STEP, joined, 0)

    n = geo.band[1][1]
    pairs = geo.band_cells[1][1]
    edge = 2 * LANES
    shift = (geo.cells[1] // 2) * LANES
    for b in range(3):
        at = slice(b * edge, (b + 1) * edge)
        even, odd = e1[:, at].astype(F32), o1[:, at].astype(F32)
        sides[b, 0] = jnp.where(parity == 0, odd, even)
        sides[b, 1] = jnp.where(parity == 0, even, odd)
    half = geo.rows[0] // 2
    for block in range(2):
        w = 0 if block == 0 else n - LANES
        window = slice(w, w + LANES)
        sh, sl = two_terms(mats[6 + block][...])
        for pieces, y in (((None, 1), ylow), ((0, 2), yhigh)):
            for i, b in enumerate(pieces):
                place_rows = slice(i * LANES, (i + 1) * LANES)
                if b is None:
                    h, l = two_terms(up1[window, :])
                    xh[place_rows, :], xl[place_rows, :] = h, l
                else:
                    for lanes, extra in (
                        (slice(0, edge), sides[b, 0, window, :]),
                        (slice(edge, shift), None),
                        (slice(shift, shift + edge), sides[b, 1, window, :]),
                    ):
                        value = d1[b, window, lanes]
                        h, l = two_terms(value if extra is None else value + extra)
                        xh[place_rows, lanes], xl[place_rows, lanes] = h, l
            y[half * block : half * (block + 1), :] = (
                mxu(sh, xh[...]) + mxu(sh, xl[...]) + mxu(sl, xh[...])
            )
    rows16 = 16
    left16 = first_half(rows16)
    wl, wh = join_weights(rows16, LOW, False), join_weights(rows16, HIGH, False)

    def last(c, carry):
        row = pl.multiple_of(c * rows16, rows16)
        lo = both_halves(columns(ylow, row, rows16), left16)
        hi = both_halves(columns(yhigh, row, rows16), left16)
        for q in range(geo.cells[0] // 2):
            put(out, row, rows16, q, join_pair(lo, hi, q, wl, wh).astype(BF16))
        return carry

    lax.fori_loop(0, geo.rows[0] // rows16, last, 0)


def call(kernel, out_shape, scratch, *args, cost=20_000_000):
    vmem = pl.BlockSpec(memory_space=pltpu.VMEM)
    smem = pl.BlockSpec(memory_space=pltpu.SMEM)
    specs = [smem if a.ndim == 1 else vmem for a in args]
    outs = jax.tree.map(lambda _: vmem, out_shape)
    return pl.pallas_call(
        kernel,
        out_shape=out_shape,
        in_specs=specs,
        out_specs=outs,
        scratch_shapes=scratch,
        compiler_params=pltpu.CompilerParams(vmem_limit_bytes=56 << 20),
        cost_estimate=pl.CostEstimate(flops=cost, bytes_accessed=1 << 20, transcendentals=0),
    )(*args)


def shape(dims, dtype=F32):
    return jax.ShapeDtypeStruct(dims, dtype)


def per_device(mesh_shape, state_field, skip_gain, embed_weight, qkv_weight, head_scale, out_weight, norm_gain, back_weight):
    lons, lats = mesh_shape["lon"], mesh_shape["lat"]
    rows, width = state_field.shape
    geo = Geometry(rows, width // C)
    lat, lon = lax.axis_index("lat"), lax.axis_index("lon")
    place = jnp.stack([lat, lon % 2]).astype(jnp.int32)
    gains = jnp.tile(skip_gain, (1, 1, 2)).reshape(-1, LANES)

    even_pairs = [(i, i ^ 1) for i in range(lons)]
    odd_pairs = [(i, (i + 1 if i % 2 else i - 1) % lons) for i in range(lons)]
    swap = [(i, lats - 1 - i) for i in range(lats)]

    def shifted(value, by):
        return lax.ppermute(value, "lon", [(i, (i + by) % lons) for i in range(lons)])

    edge = jnp.where(lat == 0, state_field[rows - HALO :], state_field[:HALO])
    edge = lax.ppermute(edge, "lat", swap)

    low_rows, band_rows = geo.low[1][1], geo.band[1][1]
    tl = analysis_matrix(LOW, geo.low[1][0], 112, 0 - LEAD - HALO, 256)
    th = analysis_matrix(HIGH, geo.band[1][0], 120, 96 - LEAD - HALO, 256)
    w1 = geo.low_cells[1][1] * LANES
    g1, d1, send_e, send_o = call(
        functools.partial(first_level_kernel, geo, lats),
        (
            shape((low_rows, w1)),
            shape((3, band_rows, geo.band_cells[1][1] * LANES)),
            shape((band_rows, 6 * LANES), BF16),
            shape((band_rows, 6 * LANES), BF16),
        ),
        [
            pltpu.VMEM((geo.extended, width), BF16),
            pltpu.VMEM((low_rows, width), F32),
            pltpu.VMEM((band_rows, width), F32),
        ],
        place,
        state_field,
        edge,
        jnp.asarray(tl),
        jnp.asarray(th),
        gains[:3],
    )
    e1 = lax.ppermute(send_e, "lon", even_pairs)
    o1 = lax.ppermute(send_o, "lon", odd_pairs)

    mats = []
    for level in (2, 3, 4):
        in_start, in_rows = geo.low[level - 1]
        mats.append(analysis_matrix(LOW, *geo.low[level], in_start, in_rows))
        mats.append(analysis_matrix(HIGH, *geo.band[level], in_start, in_rows))
    scratch = [
        pltpu.VMEM((geo.low[level][1], geo.low_cells[level][1] * LANES), F32) for level in (2, 3)
    ]
    for level in (2, 3, 4):
        w = geo.low_cells[level - 1][1] * LANES
        scratch += [pltpu.VMEM((geo.low[level][1], w), F32), pltpu.VMEM((geo.band[level][1], w), F32)]
    deep = call(
        functools.partial(deep_kernel, geo, lats),
        tuple(
            shape((3, geo.band[level][1], geo.band_cells[level][1] * LANES)) for level in (2, 3, 4)
        )
        + (shape((geo.low[4][1], geo.low_cells[4][1] * LANES)),)
        + tuple(shape(plan_shape(geo, d), BF16) for d in (1, 1, 2, 2, 3, 3)),
        scratch,
        place,
        g1,
        *[jnp.asarray(m) for m in mats],
        gains[3:],
    )
    d2, d3, d4, ll4, deep_e, deep_o, p2, m2, p3, m3 = deep

    merged, size = ll4, 1
    while size < lons:
        other = lax.ppermute(merged, "lon", [(i, i ^ size) for i in range(lons)])
        lower_half = (lon // size) % 2 == 0
        lower = jnp.where(lower_half, merged, other)
        upper = jnp.where(lower_half, other, merged)
        wide = geo.cells[4] * C * size
        merged = jnp.pad(lower, ((0, 0), (0, wide))) + jnp.pad(upper, ((0, 0), (wide, 0)))
        size *= 2
    around = geo.cells[4] * lons * C
    w = 4 * C
    core = merged[:, w : w + around]
    grid4 = jnp.concatenate(
        [
            core[:, :w] + merged[:, w + around :],
            core[:, w : around - w],
            core[:, around - w :] + merged[:, :w],
        ],
        1,
    )
    skip = -geo.low[4][0]
    tokens = grid4[skip : skip + geo.rows[4]].astype(BF16)
    others = lax.ppermute(tokens, "lat", swap)
    keys = jnp.concatenate([tokens, others], 0).reshape(-1, C)

    e2 = lax.ppermute(deep_e, "lon", even_pairs)
    o2 = lax.ppermute(deep_o, "lon", odd_pairs)
    from_m2, from_p2 = shifted(p2, 2), shifted(m2, -2)
    from_m3, from_p3 = shifted(p3, 3), shifted(m3, -3)

    ring = jnp.concatenate([grid4[:, around - w :], grid4, grid4[:, :w]], 1)
    own = lax.dynamic_slice(
        ring,
        (0, lon * geo.cells[4] * C + C),
        (geo.low[4][1], geo.band_cells[4][1] * LANES),
    )
    blocks = max(1, keys.shape[0] // 928) if keys.shape[0] % 928 == 0 else 1
    coarse = call(
        functools.partial(attention_kernel, geo, lats, blocks),
        shape(own.shape),
        [],
        place,
        keys,
        own,
        embed_weight,
        qkv_weight,
        head_scale,
        out_weight,
        norm_gain[None],
        back_weight,
        cost=200_000_000,
    )

    synth = []
    for level in (4, 3, 2):
        for taps in (LOW, HIGH):
            synth.append(synthesis_matrix(taps, *geo.band[level - 1], *geo.band[level]))
    half = rows // 2
    for block in range(2):
        begin = geo.band[1][0] + (0 if block == 0 else band_rows - LANES)
        synth.append(
            np.concatenate(
                [synthesis_matrix(taps, half * block, half, begin, LANES) for taps in (LOW, HIGH)], 1
            )
        )
    y_width = geo.band_cells[1][1] * LANES
    return call(
        functools.partial(synthesis_kernel, geo, lats),
        shape((rows, width), BF16),
        [pltpu.VMEM((geo.band[level][1], geo.band_cells[level][1] * LANES), F32) for level in (3, 2, 1)]
        + [
            pltpu.VMEM((3, 2, band_rows, 2 * LANES), F32),
            pltpu.VMEM((2 * LANES, y_width), BF16),
            pltpu.VMEM((2 * LANES, y_width), BF16),
            pltpu.VMEM((rows, y_width), F32),
            pltpu.VMEM((rows, y_width), F32),
        ],
        place,
        coarse,
        d1,
        d2,
        d3,
        d4,
        e1,
        o1,
        e2,
        o2,
        from_m2,
        from_p2,
        from_m3,
        from_p3,
        *[jnp.asarray(m) for m in synth],
    )


def solution(mesh):
    in_specs = (P("lat", ("member", "lon")), P(), P(), P(), P(), P(), P(), P())
    out_specs = P("lat", ("member", "lon"))
    return jax.shard_map(
        functools.partial(per_device, dict(mesh.shape)),
        mesh=mesh,
        in_specs=in_specs,
        out_specs=out_specs,
        check_vma=False,
    )
```

profile of v0, /device:TPU:0, one launch (start us, length us, event | category | flops | bytes accessed | tf_op | source)
XLA Modules:
  0.0 116.3 jit_solution(3686878202576997102)
XLA Ops:
  0.0 1.2 slice_select_fusion
  1.2 0.6 collective-permute-start
  1.7 0.7 slice.43
  2.4 0.7 slice.45
  3.1 0.7 tile.13.gain
  3.8 0.7 tile.15.refs_6_
  4.5 0.7 pad_add_fusion.3.place
  5.1 0.0 collective-permute-done.edge
  5.1 0.7 copy-done.2
  5.9 14.3 %shard_map.226 = (f32[336,1280]{1,0:T(8,128)}, f32[3,240,1280]{2,1,0:T(8,128)}, bf16[240,768]{1,0:T(8,128)(2,1)}, bf16[240,768]{1,0:T(8,128)(2,1)}) custom-call(s32[2]{0:T(128)} %pad_add_fusion.3.place, bf16[464,2048]{1,0:T(8,128)(2,1)} %x.13, bf16[96,2048]{1,0:T(8,128)(2,1)} %copy-done.2, f32[112,256]{1,0:T(8,128)} %constant.105.clone.tl, ...), custom_call_target="tpu_custom_call" | custom-call | flops 20000000 | bytes 1048576 | tf_op jit(solution)/shard_map/pallas_call | solution.py:553
  20.2 12.8 %shard_map.227 = (f32[3,128,896]{2,1,0:T(8,128)}, f32[3,64,640]{2,1,0:T(8,128)}, f32[3,40,512]{2,1,0:T(8,128)}, f32[40,640]{1,0:T(8,128)}, bf16[240,1152]{1,0:T(...) custom-call(s32[2]{0:T(128)} %pad_add_fusion.3.place, ...), custom_call_target="tpu_custom_call" | custom-call | flops 20000000 | bytes 1048576 | tf_op jit(solution)/shard_map/pallas_call | solution.py:553
  32.9 2.6 %collective-permute-start.1 = (f32[40,640]{1,0:T(8,128)}, f32[40,640]{1,0:T(8,128)S(1)}, u32[]{:S(2)}, u32[]{:S(2)}) collective-permute-start(f32[40,640]{1,0:T(8,128)} %get-tuple-element.20), channel_id=1, source_target_pairs={{0,2},{2,0},{4,6},{6,4},{8,10},{10,8},{12,14},{14,12},{1,3},{3,1},... | collective-permute-start | bytes 307208 | tf_op jit(solution)/shard_map/ppermute | solution.py:641
  35.5 3.7 %collective-permute-done.1 = f32[40,640]{1,0:T(8,128)S(1)} collective-permute-done((f32[40,640]{1,0:T(8,128)}, f32[40,640]{1,0:T(8,128)S(1)}, u32[]{:S(2)}, u32[]{:S(2)}) %collective-permute-start.1) | collective-permute-done | bytes 102432 | tf_op jit(solution)/shard_map/ppermute | solution.py:641
  39.2 0.9 broadcast_select_fusion.5
  40.1 0.0 copy-start.9
  40.2 1.9 %collective-permute-start.2 = (f32[40,768]{1,0:T(8,128)S(1)}, f32[40,768]{1,0:T(8,128)S(1)}, u32[]{:S(2)}, u32[]{:S(2)}) collective-permute-start(f32[40,768]{1,0:T(8,128)S(1)} %pad_add_fusion.1), channel_id=1, source_target_pairs={{0,4},{2,6},{4,0},{6,2},{8,12},{10,14},{12,8},{14,10},{1,5},{3,7},... | collective-permute-start | bytes 368648 | tf_op jit(solution)/shard_map/ppermute | solution.py:641
  42.1 3.3 %collective-permute-done.2 = f32[40,768]{1,0:T(8,128)S(1)} collective-permute-done((f32[40,768]{1,0:T(8,128)S(1)}, f32[40,768]{1,0:T(8,128)S(1)}, u32[]{:S(2)}, u32[]{:S(2)}) %collective-permute-start.2) | collective-permute-done | bytes 122912 | tf_op jit(solution)/shard_map/ppermute | solution.py:641
  45.4 2.7 %collective-permute-start.3 = (f32[40,1024]{1,0:T(8,128)S(1)}, f32[40,1024]{1,0:T(8,128)S(1)}, u32[]{:S(2)}, u32[]{:S(2)}) collective-permute-start(f32[40,1024]{1,0:T(8,128)S(1)} %pad_add_fusion), channel_id=1, source_target_pairs={{0,8},{2,10},{4,12},{6,14},{8,0},{10,2},{12,4},{14,6},{1,9},{3,11}... | collective-permute-start | bytes 491528 | tf_op jit(solution)/shard_map/ppermute | solution.py:641
  48.1 2.5 %collective-permute-start.11 = (bf16[48,384]{1,0:T(8,128)(2,1)}, bf16[48,384]{1,0:T(8,128)(2,1)S(1)}, u32[]{:S(2)}, u32[]{:S(2)}) collective-permute-start(bf16[48,384]{1,0:T(8,128)(2,1)} %get-tuple-element.31), channel_id=1, source_target_pairs={{0,6},{2,8},{4,10},{6,12},{8,14},{10,0},{12,2},{14,4},{1,7},{3,9},... | collective-permute-start | bytes 110600 | tf_op jit(solution)/shard_map/ppermute | solution.py:581
  50.6 1.3 %collective-permute-start.12 = (bf16[48,384]{1,0:T(8,128)(2,1)}, bf16[48,384]{1,0:T(8,128)(2,1)S(1)}, u32[]{:S(2)}, u32[]{:S(2)}) collective-permute-start(bf16[48,384]{1,0:T(8,128)(2,1)} %get-tuple-element.32), channel_id=1, source_target_pairs={{0,10},{2,12},{4,14},{6,0},{8,2},{10,4},{12,6},{14,8},{1,11},{3,13... | collective-permute-start | bytes 110600 | tf_op jit(solution)/shard_map/ppermute | solution.py:581
  51.9 1.6 %collective-permute-start.9 = (bf16[112,768]{1,0:T(8,128)(2,1)}, bf16[112,768]{1,0:T(8,128)(2,1)S(1)}, u32[]{:S(2)}, u32[]{:S(2)}) collective-permute-start(bf16[112,768]{1,0:T(8,128)(2,1)} %get-tuple-element.29), channel_id=1, source_target_pairs={{0,4},{2,6},{4,8},{6,10},{8,12},{10,14},{12,0},{14,2},{1,5},{3,7},... | collective-permute-start | bytes 516104 | tf_op jit(solution)/shard_map/ppermute | solution.py:581
  53.5 0.8 collective-permute-start.7
  54.3 6.6 %collective-permute-done.3 = f32[40,1024]{1,0:T(8,128)S(1)} collective-permute-done((f32[40,1024]{1,0:T(8,128)S(1)}, f32[40,1024]{1,0:T(8,128)S(1)}, u32[]{:S(2)}, u32[]{:S(2)}) %collective-permute-start.3) | collective-permute-done | bytes 163872 | tf_op jit(solution)/shard_map/ppermute | solution.py:641
  60.9 0.1 collective-permute-start.8
  61.0 0.0 collective-permute-done.11.refs_6_
  61.1 0.1 collective-permute-start.5
  61.1 0.0 collective-permute-done.12.refs_7_
  61.2 4.7 %collective-permute-start.6 = (bf16[240,768]{1,0:T(8,128)(2,1)S(1)}, bf16[240,768]{1,0:T(8,128)(2,1)S(1)}, u32[]{:S(2)}, u32[]{:S(2)}) collective-permute-start(bf16[240,768]{1,0:T(8,128)(2,1)S(1)} %copy-done.10), channel_id=1, source_target_pairs={{0,14},{2,4},{4,2},{6,8},{8,6},{10,12},{12,10},{14,0},{1,15},{3,5}... | collective-permute-start | bytes 1105928 | tf_op jit(solution)/shard_map/ppermute | solution.py:611
  65.9 0.0 collective-permute-done.9.refs_4_
  65.9 0.0 copy-start.5
  65.9 0.1 collective-permute-start.4
  66.0 0.7 copy.28.wb
  66.8 0.5 collective-permute-done.4
  67.3 0.5 collective-permute-start.10
  67.8 0.7 constant_dynamic-slice_fusion.grid
  68.6 0.9 reshape.11.keys
  69.4 6.5 %shard_map.228.coarse = f32[40,512]{1,0:T(8,128)} custom-call(s32[2]{0:T(128)} %pad_add_fusion.3.place, bf16[928,64]{1,0:T(8,128)(2,1)} %reshape.11.keys, f32[40,512]{1,0:T(8,128)} %constant_dynamic-slice_fusion.grid, bf16[64,256]{1,0:T(8,128)(2,1)} %we.1, bf16[256,768]{1,0:T(8,128)(2,1)} %wqkv.1, f32[8]{0:T(128)} %scale.1, bf16[256,256]{1,0:T(8,128)(2,1)} %wo.1, ...), custom_call_target="tpu_custom_call" | custom-call | flops 200000000 | bytes 1048576 | tf_op jit(solution)/shard_map/pallas_call | solution.py:553
  76.0 8.6 %collective-permute-done.10.refs_5_ = bf16[112,768]{1,0:T(8,128)(2,1)S(1)} collective-permute-done((bf16[112,768]{1,0:T(8,128)(2,1)}, bf16[112,768]{1,0:T(8,128)(2,1)S(1)}, u32[]{:S(2)}, u32[]{:S(2)}) %collective-permute-start.10) | collective-permute-done | bytes 172064 | tf_op jit(solution)/shard_map/ppermute | solution.py:581
  84.5 9.8 %collective-permute-done.5.refs_0_ = bf16[240,768]{1,0:T(8,128)(2,1)S(1)} collective-permute-done((bf16[240,768]{1,0:T(8,128)(2,1)S(1)}, bf16[240,768]{1,0:T(8,128)(2,1)S(1)}, u32[]{:S(2)}, u32[]{:S(2)}) %collective-permute-start.5) | collective-permute-done | bytes 368672 | tf_op jit(solution)/shard_map/ppermute | solution.py:610
  94.3 0.0 collective-permute-done.6.refs_1_
  94.3 0.0 collective-permute-done.7.refs_2_
  94.3 0.0 collective-permute-done.8.refs_3_
  94.3 0.0 copy-start.1
  94.4 0.7 copy-done.3
  95.1 0.1 copy-done.4
  95.2 0.2 copy-done
  95.4 0.2 copy-done.1
  95.6 20.7 %shard_map.229 = bf16[464,2048]{1,0:T(8,128)(2,1)} custom-call(s32[2]{0:T(128)} %pad_add_fusion.3.place, f32[40,512]{1,0:T(8,128)} %shard_map.228.coarse, f32[3,240,1280]{2,1,0:T(8,128)} %get-tuple-element.21.d1, f32[3,128,896]{2,1,0:T(8,128)} %get-tuple-element.22.d2, f32[3,64,640]{2,1,0:T(8,128)} %get-tuple-element.23.d3, ...), custom_call_target="tpu_custom_call" | custom-call | flops 20000000 | bytes 1048576 | tf_op jit(solution)/shard_map/pallas_call | solution.py:553
  (31 shorter events, 0.2 us)
Async XLA Ops:
  1.2 4.0 %collective-permute-start = (bf16[96,2048]{1,0:T(8,128)(2,1)S(1)}, bf16[96,2048]{1,0:T(8,128)(2,1)S(1)}, u32[]{:S(2)}, u32[]{:S(2)}) collective-permute-start(bf16[96,2048]{1,0:T(8,128)(2,1)S(1)} %slice_select_fusion), channel_id=1, source_target_pairs={{0,1},{1,0},{2,3},{3,2},{4,5},{5,4},{6,7},{7,6},{8,9},{9,8},{10,11... | collective-permute-start | bytes 1179656 | tf_op jit(solution)/shard_map/ppermute | solution.py:584
  5.1 0.8 copy-start.2
  32.9 6.3 %collective-permute-start.1 = (f32[40,640]{1,0:T(8,128)}, f32[40,640]{1,0:T(8,128)S(1)}, u32[]{:S(2)}, u32[]{:S(2)}) collective-permute-start(f32[40,640]{1,0:T(8,128)} %get-tuple-element.20), channel_id=1, source_target_pairs={{0,2},{2,0},{4,6},{6,4},{8,10},{10,8},{12,14},{14,12},{1,3},{3,1},... | collective-permute-start | bytes 307208 | tf_op jit(solution)/shard_map/ppermute | solution.py:641
  35.5 25.6 %copy-start.11 = (bf16[240,768]{1,0:T(8,128)(2,1)S(1)}, bf16[240,768]{1,0:T(8,128)(2,1)}, u32[]{:S(2)}) copy-start(bf16[240,768]{1,0:T(8,128)(2,1)} %get-tuple-element.25) | copy-start | bytes 1105924
  35.5 25.7 %copy-start.10 = (bf16[240,768]{1,0:T(8,128)(2,1)S(1)}, bf16[240,768]{1,0:T(8,128)(2,1)}, u32[]{:S(2)}) copy-start(bf16[240,768]{1,0:T(8,128)(2,1)} %get-tuple-element.26) | copy-start | bytes 1105924
  40.1 25.9 %copy-start.9 = (bf16[256,64]{0,1:T(8,128)(2,1)S(1)}, bf16[256,64]{0,1:T(8,128)(2,1)}, u32[]{:S(2)}) copy-start(bf16[256,64]{0,1:T(8,128)(2,1)} %param.31) | copy-start | bytes 98308
  40.2 5.2 %collective-permute-start.2 = (f32[40,768]{1,0:T(8,128)S(1)}, f32[40,768]{1,0:T(8,128)S(1)}, u32[]{:S(2)}, u32[]{:S(2)}) collective-permute-start(f32[40,768]{1,0:T(8,128)S(1)} %pad_add_fusion.1), channel_id=1, source_target_pairs={{0,4},{2,6},{4,0},{6,2},{8,12},{10,14},{12,8},{14,10},{1,5},{3,7},... | collective-permute-start | bytes 368648 | tf_op jit(solution)/shard_map/ppermute | solution.py:641
  45.4 15.5 %collective-permute-start.3 = (f32[40,1024]{1,0:T(8,128)S(1)}, f32[40,1024]{1,0:T(8,128)S(1)}, u32[]{:S(2)}, u32[]{:S(2)}) collective-permute-start(f32[40,1024]{1,0:T(8,128)S(1)} %pad_add_fusion), channel_id=1, source_target_pairs={{0,8},{2,10},{4,12},{6,14},{8,0},{10,2},{12,4},{14,6},{1,9},{3,11}... | collective-permute-start | bytes 491528 | tf_op jit(solution)/shard_map/ppermute | solution.py:641
  48.1 13.0 %collective-permute-start.11 = (bf16[48,384]{1,0:T(8,128)(2,1)}, bf16[48,384]{1,0:T(8,128)(2,1)S(1)}, u32[]{:S(2)}, u32[]{:S(2)}) collective-permute-start(bf16[48,384]{1,0:T(8,128)(2,1)} %get-tuple-element.31), channel_id=1, source_target_pairs={{0,6},{2,8},{4,10},{6,12},{8,14},{10,0},{12,2},{14,4},{1,7},{3,9},... | collective-permute-start | bytes 110600 | tf_op jit(solution)/shard_map/ppermute | solution.py:581
  50.6 10.6 %collective-permute-start.12 = (bf16[48,384]{1,0:T(8,128)(2,1)}, bf16[48,384]{1,0:T(8,128)(2,1)S(1)}, u32[]{:S(2)}, u32[]{:S(2)}) collective-permute-start(bf16[48,384]{1,0:T(8,128)(2,1)} %get-tuple-element.32), channel_id=1, source_target_pairs={{0,10},{2,12},{4,14},{6,0},{8,2},{10,4},{12,6},{14,8},{1,11},{3,13... | collective-permute-start | bytes 110600 | tf_op jit(solution)/shard_map/ppermute | solution.py:581
  51.9 14.0 %collective-permute-start.9 = (bf16[112,768]{1,0:T(8,128)(2,1)}, bf16[112,768]{1,0:T(8,128)(2,1)S(1)}, u32[]{:S(2)}, u32[]{:S(2)}) collective-permute-start(bf16[112,768]{1,0:T(8,128)(2,1)} %get-tuple-element.29), channel_id=1, source_target_pairs={{0,4},{2,6},{4,8},{6,10},{8,12},{10,14},{12,0},{14,2},{1,5},{3,7},... | collective-permute-start | bytes 516104 | tf_op jit(solution)/shard_map/ppermute | solution.py:581
  53.5 40.9 %collective-permute-start.7 = (bf16[240,1152]{1,0:T(8,128)(2,1)}, bf16[240,1152]{1,0:T(8,128)(2,1)S(1)}, u32[]{:S(2)}, u32[]{:S(2)}) collective-permute-start(bf16[240,1152]{1,0:T(8,128)(2,1)} %get-tuple-element.27), channel_id=1, source_target_pairs={{0,2},{2,0},{4,6},{6,4},{8,10},{10,8},{12,14},{14,12},{1,3},{3,1},... | collective-permute-start | bytes 1658888 | tf_op jit(solution)/shard_map/ppermute | solution.py:664
  60.9 33.5 %collective-permute-start.8 = (bf16[240,1152]{1,0:T(8,128)(2,1)}, bf16[240,1152]{1,0:T(8,128)(2,1)S(1)}, u32[]{:S(2)}, u32[]{:S(2)}) collective-permute-start(bf16[240,1152]{1,0:T(8,128)(2,1)} %get-tuple-element.28), channel_id=1, source_target_pairs={{0,14},{2,4},{4,2},{6,8},{8,6},{10,12},{12,10},{14,0},{1,15},{3,5}... | collective-permute-start | bytes 1658888 | tf_op jit(solution)/shard_map/ppermute | solution.py:665
  61.0 33.3 %copy-start.7 = (bf16[48,384]{1,0:T(8,128)(2,1)}, bf16[48,384]{1,0:T(8,128)(2,1)S(1)}, u32[]{:S(2)}) copy-start(bf16[48,384]{1,0:T(8,128)(2,1)S(1)} %collective-permute-done.11.refs_6_) | copy-start | bytes 110596
  61.1 33.3 %collective-permute-start.5 = (bf16[240,768]{1,0:T(8,128)(2,1)S(1)}, bf16[240,768]{1,0:T(8,128)(2,1)S(1)}, u32[]{:S(2)}, u32[]{:S(2)}) collective-permute-start(bf16[240,768]{1,0:T(8,128)(2,1)S(1)} %copy-done.11), channel_id=1, source_target_pairs={{0,2},{2,0},{4,6},{6,4},{8,10},{10,8},{12,14},{14,12},{1,3},{3,1},... | collective-permute-start | bytes 1105928 | tf_op jit(solution)/shard_map/ppermute | solution.py:610
  61.2 33.2 %copy-start.8 = (bf16[48,384]{1,0:T(8,128)(2,1)}, bf16[48,384]{1,0:T(8,128)(2,1)S(1)}, u32[]{:S(2)}) copy-start(bf16[48,384]{1,0:T(8,128)(2,1)S(1)} %collective-permute-done.12.refs_7_) | copy-start | bytes 110596
  61.2 33.1 %collective-permute-start.6 = (bf16[240,768]{1,0:T(8,128)(2,1)S(1)}, bf16[240,768]{1,0:T(8,128)(2,1)S(1)}, u32[]{:S(2)}, u32[]{:S(2)}) collective-permute-start(bf16[240,768]{1,0:T(8,128)(2,1)S(1)} %copy-done.10), channel_id=1, source_target_pairs={{0,14},{2,4},{4,2},{6,8},{8,6},{10,12},{12,10},{14,0},{1,15},{3,5}... | collective-permute-start | bytes 1105928 | tf_op jit(solution)/shard_map/ppermute | solution.py:611
  65.9 28.4 %copy-start.5 = (bf16[112,768]{1,0:T(8,128)(2,1)}, bf16[112,768]{1,0:T(8,128)(2,1)S(1)}, u32[]{:S(2)}) copy-start(bf16[112,768]{1,0:T(8,128)(2,1)S(1)} %collective-permute-done.9.refs_4_) | copy-start | bytes 516100
  65.9 1.3 %collective-permute-start.4 = (bf16[29,1024]{1,0:T(8,128)(2,1)S(1)}, bf16[29,1024]{1,0:T(8,128)(2,1)S(1)}, u32[]{:S(2)}, u32[]{:S(2)}) collective-permute-start(bf16[29,1024]{1,0:T(8,128)(2,1)S(1)} %pad_maximum_fusion.1), channel_id=1, source_target_pairs={{0,1},{1,0},{2,3},{3,2},{4,5},{5,4},{6,7},{7,6},{8,9},{9,8},{10,11... | collective-permute-start | bytes 178184 | tf_op jit(solution)/shard_map/ppermute | solution.py:661
  67.3 17.3 %collective-permute-start.10 = (bf16[112,768]{1,0:T(8,128)(2,1)}, bf16[112,768]{1,0:T(8,128)(2,1)S(1)}, u32[]{:S(2)}, u32[]{:S(2)}) collective-permute-start(bf16[112,768]{1,0:T(8,128)(2,1)} %get-tuple-element.30), channel_id=1, source_target_pairs={{0,12},{2,14},{4,0},{6,2},{8,4},{10,6},{12,8},{14,10},{1,13},{3,15... | collective-permute-start | bytes 516104 | tf_op jit(solution)/shard_map/ppermute | solution.py:581
  84.5 9.8 %copy-start.6 = (bf16[112,768]{1,0:T(8,128)(2,1)}, bf16[112,768]{1,0:T(8,128)(2,1)S(1)}, u32[]{:S(2)}) copy-start(bf16[112,768]{1,0:T(8,128)(2,1)S(1)} %collective-permute-done.10.refs_5_) | copy-start | bytes 516100
  94.3 0.7 copy-start.3
  94.3 0.9 copy-start.4
  94.3 1.0 copy-start
  94.3 1.2 %copy-start.1 = (bf16[240,1152]{1,0:T(8,128)(2,1)}, bf16[240,1152]{1,0:T(8,128)(2,1)S(1)}, u32[]{:S(2)}) copy-start(bf16[240,1152]{1,0:T(8,128)(2,1)S(1)} %collective-permute-done.8.refs_3_) | copy-start | bytes 1658884
where the time goes:
time: 117 us; the launch traced here: 116 us
  Pallas kernels  54.3 us (46%)
  waiting for transfers between devices  32.4 us (28%)
  starting transfers between devices  19.4 us (17%)
  local copies, waits for them, and re-layouts  7.02 us (6%)
  other arithmetic  2.92 us (2%)
    pallas_call x4, Pallas kernels, call(): pl.pallas_call(kernel, out_shape=out_shape, in_specs=specs, out_specs=out...  54.3 us
    ppermute x3, waiting for transfers between devices, per_device(): other = lax.ppermute(merged, 'lon', [(i, i ^ size) for i in range(lons)])  13.6 us
    ppermute x1, waiting for transfers between devices, per_device(): e1 = lax.ppermute(send_e, 'lon', even_pairs)  9.77 us
    ppermute x4, waiting for transfers between devices, shifted(): lax.ppermute(value, 'lon', [(i, (i + by) % lons) for i in range(lons)])  8.56 us
    ppermute x3, starting transfers between devices, per_device(): other = lax.ppermute(merged, 'lon', [(i, i ^ size) for i in range(lons)])  7.11 us
    ppermute x4, starting transfers between devices, shifted(): lax.ppermute(value, 'lon', [(i, (i + by) % lons) for i in range(lons)])  5.94 us
    ppermute x1, starting transfers between devices, per_device(): o1 = lax.ppermute(send_o, 'lon', odd_pairs)  4.73 us
    unnamed x26, local copies, waits for them, and re-layouts  2.68 us
  transfers between devices with their start and end apart: 13, of which 6 were waited for; matrix products, arithmetic and copies ran while one was open for 5% of the time, Pallas kernels for 6%

commit v1 on v0

v1 whole, which is shorter than its diff:
```python
import functools
import math

import jax
import jax.numpy as jnp
import numpy as np
from jax import lax
from jax.experimental import pallas as pl
from jax.experimental.pallas import tpu as pltpu
from jax.sharding import PartitionSpec as P


C = 64
HEADS = 8
HEAD_DIM = 32
E = 256
LANES = 128
HALO = 96
LEAD = 16

LOW = np.array(
    [
        -0.010597401784997278,
        0.032883011666982945,
        0.030841381835986965,
        -0.18703481171888114,
        -0.02798376941698385,
        0.6308807679295904,
        0.7148465705525415,
        0.23037781330885523,
    ]
)
HIGH = np.array([(-1.0) ** j * LOW[7 - j] for j in range(8)])


def lattice_factors():
    a = np.array([(LOW[2 * (3 - j)], LOW[2 * (3 - j) + 1]) for j in range(4)])
    b = np.array([(HIGH[2 * (3 - j)], HIGH[2 * (3 - j) + 1]) for j in range(4)])
    factors = {}
    for s in (3, 2, 1):
        k = (a[s] @ b[s]) / (b[s] @ b[s])
        a, b = (a - k * b) / (1 + k * k), (k * a + b) / (1 + k * k)
        a, b = a[:s], b[1 : s + 1]
        factors[s] = float(k)
    factors[0] = float(a[0][1] / a[0][0])
    return factors, float(a[0][0]), float(np.sign(b[0][1] / a[0][0]))


TURN, SCALE, SIGN = lattice_factors()
F32 = jnp.float32
BF16 = jnp.bfloat16


def analysis_matrix(taps, out_start, out_rows, in_start, in_rows):
    m = np.zeros((out_rows, in_rows), np.float32)
    for j in range(out_rows):
        for t in range(8):
            r = 2 * (out_start + j) - 3 + t - in_start
            if 0 <= r < in_rows:
                m[j, r] = taps[t]
    return m


def synthesis_matrix(taps, out_start, out_rows, in_start, in_rows):
    m = np.zeros((out_rows, in_rows), np.float32)
    for j in range(out_rows):
        for r in range(in_rows):
            t = out_start + j - 2 * (in_start + r) + 3
            if 0 <= t < 8:
                m[j, r] = taps[t]
    return m


def two_terms(value):
    top = value.astype(BF16)
    return top, (value - top.astype(F32)).astype(BF16)


def masked_rows(matrix, start, count, lat, lats):
    row = lax.broadcasted_iota(jnp.int32, matrix.shape, 0) + (start + lat * count)
    return jnp.where((row >= 0) & (row < count * lats), matrix, 0.0)


def mxu(a, b):
    return jnp.dot(a, b, preferred_element_type=F32)


def dot3(matrix, vh, vl):
    mh, ml = two_terms(matrix)
    return mxu(mh, vh) + mxu(mh, vl) + mxu(ml, vh)


def first_half(rows):
    return lax.broadcasted_iota(jnp.int32, (rows, LANES), 1) < C


def half_turn(value):
    return None if value is None else pltpu.roll(value, C, 1)


def pick(left, a, b):
    if a is None and b is None:
        return None
    return jnp.where(left, 0.0 if a is None else a, 0.0 if b is None else b)


def plus(a, b, factor):
    if b is None:
        return a
    if a is None:
        return b * factor
    return a + b * factor


class Memo:
    def __init__(self, make):
        self.make, self.known = make, {}

    def __call__(self, n):
        if n not in self.known:
            self.known[n] = self.make(n)
        return self.known[n]


def analysis(cols, start, left):
    turned = Memo(lambda i: half_turn(cols[i]) if 0 <= i < len(cols) else None)
    plain = lambda i: cols[i] if 0 <= i < len(cols) else None
    if start % 2 == 0:
        at = lambda n: n - 1 - start // 2
        u = Memo(lambda n: pick(left, turned(at(n) - 1), plain(at(n))))
        w = Memo(lambda n: pick(left, plain(at(n)), turned(at(n) + 1)))
    else:
        at = lambda n: n - (start + 3) // 2
        u = Memo(lambda n: pick(left, plain(at(n)), turned(at(n) + 1)))
        w = Memo(lambda n: pick(left, turned(at(n)), plain(at(n) + 1)))
    a = Memo(lambda n: plus(u(n), w(n), TURN[0]))
    if SIGN < 0:
        minus = lambda v: None if v is None else -v
        b = Memo(lambda n: plus(minus(w(n)), u(n), TURN[0]))
    else:
        b = Memo(lambda n: plus(w(n), u(n), -TURN[0]))

    def stage(a, b, factor):
        rolled = Memo(lambda n: half_turn(b(n)))
        late = Memo(lambda n: pick(left, rolled(n - 2), rolled(n)))
        return (
            Memo(lambda n: plus(a(n), late(n), factor)),
            Memo(lambda n: plus(late(n), a(n), -factor)),
        )

    for s in (1, 2, 3):
        a, b = stage(a, b, TURN[s])
    return (lambda k: a(k + 3)), (lambda k: b(k + 3))


def synthesis(lows, highs, start, left):
    def cells(cols):
        return lambda n: cols[(n - 3 - start) // 2] if 0 <= n - 3 - start < 2 * len(cols) else None

    a, b = cells(lows), cells(highs)

    def stage(a, b, factor):
        early = Memo(lambda n: half_turn(plus(b(n), a(n), factor)))
        return (
            Memo(lambda n: plus(a(n), b(n), -factor)),
            Memo(lambda n: pick(left, early(n), early(n + 2))),
        )

    for s in (3, 2, 1):
        a, b = stage(a, b, TURN[s])
    last_a, last_b = a, b
    u = Memo(lambda n: plus(last_a(n), last_b(n), -TURN[0] * SIGN))
    if SIGN < 0:
        w = Memo(lambda n: plus(last_a(n) * TURN[0] if last_a(n) is not None else None, last_b(n), -1.0))
    else:
        w = Memo(lambda n: plus(last_b(n), last_a(n), TURN[0]))
    u_turned, w_turned = Memo(lambda n: half_turn(u(n))), Memo(lambda n: half_turn(w(n)))
    parity = (start + 3) % 2

    def pair(m):
        if m % 2:
            n = (m + 3) // 2
            if n % 2 == parity:
                return pick(left, u(n), w_turned(n))
            return pick(left, u_turned(n - 1), w(n - 1))
        n = m // 2 + 1
        if n % 2 == parity:
            return pick(left, w(n), u(n))
        return pick(left, w_turned(n - 1), u_turned(n + 1))

    return pair


def columns(ref, row, rows, count=None):
    count = ref.shape[-1] // LANES if count is None else count
    return [ref[pl.ds(row, rows), pl.ds(LANES * p, LANES)] for p in range(count)]


def put(ref, row, p, value, lead=()):
    ref[lead + (pl.ds(row, value.shape[0]), pl.ds(LANES * p, LANES))] = value


class Geometry:
    def __init__(self, rows, cells):
        self.rows = [rows >> level for level in range(5)]
        self.cells = [cells >> level for level in range(5)]
        up = lambda value, step: -(-value // step) * step
        self.band = [
            None,
            (-4, up(self.rows[1] + 4, 120)),
            (-8, up(self.rows[2] + 11, 16)),
            (-3, up(self.rows[3] + 6, 8)),
            (-3, up(self.rows[4] + 6, 8)),
        ]
        self.low = [
            None,
            (-52, up(self.rows[1] + 97, 112)),
            (-24, up(self.rows[2] + 45, 88)),
            (-11, up(self.rows[3] + 20, 8)),
            (-3, up(self.rows[4] + 6, 8)),
        ]
        self.span = [None, (-2, self.cells[1] // 2 + 2)]
        for level in (2, 3, 4):
            self.span.append((-3, self.cells[level] // 2 + 3))
        self.extended = max(
            LEAD + 2 * HALO + rows, 2 * (self.low[1][1] - 112) + 256
        )


STEP = 8


def levels_loop(geo, level, lo, hi, source_start, gain, target, bands, extra):
    left = first_half(STEP)
    first, pairs = geo.span[level]
    low_start, low_rows = geo.low[level]
    band_start, band_rows = geo.band[level]
    skip = (band_start - low_start) // STEP
    if extra:
        def lows(c, carry):
            row = pl.multiple_of(c * STEP, STEP)
            low, _ = analysis(columns(lo, row, STEP), source_start, left)
            for q in range(pairs):
                put(target, row, q, low(first + 2 * q))
            return carry

        lax.fori_loop(0, skip, lows, 0)
        lax.fori_loop(skip + band_rows // STEP, low_rows // STEP, lows, 0)

    def both(c, carry):
        row = pl.multiple_of(c * STEP, STEP)
        g = [jnp.broadcast_to(gain[b : b + 1, :], (STEP, LANES)) for b in range(3)]
        low, high = analysis(columns(lo, row + skip * STEP, STEP), source_start, left)
        for q in range(pairs):
            put(target, row + skip * STEP, q, low(first + 2 * q))
            put(bands, row, q, high(first + 2 * q) * g[0], (0,))
        low, high = analysis(columns(hi, row, STEP), source_start, left)
        for q in range(pairs):
            put(bands, row, q, low(first + 2 * q) * g[1], (1,))
            put(bands, row, q, high(first + 2 * q) * g[2], (2,))
        return carry

    lax.fori_loop(0, band_rows // STEP, both, 0)


def first_level_kernel(geo, lats, place, edge, tl, th, gain, x, g1, d1, send_e, send_o, ext, la, ha, sems):
    lat, parity = place[0], place[1]
    rows = geo.rows[0]
    low_start, low_rows = geo.low[1]
    band_start, band_rows = geo.band[1]
    width = x.shape[1]
    begin = LEAD + HALO
    cuts = [0] + [min(rows, 224 * b + 256 - begin) for b in range(low_rows // 112 - 1)] + [rows]
    copies = []
    for i in range(len(cuts) - 1):
        part = pl.ds(cuts[i], cuts[i + 1] - cuts[i])
        to = pl.ds(begin + cuts[i], cuts[i + 1] - cuts[i])
        copies.append(pltpu.make_async_copy(x.at[part, :], ext.at[to, :], sems.at[i]))
        copies[-1].start()
    top = slice(LEAD, begin)
    bottom = slice(begin + rows, begin + rows + HALO)
    ext[0:LEAD, :] = jnp.zeros((LEAD, width), BF16)
    tail = geo.extended - (LEAD + 2 * HALO + rows)
    if tail:
        ext[geo.extended - tail :, :] = jnp.zeros((tail, width), BF16)

    @pl.when(lat == 0)
    def _():
        ext[top, :] = jnp.zeros((HALO, width), BF16)
        ext[bottom, :] = edge[...]

    @pl.when(lat != 0)
    def _():
        ext[top, :] = edge[...]
        ext[bottom, :] = jnp.zeros((HALO, width), BF16)

    for b in range(low_rows // 112):
        copies[b].wait()
        mh, ml = two_terms(masked_rows(tl[...], low_start + 112 * b, geo.rows[1], lat, lats))
        data = ext[224 * b : 224 * b + 256, :]
        la[112 * b : 112 * b + 112, :] = mxu(mh, data) + mxu(ml, data)
    for b in range(band_rows // 120):
        mh, ml = two_terms(masked_rows(th[...], band_start + 120 * b, geo.rows[1], lat, lats))
        data = ext[96 + 240 * b : 352 + 240 * b, :]
        ha[120 * b : 120 * b + 120, :] = mxu(mh, data) + mxu(ml, data)

    levels_loop(geo, 1, la, ha, 0, gain, g1, d1, True)
    edge_lanes = 2 * LANES
    shift = (geo.cells[1] // 2) * LANES

    def fill(to_left, to_right):
        for b in range(3):
            at = slice(b * edge_lanes, (b + 1) * edge_lanes)
            to_left[:, at] = d1[b, :, 0:edge_lanes].astype(BF16)
            to_right[:, at] = d1[b, :, shift : shift + edge_lanes].astype(BF16)

    @pl.when(parity == 0)
    def _():
        fill(send_o, send_e)

    @pl.when(parity != 0)
    def _():
        fill(send_e, send_o)


def deep_blocks(geo):
    in_rows = geo.low[1][1]
    lows, highs = [], []
    for b in range(geo.low[2][1] // 88):
        lows.append((88 * b, 88, min(176 * b, in_rows - 192), 192))
    half = geo.band[2][1] // 2
    for b in range(2):
        first = 2 * (geo.band[2][0] + half * b) - 3 - geo.low[1][0]
        highs.append((half * b, half, first // 16 * 16, 2 * half + 16))
    return lows, highs


def deep_kernel(geo, lats, mat_count, place, gain, g1, *refs):
    lat, parity = place[0], place[1]
    mats, refs = list(refs[:mat_count]), refs[mat_count:]
    d = {2: refs[0], 3: refs[1], 4: refs[2]}
    ll4, send_e, send_o, p2, m2, p3, m3 = refs[3:10]
    g2, g3, lo2, hi2, lo3, hi3, lo4, hi4, gh, gl = refs[10:]
    lo, hi = {2: lo2, 3: lo3, 4: lo4}, {2: hi2, 3: hi3, 4: hi4}
    grids = {1: g1, 2: g2, 3: g3, 4: ll4}
    gh[...], gl[...] = two_terms(g1[...])
    for starts, blocks, out in zip((geo.low[2][0], geo.band[2][0]), deep_blocks(geo), (lo2, hi2)):
        for at, count, begin, size in blocks:
            matrix = masked_rows(mats.pop(0)[...], starts + at, geo.rows[2], lat, lats)
            window = slice(begin, begin + size)
            out[at : at + count, :] = dot3(matrix, gh[window, :], gl[window, :])
    for level in (2, 3, 4):
        if level > 2:
            vh, vl = two_terms(grids[level - 1][...])
            for starts, out in ((geo.low[level][0], lo[level]), (geo.band[level][0], hi[level])):
                matrix = masked_rows(mats.pop(0)[...], starts, geo.rows[level], lat, lats)
                out[...] = dot3(matrix, vh, vl)
        start = geo.span[level - 1][0]
        rows = gain[3 * (level - 2) : 3 * (level - 2) + 3, :]
        levels_loop(geo, level, lo[level], hi[level], start, rows, grids[level], d[level], level < 4)

    def fill(distance, to_left, to_right):
        for level, count, row in exchange_plan(geo)[distance]:
            n = geo.band[level][1]
            move = distance * geo.cells[level] // 2
            for b in range(3):
                lanes = slice(b * count * LANES, (b + 1) * count * LANES)
                to_left[row : row + n, lanes] = d[level][b, :, 0 : count * LANES].astype(BF16)
                to_right[row : row + n, lanes] = d[level][
                    b, :, move * LANES : (move + count) * LANES
                ].astype(BF16)

    @pl.when(parity == 0)
    def _():
        fill(1, send_o, send_e)

    @pl.when(parity != 0)
    def _():
        fill(1, send_e, send_o)

    fill(2, m2, p2)
    fill(3, m3, p3)


def exchange_plan(geo):
    plan = {}
    for distance in (1, 2, 3):
        entries, row = [], 0
        for level in (2, 3, 4):
            count = geo.span[level][1] - distance * geo.cells[level] // 2
            if count > 0:
                entries.append((level, count, row))
                row += -(-geo.band[level][1] // 16) * 16
        plan[distance] = entries
    return plan


def plan_shape(geo, distance):
    entries = exchange_plan(geo)[distance]
    rows = sum(-(-geo.band[level][1] // 16) * 16 for level, _, _ in entries)
    return (rows, max(count for _, count, _ in entries) * 3 * LANES)


def attention_kernel(geo, lats, blocks, place, keys, grid, we, wqkv, scale, wo, gain, wb, out):
    lat = place[0]
    rows, width = grid.shape
    cells = width // C
    field = grid[...]
    own = jnp.concatenate([field[:, C * c : C * (c + 1)] for c in range(cells)], 0)
    count = own.shape[0]
    embedded = mxu(own.astype(BF16), we[...])
    queries = mxu(embedded.astype(BF16), wqkv[:, 0:E]).astype(BF16)
    lane = lax.broadcasted_iota(jnp.int32, (1, E), 1)
    block = keys.shape[0] // blocks
    factor = [scale[h] * (1.0 / math.sqrt(HEAD_DIM)) for h in range(HEADS)]

    def keyvals(start):
        spread = mxu(keys[pl.ds(start, block), :], we[...]).astype(BF16)
        both = mxu(spread, wqkv[:, E : 3 * E]).astype(BF16)
        return both[:, 0:E], both[:, E : 2 * E]

    def scores_of(h, k):
        mine = (lane >= h * HEAD_DIM) & (lane < (h + 1) * HEAD_DIM)
        q = jnp.where(mine, queries, jnp.zeros_like(queries))
        s = lax.dot_general(q, k, (((1,), (1,)), ((), ())), preferred_element_type=F32)
        return s * factor[h]

    def masked(h, value):
        mine = (lane >= h * HEAD_DIM) & (lane < (h + 1) * HEAD_DIM)
        return jnp.where(mine, value, jnp.zeros_like(value))

    if blocks == 1:
        k, v = keyvals(0)
        attended = jnp.zeros((count, E), F32)
        for h in range(HEADS):
            s = scores_of(h, k)
            w = jnp.exp(s - jnp.max(s, -1, keepdims=True))
            total = jnp.sum(w, -1, keepdims=True)
            attended = attended + masked(h, mxu(w.astype(BF16), v) / total)
    else:

        def one_block(b, carry):
            peaks, totals, sums = carry
            k, v = keyvals(pl.multiple_of(b * block, 16))
            new_peaks, new_totals = [], []
            shrunk = jnp.zeros((count, E), F32)
            for h in range(HEADS):
                s = scores_of(h, k)
                peak = jnp.maximum(peaks[h], jnp.max(s, -1, keepdims=True))
                shrink = jnp.exp(peaks[h] - peak)
                w = jnp.exp(s - peak)
                new_peaks.append(peak)
                new_totals.append(totals[h] * shrink + jnp.sum(w, -1, keepdims=True))
                shrunk = shrunk + masked(h, sums * shrink + mxu(w.astype(BF16), v))
            return tuple(new_peaks), tuple(new_totals), shrunk

        start = (
            tuple(jnp.full((count, 1), -1e30, F32) for _ in range(HEADS)),
            tuple(jnp.zeros((count, 1), F32) for _ in range(HEADS)),
            jnp.zeros((count, E), F32),
        )
        _, totals, sums = lax.fori_loop(0, blocks, one_block, start)
        attended = jnp.zeros((count, E), F32)
        for h in range(HEADS):
            attended = attended + masked(h, sums / totals[h])
    hidden = embedded + mxu(attended.astype(BF16), wo[...])
    square = jnp.mean(hidden * hidden, -1, keepdims=True)
    normed = (hidden * lax.rsqrt(square + 1e-06) * gain[...]).astype(BF16)
    update = mxu(normed, wb[...])
    back = [
        jnp.concatenate(
            [update[rows * c : rows * (c + 1), :], update[rows * (c + 1) : rows * (c + 2), :]], 1
        )
        for c in range(0, cells, 2)
    ]
    start = geo.band[4][0]
    for q, value in enumerate(back):
        at = slice(q * LANES, (q + 1) * LANES)
        out[:, at] = masked_rows(field[:, at] + value, start, geo.rows[4], lat, lats)


def synthesis_kernel(geo, lats, place, coarse, d1, d2, d3, d4, *refs):
    lat, parity = place[0], place[1]
    e1, o1, e2, o2, from_m2, from_p2, from_m3, from_p3 = refs[:8]
    mats, refs = refs[8:13], refs[13:]
    out, up3, up2, up1, sides, xh, xl, ylow, yhigh, done, sems = refs
    bands = {2: d2, 3: d3, 4: d4}
    plan = exchange_plan(geo)

    def from_sides(level, b):
        n = geo.band[level][1]
        cols = [bands[level][b, :, LANES * p : LANES * (p + 1)] for p in range(geo.span[level][1])]
        for distance in (1, 2, 3):
            for which, count, row in plan[distance]:
                if which != level:
                    continue
                move = distance * geo.cells[level] // 2
                for p in range(count):
                    lanes = slice((b * count + p) * LANES, (b * count + p + 1) * LANES)
                    if distance == 1:
                        even = e2[row : row + n, lanes].astype(F32)
                        odd = o2[row : row + n, lanes].astype(F32)
                        low = jnp.where(parity == 0, odd, even)
                        high = jnp.where(parity == 0, even, odd)
                    else:
                        lows, highs = {2: (from_m2, from_p2), 3: (from_m3, from_p3)}[distance]
                        low = lows[row : row + n, lanes].astype(F32)
                        high = highs[row : row + n, lanes].astype(F32)
                    cols[p] = cols[p] + low
                    cols[p + move] = cols[p + move] + high
        return jnp.concatenate(cols, 1)

    uppers = {4: coarse, 3: up3, 2: up2, 1: up1}
    left = first_half(STEP)
    for level in (4, 3, 2):
        begin, pairs = geo.span[level]
        below = level - 1
        start, rows = geo.band[below]
        matrix = masked_rows(mats[4 - level][...], start, geo.rows[below], lat, lats)
        width = pairs * LANES
        for one, two, y in (
            (uppers[level][...], from_sides(level, 1), ylow),
            (from_sides(level, 0), from_sides(level, 2), yhigh),
        ):
            h, l = two_terms(jnp.concatenate([one, two], 0))
            y[0:rows, 0:width] = dot3(matrix, h, l)
        target = uppers[below]
        first, out_pairs = geo.span[below]

        def joined(c, carry):
            row = pl.multiple_of(c * STEP, STEP)
            pair = synthesis(
                columns(ylow, row, STEP, pairs), columns(yhigh, row, STEP, pairs), begin, left
            )
            for q in range(out_pairs):
                put(target, row, q, pair(first + 2 * q))
            return carry

        lax.fori_loop(0, rows // STEP, joined, 0)

    n = geo.band[1][1]
    edge = 2 * LANES
    shift = (geo.cells[1] // 2) * LANES
    for b in range(3):
        at = slice(b * edge, (b + 1) * edge)
        even, odd = e1[:, at].astype(F32), o1[:, at].astype(F32)
        sides[b, 0] = jnp.where(parity == 0, odd, even)
        sides[b, 1] = jnp.where(parity == 0, even, odd)
    half = geo.rows[0] // 2
    for block in range(2):
        w = 0 if block == 0 else n - LANES
        window = slice(w, w + LANES)
        sh, sl = two_terms(mats[3 + block][...])
        for pieces, y in (((None, 1), ylow), ((0, 2), yhigh)):
            for i, b in enumerate(pieces):
                place_rows = slice(i * LANES, (i + 1) * LANES)
                if b is None:
                    h, l = two_terms(up1[window, :])
                    xh[place_rows, :], xl[place_rows, :] = h, l
                else:
                    for lanes, extra in (
                        (slice(0, edge), sides[b, 0, window, :]),
                        (slice(edge, shift), None),
                        (slice(shift, shift + edge), sides[b, 1, window, :]),
                    ):
                        value = d1[b, window, lanes]
                        h, l = two_terms(value if extra is None else value + extra)
                        xh[place_rows, lanes], xl[place_rows, lanes] = h, l
            y[half * block : half * (block + 1), :] = (
                mxu(sh, xh[...]) + mxu(sh, xl[...]) + mxu(sl, xh[...])
            )
    rows16 = 16
    left16 = first_half(rows16)
    begin, pairs = geo.span[1]

    def last(c, carry):
        row = pl.multiple_of(c * rows16, rows16)
        pair = synthesis(columns(ylow, row, rows16), columns(yhigh, row, rows16), begin, left16)
        for q in range(geo.cells[0] // 2):
            put(done, row, q, pair(2 * q).astype(BF16))
        return carry

    chunks = geo.rows[0] // rows16
    cuts = [chunks * i // 4 for i in range(5)]
    copies = []
    for i in range(4):
        lax.fori_loop(cuts[i], cuts[i + 1], last, 0)
        part = pl.ds(cuts[i] * rows16, (cuts[i + 1] - cuts[i]) * rows16)
        copies.append(pltpu.make_async_copy(done.at[part, :], out.at[part, :], sems.at[i]))
        copies[-1].start()
    for copy in copies:
        copy.wait()


def call(kernel, out_shape, scratch, *args, cost=20_000_000, grant=24, raw=0, raw_out=False):
    vmem = pl.BlockSpec(memory_space=pltpu.VMEM)
    smem = pl.BlockSpec(memory_space=pltpu.SMEM)
    anywhere = pl.BlockSpec(memory_space=pl.ANY)
    specs = [smem if a.ndim == 1 and a.size < 16 else vmem for a in args]
    if raw:
        specs[-raw:] = [anywhere] * raw
    outs = jax.tree.map(lambda _: anywhere if raw_out else vmem, out_shape)
    return pl.pallas_call(
        kernel,
        out_shape=out_shape,
        in_specs=specs,
        out_specs=outs,
        scratch_shapes=scratch,
        compiler_params=pltpu.CompilerParams(vmem_limit_bytes=grant << 20),
        cost_estimate=pl.CostEstimate(flops=cost, bytes_accessed=1 << 20, transcendentals=0),
    )(*args)


def shape(dims, dtype=F32):
    return pltpu.VMEM(dims, dtype)


def constant(matrix):
    return jnp.asarray(matrix)


def per_device(mesh_shape, state_field, skip_gain, embed_weight, qkv_weight, head_scale, out_weight, norm_gain, back_weight):
    return program(
        mesh_shape, state_field, skip_gain, embed_weight, qkv_weight, head_scale, out_weight, norm_gain, back_weight
    )


def program(mesh_shape, state_field, skip_gain, embed_weight, qkv_weight, head_scale, out_weight, norm_gain, back_weight):
    lons, lats = mesh_shape["lon"], mesh_shape["lat"]
    rows, width = state_field.shape
    geo = Geometry(rows, width // C)
    lat, lon = lax.axis_index("lat"), lax.axis_index("lon")
    place = jnp.stack([lat, lon % 2]).astype(jnp.int32)
    gains = jnp.concatenate([skip_gain, skip_gain], 2).reshape(-1, LANES)

    even_pairs = [(i, i ^ 1) for i in range(lons)]
    odd_pairs = [(i, (i + 1 if i % 2 else i - 1) % lons) for i in range(lons)]
    swap = [(i, lats - 1 - i) for i in range(lats)]

    def shifted(value, by):
        return lax.ppermute(value, "lon", [(i, (i + by) % lons) for i in range(lons)])

    edge = jnp.where(lat == 0, state_field[rows - HALO :], state_field[:HALO])
    edge = lax.ppermute(edge, "lat", swap)

    low_rows, band_rows = geo.low[1][1], geo.band[1][1]
    tl = SCALE * analysis_matrix(LOW, geo.low[1][0], 112, 0 - LEAD - HALO, 256)
    th = SCALE * analysis_matrix(HIGH, geo.band[1][0], 120, 96 - LEAD - HALO, 256)
    w1 = geo.span[1][1] * LANES
    g1, d1, send_e, send_o = call(
        functools.partial(first_level_kernel, geo, lats),
        (
            shape((low_rows, w1)),
            shape((3, band_rows, w1)),
            shape((band_rows, 6 * LANES), BF16),
            shape((band_rows, 6 * LANES), BF16),
        ),
        [
            pltpu.VMEM((geo.extended, width), BF16),
            pltpu.VMEM((low_rows, width), F32),
            pltpu.VMEM((band_rows, width), F32),
            pltpu.SemaphoreType.DMA((low_rows // 112,)),
        ],
        place,
        edge,
        constant(tl),
        constant(th),
        gains[:3],
        state_field,
        raw=1,
    )
    e1 = lax.ppermute(send_e, "lon", even_pairs)
    o1 = lax.ppermute(send_o, "lon", odd_pairs)

    mats = []
    for taps, start, blocks in zip((LOW, HIGH), (geo.low[2][0], geo.band[2][0]), deep_blocks(geo)):
        for at, count, begin, size in blocks:
            mats.append(analysis_matrix(taps, start + at, count, geo.low[1][0] + begin, size))
    for level in (3, 4):
        in_start, in_rows = geo.low[level - 1]
        mats.append(analysis_matrix(LOW, *geo.low[level], in_start, in_rows))
        mats.append(analysis_matrix(HIGH, *geo.band[level], in_start, in_rows))
    scratch = [pltpu.VMEM((geo.low[level][1], geo.span[level][1] * LANES), F32) for level in (2, 3)]
    for level in (2, 3, 4):
        w = geo.span[level - 1][1] * LANES
        scratch += [pltpu.VMEM((geo.low[level][1], w), F32), pltpu.VMEM((geo.band[level][1], w), F32)]
    scratch += [pltpu.VMEM((low_rows, w1), BF16), pltpu.VMEM((low_rows, w1), BF16)]
    deep = call(
        functools.partial(deep_kernel, geo, lats, len(mats)),
        tuple(shape((3, geo.band[level][1], geo.span[level][1] * LANES)) for level in (2, 3, 4))
        + (shape((geo.low[4][1], geo.span[4][1] * LANES)),)
        + tuple(shape(plan_shape(geo, d), BF16) for d in (1, 1, 2, 2, 3, 3)),
        scratch,
        place,
        gains[3:],
        g1,
        *[constant(SCALE * m) for m in mats],
    )
    d2, d3, d4, ll4, deep_e, deep_o, p2, m2, p3, m3 = deep

    merged, size = ll4, 1
    while size < lons:
        other = lax.ppermute(merged, "lon", [(i, i ^ size) for i in range(lons)])
        lower_half = (lon // size) % 2 == 0
        lower = jnp.where(lower_half, merged, other)
        upper = jnp.where(lower_half, other, merged)
        wide = geo.cells[4] * C * size
        merged = jnp.pad(lower, ((0, 0), (0, wide))) + jnp.pad(upper, ((0, 0), (wide, 0)))
        size = 2 * size
    around = geo.cells[4] * lons * C
    w = 6 * C
    ring = jnp.concatenate([merged[:, :w] + merged[:, around:], merged[:, w:around]], 1)
    skip = -geo.low[4][0]
    tokens = ring[skip : skip + geo.rows[4]].astype(BF16)
    others = lax.ppermute(tokens, "lat", swap)
    keys = jnp.concatenate([tokens, others], 0).reshape(-1, C)

    e2 = lax.ppermute(deep_e, "lon", even_pairs)
    o2 = lax.ppermute(deep_o, "lon", odd_pairs)
    from_m2, from_p2 = shifted(p2, 2), shifted(m2, -2)
    from_m3, from_p3 = shifted(p3, 3), shifted(m3, -3)

    own = lax.dynamic_slice(
        jnp.concatenate([ring, ring[:, :w]], 1),
        (0, lon * geo.cells[4] * C),
        (geo.low[4][1], geo.span[4][1] * LANES),
    )
    blocks = max(1, keys.shape[0] // 928) if keys.shape[0] % 928 == 0 else 1
    coarse = call(
        functools.partial(attention_kernel, geo, lats, blocks),
        shape(own.shape),
        [],
        place,
        keys,
        own,
        embed_weight,
        qkv_weight,
        head_scale,
        out_weight,
        norm_gain[None],
        back_weight,
        cost=200_000_000,
    )

    synth = []
    for level in (4, 3, 2):
        synth.append(
            np.concatenate(
                [synthesis_matrix(t, *geo.band[level - 1], *geo.band[level]) for t in (LOW, HIGH)], 1
            )
        )
    half = rows // 2
    for block in range(2):
        begin = geo.band[1][0] + (0 if block == 0 else band_rows - LANES)
        synth.append(
            np.concatenate(
                [synthesis_matrix(t, half * block, half, begin, LANES) for t in (LOW, HIGH)], 1
            )
        )
    return call(
        functools.partial(synthesis_kernel, geo, lats),
        jax.ShapeDtypeStruct((rows, width), BF16),
        [pltpu.VMEM((geo.band[level][1], geo.span[level][1] * LANES), F32) for level in (3, 2, 1)]
        + [
            pltpu.VMEM((3, 2, band_rows, 2 * LANES), F32),
            pltpu.VMEM((2 * LANES, w1), BF16),
            pltpu.VMEM((2 * LANES, w1), BF16),
            pltpu.VMEM((rows, w1), F32),
            pltpu.VMEM((rows, w1), F32),
            pltpu.VMEM((rows, width), BF16),
            pltpu.SemaphoreType.DMA((4,)),
        ],
        place,
        coarse,
        d1,
        d2,
        d3,
        d4,
        e1,
        o1,
        e2,
        o2,
        from_m2,
        from_p2,
        from_m3,
        from_p3,
        *[constant(SCALE * m) for m in synth],
        raw_out=True,
    )


def solution(mesh):
    in_specs = (P("lat", ("member", "lon")), P(), P(), P(), P(), P(), P(), P())
    out_specs = P("lat", ("member", "lon"))
    return jax.shard_map(
        functools.partial(per_device, dict(mesh.shape)),
        mesh=mesh,
        in_specs=in_specs,
        out_specs=out_specs,
        check_vma=False,
    )
```

time: 117 us -> 140 us (1.20)
  local copies, waits for them, and re-layouts: 7.02 us -> 21.6 us
  Pallas kernels: 54.3 us -> 66.1 us
  waiting for transfers between devices: 32.4 us -> 25.8 us
  other arithmetic: 2.92 us -> 5.33 us
    unnamed x26 -> x70, local copies, waits for them, and re-layouts: 2.68 us -> 20.4 us
    pallas_call x4, Pallas kernels: 54.3 us -> 66.1 us  [call(): pl.pallas_call(kernel, out_shape=out_shape, in_specs=specs, out_specs=out...]
    ppermute x4, waiting for transfers between devices: 8.56 us -> 5.12 us  [shifted(): lax.ppermute(value, 'lon', [(i, (i + by) % lons) for i in range(lons)])]
    ppermute x9, waiting for transfers between devices: 23.8 us -> 20.6 us  [the longest x1 11.4 us: program(): e1 = lax.ppermute(send_e, 'lon', even_pairs)]
    concatenate x3 -> x4, other arithmetic: 0.05 us -> 1.62 us  [the longest x1 0.85 us: program(): jnp.concatenate([ring, ring[:, :w]], 1)]
  transfers between devices with their start and end apart: 13 -> 13, of which waited for: 6 -> 7; matrix products, arithmetic and copies ran while one was open for 5% -> 5% of each run, Pallas kernels for 6% -> 4%
where the time goes in v1:
time: 140 us; the launch traced here: 139 us
  Pallas kernels  66.1 us (47%)
  waiting for transfers between devices  25.8 us (18%)
  local copies, waits for them, and re-layouts  21.6 us (15%)
  starting transfers between devices  19.8 us (14%)
  other arithmetic  5.33 us (4%)
    pallas_call x4, Pallas kernels, call(): pl.pallas_call(kernel, out_shape=out_shape, in_specs=specs, out_specs=out...  66.1 us
    unnamed x70, local copies, waits for them, and re-layouts  20.4 us
    ppermute x1, waiting for transfers between devices, program(): e1 = lax.ppermute(send_e, 'lon', even_pairs)  11.4 us
    ppermute x3, waiting for transfers between devices, program(): other = lax.ppermute(merged, 'lon', [(i, i ^ size) for i in range(lons)])  8.45 us
    ppermute x3, starting transfers between devices, program(): other = lax.ppermute(merged, 'lon', [(i, i ^ size) for i in range(lons)])  7.67 us
    ppermute x4, starting transfers between devices, shifted(): lax.ppermute(value, 'lon', [(i, (i + by) % lons) for i in range(lons)])  5.89 us
    ppermute x4, waiting for transfers between devices, shifted(): lax.ppermute(value, 'lon', [(i, (i + by) % lons) for i in range(lons)])  5.12 us
    ppermute x1, starting transfers between devices, program(): o2 = lax.ppermute(deep_o, 'lon', odd_pairs)  3.07 us
  transfers between devices with their start and end apart: 13, of which 7 were waited for; matrix products, arithmetic and copies ran while one was open for 5% of the time, Pallas kernels for 4%

profile of v1, /device:TPU:0, one launch (start us, length us, event | category | flops | bytes accessed | tf_op | source)
XLA Modules:
  0.0 139.0 jit_solution(8553423279416653717)
XLA Ops:
  0.0 1.2 slice_select_fusion
  1.3 0.6 collective-permute-start
  1.9 0.7 copy.27
  3.2 1.5 %copy-done = bf16[464,2048]{1,0:T(8,128)(2,1)S(1)} copy-done((bf16[464,2048]{1,0:T(8,128)(2,1)S(1)}, bf16[464,2048]{1,0:T(8,128)(2,1)}, u32[]{:S(2)}) %copy-start) | copy-done | bytes 1900568
  4.7 0.9 copy-done.11
  5.6 0.9 copy-done.12
  6.5 15.9 %shard_map.217 = (f32[336,1280]{1,0:T(8,128)S(1)}, f32[3,240,1280]{2,1,0:T(8,128)S(1)}, bf16[240,768]{1,0:T(8,128)(2,1)S(1)}, bf16[240,768]{1,0:T(8,128)(2,1)S(1)}) custom-call(s32[2]{0:T(128)S(1)} %pad_add_fusion.3.place, bf16[96,2048]{1,0:T(8,128)(2,1)S(1)} %collective-permute-done.edge, f32[112,256]{1,0:T(8,128)S(1)} %copy-done.12, ...), custom_call_target="tpu_custom_call" | custom-call | flops 20000000 | bytes 1048576 | tf_op jit(solution)/shard_map/pallas_call | solution.py:603
  22.4 1.8 %copy-done.1 = f32[3,240,1280]{2,1,0:T(8,128)} copy-done((f32[3,240,1280]{2,1,0:T(8,128)}, f32[3,240,1280]{2,1,0:T(8,128)S(1)}, u32[]{:S(2)}) %copy-start.1) | copy-done | bytes 3686424
  24.3 13.9 %shard_map.218 = (f32[3,128,896]{2,1,0:T(8,128)S(1)}, f32[3,64,640]{2,1,0:T(8,128)S(1)}, f32[3,40,512]{2,1,0:T(8,128)S(1)}, f32[40,512]{1,0:T(8,128)S(1)}, bf16[...) custom-call(s32[2]{0:T(128)S(1)} %pad_add_fusion.3.place, ...), custom_call_target="tpu_custom_call" | custom-call | flops 20000000 | bytes 1048576 | tf_op jit(solution)/shard_map/pallas_call | solution.py:603
  38.2 0.8 copy-done.28
  39.0 0.7 copy-done.31
  39.7 2.8 %collective-permute-start.1 = (f32[40,512]{1,0:T(8,128)S(1)}, f32[40,512]{1,0:T(8,128)S(1)}, u32[]{:S(2)}, u32[]{:S(2)}) collective-permute-start(f32[40,512]{1,0:T(8,128)S(1)} %get-tuple-element.20), channel_id=1, source_target_pairs={{0,2},{2,0},{4,6},{6,4},{8,10},{10,8},{12,14},{14,12},{1,3},{3,1},... | collective-permute-start | bytes 245768 | tf_op jit(solution)/shard_map/ppermute | solution.py:703
  42.5 2.7 %collective-permute-done.1 = f32[40,512]{1,0:T(8,128)S(1)} collective-permute-done((f32[40,512]{1,0:T(8,128)S(1)}, f32[40,512]{1,0:T(8,128)S(1)}, u32[]{:S(2)}, u32[]{:S(2)}) %collective-permute-start.1) | collective-permute-done | bytes 81952 | tf_op jit(solution)/shard_map/ppermute | solution.py:703
  45.3 1.9 %collective-permute-start.2 = (f32[40,640]{1,0:T(8,128)S(1)}, f32[40,640]{1,0:T(8,128)S(1)}, u32[]{:S(2)}, u32[]{:S(2)}) collective-permute-start(f32[40,640]{1,0:T(8,128)S(1)} %pad_add_fusion.2), channel_id=1, source_target_pairs={{0,4},{2,6},{4,0},{6,2},{8,12},{10,14},{12,8},{14,10},{1,5},{3,7},... | collective-permute-start | bytes 307208 | tf_op jit(solution)/shard_map/ppermute | solution.py:703
  47.2 2.8 %collective-permute-done.2 = f32[40,640]{1,0:T(8,128)S(1)} collective-permute-done((f32[40,640]{1,0:T(8,128)S(1)}, f32[40,640]{1,0:T(8,128)S(1)}, u32[]{:S(2)}, u32[]{:S(2)}) %collective-permute-start.2) | collective-permute-done | bytes 102432 | tf_op jit(solution)/shard_map/ppermute | solution.py:703
  50.1 2.9 %collective-permute-start.3 = (f32[40,896]{1,0:T(8,128)S(1)}, f32[40,896]{1,0:T(8,128)S(1)}, u32[]{:S(2)}, u32[]{:S(2)}) collective-permute-start(f32[40,896]{1,0:T(8,128)S(1)} %pad_add_fusion), channel_id=1, source_target_pairs={{0,8},{2,10},{4,12},{6,14},{8,0},{10,2},{12,4},{14,6},{1,9},{3,11}... | collective-permute-start | bytes 430088 | tf_op jit(solution)/shard_map/ppermute | solution.py:703
  53.0 2.5 %collective-permute-start.11 = (bf16[48,384]{1,0:T(8,128)(2,1)S(1)}, bf16[48,384]{1,0:T(8,128)(2,1)S(1)}, u32[]{:S(2)}, u32[]{:S(2)}) collective-permute-start(bf16[48,384]{1,0:T(8,128)(2,1)S(1)} %get-tuple-element.31), channel_id=1, source_target_pairs={{0,6},{2,8},{4,10},{6,12},{8,14},{10,0},{12,2},{14,4},{1,7},{3,9},... | collective-permute-start | bytes 110600 | tf_op jit(solution)/shard_map/ppermute | solution.py:641
  55.5 1.3 collective-permute-start.12
  56.8 1.6 %collective-permute-start.9 = (bf16[112,768]{1,0:T(8,128)(2,1)}, bf16[112,768]{1,0:T(8,128)(2,1)S(1)}, u32[]{:S(2)}, u32[]{:S(2)}) collective-permute-start(bf16[112,768]{1,0:T(8,128)(2,1)} %get-tuple-element.29), channel_id=1, source_target_pairs={{0,4},{2,6},{4,8},{6,10},{8,12},{10,14},{12,0},{14,2},{1,5},{3,7},... | collective-permute-start | bytes 516104 | tf_op jit(solution)/shard_map/ppermute | solution.py:641
  58.4 0.8 collective-permute-start.7
  59.2 2.9 %collective-permute-done.3 = f32[40,896]{1,0:T(8,128)S(1)} collective-permute-done((f32[40,896]{1,0:T(8,128)S(1)}, f32[40,896]{1,0:T(8,128)S(1)}, u32[]{:S(2)}, u32[]{:S(2)}) %collective-permute-start.3) | collective-permute-done | bytes 143392 | tf_op jit(solution)/shard_map/ppermute | solution.py:703
  62.1 0.7 copy-done.33
  62.8 3.1 %collective-permute-start.8 = (bf16[240,1152]{1,0:T(8,128)(2,1)}, bf16[240,1152]{1,0:T(8,128)(2,1)S(1)}, u32[]{:S(2)}, u32[]{:S(2)}) collective-permute-start(bf16[240,1152]{1,0:T(8,128)(2,1)} %copy-done.28), channel_id=1, source_target_pairs={{0,14},{2,4},{4,2},{6,8},{8,6},{10,12},{12,10},{14,0},{1,15},{3,5}... | collective-permute-start | bytes 1658888 | tf_op jit(solution)/shard_map/ppermute | solution.py:719
  65.9 1.0 broadcast_select_fusion.1
  66.9 0.6 fusion.5
  67.5 0.6 fusion.4
  68.2 1.7 %collective-permute-start.6 = (bf16[240,768]{1,0:T(8,128)(2,1)}, bf16[240,768]{1,0:T(8,128)(2,1)}, u32[]{:S(2)}, u32[]{:S(2)}) collective-permute-start(bf16[240,768]{1,0:T(8,128)(2,1)} %copy-done.29), channel_id=1, source_target_pairs={{0,14},{2,4},{4,2},{6,8},{8,6},{10,12},{12,10},{14,0},{1,15},{3,5}... | collective-permute-start | bytes 1105928 | tf_op jit(solution)/shard_map/ppermute | solution.py:673
  70.0 0.9 copy.29.wb
  71.3 0.5 collective-permute-start.10
  71.7 0.8 fusion.1.grid
  72.6 0.7 pad_maximum_fusion
  73.3 1.1 reshape.6.keys
  74.4 1.0 copy-done.3
  75.4 0.9 copy-done.10
  76.3 0.8 copy-done.23
  77.1 5.2 %shard_map.219.coarse = f32[40,512]{1,0:T(8,128)S(1)} custom-call(s32[2]{0:T(128)S(1)} %pad_add_fusion.3.place, bf16[928,64]{1,0:T(8,128)(2,1)S(1)} %reshape.6.keys, f32[40,512]{1,0:T(8,128)S(1)} %fusion.1.grid, bf16[64,256]{1,0:T(8,128)(2,1)S(1)} %copy-done.23, bf16[256,768]{1,0:T(8,128)(2,1)S(1)} %copy-done.3, f32[8]{0:T(128)S(1)} %copy-done.27, ...), custom_call_target="tpu_custom_call" | custom-call | flops 200000000 | bytes 1048576 | tf_op jit(solution)/shard_map/pallas_call | solution.py:603
  82.3 5.1 %collective-permute-done.10.refs_5_ = bf16[112,768]{1,0:T(8,128)(2,1)} collective-permute-done((bf16[112,768]{1,0:T(8,128)(2,1)}, bf16[112,768]{1,0:T(8,128)(2,1)}, u32[]{:S(2)}, u32[]{:S(2)}) %collective-permute-start.10) | collective-permute-done | bytes 172064 | tf_op jit(solution)/shard_map/ppermute | solution.py:641
  87.4 11.4 %collective-permute-done.5.refs_0_ = bf16[240,768]{1,0:T(8,128)(2,1)} collective-permute-done((bf16[240,768]{1,0:T(8,128)(2,1)}, bf16[240,768]{1,0:T(8,128)(2,1)}, u32[]{:S(2)}, u32[]{:S(2)}) %collective-permute-start.5) | collective-permute-done | bytes 368672 | tf_op jit(solution)/shard_map/ppermute | solution.py:672
  98.8 2.0 %copy-done.2 = f32[3,240,1280]{2,1,0:T(8,128)S(1)} copy-done((f32[3,240,1280]{2,1,0:T(8,128)S(1)}, f32[3,240,1280]{2,1,0:T(8,128)}, u32[]{:S(2)}) %copy-start.2) | copy-done | bytes 3686424
  100.9 0.9 copy-done.5
  101.8 0.9 copy-done.7
  102.8 0.9 copy-done.8
  103.7 0.9 copy-done.9
  104.7 0.8 copy-done.16
  105.5 0.8 copy-done.19
  106.3 0.8 copy-done.21
  107.0 0.8 copy-done.22
  107.8 31.1 %shard_map.220 = bf16[464,2048]{1,0:T(8,128)(2,1)} custom-call(s32[2]{0:T(128)S(1)} %pad_add_fusion.3.place, f32[40,512]{1,0:T(8,128)S(1)} %shard_map.219.coarse, f32[3,240,1280]{2,1,0:T(8,128)S(1)} %copy-done.2, f32[3,128,896]{2,1,0:T(8,128)S(1)} %get-tuple-element.22.d2, f32[3,64,640]{2,1,0:T(8,128)S(1)} %get-tuple-element.23.d3, ...), custom_call_target="tpu_custom_call" | custom-call | flops 20000000 | bytes 1048576 | tf_op jit(solution)/shard_map/pallas_call | solution.py:603
  (68 shorter events, 1.3 us)
Async XLA Ops:
  0.0 24.2 %copy-start.4 = (f32[64,144]{1,0:T(8,128)S(1)}, f32[64,144]{1,0:T(8,128)}, u32[]{:S(2)}) copy-start(f32[64,144]{1,0:T(8,128)} %constant.103.clone.refs_2_.refs_3_) | copy-start | bytes 110596
  0.0 24.2 %copy-start.13 = (f32[88,192]{1,0:T(8,128)S(1)}, f32[88,192]{1,0:T(8,128)}, u32[]{:S(2)}) copy-start(f32[88,192]{1,0:T(8,128)} %constant.102.clone.refs_1_) | copy-start | bytes 202756
  0.0 24.2 %copy-start.14 = (f32[88,192]{1,0:T(8,128)S(1)}, f32[88,192]{1,0:T(8,128)}, u32[]{:S(2)}) copy-start(f32[88,192]{1,0:T(8,128)} %constant.101.clone.refs_0_) | copy-start | bytes 202756
  0.0 24.2 %copy-start.15 = (f32[80,176]{1,0:T(8,128)S(1)}, f32[80,176]{1,0:T(8,128)}, u32[]{:S(2)}) copy-start(f32[80,176]{1,0:T(8,128)} %constant.104.clone.refs_4_) | copy-start | bytes 168964
  0.0 24.2 %copy-start.17 = (f32[64,176]{1,0:T(8,128)S(1)}, f32[64,176]{1,0:T(8,128)}, u32[]{:S(2)}) copy-start(f32[64,176]{1,0:T(8,128)} %constant.105.clone.refs_5_) | copy-start | bytes 135172
  0.0 24.2 %copy-start.24 = (f32[40,80]{1,0:T(8,128)S(1)}, f32[40,80]{1,0:T(8,128)}, u32[]{:S(2)}) copy-start(f32[40,80]{1,0:T(8,128)} %constant.107.clone.refs_7_) | copy-start | bytes 38404
  0.0 24.2 %copy-start.25 = (f32[40,80]{1,0:T(8,128)S(1)}, f32[40,80]{1,0:T(8,128)}, u32[]{:S(2)}) copy-start(f32[40,80]{1,0:T(8,128)} %constant.106.clone.refs_6_) | copy-start | bytes 38404
  1.3 1.9 %collective-permute-start = (bf16[96,2048]{1,0:T(8,128)(2,1)S(1)}, bf16[96,2048]{1,0:T(8,128)(2,1)S(1)}, u32[]{:S(2)}, u32[]{:S(2)}) collective-permute-start(bf16[96,2048]{1,0:T(8,128)(2,1)S(1)} %slice_select_fusion), channel_id=1, source_target_pairs={{0,1},{1,0},{2,3},{3,2},{4,5},{5,4},{6,7},{7,6},{8,9},{9,8},{10,11... | collective-permute-start | bytes 1179656 | tf_op jit(solution)/shard_map/ppermute | solution.py:644
  3.2 1.5 %copy-start = (bf16[464,2048]{1,0:T(8,128)(2,1)S(1)}, bf16[464,2048]{1,0:T(8,128)(2,1)}, u32[]{:S(2)}) copy-start(bf16[464,2048]{1,0:T(8,128)(2,1)} %x.13) | copy-start | bytes 5701636
  4.7 0.9 copy-start.11
  5.6 0.9 copy-start.12
  22.4 1.8 %copy-start.1 = (f32[3,240,1280]{2,1,0:T(8,128)}, f32[3,240,1280]{2,1,0:T(8,128)S(1)}, u32[]{:S(2)}) copy-start(f32[3,240,1280]{2,1,0:T(8,128)S(1)} %get-tuple-element.21.d1) | copy-start | bytes 11059204
  24.2 14.8 %copy-start.29 = (bf16[240,768]{1,0:T(8,128)(2,1)}, bf16[240,768]{1,0:T(8,128)(2,1)S(1)}, u32[]{:S(2)}) copy-start(bf16[240,768]{1,0:T(8,128)(2,1)S(1)} %get-tuple-element.26) | copy-start | bytes 1105924
  24.2 14.8 %copy-start.30 = (bf16[240,768]{1,0:T(8,128)(2,1)}, bf16[240,768]{1,0:T(8,128)(2,1)S(1)}, u32[]{:S(2)}) copy-start(bf16[240,768]{1,0:T(8,128)(2,1)S(1)} %get-tuple-element.25) | copy-start | bytes 1105924
  38.2 0.8 copy-start.28
  39.0 0.7 copy-start.31
  39.0 19.4 %copy-start.6 = (f32[3,40,512]{2,1,0:T(8,128)}, f32[3,40,512]{2,1,0:T(8,128)S(1)}, u32[]{:S(2)}) copy-start(f32[3,40,512]{2,1,0:T(8,128)S(1)} %get-tuple-element.24.d4) | copy-start | bytes 737284
  39.7 5.6 %collective-permute-start.1 = (f32[40,512]{1,0:T(8,128)S(1)}, f32[40,512]{1,0:T(8,128)S(1)}, u32[]{:S(2)}, u32[]{:S(2)}) collective-permute-start(f32[40,512]{1,0:T(8,128)S(1)} %get-tuple-element.20), channel_id=1, source_target_pairs={{0,2},{2,0},{4,6},{6,4},{8,10},{10,8},{12,14},{14,12},{1,3},{3,1},... | collective-permute-start | bytes 245768 | tf_op jit(solution)/shard_map/ppermute | solution.py:703
  45.3 29.1 %copy-start.26 = (f32[256]{0:T(256)S(1)}, f32[256]{0:T(256)}, u32[]{:S(2)}) copy-start(f32[256]{0:T(256)} %param.29) | copy-start | bytes 3076
  45.3 29.1 %copy-start.27 = (f32[8]{0:T(128)S(1)}, f32[8]{0:T(128)}, u32[]{:S(2)}) copy-start(f32[8]{0:T(128)} %scale.1) | copy-start | bytes 100
  45.3 4.7 %collective-permute-start.2 = (f32[40,640]{1,0:T(8,128)S(1)}, f32[40,640]{1,0:T(8,128)S(1)}, u32[]{:S(2)}, u32[]{:S(2)}) collective-permute-start(f32[40,640]{1,0:T(8,128)S(1)} %pad_add_fusion.2), channel_id=1, source_target_pairs={{0,4},{2,6},{4,0},{6,2},{8,12},{10,14},{12,8},{14,10},{1,5},{3,7},... | collective-permute-start | bytes 307208 | tf_op jit(solution)/shard_map/ppermute | solution.py:703
  50.1 12.0 %copy-start.32 = (f32[40,896]{1,0:T(8,128)}, f32[40,896]{1,0:T(8,128)S(1)}, u32[]{:S(2)}) copy-start(f32[40,896]{1,0:T(8,128)S(1)} %pad_add_fusion) | copy-start | bytes 430084
  50.1 12.0 %collective-permute-start.3 = (f32[40,896]{1,0:T(8,128)S(1)}, f32[40,896]{1,0:T(8,128)S(1)}, u32[]{:S(2)}, u32[]{:S(2)}) collective-permute-start(f32[40,896]{1,0:T(8,128)S(1)} %pad_add_fusion), channel_id=1, source_target_pairs={{0,8},{2,10},{4,12},{6,14},{8,0},{10,2},{12,4},{14,6},{1,9},{3,11}... | collective-permute-start | bytes 430088 | tf_op jit(solution)/shard_map/ppermute | solution.py:703
  53.0 15.1 %collective-permute-start.11 = (bf16[48,384]{1,0:T(8,128)(2,1)S(1)}, bf16[48,384]{1,0:T(8,128)(2,1)S(1)}, u32[]{:S(2)}, u32[]{:S(2)}) collective-permute-start(bf16[48,384]{1,0:T(8,128)(2,1)S(1)} %get-tuple-element.31), channel_id=1, source_target_pairs={{0,6},{2,8},{4,10},{6,12},{8,14},{10,0},{12,2},{14,4},{1,7},{3,9},... | collective-permute-start | bytes 110600 | tf_op jit(solution)/shard_map/ppermute | solution.py:641
  55.5 12.6 %collective-permute-start.12 = (bf16[48,384]{1,0:T(8,128)(2,1)S(1)}, bf16[48,384]{1,0:T(8,128)(2,1)S(1)}, u32[]{:S(2)}, u32[]{:S(2)}) collective-permute-start(bf16[48,384]{1,0:T(8,128)(2,1)S(1)} %get-tuple-element.32), channel_id=1, source_target_pairs={{0,10},{2,12},{4,14},{6,0},{8,2},{10,4},{12,6},{14,8},{1,11},{3,13... | collective-permute-start | bytes 110600 | tf_op jit(solution)/shard_map/ppermute | solution.py:641
  56.8 13.1 %collective-permute-start.9 = (bf16[112,768]{1,0:T(8,128)(2,1)}, bf16[112,768]{1,0:T(8,128)(2,1)S(1)}, u32[]{:S(2)}, u32[]{:S(2)}) collective-permute-start(bf16[112,768]{1,0:T(8,128)(2,1)} %get-tuple-element.29), channel_id=1, source_target_pairs={{0,4},{2,6},{4,8},{6,10},{8,12},{10,14},{12,0},{14,2},{1,5},{3,7},... | collective-permute-start | bytes 516104 | tf_op jit(solution)/shard_map/ppermute | solution.py:641
  58.4 40.4 %collective-permute-start.7 = (bf16[240,1152]{1,0:T(8,128)(2,1)}, bf16[240,1152]{1,0:T(8,128)(2,1)S(1)}, u32[]{:S(2)}, u32[]{:S(2)}) collective-permute-start(bf16[240,1152]{1,0:T(8,128)(2,1)} %get-tuple-element.27), channel_id=1, source_target_pairs={{0,2},{2,0},{4,6},{6,4},{8,10},{10,8},{12,14},{14,12},{1,3},{3,1},... | collective-permute-start | bytes 1658888 | tf_op jit(solution)/shard_map/ppermute | solution.py:718
  62.1 0.7 copy-start.33
  62.8 36.0 %collective-permute-start.8 = (bf16[240,1152]{1,0:T(8,128)(2,1)}, bf16[240,1152]{1,0:T(8,128)(2,1)S(1)}, u32[]{:S(2)}, u32[]{:S(2)}) collective-permute-start(bf16[240,1152]{1,0:T(8,128)(2,1)} %copy-done.28), channel_id=1, source_target_pairs={{0,14},{2,4},{4,2},{6,8},{8,6},{10,12},{12,10},{14,0},{1,15},{3,5}... | collective-permute-start | bytes 1658888 | tf_op jit(solution)/shard_map/ppermute | solution.py:719
  68.1 4.4 %copy-start.18 = (bf16[48,384]{1,0:T(8,128)(2,1)}, bf16[48,384]{1,0:T(8,128)(2,1)S(1)}, u32[]{:S(2)}) copy-start(bf16[48,384]{1,0:T(8,128)(2,1)S(1)} %collective-permute-done.11.refs_6_) | copy-start | bytes 110596
  68.2 30.7 %collective-permute-start.5 = (bf16[240,768]{1,0:T(8,128)(2,1)}, bf16[240,768]{1,0:T(8,128)(2,1)}, u32[]{:S(2)}, u32[]{:S(2)}) collective-permute-start(bf16[240,768]{1,0:T(8,128)(2,1)} %copy-done.30), channel_id=1, source_target_pairs={{0,2},{2,0},{4,6},{6,4},{8,10},{10,8},{12,14},{14,12},{1,3},{3,1},... | collective-permute-start | bytes 1105928 | tf_op jit(solution)/shard_map/ppermute | solution.py:672
  68.2 3.6 %copy-start.20 = (bf16[48,384]{1,0:T(8,128)(2,1)}, bf16[48,384]{1,0:T(8,128)(2,1)S(1)}, u32[]{:S(2)}) copy-start(bf16[48,384]{1,0:T(8,128)(2,1)S(1)} %collective-permute-done.12.refs_7_) | copy-start | bytes 110596
  68.2 30.7 %collective-permute-start.6 = (bf16[240,768]{1,0:T(8,128)(2,1)}, bf16[240,768]{1,0:T(8,128)(2,1)}, u32[]{:S(2)}, u32[]{:S(2)}) collective-permute-start(bf16[240,768]{1,0:T(8,128)(2,1)} %copy-done.29), channel_id=1, source_target_pairs={{0,14},{2,4},{4,2},{6,8},{8,6},{10,12},{12,10},{14,0},{1,15},{3,5}... | collective-permute-start | bytes 1105928 | tf_op jit(solution)/shard_map/ppermute | solution.py:673
  69.9 1.3 collective-permute-start.4
  71.3 16.2 %collective-permute-start.10 = (bf16[112,768]{1,0:T(8,128)(2,1)}, bf16[112,768]{1,0:T(8,128)(2,1)}, u32[]{:S(2)}, u32[]{:S(2)}) collective-permute-start(bf16[112,768]{1,0:T(8,128)(2,1)} %copy-done.31), channel_id=1, source_target_pairs={{0,12},{2,14},{4,0},{6,2},{8,4},{10,6},{12,8},{14,10},{1,13},{3,15... | collective-permute-start | bytes 516104 | tf_op jit(solution)/shard_map/ppermute | solution.py:641
  74.4 1.0 copy-start.3
  75.4 0.9 copy-start.10
  76.3 0.8 copy-start.23
  98.8 2.0 %copy-start.2 = (f32[3,240,1280]{2,1,0:T(8,128)S(1)}, f32[3,240,1280]{2,1,0:T(8,128)}, u32[]{:S(2)}) copy-start(f32[3,240,1280]{2,1,0:T(8,128)} %copy-done.1) | copy-start | bytes 11059204
  100.9 0.9 copy-start.5
  101.8 0.9 copy-start.7
  102.8 0.9 copy-start.8
  103.7 0.9 copy-start.9
  104.7 0.8 copy-start.16
  105.5 0.8 copy-start.19
  106.3 0.8 copy-start.21
  107.0 0.8 copy-start.22

commit v2 on v1

--- a/solution.py
+++ b/solution.py
@@ -51,26 +51,6 @@
 BF16 = jnp.bfloat16
 
 
-def analysis_matrix(taps, out_start, out_rows, in_start, in_rows):
-    m = np.zeros((out_rows, in_rows), np.float32)
-    for j in range(out_rows):
-        for t in range(8):
-            r = 2 * (out_start + j) - 3 + t - in_start
-            if 0 <= r < in_rows:
-                m[j, r] = taps[t]
-    return m
-
-
-def synthesis_matrix(taps, out_start, out_rows, in_start, in_rows):
-    m = np.zeros((out_rows, in_rows), np.float32)
-    for j in range(out_rows):
-        for r in range(in_rows):
-            t = out_start + j - 2 * (in_start + r) + 3
-            if 0 <= t < 8:
-                m[j, r] = taps[t]
-    return m
-
-
 def two_terms(value):
     top = value.astype(BF16)
     return top, (value - top.astype(F32)).astype(BF16)
@@ -79,6 +59,29 @@
 def masked_rows(matrix, start, count, lat, lats):
     row = lax.broadcasted_iota(jnp.int32, matrix.shape, 0) + (start + lat * count)
     return jnp.where((row >= 0) & (row < count * lats), matrix, 0.0)
+
+
+def banded(shape, low, high, row_factor, column_factor, offset):
+    row = lax.broadcasted_iota(jnp.int32, shape, 0)
+    column = lax.broadcasted_iota(jnp.int32, shape, 1)
+    tap = row_factor * row + column_factor * column + offset
+    if high is not None:
+        second = column >= shape[1] // 2
+        tap = jnp.where(second, tap - column_factor * (shape[1] // 2), tap)
+    matrix = jnp.zeros(shape, F32)
+    for t in range(8):
+        value = F32(low[t]) if high is None else jnp.where(second, F32(high[t]), F32(low[t]))
+        matrix = jnp.where(tap == t, value, matrix)
+    return matrix
+
+
+def analysis_matrix(taps, out_start, out_rows, in_start, in_rows):
+    return banded((out_rows, in_rows), taps, None, -2, 1, in_start + 3 - 2 * out_start)
+
+
+def synthesis_matrix(out_start, out_rows, in_start, in_rows):
+    shape = (out_rows, 2 * in_rows)
+    return banded(shape, SCALE * LOW, SCALE * HIGH, 1, -2, out_start - 2 * in_start + 3)
 
 
 def mxu(a, b):
@@ -133,24 +136,18 @@
         at = lambda n: n - (start + 3) // 2
         u = Memo(lambda n: pick(left, plain(at(n)), turned(at(n) + 1)))
         w = Memo(lambda n: pick(left, turned(at(n)), plain(at(n) + 1)))
-    a = Memo(lambda n: plus(u(n), w(n), TURN[0]))
-    if SIGN < 0:
-        minus = lambda v: None if v is None else -v
-        b = Memo(lambda n: plus(minus(w(n)), u(n), TURN[0]))
-    else:
-        b = Memo(lambda n: plus(w(n), u(n), -TURN[0]))
-
-    def stage(a, b, factor):
-        rolled = Memo(lambda n: half_turn(b(n)))
-        late = Memo(lambda n: pick(left, rolled(n - 2), rolled(n)))
-        return (
-            Memo(lambda n: plus(a(n), late(n), factor)),
-            Memo(lambda n: plus(late(n), a(n), -factor)),
-        )
-
-    for s in (1, 2, 3):
-        a, b = stage(a, b, TURN[s])
-    return (lambda k: a(k + 3)), (lambda k: b(k + 3))
+
+    def band(taps):
+        def make(k):
+            total = None
+            for step in range(4):
+                total = plus(total, u(k + step), float(taps[2 * step]))
+                total = plus(total, w(k + step), float(taps[2 * step + 1]))
+            return total
+
+        return make
+
+    return band(LOW), band(HIGH)
 
 
 def synthesis(lows, highs, start, left):
@@ -227,52 +224,66 @@
         )
 
 
-STEP = 8
-
-
-def levels_loop(geo, level, lo, hi, source_start, gain, target, bands, extra):
-    left = first_half(STEP)
+STEP = 240
+SIDE = 8
+NEAR = 16
+
+
+def best_step(rows, most=None):
+    return max(s for s in range(8, (most or STEP) + 1, 8) if rows % s == 0)
+
+
+def low_rows(geo, level, source, source_start, target):
     first, pairs = geo.span[level]
-    low_start, low_rows = geo.low[level]
-    band_start, band_rows = geo.band[level]
-    skip = (band_start - low_start) // STEP
-    if extra:
-        def lows(c, carry):
-            row = pl.multiple_of(c * STEP, STEP)
-            low, _ = analysis(columns(lo, row, STEP), source_start, left)
-            for q in range(pairs):
-                put(target, row, q, low(first + 2 * q))
-            return carry
-
-        lax.fori_loop(0, skip, lows, 0)
-        lax.fori_loop(skip + band_rows // STEP, low_rows // STEP, lows, 0)
-
-    def both(c, carry):
-        row = pl.multiple_of(c * STEP, STEP)
-        g = [jnp.broadcast_to(gain[b : b + 1, :], (STEP, LANES)) for b in range(3)]
-        low, high = analysis(columns(lo, row + skip * STEP, STEP), source_start, left)
+    rows = geo.low[level][1]
+    step = best_step(rows, 168)
+    left = first_half(step)
+
+    def body(c, carry):
+        row = pl.multiple_of(c * step, step)
+        low, _ = analysis(columns(source, row, step), source_start, left)
         for q in range(pairs):
-            put(target, row + skip * STEP, q, low(first + 2 * q))
+            put(target, row, q, low(first + 2 * q))
+        return carry
+
+    lax.fori_loop(0, rows // step, body, 0)
+
+
+def band_rows(geo, level, lo, skip, hi, source_start, gain, bands):
+    first, pairs = geo.span[level]
+    rows = geo.band[level][1]
+    step = best_step(rows)
+    left = first_half(step)
+
+    def body(c, carry):
+        row = pl.multiple_of(c * step, step)
+        g = [jnp.broadcast_to(gain[b : b + 1, :], (step, LANES)) for b in range(3)]
+        _, high = analysis(columns(lo, row + skip, step), source_start, left)
+        for q in range(pairs):
             put(bands, row, q, high(first + 2 * q) * g[0], (0,))
-        low, high = analysis(columns(hi, row, STEP), source_start, left)
+        low, high = analysis(columns(hi, row, step), source_start, left)
         for q in range(pairs):
             put(bands, row, q, low(first + 2 * q) * g[1], (1,))
             put(bands, row, q, high(first + 2 * q) * g[2], (2,))
         return carry
 
-    lax.fori_loop(0, band_rows // STEP, both, 0)
-
-
-def first_level_kernel(geo, lats, place, edge, tl, th, gain, x, g1, d1, send_e, send_o, ext, la, ha, sems):
-    lat, parity = place[0], place[1]
+    lax.fori_loop(0, rows // step, body, 0)
+
+
+def coarse_kernel(geo, lats, place, edge, x, *refs):
+    lat = place[0]
+    weights, copies_of = refs[:4], refs[4:8]
+    g1, lo2, g2, lo3, g3, lo4, ll4, ext, la, gh, gl, sems, weight_sems = refs[8:]
+    for i in range(4):
+        pltpu.make_async_copy(weights[i], copies_of[i], weight_sems.at[i]).start()
     rows = geo.rows[0]
-    low_start, low_rows = geo.low[1]
-    band_start, band_rows = geo.band[1]
+    start, count = geo.low[1]
     width = x.shape[1]
     begin = LEAD + HALO
-    cuts = [0] + [min(rows, 224 * b + 256 - begin) for b in range(low_rows // 112 - 1)] + [rows]
+    blocks = count // 112
+    cuts = [0] + [min(rows, 224 * b + 256 - begin) for b in range(blocks - 1)] + [rows]
     copies = []
-    for i in range(len(cuts) - 1):
+    for i in range(blocks):
         part = pl.ds(cuts[i], cuts[i + 1] - cuts[i])
         to = pl.ds(begin + cuts[i], cuts[i + 1] - cuts[i])
         copies.append(pltpu.make_async_copy(x.at[part, :], ext.at[to, :], sems.at[i]))
@@ -294,70 +305,98 @@
         ext[top, :] = edge[...]
         ext[bottom, :] = jnp.zeros((HALO, width), BF16)
 
-    for b in range(low_rows // 112):
+    base = analysis_matrix(LOW, start, 112, 0 - LEAD - HALO, 256)
+    for b in range(blocks):
         copies[b].wait()
-        mh, ml = two_terms(masked_rows(tl[...], low_start + 112 * b, geo.rows[1], lat, lats))
+        mh, ml = two_terms(masked_rows(base, start + 112 * b, geo.rows[1], lat, lats))
         data = ext[224 * b : 224 * b + 256, :]
         la[112 * b : 112 * b + 112, :] = mxu(mh, data) + mxu(ml, data)
-    for b in range(band_rows // 120):
-        mh, ml = two_terms(masked_rows(th[...], band_start + 120 * b, geo.rows[1], lat, lats))
-        data = ext[96 + 240 * b : 352 + 240 * b, :]
-        ha[120 * b : 120 * b + 120, :] = mxu(mh, data) + mxu(ml, data)
-
-    levels_loop(geo, 1, la, ha, 0, gain, g1, d1, True)
-    edge_lanes = 2 * LANES
-    shift = (geo.cells[1] // 2) * LANES
-
-    def fill(to_left, to_right):
-        for b in range(3):
-            at = slice(b * edge_lanes, (b + 1) * edge_lanes)
-            to_left[:, at] = d1[b, :, 0:edge_lanes].astype(BF16)
-            to_right[:, at] = d1[b, :, shift : shift + edge_lanes].astype(BF16)
+    low_rows(geo, 1, la, 0, g1)
+    gh[...], gl[...] = two_terms(g1[...])
+    out_start, out_rows = geo.low[2]
+    for b in range(out_rows // 88):
+        at = min(176 * b, count - 192)
+        window = slice(at, at + 192)
+        matrix = analysis_matrix(LOW, out_start + 88 * b, 88, start + at, 192)
+        matrix = masked_rows(matrix, out_start + 88 * b, geo.rows[2], lat, lats)
+        lo2[88 * b : 88 * b + 88, :] = dot3(matrix, gh[window, :], gl[window, :])
+    low_rows(geo, 2, lo2, geo.span[1][0], g2)
+    for level, source, lo, target in ((3, g2, lo3, g3), (4, g3, lo4, ll4)):
+        vh, vl = two_terms(source[...])
+        matrix = analysis_matrix(LOW, *geo.low[level], *geo.low[level - 1])
+        matrix = masked_rows(matrix, geo.low[level][0], geo.rows[level], lat, lats)
+        lo[...] = dot3(matrix, vh, vl)
+        low_rows(geo, level, lo, geo.span[level - 1][0], target)
+    for i in range(4):
+        pltpu.make_async_copy(weights[i], copies_of[i], weight_sems.at[i]).wait()
+
+
+def first_bands_kernel(geo, lats, place, edge, side_e, side_o, gain, x, d1, ext, la, ha, sem):
+    lat, parity = place[0], place[1]
+    rows, width = x.shape
+    lanes = SIDE * C
+    copy = pltpu.make_async_copy(x, ext.at[pl.ds(NEAR, rows), pl.ds(lanes, width)], sem)
+    copy.start()
+    own = slice(lanes, lanes + width)
+
+    @pl.when(lat == 0)
+    def _():
+        ext[0:NEAR, own] = jnp.zeros((NEAR, width), BF16)
+        ext[NEAR + rows :, own] = edge[0:NEAR, :]
+
+    @pl.when(lat != 0)
+    def _():
+        ext[0:NEAR, own] = edge[HALO - NEAR :, :]
+        ext[NEAR + rows :, own] = jnp.zeros((NEAR, width), BF16)
 
     @pl.when(parity == 0)
     def _():
-        fill(send_o, send_e)
+        ext[:, 0:lanes] = side_o[...]
+        ext[:, lanes + width :] = side_e[...]
 
     @pl.when(parity != 0)
     def _():
-        fill(send_e, send_o)
-
-
-def deep_blocks(geo):
-    in_rows = geo.low[1][1]
-    lows, highs = [], []
-    for b in range(geo.low[2][1] // 88):
-        lows.append((88 * b, 88, min(176 * b, in_rows - 192), 192))
-    half = geo.band[2][1] // 2
-    for b in range(2):
-        first = 2 * (geo.band[2][0] + half * b) - 3 - geo.low[1][0]
-        highs.append((half * b, half, first // 16 * 16, 2 * half + 16))
-    return lows, highs
-
-
-def deep_kernel(geo, lats, mat_count, place, gain, g1, *refs):
+        ext[:, 0:lanes] = side_e[...]
+        ext[:, lanes + width :] = side_o[...]
+
+    start, count = geo.band[1]
+    low = analysis_matrix(LOW, start, 120, -NEAR, 256)
+    high = analysis_matrix(HIGH, start, 120, -NEAR, 256)
+    copy.wait()
+    for b in range(count // 120):
+        data = ext[240 * b : 240 * b + 256, :]
+        for matrix, out in ((low, la), (high, ha)):
+            mh, ml = two_terms(masked_rows(matrix, start + 120 * b, geo.rows[1], lat, lats))
+            out[120 * b : 120 * b + 120, :] = mxu(mh, data) + mxu(ml, data)
+    band_rows(geo, 1, la, 0, ha, -SIDE, gain, d1)
+
+
+def deep_kernel(geo, lats, place, gain, *refs):
     lat, parity = place[0], place[1]
-    mats, refs = list(refs[:mat_count]), refs[mat_count:]
-    d = {2: refs[0], 3: refs[1], 4: refs[2]}
-    ll4, send_e, send_o, p2, m2, p3, m3 = refs[3:10]
-    g2, g3, lo2, hi2, lo3, hi3, lo4, hi4, gh, gl = refs[10:]
-    lo, hi = {2: lo2, 3: lo3, 4: lo4}, {2: hi2, 3: hi3, 4: hi4}
-    grids = {1: g1, 2: g2, 3: g3, 4: ll4}
-    gh[...], gl[...] = two_terms(g1[...])
-    for starts, blocks, out in zip((geo.low[2][0], geo.band[2][0]), deep_blocks(geo), (lo2, hi2)):
-        for at, count, begin, size in blocks:
-            matrix = masked_rows(mats.pop(0)[...], starts + at, geo.rows[2], lat, lats)
-            window = slice(begin, begin + size)
-            out[at : at + count, :] = dot3(matrix, gh[window, :], gl[window, :])
+    g1, lo2, g2, lo3, g3, lo4 = refs[:6]
+    d = {2: refs[6], 3: refs[7], 4: refs[8]}
+    send_e, send_o, p2, m2, p3, m3, hi2, hi3, hi4 = refs[9:]
+    grids = {1: g1, 2: g2, 3: g3}
+    los, his = {2: lo2, 3: lo3, 4: lo4}, {2: hi2, 3: hi3, 4: hi4}
     for level in (2, 3, 4):
-        if level > 2:
-            vh, vl = two_terms(grids[level - 1][...])
-            for starts, out in ((geo.low[level][0], lo[level]), (geo.band[level][0], hi[level])):
-                matrix = masked_rows(mats.pop(0)[...], starts, geo.rows[level], lat, lats)
-                out[...] = dot3(matrix, vh, vl)
-        start = geo.span[level - 1][0]
+        start, count = geo.band[level]
+        source, in_start = grids[level - 1], geo.low[level - 1][0]
+        parts = 2 if level == 2 else 1
+        half = count // parts
+        for b in range(parts):
+            if parts == 1:
+                at, size = 0, source.shape[0]
+            else:
+                at = (2 * (start + half * b) - 3 - in_start) // 16 * 16
+                size = 2 * half + 16
+            vh, vl = two_terms(source[at : at + size, :])
+            matrix = analysis_matrix(HIGH, start + half * b, half, in_start + at, size)
+            matrix = masked_rows(matrix, start + half * b, geo.rows[level], lat, lats)
+            his[level][half * b : half * (b + 1), :] = dot3(matrix, vh, vl)
         rows = gain[3 * (level - 2) : 3 * (level - 2) + 3, :]
-        levels_loop(geo, level, lo[level], hi[level], start, rows, grids[level], d[level], level < 4)
+        skip = start - geo.low[level][0]
+        begin = geo.span[level - 1][0]
+        band_rows(geo, level, los[level], skip, his[level], begin, rows, d[level])
 
     def fill(distance, to_left, to_right):
         for level, count, row in exchange_plan(geo)[distance]:
@@ -466,7 +505,9 @@
     hidden = embedded + mxu(attended.astype(BF16), wo[...])
     square = jnp.mean(hidden * hidden, -1, keepdims=True)
     normed = (hidden * lax.rsqrt(square + 1e-06) * gain[...]).astype(BF16)
-    update = mxu(normed, wb[...])
+    update = lax.dot_general(
+        normed, wb[...], (((1,), (1,)), ((), ())), preferred_element_type=F32
+    )
     back = [
         jnp.concatenate(
             [update[rows * c : rows * (c + 1), :], update[rows * (c + 1) : rows * (c + 2), :]], 1
@@ -481,9 +522,8 @@
 
 def synthesis_kernel(geo, lats, place, coarse, d1, d2, d3, d4, *refs):
     lat, parity = place[0], place[1]
-    e1, o1, e2, o2, from_m2, from_p2, from_m3, from_p3 = refs[:8]
-    mats, refs = refs[8:13], refs[13:]
-    out, up3, up2, up1, sides, xh, xl, ylow, yhigh, done, sems = refs
+    e2, o2, from_m2, from_p2, from_m3, from_p3 = refs[:6]
+    out, up3, up2, up1, xh, xl, ylow, yhigh, done, sems = refs[6:]
     bands = {2: d2, 3: d3, 4: d4}
     plan = exchange_plan(geo)
 
@@ -511,12 +551,12 @@
         return jnp.concatenate(cols, 1)
 
     uppers = {4: coarse, 3: up3, 2: up2, 1: up1}
-    left = first_half(STEP)
     for level in (4, 3, 2):
         begin, pairs = geo.span[level]
         below = level - 1
         start, rows = geo.band[below]
-        matrix = masked_rows(mats[4 - level][...], start, geo.rows[below], lat, lats)
+        matrix = synthesis_matrix(start, rows, *geo.band[level])
+        matrix = masked_rows(matrix, start, geo.rows[below], lat, lats)
         width = pairs * LANES
         for one, two, y in (
             (uppers[level][...], from_sides(level, 1), ylow),
@@ -527,79 +567,72 @@
         target = uppers[below]
         first, out_pairs = geo.span[below]
 
+        step = best_step(rows)
+        left = first_half(step)
+
         def joined(c, carry):
-            row = pl.multiple_of(c * STEP, STEP)
+            row = pl.multiple_of(c * step, step)
             pair = synthesis(
-                columns(ylow, row, STEP, pairs), columns(yhigh, row, STEP, pairs), begin, left
+                columns(ylow, row, step, pairs), columns(yhigh, row, step, pairs), begin, left
             )
             for q in range(out_pairs):
                 put(target, row, q, pair(first + 2 * q))
             return carry
 
-        lax.fori_loop(0, rows // STEP, joined, 0)
+        lax.fori_loop(0, rows // step, joined, 0)
 
     n = geo.band[1][1]
-    edge = 2 * LANES
-    shift = (geo.cells[1] // 2) * LANES
-    for b in range(3):
-        at = slice(b * edge, (b + 1) * edge)
-        even, odd = e1[:, at].astype(F32), o1[:, at].astype(F32)
-        sides[b, 0] = jnp.where(parity == 0, odd, even)
-        sides[b, 1] = jnp.where(parity == 0, even, odd)
     half = geo.rows[0] // 2
     for block in range(2):
         w = 0 if block == 0 else n - LANES
         window = slice(w, w + LANES)
-        sh, sl = two_terms(mats[3 + block][...])
-        for pieces, y in (((None, 1), ylow), ((0, 2), yhigh)):
-            for i, b in enumerate(pieces):
-                place_rows = slice(i * LANES, (i + 1) * LANES)
-                if b is None:
-                    h, l = two_terms(up1[window, :])
-                    xh[place_rows, :], xl[place_rows, :] = h, l
-                else:
-                    for lanes, extra in (
-                        (slice(0, edge), sides[b, 0, window, :]),
-                        (slice(edge, shift), None),
-                        (slice(shift, shift + edge), sides[b, 1, window, :]),
-                    ):
-                        value = d1[b, window, lanes]
-                        h, l = two_terms(value if extra is None else value + extra)
-                        xh[place_rows, lanes], xl[place_rows, lanes] = h, l
+        sh, sl = two_terms(synthesis_matrix(half * block, half, geo.band[1][0] + w, LANES))
+        for one, two, y in (
+            (up1[window, :], d1[1, window, :], ylow),
+            (d1[0, window, :], d1[2, window, :], yhigh),
+        ):
+            xh[0:LANES, :], xl[0:LANES, :] = two_terms(one)
+            xh[LANES:, :], xl[LANES:, :] = two_terms(two)
             y[half * block : half * (block + 1), :] = (
                 mxu(sh, xh[...]) + mxu(sh, xl[...]) + mxu(sl, xh[...])
             )
-    rows16 = 16
-    left16 = first_half(rows16)
     begin, pairs = geo.span[1]
-
-    def last(c, carry):
-        row = pl.multiple_of(c * rows16, rows16)
-        pair = synthesis(columns(ylow, row, rows16), columns(yhigh, row, rows16), begin, left16)
+    most = 112
+
+    def last(row, count):
+        left = first_half(count)
+        pair = synthesis(columns(ylow, row, count), columns(yhigh, row, count), begin, left)
         for q in range(geo.cells[0] // 2):
             put(done, row, q, pair(2 * q).astype(BF16))
+
+    def store(i, count):
+        part = pl.ds(pl.multiple_of(i * most, 16), count)
+        return pltpu.make_async_copy(done.at[part, :], out.at[part, :], sems.at[i])
+
+    whole, rest = geo.rows[0] // most, geo.rows[0] % most
+
+    def chunk(i, carry):
+        last(pl.multiple_of(i * most, 16), most)
+        store(i, most).start()
         return carry
 
-    chunks = geo.rows[0] // rows16
-    cuts = [chunks * i // 4 for i in range(5)]
-    copies = []
-    for i in range(4):
-        lax.fori_loop(cuts[i], cuts[i + 1], last, 0)
-        part = pl.ds(cuts[i] * rows16, (cuts[i + 1] - cuts[i]) * rows16)
-        copies.append(pltpu.make_async_copy(done.at[part, :], out.at[part, :], sems.at[i]))
-        copies[-1].start()
-    for copy in copies:
-        copy.wait()
-
-
-def call(kernel, out_shape, scratch, *args, cost=20_000_000, grant=24, raw=0, raw_out=False):
+    lax.fori_loop(0, whole, chunk, 0)
+    if rest:
+        last(whole * most, rest)
+        store(whole, rest).start()
+    for i in range(whole):
+        store(i, most).wait()
+    if rest:
+        store(whole, rest).wait()
+
+
+def call(kernel, out_shape, scratch, *args, cost=20_000_000, grant=24, raw=(), raw_out=False):
     vmem = pl.BlockSpec(memory_space=pltpu.VMEM)
     smem = pl.BlockSpec(memory_space=pltpu.SMEM)
-    anywhere = pl.BlockSpec(memory_space=pl.ANY)
     specs = [smem if a.ndim == 1 and a.size < 16 else vmem for a in args]
-    if raw:
-        specs[-raw:] = [anywhere] * raw
-    outs = jax.tree.map(lambda _: anywhere if raw_out else vmem, out_shape)
+    for at in raw:
+        specs[at] = pl.BlockSpec(memory_space=pltpu.HBM)
+    outs = jax.tree.map(lambda _: pl.BlockSpec(memory_space=pl.ANY) if raw_out else vmem, out_shape)
     return pl.pallas_call(
         kernel,
         out_shape=out_shape,
@@ -615,10 +648,6 @@
     return pltpu.VMEM(dims, dtype)
 
 
-def constant(matrix):
-    return jnp.asarray(matrix)
-
-
 def per_device(mesh_shape, state_field, skip_gain, embed_weight, qkv_weight, head_scale, out_weight, norm_gain, back_weight):
     return program(
         mesh_shape, state_field, skip_gain, embed_weight, qkv_weight, head_scale, out_weight, norm_gain, back_weight
@@ -643,60 +672,75 @@
     edge = jnp.where(lat == 0, state_field[rows - HALO :], state_field[:HALO])
     edge = lax.ppermute(edge, "lat", swap)
 
-    low_rows, band_rows = geo.low[1][1], geo.band[1][1]
-    tl = SCALE * analysis_matrix(LOW, geo.low[1][0], 112, 0 - LEAD - HALO, 256)
-    th = SCALE * analysis_matrix(HIGH, geo.band[1][0], 120, 96 - LEAD - HALO, 256)
-    w1 = geo.span[1][1] * LANES
-    g1, d1, send_e, send_o = call(
-        functools.partial(first_level_kernel, geo, lats),
-        (
-            shape((low_rows, w1)),
-            shape((3, band_rows, w1)),
-            shape((band_rows, 6 * LANES), BF16),
-            shape((band_rows, 6 * LANES), BF16),
-        ),
+    even_lon = lon % 2 == 0
+    wide = SIDE * C
+
+    def beside(value, first):
+        return jnp.where(first, value[:, width - wide :], value[:, :wide])
+
+    def with_rows(first):
+        near = beside(edge, first)
+        none = jnp.zeros((NEAR, wide), BF16)
+        top = jnp.where(lat == 0, none, near[HALO - NEAR :])
+        bottom = jnp.where(lat == 0, near[:NEAR], none)
+        return jnp.concatenate([top, beside(state_field, first), bottom], 0)
+
+    side_e = lax.ppermute(with_rows(even_lon), "lon", even_pairs)
+    side_o = lax.ppermute(with_rows(~even_lon), "lon", odd_pairs)
+
+    w = [None] + [geo.span[level][1] * LANES for level in (1, 2, 3, 4)]
+    weights = (embed_weight, qkv_weight, out_weight, back_weight.T)
+    low = lambda level, lanes: shape((geo.low[level][1], w[lanes]))
+    *weights, g1, lo2, g2, lo3, g3, lo4, ll4 = call(
+        functools.partial(coarse_kernel, geo, lats),
+        tuple(shape(a.shape, BF16) for a in weights)
+        + (low(1, 1), low(2, 1), low(2, 2), low(3, 2), low(3, 3), low(4, 3), low(4, 4)),
         [
             pltpu.VMEM((geo.extended, width), BF16),
-            pltpu.VMEM((low_rows, width), F32),
-            pltpu.VMEM((band_rows, width), F32),
-            pltpu.SemaphoreType.DMA((low_rows // 112,)),
+            pltpu.VMEM((geo.low[1][1], width), F32),
+            pltpu.VMEM((geo.low[1][1], w[1]), BF16),
+            pltpu.VMEM((geo.low[1][1], w[1]), BF16),
+            pltpu.SemaphoreType.DMA((geo.low[1][1] // 112,)),
+            pltpu.SemaphoreType.DMA((4,)),
         ],
         place,
         edge,
-        constant(tl),
-        constant(th),
+        state_field,
+        *weights,
+        raw=(2, 3, 4, 5, 6),
+    )
+    extended = NEAR + rows + NEAR
+    d1 = call(
+        functools.partial(first_bands_kernel, geo, lats),
+        shape((3, geo.band[1][1], w[1])),
+        [
+            pltpu.VMEM((extended, width + 2 * wide), BF16),
+            pltpu.VMEM((geo.band[1][1], width + 2 * wide), F32),
+            pltpu.VMEM((geo.band[1][1], width + 2 * wide), F32),
+            pltpu.SemaphoreType.DMA,
+        ],
+        place,
+        edge,
+        side_e,
+        side_o,
         gains[:3],
         state_field,
-        raw=1,
+        raw=(5,),
     )
-    e1 = lax.ppermute(send_e, "lon", even_pairs)
-    o1 = lax.ppermute(send_o, "lon", odd_pairs)
-
-    mats = []
-    for taps, start, blocks in zip((LOW, HIGH), (geo.low[2][0], geo.band[2][0]), deep_blocks(geo)):
-        for at, count, begin, size in blocks:
-            mats.append(analysis_matrix(taps, start + at, count, geo.low[1][0] + begin, size))
-    for level in (3, 4):
-        in_start, in_rows = geo.low[level - 1]
-        mats.append(analysis_matrix(LOW, *geo.low[level], in_start, in_rows))
-        mats.append(analysis_matrix(HIGH, *geo.band[level], in_start, in_rows))
-    scratch = [pltpu.VMEM((geo.low[level][1], geo.span[level][1] * LANES), F32) for level in (2, 3)]
-    for level in (2, 3, 4):
-        w = geo.span[level - 1][1] * LANES
-        scratch += [pltpu.VMEM((geo.low[level][1], w), F32), pltpu.VMEM((geo.band[level][1], w), F32)]
-    scratch += [pltpu.VMEM((low_rows, w1), BF16), pltpu.VMEM((low_rows, w1), BF16)]
-    deep = call(
-        functools.partial(deep_kernel, geo, lats, len(mats)),
-        tuple(shape((3, geo.band[level][1], geo.span[level][1] * LANES)) for level in (2, 3, 4))
-        + (shape((geo.low[4][1], geo.span[4][1] * LANES)),)
+    d2, d3, d4, deep_e, deep_o, p2, m2, p3, m3 = call(
+        functools.partial(deep_kernel, geo, lats),
+        tuple(shape((3, geo.band[level][1], w[level])) for level in (2, 3, 4))
         + tuple(shape(plan_shape(geo, d), BF16) for d in (1, 1, 2, 2, 3, 3)),
-        scratch,
+        [pltpu.VMEM((geo.band[level][1], w[level - 1]), F32) for level in (2, 3, 4)],
         place,
         gains[3:],
         g1,
-        *[constant(SCALE * m) for m in mats],
+        lo2,
+        g2,
+        lo3,
+        g3,
+        lo4,
     )
-    d2, d3, d4, ll4, deep_e, deep_o, p2, m2, p3, m3 = deep
 
     merged, size = ll4, 1
     while size < lons:
@@ -704,24 +748,24 @@
         lower_half = (lon // size) % 2 == 0
         lower = jnp.where(lower_half, merged, other)
         upper = jnp.where(lower_half, other, merged)
-        wide = geo.cells[4] * C * size
-        merged = jnp.pad(lower, ((0, 0), (0, wide))) + jnp.pad(upper, ((0, 0), (wide, 0)))
+        more = geo.cells[4] * C * size
+        merged = jnp.pad(lower, ((0, 0), (0, more))) + jnp.pad(upper, ((0, 0), (more, 0)))
         size = 2 * size
     around = geo.cells[4] * lons * C
-    w = 6 * C
-    ring = jnp.concatenate([merged[:, :w] + merged[:, around:], merged[:, w:around]], 1)
+    fold = 6 * C
+    ring = jnp.concatenate([merged[:, :fold] + merged[:, around:], merged[:, fold:around]], 1)
     skip = -geo.low[4][0]
     tokens = ring[skip : skip + geo.rows[4]].astype(BF16)
     others = lax.ppermute(tokens, "lat", swap)
     keys = jnp.concatenate([tokens, others], 0).reshape(-1, C)
 
-    e2 = lax.ppermute(deep_e, "lon", even_pairs)
-    o2 = lax.ppermute(deep_o, "lon", odd_pairs)
+    deep_e = lax.ppermute(deep_e, "lon", even_pairs)
+    deep_o = lax.ppermute(deep_o, "lon", odd_pairs)
     from_m2, from_p2 = shifted(p2, 2), shifted(m2, -2)
     from_m3, from_p3 = shifted(p3, 3), shifted(m3, -3)
 
     own = lax.dynamic_slice(
-        jnp.concatenate([ring, ring[:, :w]], 1),
+        jnp.concatenate([ring, ring[:, :fold]], 1),
         (0, lon * geo.cells[4] * C),
         (geo.low[4][1], geo.span[4][1] * LANES),
     )
@@ -733,42 +777,26 @@
         place,
         keys,
         own,
-        embed_weight,
-        qkv_weight,
+        weights[0],
+        weights[1],
         head_scale,
-        out_weight,
+        weights[2],
         norm_gain[None],
-        back_weight,
+        weights[3],
         cost=200_000_000,
     )
 
-    synth = []
-    for level in (4, 3, 2):
-        synth.append(
-            np.concatenate(
-                [synthesis_matrix(t, *geo.band[level - 1], *geo.band[level]) for t in (LOW, HIGH)], 1
-            )
-        )
-    half = rows // 2
-    for block in range(2):
-        begin = geo.band[1][0] + (0 if block == 0 else band_rows - LANES)
-        synth.append(
-            np.concatenate(
-                [synthesis_matrix(t, half * block, half, begin, LANES) for t in (LOW, HIGH)], 1
-            )
-        )
     return call(
         functools.partial(synthesis_kernel, geo, lats),
         jax.ShapeDtypeStruct((rows, width), BF16),
-        [pltpu.VMEM((geo.band[level][1], geo.span[level][1] * LANES), F32) for level in (3, 2, 1)]
+        [pltpu.VMEM((geo.band[level][1], w[level]), F32) for level in (3, 2, 1)]
         + [
-            pltpu.VMEM((3, 2, band_rows, 2 * LANES), F32),
-            pltpu.VMEM((2 * LANES, w1), BF16),
-            pltpu.VMEM((2 * LANES, w1), BF16),
-            pltpu.VMEM((rows, w1), F32),
-            pltpu.VMEM((rows, w1), F32),
+            pltpu.VMEM((2 * LANES, w[1]), BF16),
+            pltpu.VMEM((2 * LANES, w[1]), BF16),
+            pltpu.VMEM((rows, w[1]), F32),
+            pltpu.VMEM((rows, w[1]), F32),
             pltpu.VMEM((rows, width), BF16),
-            pltpu.SemaphoreType.DMA((4,)),
+            pltpu.SemaphoreType.DMA((rows // 112 + 1,)),
         ],
         place,
         coarse,
@@ -776,15 +804,12 @@
         d2,
         d3,
         d4,
-        e1,
-        o1,
-        e2,
-        o2,
+        deep_e,
+        deep_o,
         from_m2,
         from_p2,
         from_m3,
         from_p3,
-        *[constant(SCALE * m) for m in synth],
         raw_out=True,
     )
 

time: 140 us -> 115 us (0.82)
  Pallas kernels: 66.1 us -> 35.1 us
  waiting for transfers between devices: 25.8 us -> 41.3 us
  local copies, waits for them, and re-layouts: 21.6 us -> 10.8 us
    pallas_call x4 -> x5, Pallas kernels: 66.1 us -> 35.1 us  [call(): pl.pallas_call(kernel, out_shape=out_shape, in_specs=specs, out_specs=out...]
    ppermute x3, waiting for transfers between devices: 8.45 us -> 30.5 us  [program(): other = lax.ppermute(merged, 'lon', [(i, i ^ size) for i in range(lons)])]
    unnamed x70 -> x51, local copies, waits for them, and re-layouts: 20.4 us -> 9.7 us
    ppermute x4, starting transfers between devices: 5.59 us -> 12.2 us  [the longest x1 4.55 us: program(): side_o = lax.ppermute(with_rows(~even_lon), 'lon', odd_pairs)]
    ppermute x4, waiting for transfers between devices: 5.12 us -> 0.01 us  [shifted(): lax.ppermute(value, 'lon', [(i, (i + by) % lons) for i in range(lons)])]
    ppermute x4, starting transfers between devices: 5.89 us -> 2.56 us  [shifted(): lax.ppermute(value, 'lon', [(i, (i + by) % lons) for i in range(lons)])]
    ppermute x3, starting transfers between devices: 7.67 us -> 5.12 us  [program(): other = lax.ppermute(merged, 'lon', [(i, i ^ size) for i in range(lons)])]
  transfers between devices with their start and end apart: 13 -> 13, of which waited for: 7 -> 5; matrix products, arithmetic and copies ran while one was open for 5% -> 5% of each run, Pallas kernels for 4% -> 9%
where the time goes in v2:
time: 115 us; the launch traced here: 113 us
  waiting for transfers between devices  41.3 us (36%)
  Pallas kernels  35.1 us (31%)
  starting transfers between devices  20.6 us (18%)
  local copies, waits for them, and re-layouts  10.8 us (9%)
  other arithmetic  4.96 us (4%)
    pallas_call x5, Pallas kernels, call(): pl.pallas_call(kernel, out_shape=out_shape, in_specs=specs, out_specs=out...  35.1 us
    ppermute x3, waiting for transfers between devices, program(): other = lax.ppermute(merged, 'lon', [(i, i ^ size) for i in range(lons)])  30.5 us
    ppermute x1, waiting for transfers between devices, program(): side_e = lax.ppermute(with_rows(even_lon), 'lon', even_pairs)  10.2 us
    unnamed x51, local copies, waits for them, and re-layouts  9.7 us
    ppermute x3, starting transfers between devices, program(): other = lax.ppermute(merged, 'lon', [(i, i ^ size) for i in range(lons)])  5.12 us
    ppermute x1, starting transfers between devices, program(): side_o = lax.ppermute(with_rows(~even_lon), 'lon', odd_pairs)  4.55 us
    ppermute x1, starting transfers between devices, program(): deep_o = lax.ppermute(deep_o, 'lon', odd_pairs)  3.56 us
    ppermute x4, starting transfers between devices, shifted(): lax.ppermute(value, 'lon', [(i, (i + by) % lons) for i in range(lons)])  2.56 us
  transfers between devices with their start and end apart: 13, of which 5 were waited for; matrix products, arithmetic and copies ran while one was open for 5% of the time, Pallas kernels for 9%

profile of v2, /device:TPU:0, one launch (start us, length us, event | category | flops | bytes accessed | tf_op | source)
XLA Modules:
  0.0 113.3 jit_solution(7295051074487296931)
XLA Ops:
  0.0 1.3 %slice_select_fusion = bf16[96,2048]{1,0:T(8,128)(2,1)S(1)} fusion(bf16[464,2048]{1,0:T(8,128)(2,1)} %x.15, pred[]{:T(512)S(6)} %eq.26), kind=kLoop, calls=%fused_computation.4 | loop fusion | flops 196608 | bytes 1179649 | tf_op jit(solution)/shard_map/jit(_where)/select_n | solution.py:672
  1.3 0.6 collective-permute-start
  1.9 0.7 copy.11
  2.6 0.1 pad_maximum_fusion.4
  2.7 0.1 pad_add_fusion.3.place
  2.8 1.2 %broadcast_select_fusion = (bf16[464,512]{1,0:T(8,128)(2,1)S(1)}, bf16[464,512]{1,0:T(8,128)(2,1)S(1)}) fusion(pred[]{:T(512)S(6)} %not.3, bf16[464,2048]{1,0:T(8,128)(2,1)} %x.15, pred[]{:T(512)S(6)} %eq.25), kind=kLoop, calls=%fused_computation.2 | loop fusion | flops 475136 | bytes 1900546 | tf_op jit(solution)/shard_map/jit(_where)/select_n | solution.py:679
  4.0 0.0 collective-permute-done.edge
  4.1 6.4 %shard_map.82 = (bf16[64,256]{1,0:T(8,128)(2,1)S(1)}, bf16[256,768]{1,0:T(8,128)(2,1)S(1)}, bf16[256,256]{1,0:T(8,128)(2,1)S(1)}, bf16[64,256]{1,0:T(8,128)(2,1)...) custom-call(s32[2]{0:T(128)S(1)} %pad_add_fusion.3.place, ...), custom_call_target="tpu_custom_call" | custom-call | flops 20000000 | bytes 1048576 | tf_op jit(solution)/shard_map/pallas_call | solution.py:636
  10.6 3.5 %shard_map.85 = (f32[3,128,896]{2,1,0:T(8,128)S(1)}, f32[3,64,640]{2,1,0:T(8,128)S(1)}, f32[3,40,512]{2,1,0:T(8,128)S(1)}, bf16[240,1152]{1,0:T(8,128)(2,1)}, bf...) custom-call(s32[2]{0:T(128)S(1)} %pad_add_fusion.3.place, ...), custom_call_target="tpu_custom_call" | custom-call | flops 20000000 | bytes 1048576 | tf_op jit(solution)/shard_map/pallas_call | solution.py:636
  14.1 0.0 copy-start.1
  14.1 2.6 %collective-permute-start.7 = (bf16[240,1152]{1,0:T(8,128)(2,1)}, bf16[240,1152]{1,0:T(8,128)(2,1)S(1)}, u32[]{:S(2)}, u32[]{:S(2)}) collective-permute-start(bf16[240,1152]{1,0:T(8,128)(2,1)} %get-tuple-element.39), channel_id=1, source_target_pairs={{0,2},{2,0},{4,6},{6,4},{8,10},{10,8},{12,14},{14,12},{1,3},{3,1},... | collective-permute-start | bytes 1658888 | tf_op jit(solution)/shard_map/ppermute | solution.py:762
  16.7 3.6 %collective-permute-start.8 = (bf16[240,1152]{1,0:T(8,128)(2,1)}, bf16[240,1152]{1,0:T(8,128)(2,1)}, u32[]{:S(2)}, u32[]{:S(2)}) collective-permute-start(bf16[240,1152]{1,0:T(8,128)(2,1)} %get-tuple-element.40), channel_id=1, source_target_pairs={{0,14},{2,4},{4,2},{6,8},{8,6},{10,12},{12,10},{14,0},{1,15},{3,5}... | collective-permute-start | bytes 1658888 | tf_op jit(solution)/shard_map/ppermute | solution.py:763
  20.3 0.5 collective-permute-start.11
  20.8 0.4 collective-permute-start.1
  21.2 23.3 %collective-permute-done.1 = f32[40,512]{1,0:T(8,128)S(1)} collective-permute-done((f32[40,512]{1,0:T(8,128)S(1)}, f32[40,512]{1,0:T(8,128)S(1)}, u32[]{:S(2)}, u32[]{:S(2)}) %collective-permute-start.1) | collective-permute-done | bytes 81952 | tf_op jit(solution)/shard_map/ppermute | solution.py:747
  44.6 1.9 %collective-permute-start.2 = (f32[40,640]{1,0:T(8,128)S(1)}, f32[40,640]{1,0:T(8,128)S(1)}, u32[]{:S(2)}, u32[]{:S(2)}) collective-permute-start(f32[40,640]{1,0:T(8,128)S(1)} %pad_add_fusion.2), channel_id=1, source_target_pairs={{0,4},{2,6},{4,0},{6,2},{8,12},{10,14},{12,8},{14,10},{1,5},{3,7},... | collective-permute-start | bytes 307208 | tf_op jit(solution)/shard_map/ppermute | solution.py:747
  46.4 2.9 %collective-permute-done.2 = f32[40,640]{1,0:T(8,128)S(1)} collective-permute-done((f32[40,640]{1,0:T(8,128)S(1)}, f32[40,640]{1,0:T(8,128)S(1)}, u32[]{:S(2)}, u32[]{:S(2)}) %collective-permute-start.2) | collective-permute-done | bytes 102432 | tf_op jit(solution)/shard_map/ppermute | solution.py:747
  49.4 2.8 %collective-permute-start.3 = (f32[40,896]{1,0:T(8,128)S(1)}, f32[40,896]{1,0:T(8,128)S(1)}, u32[]{:S(2)}, u32[]{:S(2)}) collective-permute-start(f32[40,896]{1,0:T(8,128)S(1)} %pad_add_fusion), channel_id=1, source_target_pairs={{0,8},{2,10},{4,12},{6,14},{8,0},{10,2},{12,4},{14,6},{1,9},{3,11}... | collective-permute-start | bytes 430088 | tf_op jit(solution)/shard_map/ppermute | solution.py:747
  52.3 1.6 %collective-permute-start.5 = (bf16[496,512]{1,0:T(8,128)(2,1)S(1)}, bf16[496,512]{1,0:T(8,128)(2,1)S(1)}, u32[]{:S(2)}, u32[]{:S(2)}) collective-permute-start(bf16[496,512]{1,0:T(8,128)(2,1)S(1)} %pad_maximum_fusion), channel_id=1, source_target_pairs={{0,2},{2,0},{4,6},{6,4},{8,10},{10,8},{12,14},{14,12},{1,3},{3,1},... | collective-permute-start | bytes 1523720 | tf_op jit(solution)/shard_map/ppermute | solution.py:688
  53.9 4.3 %collective-permute-done.3 = f32[40,896]{1,0:T(8,128)S(1)} collective-permute-done((f32[40,896]{1,0:T(8,128)S(1)}, f32[40,896]{1,0:T(8,128)S(1)}, u32[]{:S(2)}, u32[]{:S(2)}) %collective-permute-start.3) | collective-permute-done | bytes 143392 | tf_op jit(solution)/shard_map/ppermute | solution.py:747
  58.2 4.6 %collective-permute-start.6 = (bf16[496,512]{1,0:T(8,128)(2,1)S(1)}, bf16[496,512]{1,0:T(8,128)(2,1)S(1)}, u32[]{:S(2)}, u32[]{:S(2)}) collective-permute-start(bf16[496,512]{1,0:T(8,128)(2,1)S(1)} %pad_maximum_fusion.1), channel_id=1, source_target_pairs={{0,14},{2,4},{4,2},{6,8},{8,6},{10,12},{12,10},{14,0},{1,15},{3,5}... | collective-permute-start | bytes 1523720 | tf_op jit(solution)/shard_map/ppermute | solution.py:689
  62.8 0.0 collective-permute-done.11.refs_4_
  62.8 0.1 collective-permute-start.4
  62.9 0.7 maximum_bitcast_fusion.gain
  63.6 0.6 collective-permute-done.4
  64.1 0.0 collective-permute-start.10
  64.1 10.2 %collective-permute-done.5.side_e = bf16[496,512]{1,0:T(8,128)(2,1)S(1)} collective-permute-done((bf16[496,512]{1,0:T(8,128)(2,1)S(1)}, bf16[496,512]{1,0:T(8,128)(2,1)S(1)}, u32[]{:S(2)}, u32[]{:S(2)}) %collective-permute-start.5) | collective-permute-done | bytes 507936 | tf_op jit(solution)/shard_map/ppermute | solution.py:688
  74.4 0.8 copy-done.3
  75.2 2.1 %collective-permute-start.9 = (bf16[112,768]{1,0:T(8,128)(2,1)}, bf16[112,768]{1,0:T(8,128)(2,1)}, u32[]{:S(2)}, u32[]{:S(2)}) collective-permute-start(bf16[112,768]{1,0:T(8,128)(2,1)} %get-tuple-element.41), channel_id=1, source_target_pairs={{0,4},{2,6},{4,8},{6,10},{8,12},{10,14},{12,0},{14,2},{1,5},{3,7},... | collective-permute-start | bytes 516104 | tf_op jit(solution)/shard_map/ppermute | solution.py:670
  77.3 0.6 fusion.1.grid
  77.9 0.8 copy-done.5
  78.7 0.0 collective-permute-start.12
  78.7 0.7 pad_maximum_fusion.2
  79.4 1.1 reshape.6.keys
  80.5 0.9 copy-done.10
  81.4 0.9 copy-done.15
  82.3 0.8 copy-done.19
  83.1 0.8 copy-done.21
  83.8 0.7 copy-done.23
  84.5 0.7 copy-done.24
  85.2 5.2 %shard_map.83.coarse = f32[40,512]{1,0:T(8,128)S(1)} custom-call(s32[2]{0:T(128)S(1)} %pad_add_fusion.3.place, bf16[928,64]{1,0:T(8,128)(2,1)S(1)} %reshape.6.keys, f32[40,512]{1,0:T(8,128)S(1)} %copy-done.10, bf16[64,256]{1,0:T(8,128)(2,1)S(1)} %copy-done.19, bf16[256,768]{1,0:T(8,128)(2,1)S(1)} %get-tuple-element.27.wqkv, f32[8]{0:T(128)S(1)} %copy-done.24, ...), custom_call_target="tpu_custom_call" | custom-call | flops 200000000 | bytes 1048576 | tf_op jit(solution)/shard_map/pallas_call | solution.py:636
  90.4 1.0 copy-done.4
  91.4 1.0 copy-done.6
  92.5 0.7 copy-done.22
  93.1 4.6 %shard_map.84.d1 = f32[3,240,1280]{2,1,0:T(8,128)S(1)} custom-call(s32[2]{0:T(128)S(1)} %pad_add_fusion.3.place, bf16[96,2048]{1,0:T(8,128)(2,1)S(1)} %collective-permute-done.edge, bf16[496,512]{1,0:T(8,128)(2,1)S(1)} %copy-done.4, bf16[496,512]{1,0:T(8,128)(2,1)S(1)} %copy-done.6, f32[3,128]{1,0:T(4,128)S(1)} %copy-done.22, bf16[464,2048]{1,0:T(8,128)(2,1)S(1)} %copy-done), custom_call_target="tpu_custom_call" | custom-call | flops 20000000 | bytes 1048576 | tf_op jit(solution)/shard_map/pallas_call | solution.py:636
  97.8 0.0 collective-permute-done.10.refs_3_
  97.8 0.0 collective-permute-done.8.refs_1_
  97.9 15.2 %shard_map.86 = bf16[464,2048]{1,0:T(8,128)(2,1)} custom-call(s32[2]{0:T(128)S(1)} %pad_add_fusion.3.place, f32[40,512]{1,0:T(8,128)S(1)} %shard_map.83.coarse, f32[3,240,1280]{2,1,0:T(8,128)S(1)} %shard_map.84.d1, f32[3,128,896]{2,1,0:T(8,128)S(1)} %copy-done.2, f32[3,64,640]{2,1,0:T(8,128)S(1)} %copy-done.8, f32[3,40,512]{2,1,0:T(8,128)S(1)} %copy-done.12, ...), custom_call_target="tpu_custom_call" | custom-call | flops 20000000 | bytes 1048576 | tf_op jit(solution)/shard_map/pallas_call | solution.py:636
  (55 shorter events, 0.3 us)
Async XLA Ops:
  0.0 4.0 %copy-start = (bf16[464,2048]{1,0:T(8,128)(2,1)S(1)}, bf16[464,2048]{1,0:T(8,128)(2,1)}, u32[]{:S(2)}) copy-start(bf16[464,2048]{1,0:T(8,128)(2,1)} %x.15) | copy-start | bytes 5701636
  0.0 4.1 %copy-start.17 = (bf16[256,64]{0,1:T(8,128)(2,1)S(1)}, bf16[256,64]{0,1:T(8,128)(2,1)}, u32[]{:S(2)}) copy-start(bf16[256,64]{0,1:T(8,128)(2,1)} %param.15) | copy-start | bytes 98308
  0.0 4.1 %copy-start.16 = (bf16[64,256]{1,0:T(8,128)(2,1)S(1)}, bf16[64,256]{1,0:T(8,128)(2,1)}, u32[]{:S(2)}) copy-start(bf16[64,256]{1,0:T(8,128)(2,1)} %refs_0_.1) | copy-start | bytes 98308
  0.0 4.1 %copy-start.9 = (bf16[256,768]{1,0:T(8,128)(2,1)S(1)}, bf16[256,768]{1,0:T(8,128)(2,1)}, u32[]{:S(2)}) copy-start(bf16[256,768]{1,0:T(8,128)(2,1)} %refs_1_.1) | copy-start | bytes 1179652
  0.0 4.1 %copy-start.13 = (bf16[256,256]{1,0:T(8,128)(2,1)S(1)}, bf16[256,256]{1,0:T(8,128)(2,1)}, u32[]{:S(2)}) copy-start(bf16[256,256]{1,0:T(8,128)(2,1)} %refs_2_.1) | copy-start | bytes 393220
  1.3 2.7 %collective-permute-start = (bf16[96,2048]{1,0:T(8,128)(2,1)S(1)}, bf16[96,2048]{1,0:T(8,128)(2,1)S(1)}, u32[]{:S(2)}, u32[]{:S(2)}) collective-permute-start(bf16[96,2048]{1,0:T(8,128)(2,1)S(1)} %slice_select_fusion), channel_id=1, source_target_pairs={{0,1},{1,0},{2,3},{3,2},{4,5},{5,4},{6,7},{7,6},{8,9},{9,8},{10,11... | collective-permute-start | bytes 1179656 | tf_op jit(solution)/shard_map/ppermute | solution.py:673
  10.5 3.6 %copy-start.14 = (bf16[256,256]{1,0:T(8,128)(2,1)}, bf16[256,256]{1,0:T(8,128)(2,1)S(1)}, u32[]{:S(2)}) copy-start(bf16[256,256]{1,0:T(8,128)(2,1)S(1)} %get-tuple-element.28.wo) | copy-start | bytes 393220
  10.6 3.6 %copy-start.18 = (bf16[64,256]{1,0:T(8,128)(2,1)}, bf16[64,256]{1,0:T(8,128)(2,1)S(1)}, u32[]{:S(2)}) copy-start(bf16[64,256]{1,0:T(8,128)(2,1)S(1)} %get-tuple-element.26.we) | copy-start | bytes 98308
  10.6 3.5 %copy-start.20 = (bf16[64,256]{1,0:T(8,128)(2,1)}, bf16[64,256]{1,0:T(8,128)(2,1)S(1)}, u32[]{:S(2)}) copy-start(bf16[64,256]{1,0:T(8,128)(2,1)S(1)} %get-tuple-element.29.wb) | copy-start | bytes 98308
  14.1 39.7 %copy-start.1 = (f32[3,128,896]{2,1,0:T(8,128)}, f32[3,128,896]{2,1,0:T(8,128)S(1)}, u32[]{:S(2)}) copy-start(f32[3,128,896]{2,1,0:T(8,128)S(1)} %get-tuple-element.36.d2) | copy-start | bytes 4128772
  14.1 39.7 %copy-start.7 = (f32[3,64,640]{2,1,0:T(8,128)}, f32[3,64,640]{2,1,0:T(8,128)S(1)}, u32[]{:S(2)}) copy-start(f32[3,64,640]{2,1,0:T(8,128)S(1)} %get-tuple-element.37.d3) | copy-start | bytes 1474564
  14.1 39.7 %copy-start.11 = (f32[3,40,512]{2,1,0:T(8,128)}, f32[3,40,512]{2,1,0:T(8,128)S(1)}, u32[]{:S(2)}) copy-start(f32[3,40,512]{2,1,0:T(8,128)S(1)} %get-tuple-element.38.d4) | copy-start | bytes 737284
  14.1 83.7 %collective-permute-start.7 = (bf16[240,1152]{1,0:T(8,128)(2,1)}, bf16[240,1152]{1,0:T(8,128)(2,1)S(1)}, u32[]{:S(2)}, u32[]{:S(2)}) collective-permute-start(bf16[240,1152]{1,0:T(8,128)(2,1)} %get-tuple-element.39), channel_id=1, source_target_pairs={{0,2},{2,0},{4,6},{6,4},{8,10},{10,8},{12,14},{14,12},{1,3},{3,1},... | collective-permute-start | bytes 1658888 | tf_op jit(solution)/shard_map/ppermute | solution.py:762
  16.7 81.1 %collective-permute-start.8 = (bf16[240,1152]{1,0:T(8,128)(2,1)}, bf16[240,1152]{1,0:T(8,128)(2,1)}, u32[]{:S(2)}, u32[]{:S(2)}) collective-permute-start(bf16[240,1152]{1,0:T(8,128)(2,1)} %get-tuple-element.40), channel_id=1, source_target_pairs={{0,14},{2,4},{4,2},{6,8},{8,6},{10,12},{12,10},{14,0},{1,15},{3,5}... | collective-permute-start | bytes 1658888 | tf_op jit(solution)/shard_map/ppermute | solution.py:763
  20.3 42.5 %collective-permute-start.11 = (bf16[48,384]{1,0:T(8,128)(2,1)S(1)}, bf16[48,384]{1,0:T(8,128)(2,1)S(1)}, u32[]{:S(2)}, u32[]{:S(2)}) collective-permute-start(bf16[48,384]{1,0:T(8,128)(2,1)S(1)} %get-tuple-element.43), channel_id=1, source_target_pairs={{0,6},{2,8},{4,10},{6,12},{8,14},{10,0},{12,2},{14,4},{1,7},{3,9},... | collective-permute-start | bytes 110600 | tf_op jit(solution)/shard_map/ppermute | solution.py:670
  20.8 23.8 %collective-permute-start.1 = (f32[40,512]{1,0:T(8,128)S(1)}, f32[40,512]{1,0:T(8,128)S(1)}, u32[]{:S(2)}, u32[]{:S(2)}) collective-permute-start(f32[40,512]{1,0:T(8,128)S(1)} %get-tuple-element.25), channel_id=1, source_target_pairs={{0,2},{2,0},{4,6},{6,4},{8,10},{10,8},{12,14},{14,12},{1,3},{3,1},... | collective-permute-start | bytes 245768 | tf_op jit(solution)/shard_map/ppermute | solution.py:747
  44.6 4.8 %collective-permute-start.2 = (f32[40,640]{1,0:T(8,128)S(1)}, f32[40,640]{1,0:T(8,128)S(1)}, u32[]{:S(2)}, u32[]{:S(2)}) collective-permute-start(f32[40,640]{1,0:T(8,128)S(1)} %pad_add_fusion.2), channel_id=1, source_target_pairs={{0,4},{2,6},{4,0},{6,2},{8,12},{10,14},{12,8},{14,10},{1,5},{3,7},... | collective-permute-start | bytes 307208 | tf_op jit(solution)/shard_map/ppermute | solution.py:747
  49.4 8.8 %collective-permute-start.3 = (f32[40,896]{1,0:T(8,128)S(1)}, f32[40,896]{1,0:T(8,128)S(1)}, u32[]{:S(2)}, u32[]{:S(2)}) collective-permute-start(f32[40,896]{1,0:T(8,128)S(1)} %pad_add_fusion), channel_id=1, source_target_pairs={{0,8},{2,10},{4,12},{6,14},{8,0},{10,2},{12,4},{14,6},{1,9},{3,11}... | collective-permute-start | bytes 430088 | tf_op jit(solution)/shard_map/ppermute | solution.py:747
  52.3 22.1 %collective-permute-start.5 = (bf16[496,512]{1,0:T(8,128)(2,1)S(1)}, bf16[496,512]{1,0:T(8,128)(2,1)S(1)}, u32[]{:S(2)}, u32[]{:S(2)}) collective-permute-start(bf16[496,512]{1,0:T(8,128)(2,1)S(1)} %pad_maximum_fusion), channel_id=1, source_target_pairs={{0,2},{2,0},{4,6},{6,4},{8,10},{10,8},{12,14},{14,12},{1,3},{3,1},... | collective-permute-start | bytes 1523720 | tf_op jit(solution)/shard_map/ppermute | solution.py:688
  58.2 19.7 %collective-permute-start.6 = (bf16[496,512]{1,0:T(8,128)(2,1)S(1)}, bf16[496,512]{1,0:T(8,128)(2,1)S(1)}, u32[]{:S(2)}, u32[]{:S(2)}) collective-permute-start(bf16[496,512]{1,0:T(8,128)(2,1)S(1)} %pad_maximum_fusion.1), channel_id=1, source_target_pairs={{0,14},{2,4},{4,2},{6,8},{8,6},{10,12},{12,10},{14,0},{1,15},{3,5}... | collective-permute-start | bytes 1523720 | tf_op jit(solution)/shard_map/ppermute | solution.py:689
  62.8 1.3 %collective-permute-start.4 = (bf16[29,1024]{1,0:T(8,128)(2,1)S(1)}, bf16[29,1024]{1,0:T(8,128)(2,1)S(1)}, u32[]{:S(2)}, u32[]{:S(2)}) collective-permute-start(bf16[29,1024]{1,0:T(8,128)(2,1)S(1)} %pad_maximum_fusion.3), channel_id=1, source_target_pairs={{0,1},{1,0},{2,3},{3,2},{4,5},{5,4},{6,7},{7,6},{8,9},{9,8},{10,11... | collective-permute-start | bytes 178184 | tf_op jit(solution)/shard_map/ppermute | solution.py:759
  64.1 33.7 %collective-permute-start.10 = (bf16[112,768]{1,0:T(8,128)(2,1)}, bf16[112,768]{1,0:T(8,128)(2,1)}, u32[]{:S(2)}, u32[]{:S(2)}) collective-permute-start(bf16[112,768]{1,0:T(8,128)(2,1)} %get-tuple-element.42), channel_id=1, source_target_pairs={{0,12},{2,14},{4,0},{6,2},{8,4},{10,6},{12,8},{14,10},{1,13},{3,15... | collective-permute-start | bytes 516104 | tf_op jit(solution)/shard_map/ppermute | solution.py:670
  74.4 0.8 copy-start.3
  75.2 22.7 %collective-permute-start.9 = (bf16[112,768]{1,0:T(8,128)(2,1)}, bf16[112,768]{1,0:T(8,128)(2,1)}, u32[]{:S(2)}, u32[]{:S(2)}) collective-permute-start(bf16[112,768]{1,0:T(8,128)(2,1)} %get-tuple-element.41), channel_id=1, source_target_pairs={{0,4},{2,6},{4,8},{6,10},{8,12},{10,14},{12,0},{14,2},{1,5},{3,7},... | collective-permute-start | bytes 516104 | tf_op jit(solution)/shard_map/ppermute | solution.py:670
  77.9 0.8 copy-start.5
  78.7 19.1 %collective-permute-start.12 = (bf16[48,384]{1,0:T(8,128)(2,1)}, bf16[48,384]{1,0:T(8,128)(2,1)S(1)}, u32[]{:S(2)}, u32[]{:S(2)}) collective-permute-start(bf16[48,384]{1,0:T(8,128)(2,1)} %get-tuple-element.44), channel_id=1, source_target_pairs={{0,10},{2,12},{4,14},{6,0},{8,2},{10,4},{12,6},{14,8},{1,11},{3,13... | collective-permute-start | bytes 110600 | tf_op jit(solution)/shard_map/ppermute | solution.py:670
  80.5 0.9 copy-start.10
  81.4 0.9 copy-start.15
  82.3 0.8 copy-start.19
  83.1 0.8 copy-start.21
  83.8 0.7 copy-start.23
  84.5 0.7 copy-start.24
  90.4 1.0 copy-start.4
  91.4 1.0 copy-start.6
  92.5 0.7 copy-start.22
  93.1 4.7 %copy-start.2 = (f32[3,128,896]{2,1,0:T(8,128)S(1)}, f32[3,128,896]{2,1,0:T(8,128)}, u32[]{:S(2)}) copy-start(f32[3,128,896]{2,1,0:T(8,128)} %copy-done.1) | copy-start | bytes 4128772
  93.1 4.7 %copy-start.8 = (f32[3,64,640]{2,1,0:T(8,128)S(1)}, f32[3,64,640]{2,1,0:T(8,128)}, u32[]{:S(2)}) copy-start(f32[3,64,640]{2,1,0:T(8,128)} %copy-done.7) | copy-start | bytes 1474564
  93.1 4.7 %copy-start.12 = (f32[3,40,512]{2,1,0:T(8,128)S(1)}, f32[3,40,512]{2,1,0:T(8,128)}, u32[]{:S(2)}) copy-start(f32[3,40,512]{2,1,0:T(8,128)} %copy-done.11) | copy-start | bytes 737284

commit v3 on v2

--- a/solution.py
+++ b/solution.py
@@ -257,7 +257,10 @@
 
     def body(c, carry):
         row = pl.multiple_of(c * step, step)
-        g = [jnp.broadcast_to(gain[b : b + 1, :], (step, LANES)) for b in range(3)]
+        g = []
+        for b in range(3):
+            one = gain[level - 1, b : b + 1, :]
+            g.append(jnp.broadcast_to(jnp.concatenate([one, one], 1), (step, LANES)))
         _, high = analysis(columns(lo, row + skip, step), source_start, left)
         for q in range(pairs):
             put(bands, row, q, high(first + 2 * q) * g[0], (0,))
@@ -270,12 +273,11 @@
     lax.fori_loop(0, rows // step, body, 0)
 
 
-def coarse_kernel(geo, lats, place, edge, x, *refs):
-    lat = place[0]
-    weights, copies_of = refs[:4], refs[4:8]
-    g1, lo2, g2, lo3, g3, lo4, ll4, ext, la, gh, gl, sems, weight_sems = refs[8:]
-    for i in range(4):
-        pltpu.make_async_copy(weights[i], copies_of[i], weight_sems.at[i]).start()
+def analysis_kernel(geo, lats, place, edge, gain, x, *refs):
+    lat, parity = place[0], place[1] % 2
+    ll4, out2, out3, out4, send_e, send_o, p2, m2, p3, m3 = refs[:10]
+    ext, la, g1, gh, gl, lo2, g2, lo3, g3, lo4, hi2, hi3, hi4, d2, d3, d4, sems, out_sems = refs[10:]
+    outs = {2: (d2, out2), 3: (d3, out3), 4: (d4, out4)}
     rows = geo.rows[0]
     start, count = geo.low[1]
     width = x.shape[1]
@@ -327,12 +329,126 @@
         matrix = masked_rows(matrix, geo.low[level][0], geo.rows[level], lat, lats)
         lo[...] = dot3(matrix, vh, vl)
         low_rows(geo, level, lo, geo.span[level - 1][0], target)
-    for i in range(4):
-        pltpu.make_async_copy(weights[i], copies_of[i], weight_sems.at[i]).wait()
-
-
-def first_bands_kernel(geo, lats, place, edge, side_e, side_o, gain, x, d1, ext, la, ha, sem):
-    lat, parity = place[0], place[1]
+    copies = []
+    for level, lo, hi in ((2, lo2, hi2), (3, lo3, hi3), (4, lo4, hi4)):
+        deep_bands(geo, lats, lat, level, {2: (gh, gl), 3: g2, 4: g3}[level], lo, hi, gain, outs[level][0])
+        copies.append(pltpu.make_async_copy(*outs[level], out_sems.at[level - 2]))
+        copies[-1].start()
+    d = {2: d2, 3: d3, 4: d4}
+
+    def fill(distance, to_left, to_right):
+        for level, count, row in exchange_plan(geo)[distance]:
+            n = geo.band[level][1]
+            move = distance * geo.cells[level] // 2
+            for b in range(3):
+                lanes = slice(b * count * LANES, (b + 1) * count * LANES)
+                to_left[row : row + n, lanes] = d[level][b, :, 0 : count * LANES].astype(BF16)
+                to_right[row : row + n, lanes] = d[level][
+                    b, :, move * LANES : (move + count) * LANES
+                ].astype(BF16)
+
+    @pl.when(parity == 0)
+    def _():
+        fill(1, send_o, send_e)
+
+    @pl.when(parity != 0)
+    def _():
+        fill(1, send_e, send_o)
+
+    fill(2, m2, p2)
+    fill(3, m3, p3)
+    for copy in copies:
+        copy.wait()
+
+
+def deep_bands(geo, lats, lat, level, source, lo, hi, gain, bands):
+    start, count = geo.band[level]
+    in_start = geo.low[level - 1][0]
+    parts = 2 if level == 2 else 1
+    half = count // parts
+    for b in range(parts):
+        if parts == 1:
+            at, size = 0, source.shape[0]
+            vh, vl = two_terms(source[...])
+        else:
+            at = (2 * (start + half * b) - 3 - in_start) // 16 * 16
+            size = 2 * half + 16
+            vh, vl = source[0][at : at + size, :], source[1][at : at + size, :]
+        matrix = analysis_matrix(HIGH, start + half * b, half, in_start + at, size)
+        matrix = masked_rows(matrix, start + half * b, geo.rows[level], lat, lats)
+        hi[half * b : half * (b + 1), :] = dot3(matrix, vh, vl)
+    skip = start - geo.low[level][0]
+    band_rows(geo, level, lo, skip, hi, geo.span[level - 1][0], gain, bands)
+
+
+def sides_kernel(place, edge, x, side_e, side_o, sems):
+    lat, parity = place[0], place[1] % 2
+    rows, width = x.shape
+    lanes = SIDE * C
+    own = pl.ds(NEAR, rows)
+
+    def fill(side, begin, sem):
+        copy = pltpu.make_async_copy(x.at[:, pl.ds(begin, lanes)], side.at[own, :], sem)
+        copy.start()
+        cols = slice(begin, begin + lanes)
+
+        @pl.when(lat == 0)
+        def _():
+            side[0:NEAR, :] = jnp.zeros((NEAR, lanes), BF16)
+            side[NEAR + rows :, :] = edge[0:NEAR, cols]
+
+        @pl.when(lat != 0)
+        def _():
+            side[0:NEAR, :] = edge[HALO - NEAR :, cols]
+            side[NEAR + rows :, :] = jnp.zeros((NEAR, lanes), BF16)
+
+        return copy
+
+    def both(low, high):
+        one, two = fill(low, 0, sems.at[0]), fill(high, width - lanes, sems.at[1])
+        one.wait()
+        two.wait()
+
+    @pl.when(parity == 0)
+    def _():
+        both(side_o, side_e)
+
+    @pl.when(parity != 0)
+    def _():
+        both(side_e, side_o)
+
+
+def merge_kernel(size, more, place, mine, other, out):
+    width = mine.shape[1]
+
+    def add(lower, upper):
+        out[:, 0:more] = lower[:, 0:more]
+        out[:, more:width] = lower[:, more:] + upper[:, 0 : width - more]
+        out[:, width:] = upper[:, width - more :]
+
+    lower_half = (place[1] // size) % 2 == 0
+
+    @pl.when(lower_half)
+    def _():
+        add(mine, other)
+
+    @pl.when(jnp.logical_not(lower_half))
+    def _():
+        add(other, mine)
+
+
+def last_merge_kernel(geo, size, more, place, mine, other, ring, tokens, merged):
+    merge_kernel(size, more, place, mine, other, merged)
+    around = ring.shape[1]
+    fold = merged.shape[1] - around
+    ring[:, 0:fold] = merged[:, 0:fold] + merged[:, around:]
+    ring[:, fold:] = merged[:, fold:around]
+    skip = -geo.low[4][0]
+    tokens[...] = ring[skip : skip + geo.rows[4], :].astype(BF16)
+
+
+def first_bands_kernel(geo, lats, place, edge, side_e, side_o, gain, x, held, ext, la, ha, d1, sem):
+    lat, parity = place[0], place[1] % 2
     rows, width = x.shape
     lanes = SIDE * C
     copy = pltpu.make_async_copy(x, ext.at[pl.ds(NEAR, rows), pl.ds(lanes, width)], sem)
@@ -369,56 +485,9 @@
             mh, ml = two_terms(masked_rows(matrix, start + 120 * b, geo.rows[1], lat, lats))
             out[120 * b : 120 * b + 120, :] = mxu(mh, data) + mxu(ml, data)
     band_rows(geo, 1, la, 0, ha, -SIDE, gain, d1)
-
-
-def deep_kernel(geo, lats, place, gain, *refs):
-    lat, parity = place[0], place[1]
-    g1, lo2, g2, lo3, g3, lo4 = refs[:6]
-    d = {2: refs[6], 3: refs[7], 4: refs[8]}
-    send_e, send_o, p2, m2, p3, m3, hi2, hi3, hi4 = refs[9:]
-    grids = {1: g1, 2: g2, 3: g3}
-    los, his = {2: lo2, 3: lo3, 4: lo4}, {2: hi2, 3: hi3, 4: hi4}
-    for level in (2, 3, 4):
-        start, count = geo.band[level]
-        source, in_start = grids[level - 1], geo.low[level - 1][0]
-        parts = 2 if level == 2 else 1
-        half = count // parts
-        for b in range(parts):
-            if parts == 1:
-                at, size = 0, source.shape[0]
-            else:
-                at = (2 * (start + half * b) - 3 - in_start) // 16 * 16
-                size = 2 * half + 16
-            vh, vl = two_terms(source[at : at + size, :])
-            matrix = analysis_matrix(HIGH, start + half * b, half, in_start + at, size)
-            matrix = masked_rows(matrix, start + half * b, geo.rows[level], lat, lats)
-            his[level][half * b : half * (b + 1), :] = dot3(matrix, vh, vl)
-        rows = gain[3 * (level - 2) : 3 * (level - 2) + 3, :]
-        skip = start - geo.low[level][0]
-        begin = geo.span[level - 1][0]
-        band_rows(geo, level, los[level], skip, his[level], begin, rows, d[level])
-
-    def fill(distance, to_left, to_right):
-        for level, count, row in exchange_plan(geo)[distance]:
-            n = geo.band[level][1]
-            move = distance * geo.cells[level] // 2
-            for b in range(3):
-                lanes = slice(b * count * LANES, (b + 1) * count * LANES)
-                to_left[row : row + n, lanes] = d[level][b, :, 0 : count * LANES].astype(BF16)
-                to_right[row : row + n, lanes] = d[level][
-                    b, :, move * LANES : (move + count) * LANES
-                ].astype(BF16)
-
-    @pl.when(parity == 0)
-    def _():
-        fill(1, send_o, send_e)
-
-    @pl.when(parity != 0)
-    def _():
-        fill(1, send_e, send_o)
-
-    fill(2, m2, p2)
-    fill(3, m3, p3)
+    copy = pltpu.make_async_copy(d1, held, sem)
+    copy.start()
+    copy.wait()
 
 
 def exchange_plan(geo):
@@ -440,11 +509,22 @@
     return (rows, max(count for _, count, _ in entries) * 3 * LANES)
 
 
-def attention_kernel(geo, lats, blocks, place, keys, grid, we, wqkv, scale, wo, gain, wb, out):
-    lat = place[0]
-    rows, width = grid.shape
+def attention_kernel(geo, lats, blocks, place, ring, own, others, we, wqkv, scale, wo, gain, wb, out, around, listed, keys):
+    lat, lon = place[0], place[1]
+    rows, width = out.shape
     cells = width // C
-    field = grid[...]
+    total = ring.shape[1]
+    around[:, 0:total] = ring[...]
+    around[:, total:] = ring[:, 0 : around.shape[1] - total]
+    field = around[:, pl.ds(pl.multiple_of(lon * (geo.cells[4] * C), LANES), width)]
+    count = geo.rows[4]
+    for source, shift in ((own, 0), (others, count)):
+        for pair in range(total // LANES):
+            value = source[:, pair * LANES : (pair + 1) * LANES].astype(F32)
+            for side in range(2):
+                at = 2 * count * (2 * pair + side) + shift
+                listed[at : at + count, :] = value[:, side * C : (side + 1) * C]
+    keys[...] = listed[...].astype(BF16)
     own = jnp.concatenate([field[:, C * c : C * (c + 1)] for c in range(cells)], 0)
     count = own.shape[0]
     embedded = mxu(own.astype(BF16), we[...])
@@ -520,10 +600,16 @@
         out[:, at] = masked_rows(field[:, at] + value, start, geo.rows[4], lat, lats)
 
 
-def synthesis_kernel(geo, lats, place, coarse, d1, d2, d3, d4, *refs):
-    lat, parity = place[0], place[1]
-    e2, o2, from_m2, from_p2, from_m3, from_p3 = refs[:6]
-    out, up3, up2, up1, xh, xl, ylow, yhigh, done, sems = refs[6:]
+def synthesis_kernel(geo, lats, place, coarse, e2, o2, from_m2, from_p2, from_m3, from_p3, *refs):
+    lat, parity = place[0], place[1] % 2
+    held, (out, up3, up2, up1, xh, xl, ylow, yhigh, done), refs = refs[:4], refs[4:13], refs[13:]
+    d1, d2, d3, d4, sems, in_sems = refs
+    arrive = [
+        pltpu.make_async_copy(source, to, in_sems.at[i])
+        for i, (source, to) in enumerate(zip(held, (d1, d2, d3, d4)))
+    ]
+    for level in (4, 3, 2, 1):
+        arrive[level - 1].start()
     bands = {2: d2, 3: d3, 4: d4}
     plan = exchange_plan(geo)
 
@@ -552,6 +638,7 @@
 
     uppers = {4: coarse, 3: up3, 2: up2, 1: up1}
     for level in (4, 3, 2):
+        arrive[level - 1].wait()
         begin, pairs = geo.span[level]
         below = level - 1
         start, rows = geo.band[below]
@@ -581,6 +668,7 @@
 
         lax.fori_loop(0, rows // step, joined, 0)
 
+    arrive[0].wait()
     n = geo.band[1][1]
     half = geo.rows[0] // 2
     for block in range(2):
@@ -626,18 +714,19 @@
         store(whole, rest).wait()
 
 
-def call(kernel, out_shape, scratch, *args, cost=20_000_000, grant=24, raw=(), raw_out=False):
+def call(kernel, out_shape, scratch, *args, cost=20_000_000, grant=24, raw=(), raw_out=()):
     vmem = pl.BlockSpec(memory_space=pltpu.VMEM)
     smem = pl.BlockSpec(memory_space=pltpu.SMEM)
+    anywhere = pl.BlockSpec(memory_space=pl.ANY)
     specs = [smem if a.ndim == 1 and a.size < 16 else vmem for a in args]
     for at in raw:
-        specs[at] = pl.BlockSpec(memory_space=pltpu.HBM)
-    outs = jax.tree.map(lambda _: pl.BlockSpec(memory_space=pl.ANY) if raw_out else vmem, out_shape)
+        specs[at] = anywhere
+    outs = [anywhere if i in raw_out else vmem for i in range(len(out_shape))]
     return pl.pallas_call(
         kernel,
-        out_shape=out_shape,
+        out_shape=tuple(out_shape),
         in_specs=specs,
-        out_specs=outs,
+        out_specs=tuple(outs),
         scratch_shapes=scratch,
         compiler_params=pltpu.CompilerParams(vmem_limit_bytes=grant << 20),
         cost_estimate=pl.CostEstimate(flops=cost, bytes_accessed=1 << 20, transcendentals=0),
@@ -645,7 +734,7 @@
 
 
 def shape(dims, dtype=F32):
-    return pltpu.VMEM(dims, dtype)
+    return jax.ShapeDtypeStruct(dims, dtype)
 
 
 def per_device(mesh_shape, state_field, skip_gain, embed_weight, qkv_weight, head_scale, out_weight, norm_gain, back_weight):
@@ -659,8 +748,7 @@
     rows, width = state_field.shape
     geo = Geometry(rows, width // C)
     lat, lon = lax.axis_index("lat"), lax.axis_index("lon")
-    place = jnp.stack([lat, lon % 2]).astype(jnp.int32)
-    gains = jnp.concatenate([skip_gain, skip_gain], 2).reshape(-1, LANES)
+    place = jnp.stack([lat, lon]).astype(jnp.int32)
 
     even_pairs = [(i, i ^ 1) for i in range(lons)]
     odd_pairs = [(i, (i + 1 if i % 2 else i - 1) % lons) for i in range(lons)]
@@ -669,126 +757,134 @@
     def shifted(value, by):
         return lax.ppermute(value, "lon", [(i, (i + by) % lons) for i in range(lons)])
 
-    edge = jnp.where(lat == 0, state_field[rows - HALO :], state_field[:HALO])
+    edge = lax.dynamic_slice(
+        state_field, (jnp.where(lat == 0, rows - HALO, 0), 0), (HALO, width)
+    )
     edge = lax.ppermute(edge, "lat", swap)
 
-    even_lon = lon % 2 == 0
     wide = SIDE * C
-
-    def beside(value, first):
-        return jnp.where(first, value[:, width - wide :], value[:, :wide])
-
-    def with_rows(first):
-        near = beside(edge, first)
-        none = jnp.zeros((NEAR, wide), BF16)
-        top = jnp.where(lat == 0, none, near[HALO - NEAR :])
-        bottom = jnp.where(lat == 0, near[:NEAR], none)
-        return jnp.concatenate([top, beside(state_field, first), bottom], 0)
-
-    side_e = lax.ppermute(with_rows(even_lon), "lon", even_pairs)
-    side_o = lax.ppermute(with_rows(~even_lon), "lon", odd_pairs)
+    extended = NEAR + rows + NEAR
+    side_e, side_o = call(
+        sides_kernel,
+        [shape((extended, wide), BF16)] * 2,
+        [pltpu.SemaphoreType.DMA((2,))],
+        place,
+        edge,
+        state_field,
+        raw=(2,),
+        cost=1_000_000,
+    )
+    side_e = lax.ppermute(side_e, "lon", even_pairs)
+    side_o = lax.ppermute(side_o, "lon", odd_pairs)
 
     w = [None] + [geo.span[level][1] * LANES for level in (1, 2, 3, 4)]
-    weights = (embed_weight, qkv_weight, out_weight, back_weight.T)
-    low = lambda level, lanes: shape((geo.low[level][1], w[lanes]))
-    *weights, g1, lo2, g2, lo3, g3, lo4, ll4 = call(
-        functools.partial(coarse_kernel, geo, lats),
-        tuple(shape(a.shape, BF16) for a in weights)
-        + (low(1, 1), low(2, 1), low(2, 2), low(3, 2), low(3, 3), low(4, 3), low(4, 4)),
+    low = lambda level, lanes: pltpu.VMEM((geo.low[level][1], w[lanes]), F32)
+    bands = [(3, geo.band[level][1], w[level]) for level in (1, 2, 3, 4)]
+    ll4, d2, d3, d4, deep_e, deep_o, p2, m2, p3, m3 = call(
+        functools.partial(analysis_kernel, geo, lats),
+        [shape((geo.low[4][1], w[4]))]
+        + [shape(dims) for dims in bands[1:]]
+        + [shape(plan_shape(geo, d), BF16) for d in (1, 1, 2, 2, 3, 3)],
         [
             pltpu.VMEM((geo.extended, width), BF16),
             pltpu.VMEM((geo.low[1][1], width), F32),
+            low(1, 1),
             pltpu.VMEM((geo.low[1][1], w[1]), BF16),
             pltpu.VMEM((geo.low[1][1], w[1]), BF16),
+            low(2, 1),
+            low(2, 2),
+            low(3, 2),
+            low(3, 3),
+            low(4, 3),
+        ]
+        + [pltpu.VMEM((geo.band[level][1], w[level - 1]), F32) for level in (2, 3, 4)]
+        + [pltpu.VMEM(dims, F32) for dims in bands[1:]]
+        + [
             pltpu.SemaphoreType.DMA((geo.low[1][1] // 112,)),
-            pltpu.SemaphoreType.DMA((4,)),
+            pltpu.SemaphoreType.DMA((3,)),
         ],
         place,
         edge,
+        skip_gain,
         state_field,
-        *weights,
-        raw=(2, 3, 4, 5, 6),
+        raw=(3,),
+        raw_out=(1, 2, 3),
     )
-    extended = NEAR + rows + NEAR
-    d1 = call(
+    (d1,) = call(
         functools.partial(first_bands_kernel, geo, lats),
-        shape((3, geo.band[1][1], w[1])),
+        [shape(bands[0])],
         [
             pltpu.VMEM((extended, width + 2 * wide), BF16),
             pltpu.VMEM((geo.band[1][1], width + 2 * wide), F32),
             pltpu.VMEM((geo.band[1][1], width + 2 * wide), F32),
+            pltpu.VMEM(bands[0], F32),
             pltpu.SemaphoreType.DMA,
         ],
         place,
         edge,
         side_e,
         side_o,
-        gains[:3],
+        skip_gain,
         state_field,
         raw=(5,),
+        raw_out=(0,),
     )
-    d2, d3, d4, deep_e, deep_o, p2, m2, p3, m3 = call(
-        functools.partial(deep_kernel, geo, lats),
-        tuple(shape((3, geo.band[level][1], w[level])) for level in (2, 3, 4))
-        + tuple(shape(plan_shape(geo, d), BF16) for d in (1, 1, 2, 2, 3, 3)),
-        [pltpu.VMEM((geo.band[level][1], w[level - 1]), F32) for level in (2, 3, 4)],
-        place,
-        gains[3:],
-        g1,
-        lo2,
-        g2,
-        lo3,
-        g3,
-        lo4,
-    )
 
     merged, size = ll4, 1
+    total = geo.cells[4] * lons * C
     while size < lons:
         other = lax.ppermute(merged, "lon", [(i, i ^ size) for i in range(lons)])
-        lower_half = (lon // size) % 2 == 0
-        lower = jnp.where(lower_half, merged, other)
-        upper = jnp.where(lower_half, other, merged)
         more = geo.cells[4] * C * size
-        merged = jnp.pad(lower, ((0, 0), (0, more))) + jnp.pad(upper, ((0, 0), (more, 0)))
+        dims = (merged.shape[0], merged.shape[1] + more)
+        if 2 * size < lons:
+            (merged,) = call(
+                functools.partial(merge_kernel, size, more), [shape(dims)], [], place, merged, other, cost=100_000
+            )
+        else:
+            ring, tokens = call(
+                functools.partial(last_merge_kernel, geo, size, more),
+                [shape((dims[0], total)), shape((geo.rows[4], total), BF16)],
+                [pltpu.VMEM(dims, F32)],
+                place,
+                merged,
+                other,
+                cost=100_000,
+            )
         size = 2 * size
-    around = geo.cells[4] * lons * C
-    fold = 6 * C
-    ring = jnp.concatenate([merged[:, :fold] + merged[:, around:], merged[:, fold:around]], 1)
-    skip = -geo.low[4][0]
-    tokens = ring[skip : skip + geo.rows[4]].astype(BF16)
     others = lax.ppermute(tokens, "lat", swap)
-    keys = jnp.concatenate([tokens, others], 0).reshape(-1, C)
 
     deep_e = lax.ppermute(deep_e, "lon", even_pairs)
     deep_o = lax.ppermute(deep_o, "lon", odd_pairs)
     from_m2, from_p2 = shifted(p2, 2), shifted(m2, -2)
     from_m3, from_p3 = shifted(p3, 3), shifted(m3, -3)
 
-    own = lax.dynamic_slice(
-        jnp.concatenate([ring, ring[:, :fold]], 1),
-        (0, lon * geo.cells[4] * C),
-        (geo.low[4][1], geo.span[4][1] * LANES),
+    key_count = 2 * geo.rows[4] * geo.cells[4] * lons
+    blocks = key_count // 928 if key_count % 928 == 0 else 1
+    (coarse,) = call(
+        functools.partial(attention_kernel, geo, lats, blocks),
+        [shape((geo.low[4][1], w[4]))],
+        [
+            pltpu.VMEM((geo.low[4][1], total + 6 * C), F32),
+            pltpu.VMEM((key_count, C), F32),
+            pltpu.VMEM((key_count, C), BF16),
+        ],
+        place,
+        ring,
+        tokens,
+        others,
+        embed_weight,
+        qkv_weight,
+        head_scale,
+        out_weight,
+        norm_gain[None],
+        back_weight.T,
+        cost=200_000_000,
+        grant=40,
     )
-    blocks = max(1, keys.shape[0] // 928) if keys.shape[0] % 928 == 0 else 1
-    coarse = call(
-        functools.partial(attention_kernel, geo, lats, blocks),
-        shape(own.shape),
-        [],
-        place,
-        keys,
-        own,
-        weights[0],
-        weights[1],
-        head_scale,
-        weights[2],
-        norm_gain[None],
-        weights[3],
-        cost=200_000_000,
-    )
-
-    return call(
+
+    (out,) = call(
         functools.partial(synthesis_kernel, geo, lats),
-        jax.ShapeDtypeStruct((rows, width), BF16),
+        [shape((rows, width), BF16)],
         [pltpu.VMEM((geo.band[level][1], w[level]), F32) for level in (3, 2, 1)]
         + [
             pltpu.VMEM((2 * LANES, w[1]), BF16),
@@ -796,22 +892,29 @@
             pltpu.VMEM((rows, w[1]), F32),
             pltpu.VMEM((rows, w[1]), F32),
             pltpu.VMEM((rows, width), BF16),
+        ]
+        + [pltpu.VMEM(dims, F32) for dims in bands]
+        + [
             pltpu.SemaphoreType.DMA((rows // 112 + 1,)),
+            pltpu.SemaphoreType.DMA((4,)),
         ],
         place,
         coarse,
-        d1,
-        d2,
-        d3,
-        d4,
         deep_e,
         deep_o,
         from_m2,
         from_p2,
         from_m3,
         from_p3,
-        raw_out=True,
+        d1,
+        d2,
+        d3,
+        d4,
+        raw=(8, 9, 10, 11),
+        raw_out=(0,),
+        grant=40,
     )
+    return out
 
 
 def solution(mesh):

time: 115 us -> 98.2 us (0.85); the launches traced: 113 us -> 98.1 us
  local copies, waits for them, and re-layouts: 10.8 us -> 2.6 us
  other arithmetic: 4.96 us -> 0.07 us
  waiting for transfers between devices: 41.3 us -> 38.2 us
  Pallas kernels: 35.1 us -> 37.3 us
    ppermute x2, waiting for transfers between devices: 10.3 us -> 0.01 us  [the longest x1 0.01 us: program(): side_e = lax.ppermute(side_e, 'lon', even_pairs)]
    unnamed x51 -> x19, local copies, waits for them, and re-layouts: 9.7 us -> 1.57 us
    ppermute x4, waiting for transfers between devices: 0.01 us -> 5.02 us  [shifted(): lax.ppermute(value, 'lon', [(i, (i + by) % lons) for i in range(lons)])]
    select_n x7 -> x0, other arithmetic: 2.65 us -> none  [the longest x1 1.31 us: program(): edge = jnp.where(lat == 0, state_field[rows - HALO:], state_field[:HALO])]
    pallas_call x5 -> x8, Pallas kernels: 35.1 us -> 37.3 us  [call(): pl.pallas_call(kernel, out_shape=tuple(out_shape), in_specs=specs, out_sp...]
    ppermute x2, starting transfers between devices: 6.11 us -> 3.89 us  [the longest x1 2.91 us: program(): side_e = lax.ppermute(side_e, 'lon', even_pairs)]
    concatenate x6 -> x0, other arithmetic: 1.51 us -> none  [the longest x1 0.69 us: program(): keys = jnp.concatenate([tokens, others], 0).reshape(-1, C)]
    ppermute x4, starting transfers between devices: 2.56 us -> 3.96 us  [shifted(): lax.ppermute(value, 'lon', [(i, (i + by) % lons) for i in range(lons)])]
  transfers between devices with their start and end apart: 13 -> 13, of which waited for: 5 -> 6; matrix products, arithmetic and copies ran while one was open for 5% -> 0% of each run, Pallas kernels for 9% -> 21%
where the time goes in v3:
time: 98.2 us; the launch traced here: 98.1 us
  waiting for transfers between devices  38.2 us (39%)
  Pallas kernels  37.3 us (38%)
  starting transfers between devices  19.5 us (20%)
  local copies, waits for them, and re-layouts  2.6 us (3%)
    pallas_call x8, Pallas kernels, call(): pl.pallas_call(kernel, out_shape=tuple(out_shape), in_specs=specs, out_sp...  37.3 us
    ppermute x3, waiting for transfers between devices, program(): other = lax.ppermute(merged, 'lon', [(i, i ^ size) for i in range(lons)])  30.6 us
    ppermute x3, starting transfers between devices, program(): other = lax.ppermute(merged, 'lon', [(i, i ^ size) for i in range(lons)])  6.01 us
    ppermute x4, waiting for transfers between devices, shifted(): lax.ppermute(value, 'lon', [(i, (i + by) % lons) for i in range(lons)])  5.02 us
    ppermute x4, starting transfers between devices, shifted(): lax.ppermute(value, 'lon', [(i, (i + by) % lons) for i in range(lons)])  3.96 us
    ppermute x1, starting transfers between devices, program(): deep_o = lax.ppermute(deep_o, 'lon', odd_pairs)  3.75 us
    ppermute x1, starting transfers between devices, program(): side_e = lax.ppermute(side_e, 'lon', even_pairs)  2.91 us
  transfers between devices with their start and end apart: 13, of which 6 were waited for; matrix products, arithmetic and copies ran while one was open for 0% of the time, Pallas kernels for 21%

profile of v3, /device:TPU:0, one launch (start us, length us, event | category | flops | bytes accessed | tf_op | source)
XLA Modules:
  0.0 98.1 jit_solution(18293415074392027596)
XLA Ops:
  0.0 1.0 %constant_dynamic-slice_fusion = bf16[96,2048]{1,0:T(8,128)(2,1)S(1)} fusion(bf16[464,2048]{1,0:T(8,128)(2,1)} %x.5, s32[]{:T(128)S(6)} %select_n.5), kind=kLoop, calls=%fused_computation.1 | loop fusion | bytes 786436 | tf_op jit(solution)/shard_map/dynamic_slice | solution.py:760
  1.0 0.6 collective-permute-start
  1.6 0.1 pad_add_fusion.place
  1.7 1.3 %collective-permute-done.edge = bf16[96,2048]{1,0:T(8,128)(2,1)S(1)} collective-permute-done((bf16[96,2048]{1,0:T(8,128)(2,1)S(1)}, bf16[96,2048]{1,0:T(8,128)(2,1)S(1)}, u32[]{:S(2)}, u32[]{:S(2)}) %collective-permute-start) | collective-permute-done | bytes 393248 | tf_op jit(solution)/shard_map/ppermute | solution.py:763
  3.0 1.5 %copy-done = bf16[464,2048]{1,0:T(8,128)(2,1)S(1)} copy-done((bf16[464,2048]{1,0:T(8,128)(2,1)S(1)}, bf16[464,2048]{1,0:T(8,128)(2,1)}, u32[]{:S(2)}) %copy-start) | copy-done | bytes 1900568
  4.5 0.7 shard_map.87
  5.1 0.0 copy-start.2
  5.1 0.0 copy-start.3
  5.2 0.0 copy-start.4
  5.2 0.0 copy-start.5
  5.2 0.0 copy-start.6
  5.2 0.0 copy-start.7
  5.2 2.9 %collective-permute-start.11 = (bf16[496,512]{1,0:T(8,128)(2,1)S(1)}, bf16[496,512]{1,0:T(8,128)(2,1)S(1)}, u32[]{:S(2)}, u32[]{:S(2)}) collective-permute-start(bf16[496,512]{1,0:T(8,128)(2,1)S(1)} %get-tuple-element.28), channel_id=1, source_target_pairs={{0,2},{2,0},{4,6},{6,4},{8,10},{10,8},{12,14},{14,12},{1,3},{3,1},... | collective-permute-start | bytes 1523720 | tf_op jit(solution)/shard_map/ppermute | solution.py:777
  8.1 0.0 copy-done.8
  8.1 0.0 copy-done.1
  8.1 8.6 %shard_map.82 = (f32[40,512]{1,0:T(8,128)S(1)}, f32[3,128,896]{2,1,0:T(8,128)S(1)}, f32[3,64,640]{2,1,0:T(8,128)S(1)}, f32[3,40,512]{2,1,0:T(8,128)S(1)}, bf16[2...) custom-call(s32[2]{0:T(128)S(1)} %pad_add_fusion.place, ...), custom_call_target="tpu_custom_call" | custom-call | flops 20000000 | bytes 1048576 | tf_op jit(solution)/shard_map/pallas_call | solution.py:725
  16.7 0.8 collective-permute-start.1
  17.5 1.3 %collective-permute-start.5 = (bf16[240,1152]{1,0:T(8,128)(2,1)S(1)}, bf16[240,1152]{1,0:T(8,128)(2,1)S(1)}, u32[]{:S(2)}, u32[]{:S(2)}) collective-permute-start(bf16[240,1152]{1,0:T(8,128)(2,1)S(1)} %get-tuple-element.22), channel_id=1, source_target_pairs={{0,2},{2,0},{4,6},{6,4},{8,10},{10,8},{12,14},{14,12},{1,3},{3,1},... | collective-permute-start | bytes 1658888 | tf_op jit(solution)/shard_map/ppermute | solution.py:856
  18.8 3.7 %collective-permute-start.6 = (bf16[240,1152]{1,0:T(8,128)(2,1)S(1)}, bf16[240,1152]{1,0:T(8,128)(2,1)S(1)}, u32[]{:S(2)}, u32[]{:S(2)}) collective-permute-start(bf16[240,1152]{1,0:T(8,128)(2,1)S(1)} %get-tuple-element.23), channel_id=1, source_target_pairs={{0,14},{2,4},{4,2},{6,8},{8,6},{10,12},{12,10},{14,0},{1,15},{3,5}... | collective-permute-start | bytes 1658888 | tf_op jit(solution)/shard_map/ppermute | solution.py:857
  22.5 1.0 collective-permute-start.12
  23.5 20.9 %collective-permute-done.1.other = f32[40,512]{1,0:T(8,128)S(1)} collective-permute-done((f32[40,512]{1,0:T(8,128)S(1)}, f32[40,512]{1,0:T(8,128)S(1)}, u32[]{:S(2)}, u32[]{:S(2)}) %collective-permute-start.1) | collective-permute-done | bytes 81952 | tf_op jit(solution)/shard_map/ppermute | solution.py:836
  44.4 0.6 shard_map.83.mine
  45.0 2.8 %collective-permute-start.2 = (f32[40,640]{1,0:T(8,128)S(1)}, f32[40,640]{1,0:T(8,128)S(1)}, u32[]{:S(2)}, u32[]{:S(2)}) collective-permute-start(f32[40,640]{1,0:T(8,128)S(1)} %shard_map.83.mine), channel_id=1, source_target_pairs={{0,4},{2,6},{4,0},{6,2},{8,12},{10,14},{12,8},{14,10},{1,5},{3,7},... | collective-permute-start | bytes 307208 | tf_op jit(solution)/shard_map/ppermute | solution.py:836
  47.8 4.2 %collective-permute-done.2.other = f32[40,640]{1,0:T(8,128)S(1)} collective-permute-done((f32[40,640]{1,0:T(8,128)S(1)}, f32[40,640]{1,0:T(8,128)S(1)}, u32[]{:S(2)}, u32[]{:S(2)}) %collective-permute-start.2) | collective-permute-done | bytes 102432 | tf_op jit(solution)/shard_map/ppermute | solution.py:836
  52.0 0.6 shard_map.84.mine
  52.5 2.5 %collective-permute-start.3 = (f32[40,896]{1,0:T(8,128)S(1)}, f32[40,896]{1,0:T(8,128)S(1)}, u32[]{:S(2)}, u32[]{:S(2)}) collective-permute-start(f32[40,896]{1,0:T(8,128)S(1)} %shard_map.84.mine), channel_id=1, source_target_pairs={{0,8},{2,10},{4,12},{6,14},{8,0},{10,2},{12,4},{14,6},{1,9},{3,11}... | collective-permute-start | bytes 430088 | tf_op jit(solution)/shard_map/ppermute | solution.py:836
  55.0 5.5 %collective-permute-done.3.other = f32[40,896]{1,0:T(8,128)S(1)} collective-permute-done((f32[40,896]{1,0:T(8,128)S(1)}, f32[40,896]{1,0:T(8,128)S(1)}, u32[]{:S(2)}, u32[]{:S(2)}) %collective-permute-start.3) | collective-permute-done | bytes 143392 | tf_op jit(solution)/shard_map/ppermute | solution.py:836
  60.5 0.1 collective-permute-start.9
  60.7 0.6 shard_map.85
  61.3 5.0 %collective-permute-done.9.from_m3 = bf16[48,384]{1,0:T(8,128)(2,1)S(1)} collective-permute-done((bf16[48,384]{1,0:T(8,128)(2,1)S(1)}, bf16[48,384]{1,0:T(8,128)(2,1)S(1)}, u32[]{:S(2)}, u32[]{:S(2)}) %collective-permute-start.9) | collective-permute-done | bytes 36896 | tf_op jit(solution)/shard_map/ppermute | solution.py:758
  66.3 0.0 collective-permute-start.4
  66.3 1.3 %collective-permute-done.4.others = bf16[29,1024]{1,0:T(8,128)(2,1)S(1)} collective-permute-done((bf16[29,1024]{1,0:T(8,128)(2,1)S(1)}, bf16[29,1024]{1,0:T(8,128)(2,1)S(1)}, u32[]{:S(2)}, u32[]{:S(2)}) %collective-permute-start.4) | collective-permute-done | bytes 59424 | tf_op jit(solution)/shard_map/ppermute | solution.py:854
  67.5 0.0 collective-permute-start.7
  67.5 0.0 collective-permute-done.11.side_e
  67.5 3.8 %collective-permute-start.8 = (bf16[112,768]{1,0:T(8,128)(2,1)S(1)}, bf16[112,768]{1,0:T(8,128)(2,1)S(1)}, u32[]{:S(2)}, u32[]{:S(2)}) collective-permute-start(bf16[112,768]{1,0:T(8,128)(2,1)S(1)} %get-tuple-element.25), channel_id=1, source_target_pairs={{0,12},{2,14},{4,0},{6,2},{8,4},{10,6},{12,8},{14,10},{1,13},{3,15... | collective-permute-start | bytes 516104 | tf_op jit(solution)/shard_map/ppermute | solution.py:758
  71.4 0.0 collective-permute-done.12.side_o
  71.4 0.0 collective-permute-start.10
  71.4 0.0 copy-done.2
  71.4 0.0 copy-done.3
  71.4 0.0 copy-done.4
  71.4 5.3 %shard_map.86.coarse = f32[40,512]{1,0:T(8,128)S(1)} custom-call(s32[2]{0:T(128)S(1)} %pad_add_fusion.place, f32[40,1024]{1,0:T(8,128)S(1)} %get-tuple-element.20.ring, bf16[29,1024]{1,0:T(8,128)(2,1)S(1)} %get-tuple-element.21.own, bf16[29,1024]{1,0:T(8,128)(2,1)S(1)} %collective-permute-done.4.others, bf16[64,256]{1,0:T(8,128)(2,1)S(1)} %copy-done.4, ...), custom_call_target="tpu_custom_call" | custom-call | flops 200000000 | bytes 1048576 | tf_op jit(solution)/shard_map/pallas_call | solution.py:725
  76.7 5.0 %shard_map.88.refs_0_ = f32[3,240,1280]{2,1,0:T(8,128)S(1)} custom-call(s32[2]{0:T(128)S(1)} %pad_add_fusion.place, bf16[96,2048]{1,0:T(8,128)(2,1)S(1)} %collective-permute-done.edge, bf16[496,512]{1,0:T(8,128)(2,1)S(1)} %collective-permute-done.11.side_e, bf16[496,512]{1,0:T(8,128)(2,1)S(1)} %collective-permute-done.12.side_o, f32[4,3,64]{2,1,0:T(4,128)S(1)} %copy.9.gain, ...), custom_call_target="tpu_custom_call" | custom-call | flops 20000000 | bytes 1048576 | tf_op jit(solution)/shard_map/pallas_call | solution.py:725
  81.7 0.0 collective-permute-done.10.from_p3
  81.8 0.0 collective-permute-done.7.from_m2
  81.8 0.0 collective-permute-done.8.from_p2
  81.8 0.0 collective-permute-done.5.e2
  81.8 0.0 collective-permute-done.6.o2
  81.8 16.1 %shard_map.89 = bf16[464,2048]{1,0:T(8,128)(2,1)} custom-call(s32[2]{0:T(128)S(1)} %pad_add_fusion.place, f32[40,512]{1,0:T(8,128)S(1)} %shard_map.86.coarse, bf16[240,1152]{1,0:T(8,128)(2,1)S(1)} %collective-permute-done.5.e2, bf16[240,1152]{1,0:T(8,128)(2,1)S(1)} %collective-permute-done.6.o2, bf16[112,768]{1,0:T(8,128)(2,1)S(1)} %collective-permute-done.7.from_m2, ...), custom_call_target="tpu_custom_call" | custom-call | flops 20000000 | bytes 1048576 | tf_op jit(solution)/shard_map/pallas_call | solution.py:725
  (7 shorter events, 0.0 us)
Async XLA Ops:
  0.0 8.1 %copy-start.8 = (f32[4,3,64]{2,0,1:T(4,128)S(1)}, f32[4,3,64]{2,0,1:T(4,128)}, u32[]{:S(2)}) copy-start(f32[4,3,64]{2,0,1:T(4,128)} %param.9) | copy-start | bytes 9220
  1.0 1.9 %collective-permute-start = (bf16[96,2048]{1,0:T(8,128)(2,1)S(1)}, bf16[96,2048]{1,0:T(8,128)(2,1)S(1)}, u32[]{:S(2)}, u32[]{:S(2)}) collective-permute-start(bf16[96,2048]{1,0:T(8,128)(2,1)S(1)} %constant_dynamic-slice_fusion), channel_id=1, source_target_pairs={{0,1},{1,0},{2,3},{3,2},{4,5},{5,4},{6,7},{7,6},{8,9},{9,8},{10,11... | collective-permute-start | bytes 1179656 | tf_op jit(solution)/shard_map/ppermute | solution.py:763
  2.9 1.5 %copy-start = (bf16[464,2048]{1,0:T(8,128)(2,1)S(1)}, bf16[464,2048]{1,0:T(8,128)(2,1)}, u32[]{:S(2)}) copy-start(bf16[464,2048]{1,0:T(8,128)(2,1)} %x.5) | copy-start | bytes 5701636
  4.5 3.7 %copy-start.1 = (bf16[464,2048]{1,0:T(8,128)(2,1)S(1)}, bf16[464,2048]{1,0:T(8,128)(2,1)}, u32[]{:S(2)}) copy-start(bf16[464,2048]{1,0:T(8,128)(2,1)} %x.5) | copy-start | bytes 5701636
  5.1 66.2 %copy-start.2 = (bf16[256,768]{1,0:T(8,128)(2,1)S(1)}, bf16[256,768]{1,0:T(8,128)(2,1)}, u32[]{:S(2)}) copy-start(bf16[256,768]{1,0:T(8,128)(2,1)} %wqkv.1) | copy-start | bytes 1179652
  5.1 66.2 %copy-start.3 = (bf16[256,256]{1,0:T(8,128)(2,1)S(1)}, bf16[256,256]{1,0:T(8,128)(2,1)}, u32[]{:S(2)}) copy-start(bf16[256,256]{1,0:T(8,128)(2,1)} %wo.1) | copy-start | bytes 393220
  5.2 66.2 %copy-start.4 = (bf16[64,256]{1,0:T(8,128)(2,1)S(1)}, bf16[64,256]{1,0:T(8,128)(2,1)}, u32[]{:S(2)}) copy-start(bf16[64,256]{1,0:T(8,128)(2,1)} %we.1) | copy-start | bytes 98308
  5.2 66.2 %copy-start.5 = (bf16[256,64]{0,1:T(8,128)(2,1)S(1)}, bf16[256,64]{0,1:T(8,128)(2,1)}, u32[]{:S(2)}) copy-start(bf16[256,64]{0,1:T(8,128)(2,1)} %param.15) | copy-start | bytes 98308
  5.2 66.2 %copy-start.6 = (f32[256]{0:T(256)S(1)}, f32[256]{0:T(256)}, u32[]{:S(2)}) copy-start(f32[256]{0:T(256)} %param.14) | copy-start | bytes 3076
  5.2 66.2 %copy-start.7 = (f32[8]{0:T(128)S(1)}, f32[8]{0:T(128)}, u32[]{:S(2)}) copy-start(f32[8]{0:T(128)} %scale.1) | copy-start | bytes 100
  5.2 62.3 %collective-permute-start.11 = (bf16[496,512]{1,0:T(8,128)(2,1)S(1)}, bf16[496,512]{1,0:T(8,128)(2,1)S(1)}, u32[]{:S(2)}, u32[]{:S(2)}) collective-permute-start(bf16[496,512]{1,0:T(8,128)(2,1)S(1)} %get-tuple-element.28), channel_id=1, source_target_pairs={{0,2},{2,0},{4,6},{6,4},{8,10},{10,8},{12,14},{14,12},{1,3},{3,1},... | collective-permute-start | bytes 1523720 | tf_op jit(solution)/shard_map/ppermute | solution.py:777
  16.7 27.7 %collective-permute-start.1 = (f32[40,512]{1,0:T(8,128)S(1)}, f32[40,512]{1,0:T(8,128)S(1)}, u32[]{:S(2)}, u32[]{:S(2)}) collective-permute-start(f32[40,512]{1,0:T(8,128)S(1)} %get-tuple-element.19.mine), channel_id=1, source_target_pairs={{0,2},{2,0},{4,6},{6,4},{8,10},{10,8},{12,14},{14,12},{1,3},{3,1},... | collective-permute-start | bytes 245768 | tf_op jit(solution)/shard_map/ppermute | solution.py:836
  17.5 64.3 %collective-permute-start.5 = (bf16[240,1152]{1,0:T(8,128)(2,1)S(1)}, bf16[240,1152]{1,0:T(8,128)(2,1)S(1)}, u32[]{:S(2)}, u32[]{:S(2)}) collective-permute-start(bf16[240,1152]{1,0:T(8,128)(2,1)S(1)} %get-tuple-element.22), channel_id=1, source_target_pairs={{0,2},{2,0},{4,6},{6,4},{8,10},{10,8},{12,14},{14,12},{1,3},{3,1},... | collective-permute-start | bytes 1658888 | tf_op jit(solution)/shard_map/ppermute | solution.py:856
  18.8 63.0 %collective-permute-start.6 = (bf16[240,1152]{1,0:T(8,128)(2,1)S(1)}, bf16[240,1152]{1,0:T(8,128)(2,1)S(1)}, u32[]{:S(2)}, u32[]{:S(2)}) collective-permute-start(bf16[240,1152]{1,0:T(8,128)(2,1)S(1)} %get-tuple-element.23), channel_id=1, source_target_pairs={{0,14},{2,4},{4,2},{6,8},{8,6},{10,12},{12,10},{14,0},{1,15},{3,5}... | collective-permute-start | bytes 1658888 | tf_op jit(solution)/shard_map/ppermute | solution.py:857
  22.5 48.8 %collective-permute-start.12 = (bf16[496,512]{1,0:T(8,128)(2,1)S(1)}, bf16[496,512]{1,0:T(8,128)(2,1)S(1)}, u32[]{:S(2)}, u32[]{:S(2)}) collective-permute-start(bf16[496,512]{1,0:T(8,128)(2,1)S(1)} %get-tuple-element.29), channel_id=1, source_target_pairs={{0,14},{2,4},{4,2},{6,8},{8,6},{10,12},{12,10},{14,0},{1,15},{3,5}... | collective-permute-start | bytes 1523720 | tf_op jit(solution)/shard_map/ppermute | solution.py:778
  45.0 7.0 %collective-permute-start.2 = (f32[40,640]{1,0:T(8,128)S(1)}, f32[40,640]{1,0:T(8,128)S(1)}, u32[]{:S(2)}, u32[]{:S(2)}) collective-permute-start(f32[40,640]{1,0:T(8,128)S(1)} %shard_map.83.mine), channel_id=1, source_target_pairs={{0,4},{2,6},{4,0},{6,2},{8,12},{10,14},{12,8},{14,10},{1,5},{3,7},... | collective-permute-start | bytes 307208 | tf_op jit(solution)/shard_map/ppermute | solution.py:836
  52.5 8.0 %collective-permute-start.3 = (f32[40,896]{1,0:T(8,128)S(1)}, f32[40,896]{1,0:T(8,128)S(1)}, u32[]{:S(2)}, u32[]{:S(2)}) collective-permute-start(f32[40,896]{1,0:T(8,128)S(1)} %shard_map.84.mine), channel_id=1, source_target_pairs={{0,8},{2,10},{4,12},{6,14},{8,0},{10,2},{12,4},{14,6},{1,9},{3,11}... | collective-permute-start | bytes 430088 | tf_op jit(solution)/shard_map/ppermute | solution.py:836
  60.5 5.8 %collective-permute-start.9 = (bf16[48,384]{1,0:T(8,128)(2,1)S(1)}, bf16[48,384]{1,0:T(8,128)(2,1)S(1)}, u32[]{:S(2)}, u32[]{:S(2)}) collective-permute-start(bf16[48,384]{1,0:T(8,128)(2,1)S(1)} %get-tuple-element.26), channel_id=1, source_target_pairs={{0,6},{2,8},{4,10},{6,12},{8,14},{10,0},{12,2},{14,4},{1,7},{3,9},... | collective-permute-start | bytes 110600 | tf_op jit(solution)/shard_map/ppermute | solution.py:758
  66.3 1.3 %collective-permute-start.4 = (bf16[29,1024]{1,0:T(8,128)(2,1)S(1)}, bf16[29,1024]{1,0:T(8,128)(2,1)S(1)}, u32[]{:S(2)}, u32[]{:S(2)}) collective-permute-start(bf16[29,1024]{1,0:T(8,128)(2,1)S(1)} %get-tuple-element.21.own), channel_id=1, source_target_pairs={{0,1},{1,0},{2,3},{3,2},{4,5},{5,4},{6,7},{7,6},{8,9},{9,8},{10,11... | collective-permute-start | bytes 178184 | tf_op jit(solution)/shard_map/ppermute | solution.py:854
  67.5 14.2 %collective-permute-start.7 = (bf16[112,768]{1,0:T(8,128)(2,1)S(1)}, bf16[112,768]{1,0:T(8,128)(2,1)S(1)}, u32[]{:S(2)}, u32[]{:S(2)}) collective-permute-start(bf16[112,768]{1,0:T(8,128)(2,1)S(1)} %get-tuple-element.24), channel_id=1, source_target_pairs={{0,4},{2,6},{4,8},{6,10},{8,12},{10,14},{12,0},{14,2},{1,5},{3,7},... | collective-permute-start | bytes 516104 | tf_op jit(solution)/shard_map/ppermute | solution.py:758
  67.5 14.2 %collective-permute-start.8 = (bf16[112,768]{1,0:T(8,128)(2,1)S(1)}, bf16[112,768]{1,0:T(8,128)(2,1)S(1)}, u32[]{:S(2)}, u32[]{:S(2)}) collective-permute-start(bf16[112,768]{1,0:T(8,128)(2,1)S(1)} %get-tuple-element.25), channel_id=1, source_target_pairs={{0,12},{2,14},{4,0},{6,2},{8,4},{10,6},{12,8},{14,10},{1,13},{3,15... | collective-permute-start | bytes 516104 | tf_op jit(solution)/shard_map/ppermute | solution.py:758
  71.4 10.4 %collective-permute-start.10 = (bf16[48,384]{1,0:T(8,128)(2,1)S(1)}, bf16[48,384]{1,0:T(8,128)(2,1)S(1)}, u32[]{:S(2)}, u32[]{:S(2)}) collective-permute-start(bf16[48,384]{1,0:T(8,128)(2,1)S(1)} %get-tuple-element.27), channel_id=1, source_target_pairs={{0,10},{2,12},{4,14},{6,0},{8,2},{10,4},{12,6},{14,8},{1,11},{3,13... | collective-permute-start | bytes 110600 | tf_op jit(solution)/shard_map/ppermute | solution.py:758

commit v4 on v3

--- a/solution.py
+++ b/solution.py
@@ -152,6 +152,8 @@
 
 def synthesis(lows, highs, start, left):
     def cells(cols):
+        if cols is None:
+            return lambda n: None
         return lambda n: cols[(n - 3 - start) // 2] if 0 <= n - 3 - start < 2 * len(cols) else None
 
     a, b = cells(lows), cells(highs)
@@ -381,99 +383,99 @@
     band_rows(geo, level, lo, skip, hi, geo.span[level - 1][0], gain, bands)
 
 
-def sides_kernel(place, edge, x, side_e, side_o, sems):
+def sides_kernel(place, x, side_e, side_o, sems):
+    parity = place[1] % 2
+    width, lanes = x.shape[1], side_e.shape[1]
+
+    def both(low, high):
+        copies = [
+            pltpu.make_async_copy(x.at[:, pl.ds(0, lanes)], low, sems.at[0]),
+            pltpu.make_async_copy(x.at[:, pl.ds(width - lanes, lanes)], high, sems.at[1]),
+        ]
+        for copy in copies:
+            copy.start()
+        for copy in copies:
+            copy.wait()
+
+    @pl.when(parity == 0)
+    def _():
+        both(side_o, side_e)
+
+    @pl.when(parity != 0)
+    def _():
+        both(side_e, side_o)
+
+
+def corners_kernel(place, side_e, side_o, out):
     lat, parity = place[0], place[1] % 2
-    rows, width = x.shape
-    lanes = SIDE * C
-    own = pl.ds(NEAR, rows)
-
-    def fill(side, begin, sem):
-        copy = pltpu.make_async_copy(x.at[:, pl.ds(begin, lanes)], side.at[own, :], sem)
-        copy.start()
-        cols = slice(begin, begin + lanes)
-
-        @pl.when(lat == 0)
-        def _():
-            side[0:NEAR, :] = jnp.zeros((NEAR, lanes), BF16)
-            side[NEAR + rows :, :] = edge[0:NEAR, cols]
-
-        @pl.when(lat != 0)
-        def _():
-            side[0:NEAR, :] = edge[HALO - NEAR :, cols]
-            side[NEAR + rows :, :] = jnp.zeros((NEAR, lanes), BF16)
-
-        return copy
-
-    def both(low, high):
-        one, two = fill(low, 0, sems.at[0]), fill(high, width - lanes, sems.at[1])
-        one.wait()
-        two.wait()
+    rows, lanes = side_e.shape
+    at = jnp.where(lat == 0, rows - NEAR, 0)
+    window = pl.ds(pl.multiple_of(at, NEAR), NEAR)
 
     @pl.when(parity == 0)
     def _():
-        both(side_o, side_e)
+        out[:, 0:lanes] = side_o[window, :]
+        out[:, lanes:] = side_e[window, :]
 
     @pl.when(parity != 0)
     def _():
-        both(side_e, side_o)
-
-
-def merge_kernel(size, more, place, mine, other, out):
-    width = mine.shape[1]
-
-    def add(lower, upper):
-        out[:, 0:more] = lower[:, 0:more]
-        out[:, more:width] = lower[:, more:] + upper[:, 0 : width - more]
-        out[:, width:] = upper[:, width - more :]
-
-    lower_half = (place[1] // size) % 2 == 0
-
-    @pl.when(lower_half)
-    def _():
-        add(mine, other)
-
-    @pl.when(jnp.logical_not(lower_half))
-    def _():
-        add(other, mine)
-
-
-def last_merge_kernel(geo, size, more, place, mine, other, ring, tokens, merged):
-    merge_kernel(size, more, place, mine, other, merged)
-    around = ring.shape[1]
-    fold = merged.shape[1] - around
-    ring[:, 0:fold] = merged[:, 0:fold] + merged[:, around:]
-    ring[:, fold:] = merged[:, fold:around]
+        out[:, 0:lanes] = side_e[window, :]
+        out[:, lanes:] = side_o[window, :]
+
+
+def ring_kernel(geo, flip, place, mine, other, ring, line):
+    width, total = mine.shape[1], ring.shape[1]
+    fold = line.shape[1] - total
+    line[...] = jnp.zeros(line.shape, F32)
+    lon = place[1]
+    for part, where in ((mine, lon), (other, lon ^ flip)):
+        at = pl.ds(pl.multiple_of(where * (geo.cells[4] * C), LANES), width)
+        line[:, at] = line[:, at] + part[...]
+    ring[:, 0:fold] = line[:, 0:fold] + line[:, total:]
+    ring[:, fold:] = line[:, fold:total]
+
+
+def add_kernel(geo, place, mine, other, ring, tokens):
+    ring[...] = mine[...] + other[...]
     skip = -geo.low[4][0]
     tokens[...] = ring[skip : skip + geo.rows[4], :].astype(BF16)
 
 
-def first_bands_kernel(geo, lats, place, edge, side_e, side_o, gain, x, held, ext, la, ha, d1, sem):
+def first_level_kernel(geo, lats, place, edge, side_e, side_o, corner, gain, x, held, ext, la, ha, d1, xh, xl, part, sem):
     lat, parity = place[0], place[1] % 2
     rows, width = x.shape
     lanes = SIDE * C
     copy = pltpu.make_async_copy(x, ext.at[pl.ds(NEAR, rows), pl.ds(lanes, width)], sem)
     copy.start()
+    sides = (slice(0, lanes), slice(lanes + width, width + 2 * lanes))
     own = slice(lanes, lanes + width)
+    inner = slice(NEAR, NEAR + rows)
+
+    def rims(near, far, edges):
+        ext[far, :] = jnp.zeros((NEAR, width + 2 * lanes), BF16)
+        ext[near, own] = edges
+        ext[near, sides[0]] = corner[:, 0:lanes]
+        ext[near, sides[1]] = corner[:, lanes:]
+
+    top, bottom = slice(0, NEAR), slice(NEAR + rows, 2 * NEAR + rows)
 
     @pl.when(lat == 0)
     def _():
-        ext[0:NEAR, own] = jnp.zeros((NEAR, width), BF16)
-        ext[NEAR + rows :, own] = edge[0:NEAR, :]
+        rims(bottom, top, edge[0:NEAR, :])
 
     @pl.when(lat != 0)
     def _():
-        ext[0:NEAR, own] = edge[HALO - NEAR :, :]
-        ext[NEAR + rows :, own] = jnp.zeros((NEAR, width), BF16)
+        rims(top, bottom, edge[HALO - NEAR :, :])
 
     @pl.when(parity == 0)
     def _():
-        ext[:, 0:lanes] = side_o[...]
-        ext[:, lanes + width :] = side_e[...]
+        ext[inner, sides[0]] = side_o[...]
+        ext[inner, sides[1]] = side_e[...]
 
     @pl.when(parity != 0)
     def _():
-        ext[:, 0:lanes] = side_e[...]
-        ext[:, lanes + width :] = side_o[...]
+        ext[inner, sides[0]] = side_e[...]
+        ext[inner, sides[1]] = side_o[...]
 
     start, count = geo.band[1]
     low = analysis_matrix(LOW, start, 120, -NEAR, 256)
@@ -485,9 +487,38 @@
             mh, ml = two_terms(masked_rows(matrix, start + 120 * b, geo.rows[1], lat, lats))
             out[120 * b : 120 * b + 120, :] = mxu(mh, data) + mxu(ml, data)
     band_rows(geo, 1, la, 0, ha, -SIDE, gain, d1)
-    copy = pltpu.make_async_copy(d1, held, sem)
-    copy.start()
-    copy.wait()
+    half = rows // 2
+    ylow, yhigh = la, ha
+    used = slice(0, d1.shape[2])
+    for block in range(2):
+        w = 0 if block == 0 else count - LANES
+        window = slice(w, w + LANES)
+        target = slice(half * block, half * (block + 1))
+        matrix = synthesis_matrix(half * block, half, start + w, LANES)
+        sh, sl = two_terms(matrix)
+        xh[0:LANES, :], xl[0:LANES, :] = two_terms(d1[0, window, :])
+        xh[LANES:, :], xl[LANES:, :] = two_terms(d1[2, window, :])
+        yhigh[target, used] = mxu(sh, xh[...]) + mxu(sh, xl[...]) + mxu(sl, xh[...])
+        vh, vl = two_terms(d1[1, window, :])
+        sh, sl = sh[:, LANES:], sl[:, LANES:]
+        ylow[target, used] = mxu(sh, vh) + mxu(sh, vl) + mxu(sl, vh)
+
+    begin, pairs = geo.span[1]
+    most = 232
+
+    def chunk(i, carry):
+        row = pl.multiple_of(i * most, 8)
+        pair = synthesis(
+            columns(ylow, row, most, pairs), columns(yhigh, row, most, pairs), begin, first_half(most)
+        )
+        for q in range(geo.cells[0] // 2):
+            put(part, row, q, pair(2 * q))
+        copy = pltpu.make_async_copy(part.at[pl.ds(row, most), :], held.at[pl.ds(row, most), :], sem)
+        copy.start()
+        copy.wait()
+        return carry
+
+    lax.fori_loop(0, rows // most, chunk, 0)
 
 
 def exchange_plan(geo):
@@ -602,11 +633,11 @@
 
 def synthesis_kernel(geo, lats, place, coarse, e2, o2, from_m2, from_p2, from_m3, from_p3, *refs):
     lat, parity = place[0], place[1] % 2
-    held, (out, up3, up2, up1, xh, xl, ylow, yhigh, done), refs = refs[:4], refs[4:13], refs[13:]
-    d1, d2, d3, d4, sems, in_sems = refs
+    held, (out, up3, up2, up1, ylow, yhigh, done), refs = refs[:4], refs[4:11], refs[11:]
+    part, d2, d3, d4, sems, in_sems = refs
     arrive = [
         pltpu.make_async_copy(source, to, in_sems.at[i])
-        for i, (source, to) in enumerate(zip(held, (d1, d2, d3, d4)))
+        for i, (source, to) in enumerate(zip(held, (part, d2, d3, d4)))
     ]
     for level in (4, 3, 2, 1):
         arrive[level - 1].start()
@@ -668,30 +699,23 @@
 
         lax.fori_loop(0, rows // step, joined, 0)
 
-    arrive[0].wait()
     n = geo.band[1][1]
     half = geo.rows[0] // 2
     for block in range(2):
         w = 0 if block == 0 else n - LANES
-        window = slice(w, w + LANES)
-        sh, sl = two_terms(synthesis_matrix(half * block, half, geo.band[1][0] + w, LANES))
-        for one, two, y in (
-            (up1[window, :], d1[1, window, :], ylow),
-            (d1[0, window, :], d1[2, window, :], yhigh),
-        ):
-            xh[0:LANES, :], xl[0:LANES, :] = two_terms(one)
-            xh[LANES:, :], xl[LANES:, :] = two_terms(two)
-            y[half * block : half * (block + 1), :] = (
-                mxu(sh, xh[...]) + mxu(sh, xl[...]) + mxu(sl, xh[...])
-            )
+        matrix = synthesis_matrix(half * block, half, geo.band[1][0] + w, LANES)
+        h, l = two_terms(up1[w : w + LANES, :])
+        ylow[half * block : half * (block + 1), :] = dot3(matrix[:, 0:LANES], h, l)
+    arrive[0].wait()
     begin, pairs = geo.span[1]
     most = 112
 
     def last(row, count):
         left = first_half(count)
-        pair = synthesis(columns(ylow, row, count), columns(yhigh, row, count), begin, left)
+        pair = synthesis(columns(ylow, row, count), None, begin, left)
         for q in range(geo.cells[0] // 2):
-            put(done, row, q, pair(2 * q).astype(BF16))
+            more = part[pl.ds(row, count), pl.ds(LANES * q, LANES)]
+            put(done, row, q, (pair(2 * q) + more).astype(BF16))
 
     def store(i, count):
         part = pl.ds(pl.multiple_of(i * most, 16), count)
@@ -766,12 +790,11 @@
     extended = NEAR + rows + NEAR
     side_e, side_o = call(
         sides_kernel,
-        [shape((extended, wide), BF16)] * 2,
+        [shape((rows, wide), BF16)] * 2,
         [pltpu.SemaphoreType.DMA((2,))],
         place,
-        edge,
         state_field,
-        raw=(2,),
+        raw=(1,),
         cost=1_000_000,
     )
     side_e = lax.ppermute(side_e, "lon", even_pairs)
@@ -810,47 +833,59 @@
         raw=(3,),
         raw_out=(1, 2, 3),
     )
-    (d1,) = call(
-        functools.partial(first_bands_kernel, geo, lats),
-        [shape(bands[0])],
+    (corner,) = call(
+        corners_kernel, [shape((NEAR, 2 * wide), BF16)], [], place, side_e, side_o, cost=100_000
+    )
+    corner = lax.ppermute(corner, "lat", swap)
+    (part,) = call(
+        functools.partial(first_level_kernel, geo, lats),
+        [shape((rows, width))],
         [
             pltpu.VMEM((extended, width + 2 * wide), BF16),
-            pltpu.VMEM((geo.band[1][1], width + 2 * wide), F32),
-            pltpu.VMEM((geo.band[1][1], width + 2 * wide), F32),
+            pltpu.VMEM((rows, width + 2 * wide), F32),
+            pltpu.VMEM((rows, width + 2 * wide), F32),
             pltpu.VMEM(bands[0], F32),
+            pltpu.VMEM((2 * LANES, w[1]), BF16),
+            pltpu.VMEM((2 * LANES, w[1]), BF16),
+            pltpu.VMEM((rows, width), F32),
             pltpu.SemaphoreType.DMA,
         ],
         place,
         edge,
         side_e,
         side_o,
+        corner,
         skip_gain,
         state_field,
-        raw=(5,),
+        raw=(6,),
         raw_out=(0,),
-    )
-
-    merged, size = ll4, 1
+        grant=40,
+    )
+
     total = geo.cells[4] * lons * C
-    while size < lons:
-        other = lax.ppermute(merged, "lon", [(i, i ^ size) for i in range(lons)])
-        more = geo.cells[4] * C * size
-        dims = (merged.shape[0], merged.shape[1] + more)
-        if 2 * size < lons:
-            (merged,) = call(
-                functools.partial(merge_kernel, size, more), [shape(dims)], [], place, merged, other, cost=100_000
-            )
-        else:
-            ring, tokens = call(
-                functools.partial(last_merge_kernel, geo, size, more),
-                [shape((dims[0], total)), shape((geo.rows[4], total), BF16)],
-                [pltpu.VMEM(dims, F32)],
-                place,
-                merged,
-                other,
-                cost=100_000,
-            )
-        size = 2 * size
+    flip = lons // 2
+    other = lax.ppermute(ll4, "lon", [(i, i ^ flip) for i in range(lons)])
+    (ring,) = call(
+        functools.partial(ring_kernel, geo, flip),
+        [shape((ll4.shape[0], total))],
+        [pltpu.VMEM((ll4.shape[0], total + 6 * C), F32)],
+        place,
+        ll4,
+        other,
+        cost=100_000,
+    )
+    while flip > 1:
+        flip = flip // 2
+        other = lax.ppermute(ring, "lon", [(i, i ^ flip) for i in range(lons)])
+        ring, tokens = call(
+            functools.partial(add_kernel, geo),
+            [shape(ring.shape), shape((geo.rows[4], total), BF16)],
+            [],
+            place,
+            ring,
+            other,
+            cost=100_000,
+        )
     others = lax.ppermute(tokens, "lat", swap)
 
     deep_e = lax.ppermute(deep_e, "lon", even_pairs)
@@ -887,13 +922,12 @@
         [shape((rows, width), BF16)],
         [pltpu.VMEM((geo.band[level][1], w[level]), F32) for level in (3, 2, 1)]
         + [
-            pltpu.VMEM((2 * LANES, w[1]), BF16),
-            pltpu.VMEM((2 * LANES, w[1]), BF16),
             pltpu.VMEM((rows, w[1]), F32),
-            pltpu.VMEM((rows, w[1]), F32),
+            pltpu.VMEM((geo.band[1][1], w[2]), F32),
             pltpu.VMEM((rows, width), BF16),
+            pltpu.VMEM((rows, width), F32),
         ]
-        + [pltpu.VMEM(dims, F32) for dims in bands]
+        + [pltpu.VMEM(dims, F32) for dims in bands[1:]]
         + [
             pltpu.SemaphoreType.DMA((rows // 112 + 1,)),
             pltpu.SemaphoreType.DMA((4,)),
@@ -906,7 +940,7 @@
         from_p2,
         from_m3,
         from_p3,
-        d1,
+        part,
         d2,
         d3,
         d4,

time: 98.2 us -> 96.1 us (0.979)
  waiting for transfers between devices: 38.2 us -> 15 us
  starting transfers between devices: 19.5 us -> 32.6 us
  Pallas kernels: 37.3 us -> 45.3 us
    ppermute x3 -> x4, waiting for transfers between devices: 30.6 us -> 9.92 us  [the longest x2 5.7 us: program(): other = lax.ppermute(ring, 'lon', [(i, i ^ flip) for i in range(lons)])]
    ppermute x3 -> x4, starting transfers between devices: 6.01 us -> 14.6 us  [the longest x2 14.5 us: program(): other = lax.ppermute(ring, 'lon', [(i, i ^ flip) for i in range(lons)])]
    pallas_call x8 -> x9, Pallas kernels: 37.3 us -> 45.3 us  [call(): pl.pallas_call(kernel, out_shape=tuple(out_shape), in_specs=specs, out_sp...]
    ppermute x4, starting transfers between devices: 3.96 us -> 8.37 us  [shifted(): lax.ppermute(value, 'lon', [(i, (i + by) % lons) for i in range(lons)])]
    ppermute x1, starting transfers between devices: 3.75 us -> 0.79 us  [program(): deep_o = lax.ppermute(deep_o, 'lon', odd_pairs)]
    ppermute x1, starting transfers between devices: 0.98 us -> 3.57 us  [program(): side_o = lax.ppermute(side_o, 'lon', odd_pairs)]
    ppermute x1, waiting for transfers between devices: 1.27 us -> 0.01 us  [program(): edge = lax.ppermute(edge, 'lat', swap)]
    ppermute x4, waiting for transfers between devices: 5.02 us -> 3.92 us  [shifted(): lax.ppermute(value, 'lon', [(i, (i + by) % lons) for i in range(lons)])]
  transfers between devices with their start and end apart: 13 -> 14, of which waited for: 6 -> 6; matrix products, arithmetic and copies ran while one was open for 0% -> 0% of each run, Pallas kernels for 21% -> 31%
where the time goes in v4:
time: 96.1 us; the launch traced here: 95.9 us
  Pallas kernels  45.3 us (47%)
  starting transfers between devices  32.6 us (34%)
  waiting for transfers between devices  15 us (16%)
  local copies, waits for them, and re-layouts  2.59 us (3%)
    pallas_call x9, Pallas kernels, call(): pl.pallas_call(kernel, out_shape=tuple(out_shape), in_specs=specs, out_sp...  45.3 us
    ppermute x2, starting transfers between devices, program(): other = lax.ppermute(ring, 'lon', [(i, i ^ flip) for i in range(lons)])  14.5 us
    ppermute x4, starting transfers between devices, shifted(): lax.ppermute(value, 'lon', [(i, (i + by) % lons) for i in range(lons)])  8.37 us
    ppermute x2, waiting for transfers between devices, program(): other = lax.ppermute(ring, 'lon', [(i, i ^ flip) for i in range(lons)])  5.7 us
    ppermute x4, waiting for transfers between devices, shifted(): lax.ppermute(value, 'lon', [(i, (i + by) % lons) for i in range(lons)])  3.92 us
    ppermute x1, waiting for transfers between devices, program(): other = lax.ppermute(ll4, 'lon', [(i, i ^ flip) for i in range(lons)])  3.61 us
    ppermute x1, starting transfers between devices, program(): side_o = lax.ppermute(side_o, 'lon', odd_pairs)  3.57 us
    ppermute x1, starting transfers between devices, program(): side_e = lax.ppermute(side_e, 'lon', even_pairs)  2.56 us
  transfers between devices with their start and end apart: 14, of which 6 were waited for; matrix products, arithmetic and copies ran while one was open for 0% of the time, Pallas kernels for 31%

profile of v4, /device:TPU:0, one launch (start us, length us, event | category | flops | bytes accessed | tf_op | source)
XLA Modules:
  0.0 95.9 jit_solution(6684317851702927202)
XLA Ops:
  0.0 1.0 %constant_dynamic-slice_fusion = bf16[96,2048]{1,0:T(8,128)(2,1)S(1)} fusion(bf16[464,2048]{1,0:T(8,128)(2,1)} %x.5, s32[]{:T(128)S(6)} %select_n.5), kind=kLoop, calls=%fused_computation.1 | loop fusion | bytes 786436 | tf_op jit(solution)/shard_map/dynamic_slice | solution.py:784
  1.0 0.6 collective-permute-start
  1.6 0.1 pad_add_fusion.place
  1.7 1.5 %copy-done = bf16[464,2048]{1,0:T(8,128)(2,1)S(1)} copy-done((bf16[464,2048]{1,0:T(8,128)(2,1)S(1)}, bf16[464,2048]{1,0:T(8,128)(2,1)}, u32[]{:S(2)}) %copy-start) | copy-done | bytes 1900568
  3.2 0.6 shard_map.87
  3.9 2.6 %collective-permute-start.11 = (bf16[464,512]{1,0:T(8,128)(2,1)S(1)}, bf16[464,512]{1,0:T(8,128)(2,1)S(1)}, u32[]{:S(2)}, u32[]{:S(2)}) collective-permute-start(bf16[464,512]{1,0:T(8,128)(2,1)S(1)} %get-tuple-element.30), channel_id=1, source_target_pairs={{0,2},{2,0},{4,6},{6,4},{8,10},{10,8},{12,14},{14,12},{1,3},{3,1},... | collective-permute-start | bytes 1425416 | tf_op jit(solution)/shard_map/ppermute | solution.py:800
  6.4 3.6 %collective-permute-start.12 = (bf16[464,512]{1,0:T(8,128)(2,1)S(1)}, bf16[464,512]{1,0:T(8,128)(2,1)S(1)}, u32[]{:S(2)}, u32[]{:S(2)}) collective-permute-start(bf16[464,512]{1,0:T(8,128)(2,1)S(1)} %get-tuple-element.31), channel_id=1, source_target_pairs={{0,14},{2,4},{4,2},{6,8},{8,6},{10,12},{12,10},{14,0},{1,15},{3,5}... | collective-permute-start | bytes 1425416 | tf_op jit(solution)/shard_map/ppermute | solution.py:801
  10.0 0.0 copy-done.8
  10.0 0.0 collective-permute-done.edge
  10.0 0.0 copy-done.1
  10.0 8.6 %shard_map.82 = (f32[40,512]{1,0:T(8,128)S(1)}, f32[3,128,896]{2,1,0:T(8,128)S(1)}, f32[3,64,640]{2,1,0:T(8,128)S(1)}, f32[3,40,512]{2,1,0:T(8,128)S(1)}, bf16[2...) custom-call(s32[2]{0:T(128)S(1)} %pad_add_fusion.place, ...), custom_call_target="tpu_custom_call" | custom-call | flops 20000000 | bytes 1048576 | tf_op jit(solution)/shard_map/pallas_call | solution.py:749
  18.6 0.1 collective-permute-start.1
  18.7 2.0 %collective-permute-start.5 = (bf16[240,1152]{1,0:T(8,128)(2,1)S(1)}, bf16[240,1152]{1,0:T(8,128)(2,1)S(1)}, u32[]{:S(2)}, u32[]{:S(2)}) collective-permute-start(bf16[240,1152]{1,0:T(8,128)(2,1)S(1)} %get-tuple-element.24), channel_id=1, source_target_pairs={{0,2},{2,0},{4,6},{6,4},{8,10},{10,8},{12,14},{14,12},{1,3},{3,1},... | collective-permute-start | bytes 1658888 | tf_op jit(solution)/shard_map/ppermute | solution.py:891
  20.7 0.8 collective-permute-start.6
  21.5 3.6 %collective-permute-done.1.other = f32[40,512]{1,0:T(8,128)S(1)} collective-permute-done((f32[40,512]{1,0:T(8,128)S(1)}, f32[40,512]{1,0:T(8,128)S(1)}, u32[]{:S(2)}, u32[]{:S(2)}) %collective-permute-start.1) | collective-permute-done | bytes 81952 | tf_op jit(solution)/shard_map/ppermute | solution.py:867
  25.1 0.6 shard_map.83.mine
  25.7 12.3 %collective-permute-start.2 = (f32[40,1024]{1,0:T(8,128)S(1)}, f32[40,1024]{1,0:T(8,128)S(1)}, u32[]{:S(2)}, u32[]{:S(2)}) collective-permute-start(f32[40,1024]{1,0:T(8,128)S(1)} %shard_map.83.mine), channel_id=1, source_target_pairs={{0,4},{2,6},{4,0},{6,2},{8,12},{10,14},{12,8},{14,10},{1,5},{3,7},... | collective-permute-start | bytes 491528 | tf_op jit(solution)/shard_map/ppermute | solution.py:879
  38.0 4.4 %collective-permute-done.2.other = f32[40,1024]{1,0:T(8,128)S(1)} collective-permute-done((f32[40,1024]{1,0:T(8,128)S(1)}, f32[40,1024]{1,0:T(8,128)S(1)}, u32[]{:S(2)}, u32[]{:S(2)}) %collective-permute-start.2) | collective-permute-done | bytes 163872 | tf_op jit(solution)/shard_map/ppermute | solution.py:879
  42.4 0.7 collective-permute-start.9
  43.1 1.2 %shard_map.84 = (f32[40,1024]{1,0:T(8,128)S(1)}, bf16[29,1024]{1,0:T(8,128)(2,1)}) custom-call(s32[2]{0:T(128)S(1)} %pad_add_fusion.place, f32[40,1024]{1,0:T(8,128)S(1)} %shard_map.83.mine, f32[40,1024]{1,0:T(8,128)S(1)} %collective-permute-done.2.other), custom_call_target="tpu_custom_call" | custom-call | flops 100000 | bytes 1048576 | tf_op jit(solution)/shard_map/pallas_call | solution.py:749
  44.3 3.9 %collective-permute-done.9.from_m3 = bf16[48,384]{1,0:T(8,128)(2,1)S(1)} collective-permute-done((bf16[48,384]{1,0:T(8,128)(2,1)S(1)}, bf16[48,384]{1,0:T(8,128)(2,1)S(1)}, u32[]{:S(2)}, u32[]{:S(2)}) %collective-permute-start.9) | collective-permute-done | bytes 36896 | tf_op jit(solution)/shard_map/ppermute | solution.py:782
  48.2 2.2 %collective-permute-start.3 = (f32[40,1024]{1,0:T(8,128)S(1)}, f32[40,1024]{1,0:T(8,128)S(1)}, u32[]{:S(2)}, u32[]{:S(2)}) collective-permute-start(f32[40,1024]{1,0:T(8,128)S(1)} %get-tuple-element.21.mine), channel_id=1, source_target_pairs={{0,2},{2,0},{4,6},{6,4},{8,10},{10,8},{12,14},{14,12},{1,3},{3,1},... | collective-permute-start | bytes 491528 | tf_op jit(solution)/shard_map/ppermute | solution.py:879
  50.4 0.0 collective-permute-done.11.side_e
  50.4 0.2 collective-permute-start.7
  50.6 0.0 collective-permute-done.12.side_o
  50.6 3.7 %collective-permute-start.8 = (bf16[112,768]{1,0:T(8,128)(2,1)S(1)}, bf16[112,768]{1,0:T(8,128)(2,1)S(1)}, u32[]{:S(2)}, u32[]{:S(2)}) collective-permute-start(bf16[112,768]{1,0:T(8,128)(2,1)S(1)} %get-tuple-element.27), channel_id=1, source_target_pairs={{0,12},{2,14},{4,0},{6,2},{8,4},{10,6},{12,8},{14,10},{1,13},{3,15... | collective-permute-start | bytes 516104 | tf_op jit(solution)/shard_map/ppermute | solution.py:782
  54.2 0.6 shard_map.88
  54.8 1.3 %collective-permute-done.3.other = f32[40,1024]{1,0:T(8,128)S(1)} collective-permute-done((f32[40,1024]{1,0:T(8,128)S(1)}, f32[40,1024]{1,0:T(8,128)S(1)}, u32[]{:S(2)}, u32[]{:S(2)}) %collective-permute-start.3) | collective-permute-done | bytes 163872 | tf_op jit(solution)/shard_map/ppermute | solution.py:879
  56.1 0.0 collective-permute-start.13
  56.1 0.6 shard_map.85
  56.7 0.6 collective-permute-done.13.corner
  57.3 0.2 collective-permute-start.4
  57.5 1.1 %collective-permute-done.4.others = bf16[29,1024]{1,0:T(8,128)(2,1)S(1)} collective-permute-done((bf16[29,1024]{1,0:T(8,128)(2,1)S(1)}, bf16[29,1024]{1,0:T(8,128)(2,1)S(1)}, u32[]{:S(2)}, u32[]{:S(2)}) %collective-permute-start.4) | collective-permute-done | bytes 59424 | tf_op jit(solution)/shard_map/ppermute | solution.py:889
  58.6 0.0 copy-start.6
  58.6 0.0 copy-start.7
  58.6 3.8 %collective-permute-start.10 = (bf16[48,384]{1,0:T(8,128)(2,1)S(1)}, bf16[48,384]{1,0:T(8,128)(2,1)S(1)}, u32[]{:S(2)}, u32[]{:S(2)}) collective-permute-start(bf16[48,384]{1,0:T(8,128)(2,1)S(1)} %get-tuple-element.29), channel_id=1, source_target_pairs={{0,10},{2,12},{4,14},{6,0},{8,2},{10,4},{12,6},{14,8},{1,11},{3,13... | collective-permute-start | bytes 110600 | tf_op jit(solution)/shard_map/ppermute | solution.py:782
  62.4 12.7 %shard_map.89.refs_0_ = f32[464,2048]{1,0:T(8,128)S(1)} custom-call(s32[2]{0:T(128)S(1)} %pad_add_fusion.place, bf16[96,2048]{1,0:T(8,128)(2,1)S(1)} %collective-permute-done.edge, bf16[464,512]{1,0:T(8,128)(2,1)S(1)} %collective-permute-done.11.side_e, bf16[464,512]{1,0:T(8,128)(2,1)S(1)} %collective-permute-done.12.side_o, ...), custom_call_target="tpu_custom_call" | custom-call | flops 20000000 | bytes 1048576 | tf_op jit(solution)/shard_map/pallas_call | solution.py:749
  75.1 0.0 copy-done.2
  75.2 0.0 copy-done.3
  75.2 0.0 copy-done.4
  75.2 0.0 copy-done.5
  75.2 5.3 %shard_map.86.coarse = f32[40,512]{1,0:T(8,128)S(1)} custom-call(s32[2]{0:T(128)S(1)} %pad_add_fusion.place, f32[40,1024]{1,0:T(8,128)S(1)} %get-tuple-element.22.ring, bf16[29,1024]{1,0:T(8,128)(2,1)S(1)} %get-tuple-element.23.own, bf16[29,1024]{1,0:T(8,128)(2,1)S(1)} %collective-permute-done.4.others, bf16[64,256]{1,0:T(8,128)(2,1)S(1)} %copy-done.4, ...), custom_call_target="tpu_custom_call" | custom-call | flops 200000000 | bytes 1048576 | tf_op jit(solution)/shard_map/pallas_call | solution.py:749
  80.5 0.0 collective-permute-done.10.from_p3
  80.5 0.0 collective-permute-done.7.from_m2
  80.5 0.0 collective-permute-done.8.from_p2
  80.5 0.0 collective-permute-done.5.e2
  80.5 0.0 collective-permute-done.6.o2
  80.5 15.2 %shard_map.90 = bf16[464,2048]{1,0:T(8,128)(2,1)} custom-call(s32[2]{0:T(128)S(1)} %pad_add_fusion.place, f32[40,512]{1,0:T(8,128)S(1)} %shard_map.86.coarse, bf16[240,1152]{1,0:T(8,128)(2,1)S(1)} %collective-permute-done.5.e2, bf16[240,1152]{1,0:T(8,128)(2,1)S(1)} %collective-permute-done.6.o2, bf16[112,768]{1,0:T(8,128)(2,1)S(1)} %collective-permute-done.7.from_m2, ...), custom_call_target="tpu_custom_call" | custom-call | flops 20000000 | bytes 1048576 | tf_op jit(solution)/shard_map/pallas_call | solution.py:749
  (10 shorter events, 0.0 us)
Async XLA Ops:
  0.0 10.0 %copy-start.8 = (f32[4,3,64]{2,0,1:T(4,128)S(1)}, f32[4,3,64]{2,0,1:T(4,128)}, u32[]{:S(2)}) copy-start(f32[4,3,64]{2,0,1:T(4,128)} %param.9) | copy-start | bytes 9220
  1.0 9.0 %collective-permute-start = (bf16[96,2048]{1,0:T(8,128)(2,1)S(1)}, bf16[96,2048]{1,0:T(8,128)(2,1)S(1)}, u32[]{:S(2)}, u32[]{:S(2)}) collective-permute-start(bf16[96,2048]{1,0:T(8,128)(2,1)S(1)} %constant_dynamic-slice_fusion), channel_id=1, source_target_pairs={{0,1},{1,0},{2,3},{3,2},{4,5},{5,4},{6,7},{7,6},{8,9},{9,8},{10,11... | collective-permute-start | bytes 1179656 | tf_op jit(solution)/shard_map/ppermute | solution.py:787
  1.7 1.5 %copy-start = (bf16[464,2048]{1,0:T(8,128)(2,1)S(1)}, bf16[464,2048]{1,0:T(8,128)(2,1)}, u32[]{:S(2)}) copy-start(bf16[464,2048]{1,0:T(8,128)(2,1)} %x.5) | copy-start | bytes 5701636
  3.2 6.8 %copy-start.1 = (bf16[464,2048]{1,0:T(8,128)(2,1)S(1)}, bf16[464,2048]{1,0:T(8,128)(2,1)}, u32[]{:S(2)}) copy-start(bf16[464,2048]{1,0:T(8,128)(2,1)} %x.5) | copy-start | bytes 5701636
  3.9 46.6 %collective-permute-start.11 = (bf16[464,512]{1,0:T(8,128)(2,1)S(1)}, bf16[464,512]{1,0:T(8,128)(2,1)S(1)}, u32[]{:S(2)}, u32[]{:S(2)}) collective-permute-start(bf16[464,512]{1,0:T(8,128)(2,1)S(1)} %get-tuple-element.30), channel_id=1, source_target_pairs={{0,2},{2,0},{4,6},{6,4},{8,10},{10,8},{12,14},{14,12},{1,3},{3,1},... | collective-permute-start | bytes 1425416 | tf_op jit(solution)/shard_map/ppermute | solution.py:800
  6.4 44.2 %collective-permute-start.12 = (bf16[464,512]{1,0:T(8,128)(2,1)S(1)}, bf16[464,512]{1,0:T(8,128)(2,1)S(1)}, u32[]{:S(2)}, u32[]{:S(2)}) collective-permute-start(bf16[464,512]{1,0:T(8,128)(2,1)S(1)} %get-tuple-element.31), channel_id=1, source_target_pairs={{0,14},{2,4},{4,2},{6,8},{8,6},{10,12},{12,10},{14,0},{1,15},{3,5}... | collective-permute-start | bytes 1425416 | tf_op jit(solution)/shard_map/ppermute | solution.py:801
  18.6 6.5 %collective-permute-start.1 = (f32[40,512]{1,0:T(8,128)S(1)}, f32[40,512]{1,0:T(8,128)S(1)}, u32[]{:S(2)}, u32[]{:S(2)}) collective-permute-start(f32[40,512]{1,0:T(8,128)S(1)} %get-tuple-element.20.mine), channel_id=1, source_target_pairs={{0,8},{2,10},{4,12},{6,14},{8,0},{10,2},{12,4},{14,6},{1,9},{3,11}... | collective-permute-start | bytes 245768 | tf_op jit(solution)/shard_map/ppermute | solution.py:867
  18.7 61.9 %collective-permute-start.5 = (bf16[240,1152]{1,0:T(8,128)(2,1)S(1)}, bf16[240,1152]{1,0:T(8,128)(2,1)S(1)}, u32[]{:S(2)}, u32[]{:S(2)}) collective-permute-start(bf16[240,1152]{1,0:T(8,128)(2,1)S(1)} %get-tuple-element.24), channel_id=1, source_target_pairs={{0,2},{2,0},{4,6},{6,4},{8,10},{10,8},{12,14},{14,12},{1,3},{3,1},... | collective-permute-start | bytes 1658888 | tf_op jit(solution)/shard_map/ppermute | solution.py:891
  20.7 59.8 %collective-permute-start.6 = (bf16[240,1152]{1,0:T(8,128)(2,1)S(1)}, bf16[240,1152]{1,0:T(8,128)(2,1)S(1)}, u32[]{:S(2)}, u32[]{:S(2)}) collective-permute-start(bf16[240,1152]{1,0:T(8,128)(2,1)S(1)} %get-tuple-element.25), channel_id=1, source_target_pairs={{0,14},{2,4},{4,2},{6,8},{8,6},{10,12},{12,10},{14,0},{1,15},{3,5}... | collective-permute-start | bytes 1658888 | tf_op jit(solution)/shard_map/ppermute | solution.py:892
  25.7 16.7 %collective-permute-start.2 = (f32[40,1024]{1,0:T(8,128)S(1)}, f32[40,1024]{1,0:T(8,128)S(1)}, u32[]{:S(2)}, u32[]{:S(2)}) collective-permute-start(f32[40,1024]{1,0:T(8,128)S(1)} %shard_map.83.mine), channel_id=1, source_target_pairs={{0,4},{2,6},{4,0},{6,2},{8,12},{10,14},{12,8},{14,10},{1,5},{3,7},... | collective-permute-start | bytes 491528 | tf_op jit(solution)/shard_map/ppermute | solution.py:879
  42.4 5.9 %collective-permute-start.9 = (bf16[48,384]{1,0:T(8,128)(2,1)S(1)}, bf16[48,384]{1,0:T(8,128)(2,1)S(1)}, u32[]{:S(2)}, u32[]{:S(2)}) collective-permute-start(bf16[48,384]{1,0:T(8,128)(2,1)S(1)} %get-tuple-element.28), channel_id=1, source_target_pairs={{0,6},{2,8},{4,10},{6,12},{8,14},{10,0},{12,2},{14,4},{1,7},{3,9},... | collective-permute-start | bytes 110600 | tf_op jit(solution)/shard_map/ppermute | solution.py:782
  48.2 7.9 %collective-permute-start.3 = (f32[40,1024]{1,0:T(8,128)S(1)}, f32[40,1024]{1,0:T(8,128)S(1)}, u32[]{:S(2)}, u32[]{:S(2)}) collective-permute-start(f32[40,1024]{1,0:T(8,128)S(1)} %get-tuple-element.21.mine), channel_id=1, source_target_pairs={{0,2},{2,0},{4,6},{6,4},{8,10},{10,8},{12,14},{14,12},{1,3},{3,1},... | collective-permute-start | bytes 491528 | tf_op jit(solution)/shard_map/ppermute | solution.py:879
  50.4 30.1 %collective-permute-start.7 = (bf16[112,768]{1,0:T(8,128)(2,1)S(1)}, bf16[112,768]{1,0:T(8,128)(2,1)S(1)}, u32[]{:S(2)}, u32[]{:S(2)}) collective-permute-start(bf16[112,768]{1,0:T(8,128)(2,1)S(1)} %get-tuple-element.26), channel_id=1, source_target_pairs={{0,4},{2,6},{4,8},{6,10},{8,12},{10,14},{12,0},{14,2},{1,5},{3,7},... | collective-permute-start | bytes 516104 | tf_op jit(solution)/shard_map/ppermute | solution.py:782
  50.6 29.9 %collective-permute-start.8 = (bf16[112,768]{1,0:T(8,128)(2,1)S(1)}, bf16[112,768]{1,0:T(8,128)(2,1)S(1)}, u32[]{:S(2)}, u32[]{:S(2)}) collective-permute-start(bf16[112,768]{1,0:T(8,128)(2,1)S(1)} %get-tuple-element.27), channel_id=1, source_target_pairs={{0,12},{2,14},{4,0},{6,2},{8,4},{10,6},{12,8},{14,10},{1,13},{3,15... | collective-permute-start | bytes 516104 | tf_op jit(solution)/shard_map/ppermute | solution.py:782
  56.1 1.2 %collective-permute-start.13 = (bf16[16,1024]{1,0:T(8,128)(2,1)S(1)}, bf16[16,1024]{1,0:T(8,128)(2,1)S(1)}, u32[]{:S(2)}, u32[]{:S(2)}) collective-permute-start(bf16[16,1024]{1,0:T(8,128)(2,1)S(1)} %shard_map.88), channel_id=1, source_target_pairs={{0,1},{1,0},{2,3},{3,2},{4,5},{5,4},{6,7},{7,6},{8,9},{9,8},{10,11... | collective-permute-start | bytes 98312 | tf_op jit(solution)/shard_map/ppermute | solution.py:839
  57.3 1.3 %collective-permute-start.4 = (bf16[29,1024]{1,0:T(8,128)(2,1)S(1)}, bf16[29,1024]{1,0:T(8,128)(2,1)S(1)}, u32[]{:S(2)}, u32[]{:S(2)}) collective-permute-start(bf16[29,1024]{1,0:T(8,128)(2,1)S(1)} %get-tuple-element.23.own), channel_id=1, source_target_pairs={{0,1},{1,0},{2,3},{3,2},{4,5},{5,4},{6,7},{7,6},{8,9},{9,8},{10,11... | collective-permute-start | bytes 178184 | tf_op jit(solution)/shard_map/ppermute | solution.py:889
  58.6 16.6 %copy-start.2 = (bf16[256,768]{1,0:T(8,128)(2,1)S(1)}, bf16[256,768]{1,0:T(8,128)(2,1)}, u32[]{:S(2)}) copy-start(bf16[256,768]{1,0:T(8,128)(2,1)} %wqkv.1) | copy-start | bytes 1179652
  58.6 16.6 %copy-start.3 = (bf16[256,256]{1,0:T(8,128)(2,1)S(1)}, bf16[256,256]{1,0:T(8,128)(2,1)}, u32[]{:S(2)}) copy-start(bf16[256,256]{1,0:T(8,128)(2,1)} %wo.1) | copy-start | bytes 393220
  58.6 16.6 %copy-start.4 = (bf16[64,256]{1,0:T(8,128)(2,1)S(1)}, bf16[64,256]{1,0:T(8,128)(2,1)}, u32[]{:S(2)}) copy-start(bf16[64,256]{1,0:T(8,128)(2,1)} %we.1) | copy-start | bytes 98308
  58.6 16.6 %copy-start.5 = (bf16[256,64]{0,1:T(8,128)(2,1)S(1)}, bf16[256,64]{0,1:T(8,128)(2,1)}, u32[]{:S(2)}) copy-start(bf16[256,64]{0,1:T(8,128)(2,1)} %param.15) | copy-start | bytes 98308
  58.6 16.6 %copy-start.6 = (f32[256]{0:T(256)S(1)}, f32[256]{0:T(256)}, u32[]{:S(2)}) copy-start(f32[256]{0:T(256)} %param.14) | copy-start | bytes 3076
  58.6 16.6 %copy-start.7 = (f32[8]{0:T(128)S(1)}, f32[8]{0:T(128)}, u32[]{:S(2)}) copy-start(f32[8]{0:T(128)} %scale.1) | copy-start | bytes 100
  58.6 21.9 %collective-permute-start.10 = (bf16[48,384]{1,0:T(8,128)(2,1)S(1)}, bf16[48,384]{1,0:T(8,128)(2,1)S(1)}, u32[]{:S(2)}, u32[]{:S(2)}) collective-permute-start(bf16[48,384]{1,0:T(8,128)(2,1)S(1)} %get-tuple-element.29), channel_id=1, source_target_pairs={{0,10},{2,12},{4,14},{6,0},{8,2},{10,4},{12,6},{14,8},{1,11},{3,13... | collective-permute-start | bytes 110600 | tf_op jit(solution)/shard_map/ppermute | solution.py:782

commit v5 on v4

--- a/solution.py
+++ b/solution.py
@@ -33,20 +33,6 @@
 HIGH = np.array([(-1.0) ** j * LOW[7 - j] for j in range(8)])
 
 
-def lattice_factors():
-    a = np.array([(LOW[2 * (3 - j)], LOW[2 * (3 - j) + 1]) for j in range(4)])
-    b = np.array([(HIGH[2 * (3 - j)], HIGH[2 * (3 - j) + 1]) for j in range(4)])
-    factors = {}
-    for s in (3, 2, 1):
-        k = (a[s] @ b[s]) / (b[s] @ b[s])
-        a, b = (a - k * b) / (1 + k * k), (k * a + b) / (1 + k * k)
-        a, b = a[:s], b[1 : s + 1]
-        factors[s] = float(k)
-    factors[0] = float(a[0][1] / a[0][0])
-    return factors, float(a[0][0]), float(np.sign(b[0][1] / a[0][0]))
-
-
-TURN, SCALE, SIGN = lattice_factors()
 F32 = jnp.float32
 BF16 = jnp.bfloat16
 
@@ -81,7 +67,7 @@
 
 def synthesis_matrix(out_start, out_rows, in_start, in_rows):
     shape = (out_rows, 2 * in_rows)
-    return banded(shape, SCALE * LOW, SCALE * HIGH, 1, -2, out_start - 2 * in_start + 3)
+    return banded(shape, LOW, HIGH, 1, -2, out_start - 2 * in_start + 3)
 
 
 def mxu(a, b):
@@ -151,30 +137,33 @@
 
 
 def synthesis(lows, highs, start, left):
+    parity = start % 2
+
     def cells(cols):
-        if cols is None:
-            return lambda n: None
-        return lambda n: cols[(n - 3 - start) // 2] if 0 <= n - 3 - start < 2 * len(cols) else None
-
-    a, b = cells(lows), cells(highs)
-
-    def stage(a, b, factor):
-        early = Memo(lambda n: half_turn(plus(b(n), a(n), factor)))
-        return (
-            Memo(lambda n: plus(a(n), b(n), -factor)),
-            Memo(lambda n: pick(left, early(n), early(n + 2))),
-        )
-
-    for s in (3, 2, 1):
-        a, b = stage(a, b, TURN[s])
-    last_a, last_b = a, b
-    u = Memo(lambda n: plus(last_a(n), last_b(n), -TURN[0] * SIGN))
-    if SIGN < 0:
-        w = Memo(lambda n: plus(last_a(n) * TURN[0] if last_a(n) is not None else None, last_b(n), -1.0))
-    else:
-        w = Memo(lambda n: plus(last_b(n), last_a(n), TURN[0]))
+        col = lambda k: cols[(k - start) // 2] if 0 <= k - start < 2 * len(cols) else None
+        turned = Memo(lambda k: half_turn(col(k)))
+
+        def at(k):
+            if k % 2 == parity:
+                return col(k)
+            return pick(left, turned(k - 1), turned(k + 1))
+
+        return Memo(at)
+
+    sources = ((cells(lows), LOW), (cells(highs), HIGH))
+
+    def output(first):
+        def make(n):
+            total = None
+            for step in range(4):
+                for source, taps in sources:
+                    total = plus(total, source(n - step), float(taps[2 * step + first]))
+            return total
+
+        return Memo(make)
+
+    u, w = output(0), output(1)
     u_turned, w_turned = Memo(lambda n: half_turn(u(n))), Memo(lambda n: half_turn(w(n)))
-    parity = (start + 3) % 2
 
     def pair(m):
         if m % 2:
@@ -186,6 +175,34 @@
         if n % 2 == parity:
             return pick(left, w(n), u(n))
         return pick(left, w_turned(n - 1), u_turned(n + 1))
+
+    return pair
+
+
+def synthesis_of_lows(lows, start, left):
+    def dup(k):
+        i = (k - start) // 2
+        if not 0 <= i < len(lows):
+            return None
+        turned = rolled(i)
+        return jnp.where(left, lows[i], turned) if (k - start) % 2 == 0 else jnp.where(left, turned, lows[i])
+
+    rolled = Memo(lambda i: half_turn(lows[i]))
+    both = Memo(dup)
+
+    def tap(t):
+        return F32(LOW[t]) if 0 <= t < 8 else F32(0.0)
+
+    weights = [jnp.where(left[0:8], tap(7 - 2 * i), tap(8 - 2 * i)) for i in range(5)]
+    weights = [jnp.concatenate([v] * (left.shape[0] // 8), 0) for v in weights]
+
+    def pair(m):
+        total = None
+        for i in range(5):
+            cell = both(m // 2 - 2 + i)
+            if cell is not None:
+                total = cell * weights[i] if total is None else total + cell * weights[i]
+        return total
 
     return pair
 
@@ -423,20 +440,31 @@
         out[:, lanes:] = side_o[window, :]
 
 
-def ring_kernel(geo, flip, place, mine, other, ring, line):
-    width, total = mine.shape[1], ring.shape[1]
-    fold = line.shape[1] - total
-    line[...] = jnp.zeros(line.shape, F32)
-    lon = place[1]
-    for part, where in ((mine, lon), (other, lon ^ flip)):
-        at = pl.ds(pl.multiple_of(where * (geo.cells[4] * C), LANES), width)
-        line[:, at] = line[:, at] + part[...]
-    ring[:, 0:fold] = line[:, 0:fold] + line[:, total:]
-    ring[:, fold:] = line[:, fold:total]
-
-
-def add_kernel(geo, place, mine, other, ring, tokens):
-    ring[...] = mine[...] + other[...]
+def merge_kernel(size, more, place, mine, other, out):
+    width = mine.shape[1]
+
+    def add(lower, upper):
+        out[:, 0:more] = lower[:, 0:more]
+        out[:, more:width] = lower[:, more:] + upper[:, 0 : width - more]
+        out[:, width:] = upper[:, width - more :]
+
+    lower_half = (place[1] // size) % 2 == 0
+
+    @pl.when(lower_half)
+    def _():
+        add(mine, other)
+
+    @pl.when(jnp.logical_not(lower_half))
+    def _():
+        add(other, mine)
+
+
+def last_merge_kernel(geo, size, more, place, mine, other, ring, tokens, merged):
+    merge_kernel(size, more, place, mine, other, merged)
+    around = ring.shape[1]
+    fold = merged.shape[1] - around
+    ring[:, 0:fold] = merged[:, 0:fold] + merged[:, around:]
+    ring[:, fold:] = merged[:, fold:around]
     skip = -geo.low[4][0]
     tokens[...] = ring[skip : skip + geo.rows[4], :].astype(BF16)
 
@@ -712,7 +740,7 @@
 
     def last(row, count):
         left = first_half(count)
-        pair = synthesis(columns(ylow, row, count), None, begin, left)
+        pair = synthesis_of_lows(columns(ylow, row, count), begin, left)
         for q in range(geo.cells[0] // 2):
             more = part[pl.ds(row, count), pl.ds(LANES * q, LANES)]
             put(done, row, q, (pair(2 * q) + more).astype(BF16))
@@ -862,30 +890,27 @@
         grant=40,
     )
 
+    merged, size = ll4, 1
     total = geo.cells[4] * lons * C
-    flip = lons // 2
-    other = lax.ppermute(ll4, "lon", [(i, i ^ flip) for i in range(lons)])
-    (ring,) = call(
-        functools.partial(ring_kernel, geo, flip),
-        [shape((ll4.shape[0], total))],
-        [pltpu.VMEM((ll4.shape[0], total + 6 * C), F32)],
-        place,
-        ll4,
-        other,
-        cost=100_000,
-    )
-    while flip > 1:
-        flip = flip // 2
-        other = lax.ppermute(ring, "lon", [(i, i ^ flip) for i in range(lons)])
-        ring, tokens = call(
-            functools.partial(add_kernel, geo),
-            [shape(ring.shape), shape((geo.rows[4], total), BF16)],
-            [],
-            place,
-            ring,
-            other,
-            cost=100_000,
-        )
+    while size < lons:
+        other = lax.ppermute(merged, "lon", [(i, i ^ size) for i in range(lons)])
+        more = geo.cells[4] * C * size
+        dims = (merged.shape[0], merged.shape[1] + more)
+        if 2 * size < lons:
+            (merged,) = call(
+                functools.partial(merge_kernel, size, more), [shape(dims)], [], place, merged, other, cost=100_000
+            )
+        else:
+            ring, tokens = call(
+                functools.partial(last_merge_kernel, geo, size, more),
+                [shape((dims[0], total)), shape((geo.rows[4], total), BF16)],
+                [pltpu.VMEM(dims, F32)],
+                place,
+                merged,
+                other,
+                cost=100_000,
+            )
+        size = 2 * size
     others = lax.ppermute(tokens, "lat", swap)
 
     deep_e = lax.ppermute(deep_e, "lon", even_pairs)

time: 96.1 us -> 108 us (1.12)
  the two profiles are of different devices: /device:TPU:0 before, /device:TPU:3 now
where the time goes in v5:
time: 108 us
  waiting for transfers between devices  45.6 us (42%)
  Pallas kernels  37.3 us (35%)
  starting transfers between devices  22.2 us (21%)
  local copies, waits for them, and re-layouts  2.59 us (2%)
    ppermute x3, waiting for transfers between devices, program(): other = lax.ppermute(merged, 'lon', [(i, i ^ size) for i in range(lons)])  41.8 us
    pallas_call x9, Pallas kernels, call(): pl.pallas_call(kernel, out_shape=tuple(out_shape), in_specs=specs, out_sp...  37.3 us
    ppermute x4, starting transfers between devices, shifted(): lax.ppermute(value, 'lon', [(i, (i + by) % lons) for i in range(lons)])  9.72 us
    ppermute x1, starting transfers between devices, program(): corner = lax.ppermute(corner, 'lat', swap)  3.24 us
    ppermute x3, starting transfers between devices, program(): other = lax.ppermute(merged, 'lon', [(i, i ^ size) for i in range(lons)])  3.02 us
    ppermute x4, waiting for transfers between devices, shifted(): lax.ppermute(value, 'lon', [(i, (i + by) % lons) for i in range(lons)])  2.66 us
    ppermute x1, starting transfers between devices, program(): side_o = lax.ppermute(side_o, 'lon', odd_pairs)  2.47 us
    ppermute x1, starting transfers between devices, program(): deep_e = lax.ppermute(deep_e, 'lon', even_pairs)  2.34 us
  transfers between devices with their start and end apart: 14, of which 6 were waited for; matrix products, arithmetic and copies ran while one was open for 0% of the time, Pallas kernels for 26%

profile of v5, /device:TPU:3, one launch (start us, length us, event | category | flops | bytes accessed | tf_op | source)
XLA Modules:
  0.0 108.1 jit_solution(516216546887063221)
XLA Ops:
  0.0 1.0 constant_dynamic-slice_fusion
  1.0 0.7 collective-permute-start
  1.8 0.1 pad_add_fusion.place
  1.9 1.5 %copy-done = bf16[464,2048]{1,0:T(8,128)(2,1)S(1)} copy-done((bf16[464,2048]{1,0:T(8,128)(2,1)S(1)}, bf16[464,2048]{1,0:T(8,128)(2,1)}, u32[]{:S(2)}) %copy-start) | copy-done | bytes 1900568
  3.4 0.7 shard_map.87
  4.0 0.1 collective-permute-start.11
  4.1 2.5 %collective-permute-start.12 = (bf16[464,512]{1,0:T(8,128)(2,1)S(1)}, bf16[464,512]{1,0:T(8,128)(2,1)S(1)}, u32[]{:S(2)}, u32[]{:S(2)}) collective-permute-start(bf16[464,512]{1,0:T(8,128)(2,1)S(1)} %get-tuple-element.29), channel_id=1, source_target_pairs={{0,14},{2,4},{4,2},{6,8},{8,6},{10,12},{12,10},{14,0},{1,15},{3,5}... | collective-permute-start | bytes 1425416 | tf_op jit(solution)/shard_map/ppermute | solution.py:829
  6.6 0.0 collective-permute-done.edge
  6.6 8.6 %shard_map.82 = (f32[40,512]{1,0:T(8,128)S(1)}, f32[3,128,896]{2,1,0:T(8,128)S(1)}, f32[3,64,640]{2,1,0:T(8,128)S(1)}, f32[3,40,512]{2,1,0:T(8,128)S(1)}, bf16[2...) custom-call(s32[2]{0:T(128)S(1)} %pad_add_fusion.place, ...), custom_call_target="tpu_custom_call" | custom-call | flops 20000000 | bytes 1048576 | tf_op jit(solution)/shard_map/pallas_call | solution.py:777
  15.2 2.3 %collective-permute-start.5 = (bf16[240,1152]{1,0:T(8,128)(2,1)S(1)}, bf16[240,1152]{1,0:T(8,128)(2,1)S(1)}, u32[]{:S(2)}, u32[]{:S(2)}) collective-permute-start(bf16[240,1152]{1,0:T(8,128)(2,1)S(1)} %get-tuple-element.22), channel_id=1, source_target_pairs={{0,2},{2,0},{4,6},{6,4},{8,10},{10,8},{12,14},{14,12},{1,3},{3,1},... | collective-permute-start | bytes 1658888 | tf_op jit(solution)/shard_map/ppermute | solution.py:916
  17.5 0.2 collective-permute-start.6
  17.7 1.2 %collective-permute-start.1 = (f32[40,512]{1,0:T(8,128)S(1)}, f32[40,512]{1,0:T(8,128)S(1)}, u32[]{:S(2)}, u32[]{:S(2)}) collective-permute-start(f32[40,512]{1,0:T(8,128)S(1)} %get-tuple-element.19.mine), channel_id=1, source_target_pairs={{0,2},{2,0},{4,6},{6,4},{8,10},{10,8},{12,14},{14,12},{1,3},{3,1},... | collective-permute-start | bytes 245768 | tf_op jit(solution)/shard_map/ppermute | solution.py:896
  18.9 33.3 %collective-permute-done.1.other = f32[40,512]{1,0:T(8,128)S(1)} collective-permute-done((f32[40,512]{1,0:T(8,128)S(1)}, f32[40,512]{1,0:T(8,128)S(1)}, u32[]{:S(2)}, u32[]{:S(2)}) %collective-permute-start.1) | collective-permute-done | bytes 81952 | tf_op jit(solution)/shard_map/ppermute | solution.py:896
  52.2 0.6 shard_map.83.mine
  52.7 1.4 %collective-permute-start.2 = (f32[40,640]{1,0:T(8,128)S(1)}, f32[40,640]{1,0:T(8,128)S(1)}, u32[]{:S(2)}, u32[]{:S(2)}) collective-permute-start(f32[40,640]{1,0:T(8,128)S(1)} %shard_map.83.mine), channel_id=1, source_target_pairs={{0,4},{2,6},{4,0},{6,2},{8,12},{10,14},{12,8},{14,10},{1,5},{3,7},... | collective-permute-start | bytes 307208 | tf_op jit(solution)/shard_map/ppermute | solution.py:896
  54.1 2.2 %collective-permute-done.2.other = f32[40,640]{1,0:T(8,128)S(1)} collective-permute-done((f32[40,640]{1,0:T(8,128)S(1)}, f32[40,640]{1,0:T(8,128)S(1)}, u32[]{:S(2)}, u32[]{:S(2)}) %collective-permute-start.2) | collective-permute-done | bytes 102432 | tf_op jit(solution)/shard_map/ppermute | solution.py:896
  56.3 2.3 %collective-permute-start.9 = (bf16[48,384]{1,0:T(8,128)(2,1)S(1)}, bf16[48,384]{1,0:T(8,128)(2,1)S(1)}, u32[]{:S(2)}, u32[]{:S(2)}) collective-permute-start(bf16[48,384]{1,0:T(8,128)(2,1)S(1)} %get-tuple-element.26), channel_id=1, source_target_pairs={{0,6},{2,8},{4,10},{6,12},{8,14},{10,0},{12,2},{14,4},{1,7},{3,9},... | collective-permute-start | bytes 110600 | tf_op jit(solution)/shard_map/ppermute | solution.py:810
  58.6 0.6 shard_map.84.mine
  59.2 2.7 %collective-permute-done.9.from_m3 = bf16[48,384]{1,0:T(8,128)(2,1)S(1)} collective-permute-done((bf16[48,384]{1,0:T(8,128)(2,1)S(1)}, bf16[48,384]{1,0:T(8,128)(2,1)S(1)}, u32[]{:S(2)}, u32[]{:S(2)}) %collective-permute-start.9) | collective-permute-done | bytes 36896 | tf_op jit(solution)/shard_map/ppermute | solution.py:810
  61.8 0.5 collective-permute-start.3
  62.3 0.0 collective-permute-done.11.side_e
  62.3 1.3 %collective-permute-start.7 = (bf16[112,768]{1,0:T(8,128)(2,1)S(1)}, bf16[112,768]{1,0:T(8,128)(2,1)S(1)}, u32[]{:S(2)}, u32[]{:S(2)}) collective-permute-start(bf16[112,768]{1,0:T(8,128)(2,1)S(1)} %get-tuple-element.24), channel_id=1, source_target_pairs={{0,4},{2,6},{4,8},{6,10},{8,12},{10,14},{12,0},{14,2},{1,5},{3,7},... | collective-permute-start | bytes 516104 | tf_op jit(solution)/shard_map/ppermute | solution.py:810
  63.6 0.0 collective-permute-done.12.side_o
  63.6 2.0 %collective-permute-start.8 = (bf16[112,768]{1,0:T(8,128)(2,1)S(1)}, bf16[112,768]{1,0:T(8,128)(2,1)S(1)}, u32[]{:S(2)}, u32[]{:S(2)}) collective-permute-start(bf16[112,768]{1,0:T(8,128)(2,1)S(1)} %get-tuple-element.25), channel_id=1, source_target_pairs={{0,12},{2,14},{4,0},{6,2},{8,4},{10,6},{12,8},{14,10},{1,13},{3,15... | collective-permute-start | bytes 516104 | tf_op jit(solution)/shard_map/ppermute | solution.py:810
  65.6 0.6 shard_map.88
  66.2 6.3 %collective-permute-done.3.other = f32[40,896]{1,0:T(8,128)S(1)} collective-permute-done((f32[40,896]{1,0:T(8,128)S(1)}, f32[40,896]{1,0:T(8,128)S(1)}, u32[]{:S(2)}, u32[]{:S(2)}) %collective-permute-start.3) | collective-permute-done | bytes 143392 | tf_op jit(solution)/shard_map/ppermute | solution.py:896
  72.4 3.2 %collective-permute-start.13 = (bf16[16,1024]{1,0:T(8,128)(2,1)S(1)}, bf16[16,1024]{1,0:T(8,128)(2,1)S(1)}, u32[]{:S(2)}, u32[]{:S(2)}) collective-permute-start(bf16[16,1024]{1,0:T(8,128)(2,1)S(1)} %shard_map.88), channel_id=1, source_target_pairs={{0,1},{1,0},{2,3},{3,2},{4,5},{5,4},{6,7},{7,6},{8,9},{9,8},{10,11... | collective-permute-start | bytes 98312 | tf_op jit(solution)/shard_map/ppermute | solution.py:867
  75.7 0.6 shard_map.85
  76.3 0.2 collective-permute-done.13.corner
  76.5 0.3 collective-permute-start.4
  76.9 0.9 collective-permute-done.4.others
  77.8 0.0 copy-start.6
  77.8 0.0 copy-start.7
  77.8 4.2 %collective-permute-start.10 = (bf16[48,384]{1,0:T(8,128)(2,1)S(1)}, bf16[48,384]{1,0:T(8,128)(2,1)S(1)}, u32[]{:S(2)}, u32[]{:S(2)}) collective-permute-start(bf16[48,384]{1,0:T(8,128)(2,1)S(1)} %get-tuple-element.27), channel_id=1, source_target_pairs={{0,10},{2,12},{4,14},{6,0},{8,2},{10,4},{12,6},{14,8},{1,11},{3,13... | collective-permute-start | bytes 110600 | tf_op jit(solution)/shard_map/ppermute | solution.py:810
  82.0 11.7 %shard_map.89.refs_0_ = f32[464,2048]{1,0:T(8,128)S(1)} custom-call(s32[2]{0:T(128)S(1)} %pad_add_fusion.place, bf16[96,2048]{1,0:T(8,128)(2,1)S(1)} %collective-permute-done.edge, bf16[464,512]{1,0:T(8,128)(2,1)S(1)} %collective-permute-done.11.side_e, bf16[464,512]{1,0:T(8,128)(2,1)S(1)} %collective-permute-done.12.side_o, ...), custom_call_target="tpu_custom_call" | custom-call | flops 20000000 | bytes 1048576 | tf_op jit(solution)/shard_map/pallas_call | solution.py:777
  93.7 0.0 copy-done.2
  93.7 0.0 copy-done.3
  93.7 0.0 copy-done.4
  93.7 0.0 copy-done.5
  93.7 0.0 copy-done.6
  93.8 0.0 copy-done.7
  93.8 5.3 %shard_map.86.coarse = f32[40,512]{1,0:T(8,128)S(1)} custom-call(s32[2]{0:T(128)S(1)} %pad_add_fusion.place, f32[40,1024]{1,0:T(8,128)S(1)} %get-tuple-element.20.ring, bf16[29,1024]{1,0:T(8,128)(2,1)S(1)} %get-tuple-element.21.own, bf16[29,1024]{1,0:T(8,128)(2,1)S(1)} %collective-permute-done.4.others, bf16[64,256]{1,0:T(8,128)(2,1)S(1)} %copy-done.4, ...), custom_call_target="tpu_custom_call" | custom-call | flops 200000000 | bytes 1048576 | tf_op jit(solution)/shard_map/pallas_call | solution.py:777
  99.1 0.0 collective-permute-done.10.from_p3
  99.1 0.0 collective-permute-done.7.from_m2
  99.1 0.0 collective-permute-done.8.from_p2
  99.1 0.0 collective-permute-done.5.e2
  99.1 0.0 collective-permute-done.6.o2
  99.1 8.9 %shard_map.90 = bf16[464,2048]{1,0:T(8,128)(2,1)} custom-call(s32[2]{0:T(128)S(1)} %pad_add_fusion.place, f32[40,512]{1,0:T(8,128)S(1)} %shard_map.86.coarse, bf16[240,1152]{1,0:T(8,128)(2,1)S(1)} %collective-permute-done.5.e2, bf16[240,1152]{1,0:T(8,128)(2,1)S(1)} %collective-permute-done.6.o2, bf16[112,768]{1,0:T(8,128)(2,1)S(1)} %collective-permute-done.7.from_m2, ...), custom_call_target="tpu_custom_call" | custom-call | flops 20000000 | bytes 1048576 | tf_op jit(solution)/shard_map/pallas_call | solution.py:777
  (10 shorter events, 0.0 us)
Async XLA Ops:
  0.0 6.6 %copy-start.8 = (f32[4,3,64]{2,0,1:T(4,128)S(1)}, f32[4,3,64]{2,0,1:T(4,128)}, u32[]{:S(2)}) copy-start(f32[4,3,64]{2,0,1:T(4,128)} %param.9) | copy-start | bytes 9220
  1.0 5.6 %collective-permute-start = (bf16[96,2048]{1,0:T(8,128)(2,1)S(1)}, bf16[96,2048]{1,0:T(8,128)(2,1)S(1)}, u32[]{:S(2)}, u32[]{:S(2)}) collective-permute-start(bf16[96,2048]{1,0:T(8,128)(2,1)S(1)} %constant_dynamic-slice_fusion), channel_id=1, source_target_pairs={{0,1},{1,0},{2,3},{3,2},{4,5},{5,4},{6,7},{7,6},{8,9},{9,8},{10,11... | collective-permute-start | bytes 1179656 | tf_op jit(solution)/shard_map/ppermute | solution.py:815
  1.9 1.5 %copy-start = (bf16[464,2048]{1,0:T(8,128)(2,1)S(1)}, bf16[464,2048]{1,0:T(8,128)(2,1)}, u32[]{:S(2)}) copy-start(bf16[464,2048]{1,0:T(8,128)(2,1)} %x.5) | copy-start | bytes 5701636
  3.4 3.2 %copy-start.1 = (bf16[464,2048]{1,0:T(8,128)(2,1)S(1)}, bf16[464,2048]{1,0:T(8,128)(2,1)}, u32[]{:S(2)}) copy-start(bf16[464,2048]{1,0:T(8,128)(2,1)} %x.5) | copy-start | bytes 5701636
  4.0 58.3 %collective-permute-start.11 = (bf16[464,512]{1,0:T(8,128)(2,1)S(1)}, bf16[464,512]{1,0:T(8,128)(2,1)S(1)}, u32[]{:S(2)}, u32[]{:S(2)}) collective-permute-start(bf16[464,512]{1,0:T(8,128)(2,1)S(1)} %get-tuple-element.28), channel_id=1, source_target_pairs={{0,2},{2,0},{4,6},{6,4},{8,10},{10,8},{12,14},{14,12},{1,3},{3,1},... | collective-permute-start | bytes 1425416 | tf_op jit(solution)/shard_map/ppermute | solution.py:828
  4.1 59.5 %collective-permute-start.12 = (bf16[464,512]{1,0:T(8,128)(2,1)S(1)}, bf16[464,512]{1,0:T(8,128)(2,1)S(1)}, u32[]{:S(2)}, u32[]{:S(2)}) collective-permute-start(bf16[464,512]{1,0:T(8,128)(2,1)S(1)} %get-tuple-element.29), channel_id=1, source_target_pairs={{0,14},{2,4},{4,2},{6,8},{8,6},{10,12},{12,10},{14,0},{1,15},{3,5}... | collective-permute-start | bytes 1425416 | tf_op jit(solution)/shard_map/ppermute | solution.py:829
  15.2 83.9 %collective-permute-start.5 = (bf16[240,1152]{1,0:T(8,128)(2,1)S(1)}, bf16[240,1152]{1,0:T(8,128)(2,1)S(1)}, u32[]{:S(2)}, u32[]{:S(2)}) collective-permute-start(bf16[240,1152]{1,0:T(8,128)(2,1)S(1)} %get-tuple-element.22), channel_id=1, source_target_pairs={{0,2},{2,0},{4,6},{6,4},{8,10},{10,8},{12,14},{14,12},{1,3},{3,1},... | collective-permute-start | bytes 1658888 | tf_op jit(solution)/shard_map/ppermute | solution.py:916
  17.5 81.6 %collective-permute-start.6 = (bf16[240,1152]{1,0:T(8,128)(2,1)S(1)}, bf16[240,1152]{1,0:T(8,128)(2,1)S(1)}, u32[]{:S(2)}, u32[]{:S(2)}) collective-permute-start(bf16[240,1152]{1,0:T(8,128)(2,1)S(1)} %get-tuple-element.23), channel_id=1, source_target_pairs={{0,14},{2,4},{4,2},{6,8},{8,6},{10,12},{12,10},{14,0},{1,15},{3,5}... | collective-permute-start | bytes 1658888 | tf_op jit(solution)/shard_map/ppermute | solution.py:917
  17.7 34.4 %collective-permute-start.1 = (f32[40,512]{1,0:T(8,128)S(1)}, f32[40,512]{1,0:T(8,128)S(1)}, u32[]{:S(2)}, u32[]{:S(2)}) collective-permute-start(f32[40,512]{1,0:T(8,128)S(1)} %get-tuple-element.19.mine), channel_id=1, source_target_pairs={{0,2},{2,0},{4,6},{6,4},{8,10},{10,8},{12,14},{14,12},{1,3},{3,1},... | collective-permute-start | bytes 245768 | tf_op jit(solution)/shard_map/ppermute | solution.py:896
  52.7 3.6 %collective-permute-start.2 = (f32[40,640]{1,0:T(8,128)S(1)}, f32[40,640]{1,0:T(8,128)S(1)}, u32[]{:S(2)}, u32[]{:S(2)}) collective-permute-start(f32[40,640]{1,0:T(8,128)S(1)} %shard_map.83.mine), channel_id=1, source_target_pairs={{0,4},{2,6},{4,0},{6,2},{8,12},{10,14},{12,8},{14,10},{1,5},{3,7},... | collective-permute-start | bytes 307208 | tf_op jit(solution)/shard_map/ppermute | solution.py:896
  56.3 5.5 %collective-permute-start.9 = (bf16[48,384]{1,0:T(8,128)(2,1)S(1)}, bf16[48,384]{1,0:T(8,128)(2,1)S(1)}, u32[]{:S(2)}, u32[]{:S(2)}) collective-permute-start(bf16[48,384]{1,0:T(8,128)(2,1)S(1)} %get-tuple-element.26), channel_id=1, source_target_pairs={{0,6},{2,8},{4,10},{6,12},{8,14},{10,0},{12,2},{14,4},{1,7},{3,9},... | collective-permute-start | bytes 110600 | tf_op jit(solution)/shard_map/ppermute | solution.py:810
  61.8 10.6 %collective-permute-start.3 = (f32[40,896]{1,0:T(8,128)S(1)}, f32[40,896]{1,0:T(8,128)S(1)}, u32[]{:S(2)}, u32[]{:S(2)}) collective-permute-start(f32[40,896]{1,0:T(8,128)S(1)} %shard_map.84.mine), channel_id=1, source_target_pairs={{0,8},{2,10},{4,12},{6,14},{8,0},{10,2},{12,4},{14,6},{1,9},{3,11}... | collective-permute-start | bytes 430088 | tf_op jit(solution)/shard_map/ppermute | solution.py:896
  62.3 36.8 %collective-permute-start.7 = (bf16[112,768]{1,0:T(8,128)(2,1)S(1)}, bf16[112,768]{1,0:T(8,128)(2,1)S(1)}, u32[]{:S(2)}, u32[]{:S(2)}) collective-permute-start(bf16[112,768]{1,0:T(8,128)(2,1)S(1)} %get-tuple-element.24), channel_id=1, source_target_pairs={{0,4},{2,6},{4,8},{6,10},{8,12},{10,14},{12,0},{14,2},{1,5},{3,7},... | collective-permute-start | bytes 516104 | tf_op jit(solution)/shard_map/ppermute | solution.py:810
  63.6 35.5 %collective-permute-start.8 = (bf16[112,768]{1,0:T(8,128)(2,1)S(1)}, bf16[112,768]{1,0:T(8,128)(2,1)S(1)}, u32[]{:S(2)}, u32[]{:S(2)}) collective-permute-start(bf16[112,768]{1,0:T(8,128)(2,1)S(1)} %get-tuple-element.25), channel_id=1, source_target_pairs={{0,12},{2,14},{4,0},{6,2},{8,4},{10,6},{12,8},{14,10},{1,13},{3,15... | collective-permute-start | bytes 516104 | tf_op jit(solution)/shard_map/ppermute | solution.py:810
  72.4 4.1 %collective-permute-start.13 = (bf16[16,1024]{1,0:T(8,128)(2,1)S(1)}, bf16[16,1024]{1,0:T(8,128)(2,1)S(1)}, u32[]{:S(2)}, u32[]{:S(2)}) collective-permute-start(bf16[16,1024]{1,0:T(8,128)(2,1)S(1)} %shard_map.88), channel_id=1, source_target_pairs={{0,1},{1,0},{2,3},{3,2},{4,5},{5,4},{6,7},{7,6},{8,9},{9,8},{10,11... | collective-permute-start | bytes 98312 | tf_op jit(solution)/shard_map/ppermute | solution.py:867
  76.5 1.3 %collective-permute-start.4 = (bf16[29,1024]{1,0:T(8,128)(2,1)S(1)}, bf16[29,1024]{1,0:T(8,128)(2,1)S(1)}, u32[]{:S(2)}, u32[]{:S(2)}) collective-permute-start(bf16[29,1024]{1,0:T(8,128)(2,1)S(1)} %get-tuple-element.21.own), channel_id=1, source_target_pairs={{0,1},{1,0},{2,3},{3,2},{4,5},{5,4},{6,7},{7,6},{8,9},{9,8},{10,11... | collective-permute-start | bytes 178184 | tf_op jit(solution)/shard_map/ppermute | solution.py:914
  77.8 15.9 %copy-start.2 = (bf16[256,768]{1,0:T(8,128)(2,1)S(1)}, bf16[256,768]{1,0:T(8,128)(2,1)}, u32[]{:S(2)}) copy-start(bf16[256,768]{1,0:T(8,128)(2,1)} %wqkv.1) | copy-start | bytes 1179652
  77.8 15.9 %copy-start.3 = (bf16[256,256]{1,0:T(8,128)(2,1)S(1)}, bf16[256,256]{1,0:T(8,128)(2,1)}, u32[]{:S(2)}) copy-start(bf16[256,256]{1,0:T(8,128)(2,1)} %wo.1) | copy-start | bytes 393220
  77.8 16.0 %copy-start.4 = (bf16[64,256]{1,0:T(8,128)(2,1)S(1)}, bf16[64,256]{1,0:T(8,128)(2,1)}, u32[]{:S(2)}) copy-start(bf16[64,256]{1,0:T(8,128)(2,1)} %we.1) | copy-start | bytes 98308
  77.8 16.0 %copy-start.5 = (bf16[256,64]{0,1:T(8,128)(2,1)S(1)}, bf16[256,64]{0,1:T(8,128)(2,1)}, u32[]{:S(2)}) copy-start(bf16[256,64]{0,1:T(8,128)(2,1)} %param.15) | copy-start | bytes 98308
  77.8 16.0 %copy-start.6 = (f32[256]{0:T(256)S(1)}, f32[256]{0:T(256)}, u32[]{:S(2)}) copy-start(f32[256]{0:T(256)} %param.14) | copy-start | bytes 3076
  77.8 16.0 %copy-start.7 = (f32[8]{0:T(128)S(1)}, f32[8]{0:T(128)}, u32[]{:S(2)}) copy-start(f32[8]{0:T(128)} %scale.1) | copy-start | bytes 100
  77.8 21.3 %collective-permute-start.10 = (bf16[48,384]{1,0:T(8,128)(2,1)S(1)}, bf16[48,384]{1,0:T(8,128)(2,1)S(1)}, u32[]{:S(2)}, u32[]{:S(2)}) collective-permute-start(bf16[48,384]{1,0:T(8,128)(2,1)S(1)} %get-tuple-element.27), channel_id=1, source_target_pairs={{0,10},{2,12},{4,14},{6,0},{8,2},{10,4},{12,6},{14,8},{1,11},{3,13... | collective-permute-start | bytes 110600 | tf_op jit(solution)/shard_map/ppermute | solution.py:810

commit v6 on v5

--- a/solution.py
+++ b/solution.py
@@ -294,9 +294,8 @@
 
 def analysis_kernel(geo, lats, place, edge, gain, x, *refs):
     lat, parity = place[0], place[1] % 2
-    ll4, out2, out3, out4, send_e, send_o, p2, m2, p3, m3 = refs[:10]
-    ext, la, g1, gh, gl, lo2, g2, lo3, g3, lo4, hi2, hi3, hi4, d2, d3, d4, sems, out_sems = refs[10:]
-    outs = {2: (d2, out2), 3: (d3, out3), 4: (d4, out4)}
+    ll4, d2, d3, d4, send_e, send_o, p2, m2, p3, m3 = refs[:10]
+    ext, la, g1, gh, gl, lo2, g2, lo3, g3, lo4, hi2, hi3, hi4, sems = refs[10:]
     rows = geo.rows[0]
     start, count = geo.low[1]
     width = x.shape[1]
@@ -348,12 +347,9 @@
         matrix = masked_rows(matrix, geo.low[level][0], geo.rows[level], lat, lats)
         lo[...] = dot3(matrix, vh, vl)
         low_rows(geo, level, lo, geo.span[level - 1][0], target)
-    copies = []
+    d = {2: d2, 3: d3, 4: d4}
     for level, lo, hi in ((2, lo2, hi2), (3, lo3, hi3), (4, lo4, hi4)):
-        deep_bands(geo, lats, lat, level, {2: (gh, gl), 3: g2, 4: g3}[level], lo, hi, gain, outs[level][0])
-        copies.append(pltpu.make_async_copy(*outs[level], out_sems.at[level - 2]))
-        copies[-1].start()
-    d = {2: d2, 3: d3, 4: d4}
+        deep_bands(geo, lats, lat, level, {2: (gh, gl), 3: g2, 4: g3}[level], lo, hi, gain, d[level])
 
     def fill(distance, to_left, to_right):
         for level, count, row in exchange_plan(geo)[distance]:
@@ -376,8 +372,6 @@
 
     fill(2, m2, p2)
     fill(3, m3, p3)
-    for copy in copies:
-        copy.wait()
 
 
 def deep_bands(geo, lats, lat, level, source, lo, hi, gain, bands):
@@ -469,7 +463,7 @@
     tokens[...] = ring[skip : skip + geo.rows[4], :].astype(BF16)
 
 
-def first_level_kernel(geo, lats, place, edge, side_e, side_o, corner, gain, x, held, ext, la, ha, d1, xh, xl, part, sem):
+def first_level_kernel(geo, lats, place, edge, side_e, side_o, corner, gain, x, part, ext, la, ha, d1, xh, xl, sem):
     lat, parity = place[0], place[1] % 2
     rows, width = x.shape
     lanes = SIDE * C
@@ -541,9 +535,6 @@
         )
         for q in range(geo.cells[0] // 2):
             put(part, row, q, pair(2 * q))
-        copy = pltpu.make_async_copy(part.at[pl.ds(row, most), :], held.at[pl.ds(row, most), :], sem)
-        copy.start()
-        copy.wait()
         return carry
 
     lax.fori_loop(0, rows // most, chunk, 0)
@@ -661,14 +652,7 @@
 
 def synthesis_kernel(geo, lats, place, coarse, e2, o2, from_m2, from_p2, from_m3, from_p3, *refs):
     lat, parity = place[0], place[1] % 2
-    held, (out, up3, up2, up1, ylow, yhigh, done), refs = refs[:4], refs[4:11], refs[11:]
-    part, d2, d3, d4, sems, in_sems = refs
-    arrive = [
-        pltpu.make_async_copy(source, to, in_sems.at[i])
-        for i, (source, to) in enumerate(zip(held, (part, d2, d3, d4)))
-    ]
-    for level in (4, 3, 2, 1):
-        arrive[level - 1].start()
+    part, d2, d3, d4, out, up3, up2, up1, ylow, yhigh, done, sems = refs
     bands = {2: d2, 3: d3, 4: d4}
     plan = exchange_plan(geo)
 
@@ -697,7 +681,6 @@
 
     uppers = {4: coarse, 3: up3, 2: up2, 1: up1}
     for level in (4, 3, 2):
-        arrive[level - 1].wait()
         begin, pairs = geo.span[level]
         below = level - 1
         start, rows = geo.band[below]
@@ -734,7 +717,6 @@
         matrix = synthesis_matrix(half * block, half, geo.band[1][0] + w, LANES)
         h, l = two_terms(up1[w : w + LANES, :])
         ylow[half * block : half * (block + 1), :] = dot3(matrix[:, 0:LANES], h, l)
-    arrive[0].wait()
     begin, pairs = geo.span[1]
     most = 112
 
@@ -766,13 +748,15 @@
         store(whole, rest).wait()
 
 
-def call(kernel, out_shape, scratch, *args, cost=20_000_000, grant=24, raw=(), raw_out=()):
+def call(kernel, out_shape, scratch, *args, cost=20_000_000, grant=24, raw=(), raw_out=(), stay=()):
     vmem = pl.BlockSpec(memory_space=pltpu.VMEM)
     smem = pl.BlockSpec(memory_space=pltpu.SMEM)
     anywhere = pl.BlockSpec(memory_space=pl.ANY)
     specs = [smem if a.ndim == 1 and a.size < 16 else vmem for a in args]
     for at in raw:
         specs[at] = anywhere
+    held = lambda a: pltpu.with_memory_space_constraint(a, pltpu.HBM)
+    args = [held(a) if i in stay else a for i, a in enumerate(args)]
     outs = [anywhere if i in raw_out else vmem for i in range(len(out_shape))]
     return pl.pallas_call(
         kernel,
@@ -823,6 +807,7 @@
         place,
         state_field,
         raw=(1,),
+        stay=(1,),
         cost=1_000_000,
     )
     side_e = lax.ppermute(side_e, "lon", even_pairs)
@@ -849,17 +834,13 @@
             low(4, 3),
         ]
         + [pltpu.VMEM((geo.band[level][1], w[level - 1]), F32) for level in (2, 3, 4)]
-        + [pltpu.VMEM(dims, F32) for dims in bands[1:]]
-        + [
-            pltpu.SemaphoreType.DMA((geo.low[1][1] // 112,)),
-            pltpu.SemaphoreType.DMA((3,)),
-        ],
+        + [pltpu.SemaphoreType.DMA((geo.low[1][1] // 112,))],
         place,
         edge,
         skip_gain,
         state_field,
         raw=(3,),
-        raw_out=(1, 2, 3),
+        stay=(3,),
     )
     (corner,) = call(
         corners_kernel, [shape((NEAR, 2 * wide), BF16)], [], place, side_e, side_o, cost=100_000
@@ -875,7 +856,6 @@
             pltpu.VMEM(bands[0], F32),
             pltpu.VMEM((2 * LANES, w[1]), BF16),
             pltpu.VMEM((2 * LANES, w[1]), BF16),
-            pltpu.VMEM((rows, width), F32),
             pltpu.SemaphoreType.DMA,
         ],
         place,
@@ -886,8 +866,8 @@
         skip_gain,
         state_field,
         raw=(6,),
-        raw_out=(0,),
-        grant=40,
+        stay=(6,),
+        grant=30,
     )
 
     merged, size = ll4, 1
@@ -950,12 +930,7 @@
             pltpu.VMEM((rows, w[1]), F32),
             pltpu.VMEM((geo.band[1][1], w[2]), F32),
             pltpu.VMEM((rows, width), BF16),
-            pltpu.VMEM((rows, width), F32),
-        ]
-        + [pltpu.VMEM(dims, F32) for dims in bands[1:]]
-        + [
             pltpu.SemaphoreType.DMA((rows // 112 + 1,)),
-            pltpu.SemaphoreType.DMA((4,)),
         ],
         place,
         coarse,
@@ -969,9 +944,8 @@
         d2,
         d3,
         d4,
-        raw=(8, 9, 10, 11),
         raw_out=(0,),
-        grant=40,
+        grant=30,
     )
     return out
 

time: 108 us -> 107 us (level)
  local copies, waits for them, and re-layouts: 2.59 us -> 1.07 us
    unnamed x19 -> x15, local copies, waits for them, and re-layouts: 1.56 us -> 0.03 us
  transfers between devices with their start and end apart: 14 -> 14, of which waited for: 6 -> 6; matrix products, arithmetic and copies ran while one was open for 0% -> 0% of each run, Pallas kernels for 26% -> 27%
where the time goes in v6:
time: 107 us
  waiting for transfers between devices  46.4 us (43%)
  Pallas kernels  36.6 us (34%)
  starting transfers between devices  22.2 us (21%)
  local copies, waits for them, and re-layouts  1.07 us (1%)
    ppermute x3, waiting for transfers between devices, program(): other = lax.ppermute(merged, 'lon', [(i, i ^ size) for i in range(lons)])  42.6 us
    pallas_call x9, Pallas kernels, call(): pl.pallas_call(kernel, out_shape=tuple(out_shape), in_specs=specs, out_sp...  36.6 us
    ppermute x4, starting transfers between devices, shifted(): lax.ppermute(value, 'lon', [(i, (i + by) % lons) for i in range(lons)])  9.73 us
    ppermute x1, starting transfers between devices, program(): corner = lax.ppermute(corner, 'lat', swap)  3.24 us
    ppermute x3, starting transfers between devices, program(): other = lax.ppermute(merged, 'lon', [(i, i ^ size) for i in range(lons)])  3.02 us
    ppermute x4, waiting for transfers between devices, shifted(): lax.ppermute(value, 'lon', [(i, (i + by) % lons) for i in range(lons)])  2.66 us
    ppermute x1, starting transfers between devices, program(): side_o = lax.ppermute(side_o, 'lon', odd_pairs)  2.47 us
    ppermute x1, starting transfers between devices, program(): deep_e = lax.ppermute(deep_e, 'lon', even_pairs)  2.33 us
  transfers between devices with their start and end apart: 14, of which 6 were waited for; matrix products, arithmetic and copies ran while one was open for 0% of the time, Pallas kernels for 27%

profile of v6, /device:TPU:3, one launch (start us, length us, event | category | flops | bytes accessed | tf_op | source)
XLA Modules:
  0.0 106.7 jit_solution(15058690116263343876)
XLA Ops:
  0.0 1.0 constant_dynamic-slice_fusion
  1.0 0.7 collective-permute-start
  1.8 0.1 pad_add_fusion.place
  1.9 1.7 %shard_map.87 = (bf16[464,512]{1,0:T(8,128)(2,1)S(1)}, bf16[464,512]{1,0:T(8,128)(2,1)S(1)}) custom-call(s32[2]{0:T(128)S(1)} %pad_add_fusion.place, bf16[464,2048]{1,0:T(8,128)(2,1)} %x.5), custom_call_target="tpu_custom_call" | custom-call | flops 1000000 | bytes 1048576 | tf_op jit(solution)/shard_map/pallas_call | solution.py:761
  3.6 0.1 collective-permute-start.11
  3.7 2.5 %collective-permute-start.12 = (bf16[464,512]{1,0:T(8,128)(2,1)S(1)}, bf16[464,512]{1,0:T(8,128)(2,1)S(1)}, u32[]{:S(2)}, u32[]{:S(2)}) collective-permute-start(bf16[464,512]{1,0:T(8,128)(2,1)S(1)} %get-tuple-element.29), channel_id=1, source_target_pairs={{0,14},{2,4},{4,2},{6,8},{8,6},{10,12},{12,10},{14,0},{1,15},{3,5}... | collective-permute-start | bytes 1425416 | tf_op jit(solution)/shard_map/ppermute | solution.py:814
  6.1 0.0 copy-done.6
  6.2 0.0 collective-permute-done.edge
  6.2 7.8 %shard_map.82 = (f32[40,512]{1,0:T(8,128)S(1)}, f32[3,128,896]{2,1,0:T(8,128)S(1)}, f32[3,64,640]{2,1,0:T(8,128)S(1)}, f32[3,40,512]{2,1,0:T(8,128)S(1)}, bf16[2...) custom-call(s32[2]{0:T(128)S(1)} %pad_add_fusion.place, ...), custom_call_target="tpu_custom_call" | custom-call | flops 20000000 | bytes 1048576 | tf_op jit(solution)/shard_map/pallas_call | solution.py:761
  13.9 2.3 %collective-permute-start.5 = (bf16[240,1152]{1,0:T(8,128)(2,1)S(1)}, bf16[240,1152]{1,0:T(8,128)(2,1)S(1)}, u32[]{:S(2)}, u32[]{:S(2)}) collective-permute-start(bf16[240,1152]{1,0:T(8,128)(2,1)S(1)} %get-tuple-element.22), channel_id=1, source_target_pairs={{0,2},{2,0},{4,6},{6,4},{8,10},{10,8},{12,14},{14,12},{1,3},{3,1},... | collective-permute-start | bytes 1658888 | tf_op jit(solution)/shard_map/ppermute | solution.py:896
  16.3 0.2 collective-permute-start.6
  16.5 1.1 %collective-permute-start.1 = (f32[40,512]{1,0:T(8,128)S(1)}, f32[40,512]{1,0:T(8,128)S(1)}, u32[]{:S(2)}, u32[]{:S(2)}) collective-permute-start(f32[40,512]{1,0:T(8,128)S(1)} %get-tuple-element.19.mine), channel_id=1, source_target_pairs={{0,2},{2,0},{4,6},{6,4},{8,10},{10,8},{12,14},{14,12},{1,3},{3,1},... | collective-permute-start | bytes 245768 | tf_op jit(solution)/shard_map/ppermute | solution.py:876
  17.6 34.1 %collective-permute-done.1.other = f32[40,512]{1,0:T(8,128)S(1)} collective-permute-done((f32[40,512]{1,0:T(8,128)S(1)}, f32[40,512]{1,0:T(8,128)S(1)}, u32[]{:S(2)}, u32[]{:S(2)}) %collective-permute-start.1) | collective-permute-done | bytes 81952 | tf_op jit(solution)/shard_map/ppermute | solution.py:876
  51.7 0.6 shard_map.83.mine
  52.3 1.4 %collective-permute-start.2 = (f32[40,640]{1,0:T(8,128)S(1)}, f32[40,640]{1,0:T(8,128)S(1)}, u32[]{:S(2)}, u32[]{:S(2)}) collective-permute-start(f32[40,640]{1,0:T(8,128)S(1)} %shard_map.83.mine), channel_id=1, source_target_pairs={{0,4},{2,6},{4,0},{6,2},{8,12},{10,14},{12,8},{14,10},{1,5},{3,7},... | collective-permute-start | bytes 307208 | tf_op jit(solution)/shard_map/ppermute | solution.py:876
  53.6 2.2 %collective-permute-done.2.other = f32[40,640]{1,0:T(8,128)S(1)} collective-permute-done((f32[40,640]{1,0:T(8,128)S(1)}, f32[40,640]{1,0:T(8,128)S(1)}, u32[]{:S(2)}, u32[]{:S(2)}) %collective-permute-start.2) | collective-permute-done | bytes 102432 | tf_op jit(solution)/shard_map/ppermute | solution.py:876
  55.9 2.3 %collective-permute-start.9 = (bf16[48,384]{1,0:T(8,128)(2,1)S(1)}, bf16[48,384]{1,0:T(8,128)(2,1)S(1)}, u32[]{:S(2)}, u32[]{:S(2)}) collective-permute-start(bf16[48,384]{1,0:T(8,128)(2,1)S(1)} %get-tuple-element.26), channel_id=1, source_target_pairs={{0,6},{2,8},{4,10},{6,12},{8,14},{10,0},{12,2},{14,4},{1,7},{3,9},... | collective-permute-start | bytes 110600 | tf_op jit(solution)/shard_map/ppermute | solution.py:794
  58.1 0.6 shard_map.84.mine
  58.7 2.6 %collective-permute-done.9.from_m3 = bf16[48,384]{1,0:T(8,128)(2,1)S(1)} collective-permute-done((bf16[48,384]{1,0:T(8,128)(2,1)S(1)}, bf16[48,384]{1,0:T(8,128)(2,1)S(1)}, u32[]{:S(2)}, u32[]{:S(2)}) %collective-permute-start.9) | collective-permute-done | bytes 36896 | tf_op jit(solution)/shard_map/ppermute | solution.py:794
  61.4 0.5 collective-permute-start.3
  61.9 0.0 collective-permute-done.11.side_e
  61.9 1.3 %collective-permute-start.7 = (bf16[112,768]{1,0:T(8,128)(2,1)S(1)}, bf16[112,768]{1,0:T(8,128)(2,1)S(1)}, u32[]{:S(2)}, u32[]{:S(2)}) collective-permute-start(bf16[112,768]{1,0:T(8,128)(2,1)S(1)} %get-tuple-element.24), channel_id=1, source_target_pairs={{0,4},{2,6},{4,8},{6,10},{8,12},{10,14},{12,0},{14,2},{1,5},{3,7},... | collective-permute-start | bytes 516104 | tf_op jit(solution)/shard_map/ppermute | solution.py:794
  63.2 0.0 collective-permute-done.12.side_o
  63.2 2.0 %collective-permute-start.8 = (bf16[112,768]{1,0:T(8,128)(2,1)S(1)}, bf16[112,768]{1,0:T(8,128)(2,1)S(1)}, u32[]{:S(2)}, u32[]{:S(2)}) collective-permute-start(bf16[112,768]{1,0:T(8,128)(2,1)S(1)} %get-tuple-element.25), channel_id=1, source_target_pairs={{0,12},{2,14},{4,0},{6,2},{8,4},{10,6},{12,8},{14,10},{1,13},{3,15... | collective-permute-start | bytes 516104 | tf_op jit(solution)/shard_map/ppermute | solution.py:794
  65.2 0.6 shard_map.88
  65.7 6.3 %collective-permute-done.3.other = f32[40,896]{1,0:T(8,128)S(1)} collective-permute-done((f32[40,896]{1,0:T(8,128)S(1)}, f32[40,896]{1,0:T(8,128)S(1)}, u32[]{:S(2)}, u32[]{:S(2)}) %collective-permute-start.3) | collective-permute-done | bytes 143392 | tf_op jit(solution)/shard_map/ppermute | solution.py:876
  72.0 3.2 %collective-permute-start.13 = (bf16[16,1024]{1,0:T(8,128)(2,1)S(1)}, bf16[16,1024]{1,0:T(8,128)(2,1)S(1)}, u32[]{:S(2)}, u32[]{:S(2)}) collective-permute-start(bf16[16,1024]{1,0:T(8,128)(2,1)S(1)} %shard_map.88), channel_id=1, source_target_pairs={{0,1},{1,0},{2,3},{3,2},{4,5},{5,4},{6,7},{7,6},{8,9},{9,8},{10,11... | collective-permute-start | bytes 98312 | tf_op jit(solution)/shard_map/ppermute | solution.py:848
  75.2 0.6 shard_map.85
  75.8 0.2 collective-permute-done.13.corner
  76.1 0.3 collective-permute-start.4
  76.4 0.9 collective-permute-done.4.others
  77.3 0.0 copy-start.4
  77.4 0.0 copy-start.5
  77.4 4.2 %collective-permute-start.10 = (bf16[48,384]{1,0:T(8,128)(2,1)S(1)}, bf16[48,384]{1,0:T(8,128)(2,1)S(1)}, u32[]{:S(2)}, u32[]{:S(2)}) collective-permute-start(bf16[48,384]{1,0:T(8,128)(2,1)S(1)} %get-tuple-element.27), channel_id=1, source_target_pairs={{0,10},{2,12},{4,14},{6,0},{8,2},{10,4},{12,6},{14,8},{1,11},{3,13... | collective-permute-start | bytes 110600 | tf_op jit(solution)/shard_map/ppermute | solution.py:794
  81.6 12.0 %shard_map.89.refs_0_ = f32[464,2048]{1,0:T(8,128)S(1)} custom-call(s32[2]{0:T(128)S(1)} %pad_add_fusion.place, bf16[96,2048]{1,0:T(8,128)(2,1)S(1)} %collective-permute-done.edge, bf16[464,512]{1,0:T(8,128)(2,1)S(1)} %collective-permute-done.11.side_e, bf16[464,512]{1,0:T(8,128)(2,1)S(1)} %collective-permute-done.12.side_o, ...), custom_call_target="tpu_custom_call" | custom-call | flops 20000000 | bytes 1048576 | tf_op jit(solution)/shard_map/pallas_call | solution.py:761
  93.6 0.0 copy-done
  93.6 0.0 copy-done.1
  93.6 0.0 copy-done.2
  93.6 0.0 copy-done.3
  93.6 0.0 copy-done.4
  93.6 0.0 copy-done.5
  93.6 5.3 %shard_map.86.coarse = f32[40,512]{1,0:T(8,128)S(1)} custom-call(s32[2]{0:T(128)S(1)} %pad_add_fusion.place, f32[40,1024]{1,0:T(8,128)S(1)} %get-tuple-element.20.ring, bf16[29,1024]{1,0:T(8,128)(2,1)S(1)} %get-tuple-element.21.own, bf16[29,1024]{1,0:T(8,128)(2,1)S(1)} %collective-permute-done.4.others, bf16[64,256]{1,0:T(8,128)(2,1)S(1)} %copy-done.2, ...), custom_call_target="tpu_custom_call" | custom-call | flops 200000000 | bytes 1048576 | tf_op jit(solution)/shard_map/pallas_call | solution.py:761
  98.9 0.0 collective-permute-done.10.from_p3
  98.9 0.0 collective-permute-done.7.from_m2
  98.9 0.0 collective-permute-done.8.from_p2
  98.9 0.0 collective-permute-done.5.e2
  98.9 0.0 collective-permute-done.6.o2
  99.0 7.5 %shard_map.90 = bf16[464,2048]{1,0:T(8,128)(2,1)} custom-call(s32[2]{0:T(128)S(1)} %pad_add_fusion.place, f32[40,512]{1,0:T(8,128)S(1)} %shard_map.86.coarse, bf16[240,1152]{1,0:T(8,128)(2,1)S(1)} %collective-permute-done.5.e2, bf16[240,1152]{1,0:T(8,128)(2,1)S(1)} %collective-permute-done.6.o2, bf16[112,768]{1,0:T(8,128)(2,1)S(1)} %collective-permute-done.7.from_m2, ...), custom_call_target="tpu_custom_call" | custom-call | flops 20000000 | bytes 1048576 | tf_op jit(solution)/shard_map/pallas_call | solution.py:761
  (6 shorter events, 0.0 us)
Async XLA Ops:
  0.0 6.2 %copy-start.6 = (f32[4,3,64]{2,0,1:T(4,128)S(1)}, f32[4,3,64]{2,0,1:T(4,128)}, u32[]{:S(2)}) copy-start(f32[4,3,64]{2,0,1:T(4,128)} %param.9) | copy-start | bytes 9220
  1.0 5.1 %collective-permute-start = (bf16[96,2048]{1,0:T(8,128)(2,1)S(1)}, bf16[96,2048]{1,0:T(8,128)(2,1)S(1)}, u32[]{:S(2)}, u32[]{:S(2)}) collective-permute-start(bf16[96,2048]{1,0:T(8,128)(2,1)S(1)} %constant_dynamic-slice_fusion), channel_id=1, source_target_pairs={{0,1},{1,0},{2,3},{3,2},{4,5},{5,4},{6,7},{7,6},{8,9},{9,8},{10,11... | collective-permute-start | bytes 1179656 | tf_op jit(solution)/shard_map/ppermute | solution.py:799
  3.6 58.3 %collective-permute-start.11 = (bf16[464,512]{1,0:T(8,128)(2,1)S(1)}, bf16[464,512]{1,0:T(8,128)(2,1)S(1)}, u32[]{:S(2)}, u32[]{:S(2)}) collective-permute-start(bf16[464,512]{1,0:T(8,128)(2,1)S(1)} %get-tuple-element.28), channel_id=1, source_target_pairs={{0,2},{2,0},{4,6},{6,4},{8,10},{10,8},{12,14},{14,12},{1,3},{3,1},... | collective-permute-start | bytes 1425416 | tf_op jit(solution)/shard_map/ppermute | solution.py:813
  3.7 59.5 %collective-permute-start.12 = (bf16[464,512]{1,0:T(8,128)(2,1)S(1)}, bf16[464,512]{1,0:T(8,128)(2,1)S(1)}, u32[]{:S(2)}, u32[]{:S(2)}) collective-permute-start(bf16[464,512]{1,0:T(8,128)(2,1)S(1)} %get-tuple-element.29), channel_id=1, source_target_pairs={{0,14},{2,4},{4,2},{6,8},{8,6},{10,12},{12,10},{14,0},{1,15},{3,5}... | collective-permute-start | bytes 1425416 | tf_op jit(solution)/shard_map/ppermute | solution.py:814
  13.9 85.0 %collective-permute-start.5 = (bf16[240,1152]{1,0:T(8,128)(2,1)S(1)}, bf16[240,1152]{1,0:T(8,128)(2,1)S(1)}, u32[]{:S(2)}, u32[]{:S(2)}) collective-permute-start(bf16[240,1152]{1,0:T(8,128)(2,1)S(1)} %get-tuple-element.22), channel_id=1, source_target_pairs={{0,2},{2,0},{4,6},{6,4},{8,10},{10,8},{12,14},{14,12},{1,3},{3,1},... | collective-permute-start | bytes 1658888 | tf_op jit(solution)/shard_map/ppermute | solution.py:896
  16.3 82.7 %collective-permute-start.6 = (bf16[240,1152]{1,0:T(8,128)(2,1)S(1)}, bf16[240,1152]{1,0:T(8,128)(2,1)S(1)}, u32[]{:S(2)}, u32[]{:S(2)}) collective-permute-start(bf16[240,1152]{1,0:T(8,128)(2,1)S(1)} %get-tuple-element.23), channel_id=1, source_target_pairs={{0,14},{2,4},{4,2},{6,8},{8,6},{10,12},{12,10},{14,0},{1,15},{3,5}... | collective-permute-start | bytes 1658888 | tf_op jit(solution)/shard_map/ppermute | solution.py:897
  16.5 35.3 %collective-permute-start.1 = (f32[40,512]{1,0:T(8,128)S(1)}, f32[40,512]{1,0:T(8,128)S(1)}, u32[]{:S(2)}, u32[]{:S(2)}) collective-permute-start(f32[40,512]{1,0:T(8,128)S(1)} %get-tuple-element.19.mine), channel_id=1, source_target_pairs={{0,2},{2,0},{4,6},{6,4},{8,10},{10,8},{12,14},{14,12},{1,3},{3,1},... | collective-permute-start | bytes 245768 | tf_op jit(solution)/shard_map/ppermute | solution.py:876
  52.3 3.6 %collective-permute-start.2 = (f32[40,640]{1,0:T(8,128)S(1)}, f32[40,640]{1,0:T(8,128)S(1)}, u32[]{:S(2)}, u32[]{:S(2)}) collective-permute-start(f32[40,640]{1,0:T(8,128)S(1)} %shard_map.83.mine), channel_id=1, source_target_pairs={{0,4},{2,6},{4,0},{6,2},{8,12},{10,14},{12,8},{14,10},{1,5},{3,7},... | collective-permute-start | bytes 307208 | tf_op jit(solution)/shard_map/ppermute | solution.py:876
  55.9 5.5 %collective-permute-start.9 = (bf16[48,384]{1,0:T(8,128)(2,1)S(1)}, bf16[48,384]{1,0:T(8,128)(2,1)S(1)}, u32[]{:S(2)}, u32[]{:S(2)}) collective-permute-start(bf16[48,384]{1,0:T(8,128)(2,1)S(1)} %get-tuple-element.26), channel_id=1, source_target_pairs={{0,6},{2,8},{4,10},{6,12},{8,14},{10,0},{12,2},{14,4},{1,7},{3,9},... | collective-permute-start | bytes 110600 | tf_op jit(solution)/shard_map/ppermute | solution.py:794
  61.4 10.6 %collective-permute-start.3 = (f32[40,896]{1,0:T(8,128)S(1)}, f32[40,896]{1,0:T(8,128)S(1)}, u32[]{:S(2)}, u32[]{:S(2)}) collective-permute-start(f32[40,896]{1,0:T(8,128)S(1)} %shard_map.84.mine), channel_id=1, source_target_pairs={{0,8},{2,10},{4,12},{6,14},{8,0},{10,2},{12,4},{14,6},{1,9},{3,11}... | collective-permute-start | bytes 430088 | tf_op jit(solution)/shard_map/ppermute | solution.py:876
  61.9 37.0 %collective-permute-start.7 = (bf16[112,768]{1,0:T(8,128)(2,1)S(1)}, bf16[112,768]{1,0:T(8,128)(2,1)S(1)}, u32[]{:S(2)}, u32[]{:S(2)}) collective-permute-start(bf16[112,768]{1,0:T(8,128)(2,1)S(1)} %get-tuple-element.24), channel_id=1, source_target_pairs={{0,4},{2,6},{4,8},{6,10},{8,12},{10,14},{12,0},{14,2},{1,5},{3,7},... | collective-permute-start | bytes 516104 | tf_op jit(solution)/shard_map/ppermute | solution.py:794
  63.2 35.7 %collective-permute-start.8 = (bf16[112,768]{1,0:T(8,128)(2,1)S(1)}, bf16[112,768]{1,0:T(8,128)(2,1)S(1)}, u32[]{:S(2)}, u32[]{:S(2)}) collective-permute-start(bf16[112,768]{1,0:T(8,128)(2,1)S(1)} %get-tuple-element.25), channel_id=1, source_target_pairs={{0,12},{2,14},{4,0},{6,2},{8,4},{10,6},{12,8},{14,10},{1,13},{3,15... | collective-permute-start | bytes 516104 | tf_op jit(solution)/shard_map/ppermute | solution.py:794
  72.0 4.1 %collective-permute-start.13 = (bf16[16,1024]{1,0:T(8,128)(2,1)S(1)}, bf16[16,1024]{1,0:T(8,128)(2,1)S(1)}, u32[]{:S(2)}, u32[]{:S(2)}) collective-permute-start(bf16[16,1024]{1,0:T(8,128)(2,1)S(1)} %shard_map.88), channel_id=1, source_target_pairs={{0,1},{1,0},{2,3},{3,2},{4,5},{5,4},{6,7},{7,6},{8,9},{9,8},{10,11... | collective-permute-start | bytes 98312 | tf_op jit(solution)/shard_map/ppermute | solution.py:848
  76.1 1.3 %collective-permute-start.4 = (bf16[29,1024]{1,0:T(8,128)(2,1)S(1)}, bf16[29,1024]{1,0:T(8,128)(2,1)S(1)}, u32[]{:S(2)}, u32[]{:S(2)}) collective-permute-start(bf16[29,1024]{1,0:T(8,128)(2,1)S(1)} %get-tuple-element.21.own), channel_id=1, source_target_pairs={{0,1},{1,0},{2,3},{3,2},{4,5},{5,4},{6,7},{7,6},{8,9},{9,8},{10,11... | collective-permute-start | bytes 178184 | tf_op jit(solution)/shard_map/ppermute | solution.py:894
  77.3 16.2 %copy-start = (bf16[256,768]{1,0:T(8,128)(2,1)S(1)}, bf16[256,768]{1,0:T(8,128)(2,1)}, u32[]{:S(2)}) copy-start(bf16[256,768]{1,0:T(8,128)(2,1)} %wqkv.1) | copy-start | bytes 1179652
  77.3 16.2 %copy-start.1 = (bf16[256,256]{1,0:T(8,128)(2,1)S(1)}, bf16[256,256]{1,0:T(8,128)(2,1)}, u32[]{:S(2)}) copy-start(bf16[256,256]{1,0:T(8,128)(2,1)} %wo.1) | copy-start | bytes 393220
  77.3 16.2 %copy-start.2 = (bf16[64,256]{1,0:T(8,128)(2,1)S(1)}, bf16[64,256]{1,0:T(8,128)(2,1)}, u32[]{:S(2)}) copy-start(bf16[64,256]{1,0:T(8,128)(2,1)} %we.1) | copy-start | bytes 98308
  77.3 16.2 %copy-start.3 = (bf16[256,64]{0,1:T(8,128)(2,1)S(1)}, bf16[256,64]{0,1:T(8,128)(2,1)}, u32[]{:S(2)}) copy-start(bf16[256,64]{0,1:T(8,128)(2,1)} %param.15) | copy-start | bytes 98308
  77.3 16.2 %copy-start.4 = (f32[256]{0:T(256)S(1)}, f32[256]{0:T(256)}, u32[]{:S(2)}) copy-start(f32[256]{0:T(256)} %param.14) | copy-start | bytes 3076
  77.4 16.2 %copy-start.5 = (f32[8]{0:T(128)S(1)}, f32[8]{0:T(128)}, u32[]{:S(2)}) copy-start(f32[8]{0:T(128)} %scale.1) | copy-start | bytes 100
  77.4 21.5 %collective-permute-start.10 = (bf16[48,384]{1,0:T(8,128)(2,1)S(1)}, bf16[48,384]{1,0:T(8,128)(2,1)S(1)}, u32[]{:S(2)}, u32[]{:S(2)}) collective-permute-start(bf16[48,384]{1,0:T(8,128)(2,1)S(1)} %get-tuple-element.27), channel_id=1, source_target_pairs={{0,10},{2,12},{4,14},{6,0},{8,2},{10,4},{12,6},{14,8},{1,11},{3,13... | collective-permute-start | bytes 110600 | tf_op jit(solution)/shard_map/ppermute | solution.py:794

commit v7 on v6

--- a/solution.py
+++ b/solution.py
@@ -463,66 +463,152 @@
     tokens[...] = ring[skip : skip + geo.rows[4], :].astype(BF16)
 
 
-def first_level_kernel(geo, lats, place, edge, side_e, side_o, corner, gain, x, part, ext, la, ha, d1, xh, xl, sem):
-    lat, parity = place[0], place[1] % 2
-    rows, width = x.shape
-    lanes = SIDE * C
-    copy = pltpu.make_async_copy(x, ext.at[pl.ds(NEAR, rows), pl.ds(lanes, width)], sem)
-    copy.start()
-    sides = (slice(0, lanes), slice(lanes + width, width + 2 * lanes))
-    own = slice(lanes, lanes + width)
-    inner = slice(NEAR, NEAR + rows)
-
-    def rims(near, far, edges):
-        ext[far, :] = jnp.zeros((NEAR, width + 2 * lanes), BF16)
-        ext[near, own] = edges
-        ext[near, sides[0]] = corner[:, 0:lanes]
-        ext[near, sides[1]] = corner[:, lanes:]
-
-    top, bottom = slice(0, NEAR), slice(NEAR + rows, 2 * NEAR + rows)
-
-    @pl.when(lat == 0)
-    def _():
-        rims(bottom, top, edge[0:NEAR, :])
-
-    @pl.when(lat != 0)
-    def _():
-        rims(top, bottom, edge[HALO - NEAR :, :])
-
-    @pl.when(parity == 0)
-    def _():
-        ext[inner, sides[0]] = side_o[...]
-        ext[inner, sides[1]] = side_e[...]
-
-    @pl.when(parity != 0)
-    def _():
-        ext[inner, sides[0]] = side_e[...]
-        ext[inner, sides[1]] = side_o[...]
-
+def latitude_bands(geo, lats, lat, ext, la, ha):
     start, count = geo.band[1]
     low = analysis_matrix(LOW, start, 120, -NEAR, 256)
     high = analysis_matrix(HIGH, start, 120, -NEAR, 256)
-    copy.wait()
     for b in range(count // 120):
         data = ext[240 * b : 240 * b + 256, :]
         for matrix, out in ((low, la), (high, ha)):
             mh, ml = two_terms(masked_rows(matrix, start + 120 * b, geo.rows[1], lat, lats))
             out[120 * b : 120 * b + 120, :] = mxu(mh, data) + mxu(ml, data)
-    band_rows(geo, 1, la, 0, ha, -SIDE, gain, d1)
+
+
+def first_bands(row, los, his, start, groups, gain, bands):
+    step = los[0].shape[0]
+    left = first_half(step)
+    g = []
+    for b in range(3):
+        one = gain[0, b : b + 1, :]
+        g.append(jnp.broadcast_to(jnp.concatenate([one, one], 1), (step, LANES)))
+    _, high = analysis(los, start, left)
+    for q, k in groups:
+        put(bands, row, q, high(k) * g[0], (0,))
+    low, high = analysis(his, start, left)
+    for q, k in groups:
+        put(bands, row, q, low(k) * g[1], (1,))
+        put(bands, row, q, high(k) * g[2], (2,))
+
+
+def edge_pairs():
+    return 2
+
+
+def inner_kernel(geo, lats, place, edge, gain, x, d1, lo_rim, hi_rim, ext, la, ha, sem):
+    lat = place[0]
+    rows, width = x.shape
+    copy = pltpu.make_async_copy(x, ext.at[pl.ds(NEAR, rows), :], sem)
+    copy.start()
+
+    @pl.when(lat == 0)
+    def _():
+        ext[0:NEAR, :] = jnp.zeros((NEAR, width), BF16)
+        ext[NEAR + rows :, :] = edge[0:NEAR, :]
+
+    @pl.when(lat != 0)
+    def _():
+        ext[0:NEAR, :] = edge[HALO - NEAR :, :]
+        ext[NEAR + rows :, :] = jnp.zeros((NEAR, width), BF16)
+
+    copy.wait()
+    latitude_bands(geo, lats, lat, ext, la, ha)
+    rim = SIDE * C
+    for out, source in ((lo_rim, la), (hi_rim, ha)):
+        out[:, 0:rim] = source[:, 0:rim]
+        out[:, rim:] = source[:, width - rim :]
+    first, pairs = geo.span[1]
+    ends = edge_pairs()
+    groups = [(q, first + 2 * q) for q in range(ends, pairs - ends)]
+    step = best_step(geo.band[1][1])
+
+    def body(c, carry):
+        row = pl.multiple_of(c * step, step)
+        first_bands(row, columns(la, row, step), columns(ha, row, step), 0, groups, gain, d1)
+        return carry
+
+    lax.fori_loop(0, geo.band[1][1] // step, body, 0)
+
+
+def first_level_kernel(geo, lats, place, side_e, side_o, corner, gain, inner, lo_rim, hi_rim, part, ext, lo_side, hi_side, d1, la, ha, xh, xl):
+    lat, parity = place[0], place[1] % 2
+    rows, _ = part.shape
+    lanes = SIDE * C
+    sides = (slice(0, lanes), slice(lanes, 2 * lanes))
+    own = slice(NEAR, NEAR + rows)
+    top, bottom = slice(0, NEAR), slice(NEAR + rows, 2 * NEAR + rows)
+
+    def rims(near, far):
+        ext[far, :] = jnp.zeros((NEAR, 2 * lanes), BF16)
+        ext[near, :] = corner[...]
+
+    @pl.when(lat == 0)
+    def _():
+        rims(bottom, top)
+
+    @pl.when(lat != 0)
+    def _():
+        rims(top, bottom)
+
+    @pl.when(parity == 0)
+    def _():
+        ext[own, sides[0]] = side_o[...]
+        ext[own, sides[1]] = side_e[...]
+
+    @pl.when(parity != 0)
+    def _():
+        ext[own, sides[0]] = side_e[...]
+        ext[own, sides[1]] = side_o[...]
+
+    start, count = geo.band[1]
+    latitude_bands(geo, lats, lat, ext, lo_side, hi_side)
+    first, pairs = geo.span[1]
+    ends = edge_pairs()
+    step = best_step(count)
+    beside = SIDE // 2
+
+    def body(c, carry):
+        row = pl.multiple_of(c * step, step)
+        sources = [columns(ref, row, step) for ref in (lo_side, hi_side, lo_rim, hi_rim)]
+        lo_s, hi_s, lo_r, hi_r = sources
+        groups = [(q, first + 2 * q) for q in range(ends)]
+        first_bands(
+            row, lo_s[:beside] + lo_r[:beside], hi_s[:beside] + hi_r[:beside], -SIDE, groups, gain, d1
+        )
+        groups = [(ends + q, first + 2 * (pairs - ends + q)) for q in range(ends)]
+        begin = geo.cells[0] - SIDE
+        first_bands(
+            row, lo_r[beside:] + lo_s[beside:], hi_r[beside:] + hi_s[beside:], begin, groups, gain, d1
+        )
+        return carry
+
+    lax.fori_loop(0, count // step, body, 0)
+    rim, whole = ends * LANES, pairs * LANES
+
+    def terms(b, window, to):
+        for lanes_to, source, lanes_from in (
+            (slice(0, rim), d1, slice(0, rim)),
+            (slice(rim, whole - rim), inner, slice(rim, whole - rim)),
+            (slice(whole - rim, whole), d1, slice(rim, 2 * rim)),
+        ):
+            h, l = two_terms(source[b, window, lanes_from])
+            xh[to, lanes_to], xl[to, lanes_to] = h, l
+
     half = rows // 2
     ylow, yhigh = la, ha
-    used = slice(0, d1.shape[2])
+    used = slice(0, whole)
+    upper, lower = slice(0, LANES), slice(LANES, 2 * LANES)
     for block in range(2):
         w = 0 if block == 0 else count - LANES
         window = slice(w, w + LANES)
         target = slice(half * block, half * (block + 1))
         matrix = synthesis_matrix(half * block, half, start + w, LANES)
         sh, sl = two_terms(matrix)
-        xh[0:LANES, :], xl[0:LANES, :] = two_terms(d1[0, window, :])
-        xh[LANES:, :], xl[LANES:, :] = two_terms(d1[2, window, :])
+        terms(0, window, upper)
+        terms(2, window, lower)
         yhigh[target, used] = mxu(sh, xh[...]) + mxu(sh, xl[...]) + mxu(sl, xh[...])
-        vh, vl = two_terms(d1[1, window, :])
+        terms(1, window, lower)
         sh, sl = sh[:, LANES:], sl[:, LANES:]
+        vh, vl = xh[lower, :], xl[lower, :]
         ylow[target, used] = mxu(sh, vh) + mxu(sh, vl) + mxu(sl, vh)
 
     begin, pairs = geo.span[1]
@@ -581,7 +667,7 @@
     queries = mxu(embedded.astype(BF16), wqkv[:, 0:E]).astype(BF16)
     lane = lax.broadcasted_iota(jnp.int32, (1, E), 1)
     block = keys.shape[0] // blocks
-    factor = [scale[h] * (1.0 / math.sqrt(HEAD_DIM)) for h in range(HEADS)]
+    factor = [scale[h] * (math.log2(math.e) / math.sqrt(HEAD_DIM)) for h in range(HEADS)]
 
     def keyvals(start):
         spread = mxu(keys[pl.ds(start, block), :], we[...]).astype(BF16)
@@ -591,8 +677,7 @@
     def scores_of(h, k):
         mine = (lane >= h * HEAD_DIM) & (lane < (h + 1) * HEAD_DIM)
         q = jnp.where(mine, queries, jnp.zeros_like(queries))
-        s = lax.dot_general(q, k, (((1,), (1,)), ((), ())), preferred_element_type=F32)
-        return s * factor[h]
+        return lax.dot_general(q, k, (((1,), (1,)), ((), ())), preferred_element_type=F32)
 
     def masked(h, value):
         mine = (lane >= h * HEAD_DIM) & (lane < (h + 1) * HEAD_DIM)
@@ -603,7 +688,7 @@
         attended = jnp.zeros((count, E), F32)
         for h in range(HEADS):
             s = scores_of(h, k)
-            w = jnp.exp(s - jnp.max(s, -1, keepdims=True))
+            w = jnp.exp2((s - jnp.max(s, -1, keepdims=True)) * factor[h])
             total = jnp.sum(w, -1, keepdims=True)
             attended = attended + masked(h, mxu(w.astype(BF16), v) / total)
     else:
@@ -616,8 +701,8 @@
             for h in range(HEADS):
                 s = scores_of(h, k)
                 peak = jnp.maximum(peaks[h], jnp.max(s, -1, keepdims=True))
-                shrink = jnp.exp(peaks[h] - peak)
-                w = jnp.exp(s - peak)
+                shrink = jnp.exp2((peaks[h] - peak) * factor[h])
+                w = jnp.exp2((s - peak) * factor[h])
                 new_peaks.append(peak)
                 new_totals.append(totals[h] * shrink + jnp.sum(w, -1, keepdims=True))
                 shrunk = shrunk + masked(h, sums * shrink + mxu(w.astype(BF16), v))
@@ -846,27 +931,45 @@
         corners_kernel, [shape((NEAR, 2 * wide), BF16)], [], place, side_e, side_o, cost=100_000
     )
     corner = lax.ppermute(corner, "lat", swap)
+    count = geo.band[1][1]
+    inner, lo_rim, hi_rim = call(
+        functools.partial(inner_kernel, geo, lats),
+        [shape(bands[0]), shape((count, 2 * wide)), shape((count, 2 * wide))],
+        [
+            pltpu.VMEM((extended, width), BF16),
+            pltpu.VMEM((count, width), F32),
+            pltpu.VMEM((count, width), F32),
+            pltpu.SemaphoreType.DMA,
+        ],
+        place,
+        edge,
+        skip_gain,
+        state_field,
+        raw=(3,),
+        stay=(3,),
+    )
+    ends = 2 * edge_pairs() * LANES
     (part,) = call(
         functools.partial(first_level_kernel, geo, lats),
         [shape((rows, width))],
         [
-            pltpu.VMEM((extended, width + 2 * wide), BF16),
-            pltpu.VMEM((rows, width + 2 * wide), F32),
-            pltpu.VMEM((rows, width + 2 * wide), F32),
-            pltpu.VMEM(bands[0], F32),
+            pltpu.VMEM((extended, 2 * wide), BF16),
+            pltpu.VMEM((count, 2 * wide), F32),
+            pltpu.VMEM((count, 2 * wide), F32),
+            pltpu.VMEM((3, count, ends), F32),
+            pltpu.VMEM((rows, w[1]), F32),
+            pltpu.VMEM((rows, w[1]), F32),
             pltpu.VMEM((2 * LANES, w[1]), BF16),
             pltpu.VMEM((2 * LANES, w[1]), BF16),
-            pltpu.SemaphoreType.DMA,
         ],
         place,
-        edge,
         side_e,
         side_o,
         corner,
         skip_gain,
-        state_field,
-        raw=(6,),
-        stay=(6,),
+        inner,
+        lo_rim,
+        hi_rim,
         grant=30,
     )
 

time: 107 us -> 107 us (level)
  the two profiles are of different devices: /device:TPU:3 before, /device:TPU:0 now
where the time goes in v7:
time: 107 us
  waiting for transfers between devices  45.3 us (42%)
  Pallas kernels  37.5 us (35%)
  starting transfers between devices  22.8 us (21%)
  local copies, waits for them, and re-layouts  1.08 us (1%)
    ppermute x3, waiting for transfers between devices, program(): other = lax.ppermute(merged, 'lon', [(i, i ^ size) for i in range(lons)])  42.5 us
    pallas_call x10, Pallas kernels, call(): pl.pallas_call(kernel, out_shape=tuple(out_shape), in_specs=specs, out_sp...  37.5 us
    ppermute x4, starting transfers between devices, shifted(): lax.ppermute(value, 'lon', [(i, (i + by) % lons) for i in range(lons)])  9.2 us
    ppermute x3, starting transfers between devices, program(): other = lax.ppermute(merged, 'lon', [(i, i ^ size) for i in range(lons)])  4.79 us
    ppermute x1, starting transfers between devices, program(): side_o = lax.ppermute(side_o, 'lon', odd_pairs)  3.57 us
    ppermute x1, starting transfers between devices, program(): side_e = lax.ppermute(side_e, 'lon', even_pairs)  2.56 us
  transfers between devices with their start and end apart: 14, of which 6 were waited for; matrix products, arithmetic and copies ran while one was open for 0% of the time, Pallas kernels for 28%

profile of v7, /device:TPU:0, one launch (start us, length us, event | category | flops | bytes accessed | tf_op | source)
XLA Modules:
  0.0 107.2 jit_solution(17600499565289330762)
XLA Ops:
  0.0 1.0 constant_dynamic-slice_fusion
  1.0 0.6 collective-permute-start
  1.6 0.1 pad_add_fusion.place
  1.7 1.7 %shard_map.87 = (bf16[464,512]{1,0:T(8,128)(2,1)S(1)}, bf16[464,512]{1,0:T(8,128)(2,1)S(1)}) custom-call(s32[2]{0:T(128)S(1)} %pad_add_fusion.place, bf16[464,2048]{1,0:T(8,128)(2,1)} %x.5), custom_call_target="tpu_custom_call" | custom-call | flops 1000000 | bytes 1048576 | tf_op jit(solution)/shard_map/pallas_call | solution.py:846
  3.4 2.6 %collective-permute-start.11 = (bf16[464,512]{1,0:T(8,128)(2,1)S(1)}, bf16[464,512]{1,0:T(8,128)(2,1)S(1)}, u32[]{:S(2)}, u32[]{:S(2)}) collective-permute-start(bf16[464,512]{1,0:T(8,128)(2,1)S(1)} %get-tuple-element.31), channel_id=1, source_target_pairs={{0,2},{2,0},{4,6},{6,4},{8,10},{10,8},{12,14},{14,12},{1,3},{3,1},... | collective-permute-start | bytes 1425416 | tf_op jit(solution)/shard_map/ppermute | solution.py:898
  6.0 3.6 %collective-permute-start.12 = (bf16[464,512]{1,0:T(8,128)(2,1)S(1)}, bf16[464,512]{1,0:T(8,128)(2,1)S(1)}, u32[]{:S(2)}, u32[]{:S(2)}) collective-permute-start(bf16[464,512]{1,0:T(8,128)(2,1)S(1)} %get-tuple-element.32), channel_id=1, source_target_pairs={{0,14},{2,4},{4,2},{6,8},{8,6},{10,12},{12,10},{14,0},{1,15},{3,5}... | collective-permute-start | bytes 1425416 | tf_op jit(solution)/shard_map/ppermute | solution.py:899
  9.5 0.0 copy-done.6
  9.6 0.0 collective-permute-done.edge
  9.6 7.8 %shard_map.82 = (f32[40,512]{1,0:T(8,128)S(1)}, f32[3,128,896]{2,1,0:T(8,128)S(1)}, f32[3,64,640]{2,1,0:T(8,128)S(1)}, f32[3,40,512]{2,1,0:T(8,128)S(1)}, bf16[2...) custom-call(s32[2]{0:T(128)S(1)} %pad_add_fusion.place, ...), custom_call_target="tpu_custom_call" | custom-call | flops 20000000 | bytes 1048576 | tf_op jit(solution)/shard_map/pallas_call | solution.py:846
  17.3 0.1 collective-permute-start.5
  17.4 1.9 %collective-permute-start.6 = (bf16[240,1152]{1,0:T(8,128)(2,1)S(1)}, bf16[240,1152]{1,0:T(8,128)(2,1)S(1)}, u32[]{:S(2)}, u32[]{:S(2)}) collective-permute-start(bf16[240,1152]{1,0:T(8,128)(2,1)S(1)} %get-tuple-element.26), channel_id=1, source_target_pairs={{0,14},{2,4},{4,2},{6,8},{8,6},{10,12},{12,10},{14,0},{1,15},{3,5}... | collective-permute-start | bytes 1658888 | tf_op jit(solution)/shard_map/ppermute | solution.py:1000
  19.3 0.6 collective-permute-start.1
  19.9 33.2 %collective-permute-done.1.other = f32[40,512]{1,0:T(8,128)S(1)} collective-permute-done((f32[40,512]{1,0:T(8,128)S(1)}, f32[40,512]{1,0:T(8,128)S(1)}, u32[]{:S(2)}, u32[]{:S(2)}) %collective-permute-start.1) | collective-permute-done | bytes 81952 | tf_op jit(solution)/shard_map/ppermute | solution.py:979
  53.1 0.6 shard_map.83.mine
  53.7 1.9 %collective-permute-start.2 = (f32[40,640]{1,0:T(8,128)S(1)}, f32[40,640]{1,0:T(8,128)S(1)}, u32[]{:S(2)}, u32[]{:S(2)}) collective-permute-start(f32[40,640]{1,0:T(8,128)S(1)} %shard_map.83.mine), channel_id=1, source_target_pairs={{0,4},{2,6},{4,0},{6,2},{8,12},{10,14},{12,8},{14,10},{1,5},{3,7},... | collective-permute-start | bytes 307208 | tf_op jit(solution)/shard_map/ppermute | solution.py:979
  55.6 2.9 %collective-permute-done.2.other = f32[40,640]{1,0:T(8,128)S(1)} collective-permute-done((f32[40,640]{1,0:T(8,128)S(1)}, f32[40,640]{1,0:T(8,128)S(1)}, u32[]{:S(2)}, u32[]{:S(2)}) %collective-permute-start.2) | collective-permute-done | bytes 102432 | tf_op jit(solution)/shard_map/ppermute | solution.py:979
  58.5 3.7 %collective-permute-start.10 = (bf16[48,384]{1,0:T(8,128)(2,1)S(1)}, bf16[48,384]{1,0:T(8,128)(2,1)S(1)}, u32[]{:S(2)}, u32[]{:S(2)}) collective-permute-start(bf16[48,384]{1,0:T(8,128)(2,1)S(1)} %get-tuple-element.30), channel_id=1, source_target_pairs={{0,10},{2,12},{4,14},{6,0},{8,2},{10,4},{12,6},{14,8},{1,11},{3,13... | collective-permute-start | bytes 110600 | tf_op jit(solution)/shard_map/ppermute | solution.py:879
  62.2 0.6 shard_map.84.mine
  62.8 1.1 collective-permute-done.10.from_p3
  63.8 2.3 %collective-permute-start.3 = (f32[40,896]{1,0:T(8,128)S(1)}, f32[40,896]{1,0:T(8,128)S(1)}, u32[]{:S(2)}, u32[]{:S(2)}) collective-permute-start(f32[40,896]{1,0:T(8,128)S(1)} %shard_map.84.mine), channel_id=1, source_target_pairs={{0,8},{2,10},{4,12},{6,14},{8,0},{10,2},{12,4},{14,6},{1,9},{3,11}... | collective-permute-start | bytes 430088 | tf_op jit(solution)/shard_map/ppermute | solution.py:979
  66.1 0.0 collective-permute-done.11.side_e
  66.1 3.4 %collective-permute-start.7 = (bf16[112,768]{1,0:T(8,128)(2,1)S(1)}, bf16[112,768]{1,0:T(8,128)(2,1)S(1)}, u32[]{:S(2)}, u32[]{:S(2)}) collective-permute-start(bf16[112,768]{1,0:T(8,128)(2,1)S(1)} %get-tuple-element.27), channel_id=1, source_target_pairs={{0,4},{2,6},{4,8},{6,10},{8,12},{10,14},{12,0},{14,2},{1,5},{3,7},... | collective-permute-start | bytes 516104 | tf_op jit(solution)/shard_map/ppermute | solution.py:879
  69.5 0.0 collective-permute-done.12.side_o
  69.5 0.5 collective-permute-start.8
  70.0 0.6 shard_map.88
  70.5 6.4 %collective-permute-done.3.other = f32[40,896]{1,0:T(8,128)S(1)} collective-permute-done((f32[40,896]{1,0:T(8,128)S(1)}, f32[40,896]{1,0:T(8,128)S(1)}, u32[]{:S(2)}, u32[]{:S(2)}) %collective-permute-start.3) | collective-permute-done | bytes 143392 | tf_op jit(solution)/shard_map/ppermute | solution.py:979
  76.9 0.0 collective-permute-start.13
  76.9 0.6 shard_map.85
  77.5 0.6 collective-permute-done.13.corner
  78.1 0.2 collective-permute-start.4
  78.3 1.1 %collective-permute-done.4.others = bf16[29,1024]{1,0:T(8,128)(2,1)S(1)} collective-permute-done((bf16[29,1024]{1,0:T(8,128)(2,1)S(1)}, bf16[29,1024]{1,0:T(8,128)(2,1)S(1)}, u32[]{:S(2)}, u32[]{:S(2)}) %collective-permute-start.4) | collective-permute-done | bytes 59424 | tf_op jit(solution)/shard_map/ppermute | solution.py:997
  79.4 1.6 %collective-permute-start.9 = (bf16[48,384]{1,0:T(8,128)(2,1)S(1)}, bf16[48,384]{1,0:T(8,128)(2,1)S(1)}, u32[]{:S(2)}, u32[]{:S(2)}) collective-permute-start(bf16[48,384]{1,0:T(8,128)(2,1)S(1)} %get-tuple-element.29), channel_id=1, source_target_pairs={{0,6},{2,8},{4,10},{6,12},{8,14},{10,0},{12,2},{14,4},{1,7},{3,9},... | collective-permute-start | bytes 110600 | tf_op jit(solution)/shard_map/ppermute | solution.py:879
  81.0 4.5 %shard_map.89 = (f32[3,240,1280]{2,1,0:T(8,128)S(1)}, f32[240,1024]{1,0:T(8,128)S(1)}, f32[240,1024]{1,0:T(8,128)S(1)}) custom-call(s32[2]{0:T(128)S(1)} %pad_add_fusion.place, bf16[96,2048]{1,0:T(8,128)(2,1)S(1)} %collective-permute-done.edge, f32[4,3,64]{2,1,0:T(4,128)S(1)} %copy.9.gain, bf16[464,2048]{1,0:T(8,128)(2,1)} %x.5), custom_call_target="tpu_custom_call" | custom-call | flops 20000000 | bytes 1048576 | tf_op jit(solution)/shard_map/pallas_call | solution.py:846
  85.5 0.0 copy-start
  85.5 0.0 copy-start.1
  85.6 0.0 copy-start.2
  85.6 0.0 copy-start.3
  85.6 0.0 copy-start.4
  85.6 0.0 copy-start.5
  85.6 8.7 %shard_map.90.refs_0_ = f32[464,2048]{1,0:T(8,128)S(1)} custom-call(s32[2]{0:T(128)S(1)} %pad_add_fusion.place, bf16[464,512]{1,0:T(8,128)(2,1)S(1)} %collective-permute-done.11.side_e, bf16[464,512]{1,0:T(8,128)(2,1)S(1)} %collective-permute-done.12.side_o, bf16[16,1024]{1,0:T(8,128)(2,1)S(1)} %collective-permute-done.13.corner, f32[4,3,64]{2,1,0:T(4,128)S(1)} %copy.9.gain, ...), custom_call_target="tpu_custom_call" | custom-call | flops 20000000 | bytes 1048576 | tf_op jit(solution)/shard_map/pallas_call | solution.py:846
  94.3 0.0 copy-done
  94.4 5.1 %shard_map.86.coarse = f32[40,512]{1,0:T(8,128)S(1)} custom-call(s32[2]{0:T(128)S(1)} %pad_add_fusion.place, f32[40,1024]{1,0:T(8,128)S(1)} %get-tuple-element.23.ring, bf16[29,1024]{1,0:T(8,128)(2,1)S(1)} %get-tuple-element.24.own, bf16[29,1024]{1,0:T(8,128)(2,1)S(1)} %collective-permute-done.4.others, bf16[64,256]{1,0:T(8,128)(2,1)S(1)} %copy-done.2, ...), custom_call_target="tpu_custom_call" | custom-call | flops 200000000 | bytes 1048576 | tf_op jit(solution)/shard_map/pallas_call | solution.py:846
  99.4 0.0 collective-permute-done.9.from_m3
  99.4 0.0 collective-permute-done.7.from_m2
  99.5 0.0 collective-permute-done.8.from_p2
  99.5 0.0 collective-permute-done.5.e2
  99.5 0.0 collective-permute-done.6.o2
  99.5 7.5 %shard_map.91 = bf16[464,2048]{1,0:T(8,128)(2,1)} custom-call(s32[2]{0:T(128)S(1)} %pad_add_fusion.place, f32[40,512]{1,0:T(8,128)S(1)} %shard_map.86.coarse, bf16[240,1152]{1,0:T(8,128)(2,1)S(1)} %collective-permute-done.5.e2, bf16[240,1152]{1,0:T(8,128)(2,1)S(1)} %collective-permute-done.6.o2, bf16[112,768]{1,0:T(8,128)(2,1)S(1)} %collective-permute-done.7.from_m2, ...), custom_call_target="tpu_custom_call" | custom-call | flops 20000000 | bytes 1048576 | tf_op jit(solution)/shard_map/pallas_call | solution.py:846
  (7 shorter events, 0.0 us)
Async XLA Ops:
  0.0 9.6 %copy-start.6 = (f32[4,3,64]{2,0,1:T(4,128)S(1)}, f32[4,3,64]{2,0,1:T(4,128)}, u32[]{:S(2)}) copy-start(f32[4,3,64]{2,0,1:T(4,128)} %param.9) | copy-start | bytes 9220
  1.0 8.5 %collective-permute-start = (bf16[96,2048]{1,0:T(8,128)(2,1)S(1)}, bf16[96,2048]{1,0:T(8,128)(2,1)S(1)}, u32[]{:S(2)}, u32[]{:S(2)}) collective-permute-start(bf16[96,2048]{1,0:T(8,128)(2,1)S(1)} %constant_dynamic-slice_fusion), channel_id=1, source_target_pairs={{0,1},{1,0},{2,3},{3,2},{4,5},{5,4},{6,7},{7,6},{8,9},{9,8},{10,11... | collective-permute-start | bytes 1179656 | tf_op jit(solution)/shard_map/ppermute | solution.py:884
  3.4 62.7 %collective-permute-start.11 = (bf16[464,512]{1,0:T(8,128)(2,1)S(1)}, bf16[464,512]{1,0:T(8,128)(2,1)S(1)}, u32[]{:S(2)}, u32[]{:S(2)}) collective-permute-start(bf16[464,512]{1,0:T(8,128)(2,1)S(1)} %get-tuple-element.31), channel_id=1, source_target_pairs={{0,2},{2,0},{4,6},{6,4},{8,10},{10,8},{12,14},{14,12},{1,3},{3,1},... | collective-permute-start | bytes 1425416 | tf_op jit(solution)/shard_map/ppermute | solution.py:898
  6.0 63.5 %collective-permute-start.12 = (bf16[464,512]{1,0:T(8,128)(2,1)S(1)}, bf16[464,512]{1,0:T(8,128)(2,1)S(1)}, u32[]{:S(2)}, u32[]{:S(2)}) collective-permute-start(bf16[464,512]{1,0:T(8,128)(2,1)S(1)} %get-tuple-element.32), channel_id=1, source_target_pairs={{0,14},{2,4},{4,2},{6,8},{8,6},{10,12},{12,10},{14,0},{1,15},{3,5}... | collective-permute-start | bytes 1425416 | tf_op jit(solution)/shard_map/ppermute | solution.py:899
  17.3 82.1 %collective-permute-start.5 = (bf16[240,1152]{1,0:T(8,128)(2,1)S(1)}, bf16[240,1152]{1,0:T(8,128)(2,1)S(1)}, u32[]{:S(2)}, u32[]{:S(2)}) collective-permute-start(bf16[240,1152]{1,0:T(8,128)(2,1)S(1)} %get-tuple-element.25), channel_id=1, source_target_pairs={{0,2},{2,0},{4,6},{6,4},{8,10},{10,8},{12,14},{14,12},{1,3},{3,1},... | collective-permute-start | bytes 1658888 | tf_op jit(solution)/shard_map/ppermute | solution.py:999
  17.4 82.1 %collective-permute-start.6 = (bf16[240,1152]{1,0:T(8,128)(2,1)S(1)}, bf16[240,1152]{1,0:T(8,128)(2,1)S(1)}, u32[]{:S(2)}, u32[]{:S(2)}) collective-permute-start(bf16[240,1152]{1,0:T(8,128)(2,1)S(1)} %get-tuple-element.26), channel_id=1, source_target_pairs={{0,14},{2,4},{4,2},{6,8},{8,6},{10,12},{12,10},{14,0},{1,15},{3,5}... | collective-permute-start | bytes 1658888 | tf_op jit(solution)/shard_map/ppermute | solution.py:1000
  19.3 33.9 %collective-permute-start.1 = (f32[40,512]{1,0:T(8,128)S(1)}, f32[40,512]{1,0:T(8,128)S(1)}, u32[]{:S(2)}, u32[]{:S(2)}) collective-permute-start(f32[40,512]{1,0:T(8,128)S(1)} %get-tuple-element.22.mine), channel_id=1, source_target_pairs={{0,2},{2,0},{4,6},{6,4},{8,10},{10,8},{12,14},{14,12},{1,3},{3,1},... | collective-permute-start | bytes 245768 | tf_op jit(solution)/shard_map/ppermute | solution.py:979
  53.7 4.8 %collective-permute-start.2 = (f32[40,640]{1,0:T(8,128)S(1)}, f32[40,640]{1,0:T(8,128)S(1)}, u32[]{:S(2)}, u32[]{:S(2)}) collective-permute-start(f32[40,640]{1,0:T(8,128)S(1)} %shard_map.83.mine), channel_id=1, source_target_pairs={{0,4},{2,6},{4,0},{6,2},{8,12},{10,14},{12,8},{14,10},{1,5},{3,7},... | collective-permute-start | bytes 307208 | tf_op jit(solution)/shard_map/ppermute | solution.py:979
  58.5 5.4 %collective-permute-start.10 = (bf16[48,384]{1,0:T(8,128)(2,1)S(1)}, bf16[48,384]{1,0:T(8,128)(2,1)S(1)}, u32[]{:S(2)}, u32[]{:S(2)}) collective-permute-start(bf16[48,384]{1,0:T(8,128)(2,1)S(1)} %get-tuple-element.30), channel_id=1, source_target_pairs={{0,10},{2,12},{4,14},{6,0},{8,2},{10,4},{12,6},{14,8},{1,11},{3,13... | collective-permute-start | bytes 110600 | tf_op jit(solution)/shard_map/ppermute | solution.py:879
  63.8 13.1 %collective-permute-start.3 = (f32[40,896]{1,0:T(8,128)S(1)}, f32[40,896]{1,0:T(8,128)S(1)}, u32[]{:S(2)}, u32[]{:S(2)}) collective-permute-start(f32[40,896]{1,0:T(8,128)S(1)} %shard_map.84.mine), channel_id=1, source_target_pairs={{0,8},{2,10},{4,12},{6,14},{8,0},{10,2},{12,4},{14,6},{1,9},{3,11}... | collective-permute-start | bytes 430088 | tf_op jit(solution)/shard_map/ppermute | solution.py:979
  66.1 33.3 %collective-permute-start.7 = (bf16[112,768]{1,0:T(8,128)(2,1)S(1)}, bf16[112,768]{1,0:T(8,128)(2,1)S(1)}, u32[]{:S(2)}, u32[]{:S(2)}) collective-permute-start(bf16[112,768]{1,0:T(8,128)(2,1)S(1)} %get-tuple-element.27), channel_id=1, source_target_pairs={{0,4},{2,6},{4,8},{6,10},{8,12},{10,14},{12,0},{14,2},{1,5},{3,7},... | collective-permute-start | bytes 516104 | tf_op jit(solution)/shard_map/ppermute | solution.py:879
  69.5 29.9 %collective-permute-start.8 = (bf16[112,768]{1,0:T(8,128)(2,1)S(1)}, bf16[112,768]{1,0:T(8,128)(2,1)S(1)}, u32[]{:S(2)}, u32[]{:S(2)}) collective-permute-start(bf16[112,768]{1,0:T(8,128)(2,1)S(1)} %get-tuple-element.28), channel_id=1, source_target_pairs={{0,12},{2,14},{4,0},{6,2},{8,4},{10,6},{12,8},{14,10},{1,13},{3,15... | collective-permute-start | bytes 516104 | tf_op jit(solution)/shard_map/ppermute | solution.py:879
  76.9 1.2 %collective-permute-start.13 = (bf16[16,1024]{1,0:T(8,128)(2,1)S(1)}, bf16[16,1024]{1,0:T(8,128)(2,1)S(1)}, u32[]{:S(2)}, u32[]{:S(2)}) collective-permute-start(bf16[16,1024]{1,0:T(8,128)(2,1)S(1)} %shard_map.88), channel_id=1, source_target_pairs={{0,1},{1,0},{2,3},{3,2},{4,5},{5,4},{6,7},{7,6},{8,9},{9,8},{10,11... | collective-permute-start | bytes 98312 | tf_op jit(solution)/shard_map/ppermute | solution.py:933
  78.1 1.3 %collective-permute-start.4 = (bf16[29,1024]{1,0:T(8,128)(2,1)S(1)}, bf16[29,1024]{1,0:T(8,128)(2,1)S(1)}, u32[]{:S(2)}, u32[]{:S(2)}) collective-permute-start(bf16[29,1024]{1,0:T(8,128)(2,1)S(1)} %get-tuple-element.24.own), channel_id=1, source_target_pairs={{0,1},{1,0},{2,3},{3,2},{4,5},{5,4},{6,7},{7,6},{8,9},{9,8},{10,11... | collective-permute-start | bytes 178184 | tf_op jit(solution)/shard_map/ppermute | solution.py:997
  79.4 20.1 %collective-permute-start.9 = (bf16[48,384]{1,0:T(8,128)(2,1)S(1)}, bf16[48,384]{1,0:T(8,128)(2,1)S(1)}, u32[]{:S(2)}, u32[]{:S(2)}) collective-permute-start(bf16[48,384]{1,0:T(8,128)(2,1)S(1)} %get-tuple-element.29), channel_id=1, source_target_pairs={{0,6},{2,8},{4,10},{6,12},{8,14},{10,0},{12,2},{14,4},{1,7},{3,9},... | collective-permute-start | bytes 110600 | tf_op jit(solution)/shard_map/ppermute | solution.py:879
  85.5 8.8 %copy-start = (bf16[256,768]{1,0:T(8,128)(2,1)S(1)}, bf16[256,768]{1,0:T(8,128)(2,1)}, u32[]{:S(2)}) copy-start(bf16[256,768]{1,0:T(8,128)(2,1)} %wqkv.1) | copy-start | bytes 1179652
  85.5 8.8 %copy-start.1 = (bf16[256,256]{1,0:T(8,128)(2,1)S(1)}, bf16[256,256]{1,0:T(8,128)(2,1)}, u32[]{:S(2)}) copy-start(bf16[256,256]{1,0:T(8,128)(2,1)} %wo.1) | copy-start | bytes 393220
  85.6 8.8 %copy-start.2 = (bf16[64,256]{1,0:T(8,128)(2,1)S(1)}, bf16[64,256]{1,0:T(8,128)(2,1)}, u32[]{:S(2)}) copy-start(bf16[64,256]{1,0:T(8,128)(2,1)} %we.1) | copy-start | bytes 98308
  85.6 8.8 %copy-start.3 = (bf16[256,64]{0,1:T(8,128)(2,1)S(1)}, bf16[256,64]{0,1:T(8,128)(2,1)}, u32[]{:S(2)}) copy-start(bf16[256,64]{0,1:T(8,128)(2,1)} %param.15) | copy-start | bytes 98308
  85.6 8.8 %copy-start.4 = (f32[256]{0:T(256)S(1)}, f32[256]{0:T(256)}, u32[]{:S(2)}) copy-start(f32[256]{0:T(256)} %param.14) | copy-start | bytes 3076
  85.6 8.8 %copy-start.5 = (f32[8]{0:T(128)S(1)}, f32[8]{0:T(128)}, u32[]{:S(2)}) copy-start(f32[8]{0:T(128)} %scale.1) | copy-start | bytes 100

commit v8 on v7

--- a/solution.py
+++ b/solution.py
@@ -394,19 +394,50 @@
     band_rows(geo, level, lo, skip, hi, geo.span[level - 1][0], gain, bands)
 
 
-def sides_kernel(place, x, side_e, side_o, sems):
-    parity = place[1] % 2
-    width, lanes = x.shape[1], side_e.shape[1]
+def side_shape(rows):
+    tall = side_split(rows)
+    return (rows + tall // 3, 3 * LANES)
+
+
+def side_split(rows):
+    return -(-(-(-rows // 2)) // 48) * 48
+
+
+def sides_kernel(place, x, side_e, side_o, edge, ends, sems):
+    lat, parity = place[0], place[1] % 2
+    rows, width = x.shape
+    lanes = 3 * LANES
+    tall = side_split(rows)
+    third = tall // 3
+    at = pl.multiple_of(jnp.where(lat == 0, rows - HALO, 0), NEAR)
+    strip = pltpu.make_async_copy(x.at[pl.ds(at, HALO), :], edge, sems.at[4])
+    strip.start()
 
     def both(low, high):
+        body = pl.ds(0, rows)
         copies = [
-            pltpu.make_async_copy(x.at[:, pl.ds(0, lanes)], low, sems.at[0]),
-            pltpu.make_async_copy(x.at[:, pl.ds(width - lanes, lanes)], high, sems.at[1]),
+            pltpu.make_async_copy(x.at[:, pl.ds(lanes, LANES)], ends.at[0], sems.at[0]),
+            pltpu.make_async_copy(x.at[:, pl.ds(width - lanes - LANES, LANES)], ends.at[1], sems.at[1]),
+            pltpu.make_async_copy(x.at[:, pl.ds(0, lanes)], low.at[body, :], sems.at[2]),
+            pltpu.make_async_copy(x.at[:, pl.ds(width - lanes, lanes)], high.at[body, :], sems.at[3]),
         ]
         for copy in copies:
             copy.start()
-        for copy in copies:
-            copy.wait()
+        for side, out in ((0, low), (1, high)):
+            copies[side].wait()
+            one = ends[side, 0:tall, :].astype(F32)
+            two = ends[side, tall:rows, :].astype(F32)
+            if side:
+                one = half_turn(one)
+            else:
+                two = half_turn(two)
+            two = jnp.concatenate([two, jnp.zeros((2 * tall - rows, LANES), F32)], 0)
+            mixed = jnp.where(lax.broadcasted_iota(jnp.int32, (tall, LANES), 1) < C, one, two)
+            for b in range(3):
+                block = mixed[third * b : third * (b + 1), :].astype(BF16)
+                out[rows : rows + third, b * LANES : (b + 1) * LANES] = block
+        copies[2].wait()
+        copies[3].wait()
 
     @pl.when(parity == 0)
     def _():
@@ -416,22 +447,46 @@
     def _():
         both(side_e, side_o)
 
-
-def corners_kernel(place, side_e, side_o, out):
+    strip.wait()
+
+
+def unpack_side(side, rows, out, row, at_left):
+    lanes = 3 * LANES
+    tall = side_split(rows)
+    third = tall // 3
+    half = jnp.concatenate(
+        [side[rows : rows + third, b * LANES : (b + 1) * LANES].astype(F32) for b in range(3)], 0
+    )
+    is_left = lax.broadcasted_iota(jnp.int32, (tall, LANES), 1) < C
+    turned = half_turn(half)
+    if at_left:
+        one, two = jnp.where(is_left, 0.0, turned), jnp.where(is_left, 0.0, half)
+        pairs, end = slice(LANES, LANES + lanes), slice(0, LANES)
+    else:
+        one, two = jnp.where(is_left, half, 0.0), jnp.where(is_left, turned, 0.0)
+        pairs, end = slice(0, lanes), slice(lanes, lanes + LANES)
+    base = 0 if at_left else SIDE * C
+    out[row : row + rows, base + pairs.start : base + pairs.stop] = side[0:rows, :]
+    out[row : row + tall, base + end.start : base + end.stop] = one.astype(BF16)
+    out[row + tall : row + rows, base + end.start : base + end.stop] = two[0 : rows - tall].astype(BF16)
+
+
+def corners_kernel(geo, place, side_e, side_o, out, ext):
     lat, parity = place[0], place[1] % 2
-    rows, lanes = side_e.shape
+    rows = geo.rows[0]
+
+    @pl.when(parity == 0)
+    def _():
+        unpack_side(side_o, rows, ext, 0, True)
+        unpack_side(side_e, rows, ext, 0, False)
+
+    @pl.when(parity != 0)
+    def _():
+        unpack_side(side_e, rows, ext, 0, True)
+        unpack_side(side_o, rows, ext, 0, False)
+
     at = jnp.where(lat == 0, rows - NEAR, 0)
-    window = pl.ds(pl.multiple_of(at, NEAR), NEAR)
-
-    @pl.when(parity == 0)
-    def _():
-        out[:, 0:lanes] = side_o[window, :]
-        out[:, lanes:] = side_e[window, :]
-
-    @pl.when(parity != 0)
-    def _():
-        out[:, 0:lanes] = side_e[window, :]
-        out[:, lanes:] = side_o[window, :]
+    out[...] = ext[pl.ds(pl.multiple_of(at, NEAR), NEAR), :]
 
 
 def merge_kernel(size, more, place, mine, other, out):
@@ -529,12 +584,10 @@
     lax.fori_loop(0, geo.band[1][1] // step, body, 0)
 
 
-def first_level_kernel(geo, lats, place, side_e, side_o, corner, gain, inner, lo_rim, hi_rim, part, ext, lo_side, hi_side, d1, la, ha, xh, xl):
-    lat, parity = place[0], place[1] % 2
+def first_level_kernel(geo, lats, place, beside, corner, gain, inner, lo_rim, hi_rim, part, ext, lo_side, hi_side, d1, la, ha, xh, xl):
+    lat = place[0]
     rows, _ = part.shape
     lanes = SIDE * C
-    sides = (slice(0, lanes), slice(lanes, 2 * lanes))
-    own = slice(NEAR, NEAR + rows)
     top, bottom = slice(0, NEAR), slice(NEAR + rows, 2 * NEAR + rows)
 
     def rims(near, far):
@@ -549,22 +602,13 @@
     def _():
         rims(top, bottom)
 
-    @pl.when(parity == 0)
-    def _():
-        ext[own, sides[0]] = side_o[...]
-        ext[own, sides[1]] = side_e[...]
-
-    @pl.when(parity != 0)
-    def _():
-        ext[own, sides[0]] = side_e[...]
-        ext[own, sides[1]] = side_o[...]
-
+    ext[NEAR : NEAR + rows, :] = beside[...]
     start, count = geo.band[1]
     latitude_bands(geo, lats, lat, ext, lo_side, hi_side)
     first, pairs = geo.span[1]
     ends = edge_pairs()
     step = best_step(count)
-    beside = SIDE // 2
+    near = SIDE // 2
 
     def body(c, carry):
         row = pl.multiple_of(c * step, step)
@@ -572,12 +616,12 @@
         lo_s, hi_s, lo_r, hi_r = sources
         groups = [(q, first + 2 * q) for q in range(ends)]
         first_bands(
-            row, lo_s[:beside] + lo_r[:beside], hi_s[:beside] + hi_r[:beside], -SIDE, groups, gain, d1
+            row, lo_s[:near] + lo_r[:near], hi_s[:near] + hi_r[:near], -SIDE, groups, gain, d1
         )
         groups = [(ends + q, first + 2 * (pairs - ends + q)) for q in range(ends)]
         begin = geo.cells[0] - SIDE
         first_bands(
-            row, lo_r[beside:] + lo_s[beside:], hi_r[beside:] + hi_s[beside:], begin, groups, gain, d1
+            row, lo_r[near:] + lo_s[near:], hi_r[near:] + hi_s[near:], begin, groups, gain, d1
         )
         return carry
 
@@ -641,7 +685,8 @@
 
 def plan_shape(geo, distance):
     entries = exchange_plan(geo)[distance]
-    rows = sum(-(-geo.band[level][1] // 16) * 16 for level, _, _ in entries)
+    level, _, row = entries[-1]
+    rows = row + geo.band[level][1]
     return (rows, max(count for _, count, _ in entries) * 3 * LANES)
 
 
@@ -878,23 +923,19 @@
     def shifted(value, by):
         return lax.ppermute(value, "lon", [(i, (i + by) % lons) for i in range(lons)])
 
-    edge = lax.dynamic_slice(
-        state_field, (jnp.where(lat == 0, rows - HALO, 0), 0), (HALO, width)
-    )
-    edge = lax.ppermute(edge, "lat", swap)
-
     wide = SIDE * C
     extended = NEAR + rows + NEAR
-    side_e, side_o = call(
+    side_e, side_o, edge = call(
         sides_kernel,
-        [shape((rows, wide), BF16)] * 2,
-        [pltpu.SemaphoreType.DMA((2,))],
+        [shape(side_shape(rows), BF16)] * 2 + [shape((HALO, width), BF16)],
+        [pltpu.VMEM((2, rows, LANES), BF16), pltpu.SemaphoreType.DMA((5,))],
         place,
         state_field,
         raw=(1,),
         stay=(1,),
         cost=1_000_000,
     )
+    edge = lax.ppermute(edge, "lat", swap)
     side_e = lax.ppermute(side_e, "lon", even_pairs)
     side_o = lax.ppermute(side_o, "lon", odd_pairs)
 
@@ -927,8 +968,14 @@
         raw=(3,),
         stay=(3,),
     )
-    (corner,) = call(
-        corners_kernel, [shape((NEAR, 2 * wide), BF16)], [], place, side_e, side_o, cost=100_000
+    corner, beside = call(
+        functools.partial(corners_kernel, geo),
+        [shape((NEAR, 2 * wide), BF16), shape((rows, 2 * wide), BF16)],
+        [],
+        place,
+        side_e,
+        side_o,
+        cost=100_000,
     )
     corner = lax.ppermute(corner, "lat", swap)
     count = geo.band[1][1]
@@ -963,8 +1010,7 @@
             pltpu.VMEM((2 * LANES, w[1]), BF16),
         ],
         place,
-        side_e,
-        side_o,
+        beside,
         corner,
         skip_gain,
         inner,

time: 107 us -> 100 us (0.935)
  waiting for transfers between devices: 45.3 us -> 36.6 us
  starting transfers between devices: 22.8 us -> 25.3 us
    ppermute x3, waiting for transfers between devices: 42.5 us -> 32.8 us  [program(): other = lax.ppermute(merged, 'lon', [(i, i ^ size) for i in range(lons)])]
    ppermute x4, starting transfers between devices: 9.2 us -> 11 us  [shifted(): lax.ppermute(value, 'lon', [(i, (i + by) % lons) for i in range(lons)])]
  transfers between devices with their start and end apart: 14 -> 14, of which waited for: 6 -> 5; matrix products, arithmetic and copies ran while one was open for 0% -> 0% of each run, Pallas kernels for 28% -> 28%
where the time goes in v8:
time: 100 us
  Pallas kernels  37.7 us (38%)
  waiting for transfers between devices  36.6 us (37%)
  starting transfers between devices  25.3 us (25%)
    pallas_call x10, Pallas kernels, call(): pl.pallas_call(kernel, out_shape=tuple(out_shape), in_specs=specs, out_sp...  37.7 us
    ppermute x3, waiting for transfers between devices, program(): other = lax.ppermute(merged, 'lon', [(i, i ^ size) for i in range(lons)])  32.8 us
    ppermute x4, starting transfers between devices, shifted(): lax.ppermute(value, 'lon', [(i, (i + by) % lons) for i in range(lons)])  11 us
    ppermute x3, starting transfers between devices, program(): other = lax.ppermute(merged, 'lon', [(i, i ^ size) for i in range(lons)])  5.39 us
    ppermute x1, starting transfers between devices, program(): side_o = lax.ppermute(side_o, 'lon', odd_pairs)  3.57 us
    ppermute x1, starting transfers between devices, program(): side_e = lax.ppermute(side_e, 'lon', even_pairs)  2.55 us
    ppermute x4, waiting for transfers between devices, shifted(): lax.ppermute(value, 'lon', [(i, (i + by) % lons) for i in range(lons)])  2.12 us
  transfers between devices with their start and end apart: 14, of which 5 were waited for; matrix products, arithmetic and copies ran while one was open for 0% of the time, Pallas kernels for 28%

profile of v8, /device:TPU:0, one launch (start us, length us, event | category | flops | bytes accessed | tf_op | source)
XLA Modules:
  0.0 100.1 jit_solution(10333287943982031774)
XLA Ops:
  0.0 0.1 pad_add_fusion.place
  0.1 1.9 %shard_map.82 = (bf16[544,384]{1,0:T(8,128)(2,1)S(1)}, bf16[544,384]{1,0:T(8,128)(2,1)S(1)}, bf16[96,2048]{1,0:T(8,128)(2,1)S(1)}) custom-call(s32[2]{0:T(128)S(1)} %pad_add_fusion.place, bf16[464,2048]{1,0:T(8,128)(2,1)} %x.5), custom_call_target="tpu_custom_call" | custom-call | flops 1000000 | bytes 1048576 | tf_op jit(solution)/shard_map/pallas_call | solution.py:891
  2.0 0.6 collective-permute-start
  2.6 2.6 %collective-permute-start.11 = (bf16[544,384]{1,0:T(8,128)(2,1)S(1)}, bf16[544,384]{1,0:T(8,128)(2,1)S(1)}, u32[]{:S(2)}, u32[]{:S(2)}) collective-permute-start(bf16[544,384]{1,0:T(8,128)(2,1)S(1)} %get-tuple-element.35), channel_id=1, source_target_pairs={{0,2},{2,0},{4,6},{6,4},{8,10},{10,8},{12,14},{14,12},{1,3},{3,1},... | collective-permute-start | bytes 1253384 | tf_op jit(solution)/shard_map/ppermute | solution.py:939
  5.1 3.6 %collective-permute-start.12 = (bf16[544,384]{1,0:T(8,128)(2,1)S(1)}, bf16[544,384]{1,0:T(8,128)(2,1)S(1)}, u32[]{:S(2)}, u32[]{:S(2)}) collective-permute-start(bf16[544,384]{1,0:T(8,128)(2,1)S(1)} %get-tuple-element.36), channel_id=1, source_target_pairs={{0,14},{2,4},{4,2},{6,8},{8,6},{10,12},{12,10},{14,0},{1,15},{3,5}... | collective-permute-start | bytes 1253384 | tf_op jit(solution)/shard_map/ppermute | solution.py:940
  8.7 0.0 copy-done.6
  8.7 0.0 collective-permute-done.edge
  8.7 7.7 %shard_map.83 = (f32[40,512]{1,0:T(8,128)S(1)}, f32[3,128,896]{2,1,0:T(8,128)S(1)}, f32[3,64,640]{2,1,0:T(8,128)S(1)}, f32[3,40,512]{2,1,0:T(8,128)S(1)}, bf16[2...) custom-call(s32[2]{0:T(128)S(1)} %pad_add_fusion.place, ...), custom_call_target="tpu_custom_call" | custom-call | flops 20000000 | bytes 1048576 | tf_op jit(solution)/shard_map/pallas_call | solution.py:891
  16.5 0.1 collective-permute-start.5
  16.5 1.9 %collective-permute-start.6 = (bf16[232,1152]{1,0:T(8,128)(2,1)S(1)}, bf16[232,1152]{1,0:T(8,128)(2,1)S(1)}, u32[]{:S(2)}, u32[]{:S(2)}) collective-permute-start(bf16[232,1152]{1,0:T(8,128)(2,1)S(1)} %get-tuple-element.30), channel_id=1, source_target_pairs={{0,14},{2,4},{4,2},{6,8},{8,6},{10,12},{12,10},{14,0},{1,15},{3,5}... | collective-permute-start | bytes 1603592 | tf_op jit(solution)/shard_map/ppermute | solution.py:1046
  18.4 0.6 collective-permute-start.1
  19.0 29.9 %collective-permute-done.1.other = f32[40,512]{1,0:T(8,128)S(1)} collective-permute-done((f32[40,512]{1,0:T(8,128)S(1)}, f32[40,512]{1,0:T(8,128)S(1)}, u32[]{:S(2)}, u32[]{:S(2)}) %collective-permute-start.1) | collective-permute-done | bytes 81952 | tf_op jit(solution)/shard_map/ppermute | solution.py:1025
  49.0 0.6 shard_map.84.mine
  49.5 1.9 %collective-permute-start.2 = (f32[40,640]{1,0:T(8,128)S(1)}, f32[40,640]{1,0:T(8,128)S(1)}, u32[]{:S(2)}, u32[]{:S(2)}) collective-permute-start(f32[40,640]{1,0:T(8,128)S(1)} %shard_map.84.mine), channel_id=1, source_target_pairs={{0,4},{2,6},{4,0},{6,2},{8,12},{10,14},{12,8},{14,10},{1,5},{3,7},... | collective-permute-start | bytes 307208 | tf_op jit(solution)/shard_map/ppermute | solution.py:1025
  51.4 2.8 %collective-permute-done.2.other = f32[40,640]{1,0:T(8,128)S(1)} collective-permute-done((f32[40,640]{1,0:T(8,128)S(1)}, f32[40,640]{1,0:T(8,128)S(1)}, u32[]{:S(2)}, u32[]{:S(2)}) %collective-permute-start.2) | collective-permute-done | bytes 102432 | tf_op jit(solution)/shard_map/ppermute | solution.py:1025
  54.3 0.6 shard_map.85.mine
  54.9 2.9 %collective-permute-start.3 = (f32[40,896]{1,0:T(8,128)S(1)}, f32[40,896]{1,0:T(8,128)S(1)}, u32[]{:S(2)}, u32[]{:S(2)}) collective-permute-start(f32[40,896]{1,0:T(8,128)S(1)} %shard_map.85.mine), channel_id=1, source_target_pairs={{0,8},{2,10},{4,12},{6,14},{8,0},{10,2},{12,4},{14,6},{1,9},{3,11}... | collective-permute-start | bytes 430088 | tf_op jit(solution)/shard_map/ppermute | solution.py:1025
  57.8 0.0 collective-permute-done.11.side_e
  57.8 1.3 %collective-permute-start.10 = (bf16[40,384]{1,0:T(8,128)(2,1)S(1)}, bf16[40,384]{1,0:T(8,128)(2,1)S(1)}, u32[]{:S(2)}, u32[]{:S(2)}) collective-permute-start(bf16[40,384]{1,0:T(8,128)(2,1)S(1)} %get-tuple-element.34), channel_id=1, source_target_pairs={{0,10},{2,12},{4,14},{6,0},{8,2},{10,4},{12,6},{14,8},{1,11},{3,13... | collective-permute-start | bytes 92168 | tf_op jit(solution)/shard_map/ppermute | solution.py:924
  59.0 0.0 collective-permute-done.12.side_o
  59.0 1.6 %collective-permute-start.7 = (bf16[104,768]{1,0:T(8,128)(2,1)S(1)}, bf16[104,768]{1,0:T(8,128)(2,1)S(1)}, u32[]{:S(2)}, u32[]{:S(2)}) collective-permute-start(bf16[104,768]{1,0:T(8,128)(2,1)S(1)} %get-tuple-element.31), channel_id=1, source_target_pairs={{0,4},{2,6},{4,8},{6,10},{8,12},{10,14},{12,0},{14,2},{1,5},{3,7},... | collective-permute-start | bytes 479240 | tf_op jit(solution)/shard_map/ppermute | solution.py:924
  60.6 2.1 %collective-permute-done.10.from_p3 = bf16[40,384]{1,0:T(8,128)(2,1)S(1)} collective-permute-done((bf16[40,384]{1,0:T(8,128)(2,1)S(1)}, bf16[40,384]{1,0:T(8,128)(2,1)S(1)}, u32[]{:S(2)}, u32[]{:S(2)}) %collective-permute-start.10) | collective-permute-done | bytes 30752 | tf_op jit(solution)/shard_map/ppermute | solution.py:924
  62.7 4.5 %collective-permute-start.8 = (bf16[104,768]{1,0:T(8,128)(2,1)S(1)}, bf16[104,768]{1,0:T(8,128)(2,1)S(1)}, u32[]{:S(2)}, u32[]{:S(2)}) collective-permute-start(bf16[104,768]{1,0:T(8,128)(2,1)S(1)} %get-tuple-element.32), channel_id=1, source_target_pairs={{0,12},{2,14},{4,0},{6,2},{8,4},{10,6},{12,8},{14,10},{1,13},{3,15... | collective-permute-start | bytes 479240 | tf_op jit(solution)/shard_map/ppermute | solution.py:924
  67.2 0.7 shard_map.88
  67.9 0.0 collective-permute-done.3.other
  67.9 0.1 collective-permute-start.13
  67.9 0.6 shard_map.86
  68.6 0.6 collective-permute-done.13.corner
  69.1 0.2 collective-permute-start.4
  69.3 1.1 %collective-permute-done.4.others = bf16[29,1024]{1,0:T(8,128)(2,1)S(1)} collective-permute-done((bf16[29,1024]{1,0:T(8,128)(2,1)S(1)}, bf16[29,1024]{1,0:T(8,128)(2,1)S(1)}, u32[]{:S(2)}, u32[]{:S(2)}) %collective-permute-start.4) | collective-permute-done | bytes 59424 | tf_op jit(solution)/shard_map/ppermute | solution.py:1043
  70.4 3.8 %collective-permute-start.9 = (bf16[40,384]{1,0:T(8,128)(2,1)S(1)}, bf16[40,384]{1,0:T(8,128)(2,1)S(1)}, u32[]{:S(2)}, u32[]{:S(2)}) collective-permute-start(bf16[40,384]{1,0:T(8,128)(2,1)S(1)} %get-tuple-element.33), channel_id=1, source_target_pairs={{0,6},{2,8},{4,10},{6,12},{8,14},{10,0},{12,2},{14,4},{1,7},{3,9},... | collective-permute-start | bytes 92168 | tf_op jit(solution)/shard_map/ppermute | solution.py:924
  74.2 4.5 %shard_map.89 = (f32[3,240,1280]{2,1,0:T(8,128)S(1)}, f32[240,1024]{1,0:T(8,128)S(1)}, f32[240,1024]{1,0:T(8,128)S(1)}) custom-call(s32[2]{0:T(128)S(1)} %pad_add_fusion.place, bf16[96,2048]{1,0:T(8,128)(2,1)S(1)} %collective-permute-done.edge, f32[4,3,64]{2,1,0:T(4,128)S(1)} %copy.9.gain, bf16[464,2048]{1,0:T(8,128)(2,1)} %x.5), custom_call_target="tpu_custom_call" | custom-call | flops 20000000 | bytes 1048576 | tf_op jit(solution)/shard_map/pallas_call | solution.py:891
  78.6 0.0 copy-start
  78.7 0.0 copy-start.1
  78.7 0.0 copy-start.2
  78.7 0.0 copy-start.3
  78.7 0.0 copy-start.4
  78.7 0.0 copy-start.5
  78.7 8.6 %shard_map.90.refs_0_ = f32[464,2048]{1,0:T(8,128)S(1)} custom-call(s32[2]{0:T(128)S(1)} %pad_add_fusion.place, bf16[464,1024]{1,0:T(8,128)(2,1)S(1)} %get-tuple-element.37.beside, bf16[16,1024]{1,0:T(8,128)(2,1)S(1)} %collective-permute-done.13.corner, f32[4,3,64]{2,1,0:T(4,128)S(1)} %copy.9.gain, f32[3,240,1280]{2,1,0:T(8,128)S(1)} %get-tuple-element.39.inner, ...), custom_call_target="tpu_custom_call" | custom-call | flops 20000000 | bytes 1048576 | tf_op jit(solution)/shard_map/pallas_call | solution.py:891
  87.3 0.0 copy-done
  87.3 0.0 copy-done.1
  87.3 5.1 %shard_map.87.coarse = f32[40,512]{1,0:T(8,128)S(1)} custom-call(s32[2]{0:T(128)S(1)} %pad_add_fusion.place, f32[40,1024]{1,0:T(8,128)S(1)} %get-tuple-element.27.ring, bf16[29,1024]{1,0:T(8,128)(2,1)S(1)} %get-tuple-element.28.own, bf16[29,1024]{1,0:T(8,128)(2,1)S(1)} %collective-permute-done.4.others, bf16[64,256]{1,0:T(8,128)(2,1)S(1)} %copy-done.2, ...), custom_call_target="tpu_custom_call" | custom-call | flops 200000000 | bytes 1048576 | tf_op jit(solution)/shard_map/pallas_call | solution.py:891
  92.4 0.0 collective-permute-done.9.from_m3
  92.4 0.0 collective-permute-done.7.from_m2
  92.4 0.0 collective-permute-done.8.from_p2
  92.4 0.0 collective-permute-done.5.e2
  92.5 0.0 collective-permute-done.6.o2
  92.5 7.5 %shard_map.91 = bf16[464,2048]{1,0:T(8,128)(2,1)} custom-call(s32[2]{0:T(128)S(1)} %pad_add_fusion.place, f32[40,512]{1,0:T(8,128)S(1)} %shard_map.87.coarse, bf16[232,1152]{1,0:T(8,128)(2,1)S(1)} %collective-permute-done.5.e2, bf16[232,1152]{1,0:T(8,128)(2,1)S(1)} %collective-permute-done.6.o2, bf16[104,768]{1,0:T(8,128)(2,1)S(1)} %collective-permute-done.7.from_m2, ...), custom_call_target="tpu_custom_call" | custom-call | flops 20000000 | bytes 1048576 | tf_op jit(solution)/shard_map/pallas_call | solution.py:891
  (6 shorter events, 0.0 us)
Async XLA Ops:
  0.0 8.7 %copy-start.6 = (f32[4,3,64]{2,0,1:T(4,128)S(1)}, f32[4,3,64]{2,0,1:T(4,128)}, u32[]{:S(2)}) copy-start(f32[4,3,64]{2,0,1:T(4,128)} %param.9) | copy-start | bytes 9220
  2.0 6.7 %collective-permute-start = (bf16[96,2048]{1,0:T(8,128)(2,1)S(1)}, bf16[96,2048]{1,0:T(8,128)(2,1)S(1)}, u32[]{:S(2)}, u32[]{:S(2)}) collective-permute-start(bf16[96,2048]{1,0:T(8,128)(2,1)S(1)} %get-tuple-element.25), channel_id=1, source_target_pairs={{0,1},{1,0},{2,3},{3,2},{4,5},{5,4},{6,7},{7,6},{8,9},{9,8},{10,11... | collective-permute-start | bytes 1179656 | tf_op jit(solution)/shard_map/ppermute | solution.py:938
  2.6 55.2 %collective-permute-start.11 = (bf16[544,384]{1,0:T(8,128)(2,1)S(1)}, bf16[544,384]{1,0:T(8,128)(2,1)S(1)}, u32[]{:S(2)}, u32[]{:S(2)}) collective-permute-start(bf16[544,384]{1,0:T(8,128)(2,1)S(1)} %get-tuple-element.35), channel_id=1, source_target_pairs={{0,2},{2,0},{4,6},{6,4},{8,10},{10,8},{12,14},{14,12},{1,3},{3,1},... | collective-permute-start | bytes 1253384 | tf_op jit(solution)/shard_map/ppermute | solution.py:939
  5.1 53.9 %collective-permute-start.12 = (bf16[544,384]{1,0:T(8,128)(2,1)S(1)}, bf16[544,384]{1,0:T(8,128)(2,1)S(1)}, u32[]{:S(2)}, u32[]{:S(2)}) collective-permute-start(bf16[544,384]{1,0:T(8,128)(2,1)S(1)} %get-tuple-element.36), channel_id=1, source_target_pairs={{0,14},{2,4},{4,2},{6,8},{8,6},{10,12},{12,10},{14,0},{1,15},{3,5}... | collective-permute-start | bytes 1253384 | tf_op jit(solution)/shard_map/ppermute | solution.py:940
  16.5 76.0 %collective-permute-start.5 = (bf16[232,1152]{1,0:T(8,128)(2,1)S(1)}, bf16[232,1152]{1,0:T(8,128)(2,1)S(1)}, u32[]{:S(2)}, u32[]{:S(2)}) collective-permute-start(bf16[232,1152]{1,0:T(8,128)(2,1)S(1)} %get-tuple-element.29), channel_id=1, source_target_pairs={{0,2},{2,0},{4,6},{6,4},{8,10},{10,8},{12,14},{14,12},{1,3},{3,1},... | collective-permute-start | bytes 1603592 | tf_op jit(solution)/shard_map/ppermute | solution.py:1045
  16.5 75.9 %collective-permute-start.6 = (bf16[232,1152]{1,0:T(8,128)(2,1)S(1)}, bf16[232,1152]{1,0:T(8,128)(2,1)S(1)}, u32[]{:S(2)}, u32[]{:S(2)}) collective-permute-start(bf16[232,1152]{1,0:T(8,128)(2,1)S(1)} %get-tuple-element.30), channel_id=1, source_target_pairs={{0,14},{2,4},{4,2},{6,8},{8,6},{10,12},{12,10},{14,0},{1,15},{3,5}... | collective-permute-start | bytes 1603592 | tf_op jit(solution)/shard_map/ppermute | solution.py:1046
  18.4 30.5 %collective-permute-start.1 = (f32[40,512]{1,0:T(8,128)S(1)}, f32[40,512]{1,0:T(8,128)S(1)}, u32[]{:S(2)}, u32[]{:S(2)}) collective-permute-start(f32[40,512]{1,0:T(8,128)S(1)} %get-tuple-element.26.mine), channel_id=1, source_target_pairs={{0,2},{2,0},{4,6},{6,4},{8,10},{10,8},{12,14},{14,12},{1,3},{3,1},... | collective-permute-start | bytes 245768 | tf_op jit(solution)/shard_map/ppermute | solution.py:1025
  49.5 4.7 %collective-permute-start.2 = (f32[40,640]{1,0:T(8,128)S(1)}, f32[40,640]{1,0:T(8,128)S(1)}, u32[]{:S(2)}, u32[]{:S(2)}) collective-permute-start(f32[40,640]{1,0:T(8,128)S(1)} %shard_map.84.mine), channel_id=1, source_target_pairs={{0,4},{2,6},{4,0},{6,2},{8,12},{10,14},{12,8},{14,10},{1,5},{3,7},... | collective-permute-start | bytes 307208 | tf_op jit(solution)/shard_map/ppermute | solution.py:1025
  54.9 13.0 %collective-permute-start.3 = (f32[40,896]{1,0:T(8,128)S(1)}, f32[40,896]{1,0:T(8,128)S(1)}, u32[]{:S(2)}, u32[]{:S(2)}) collective-permute-start(f32[40,896]{1,0:T(8,128)S(1)} %shard_map.85.mine), channel_id=1, source_target_pairs={{0,8},{2,10},{4,12},{6,14},{8,0},{10,2},{12,4},{14,6},{1,9},{3,11}... | collective-permute-start | bytes 430088 | tf_op jit(solution)/shard_map/ppermute | solution.py:1025
  57.8 5.0 %collective-permute-start.10 = (bf16[40,384]{1,0:T(8,128)(2,1)S(1)}, bf16[40,384]{1,0:T(8,128)(2,1)S(1)}, u32[]{:S(2)}, u32[]{:S(2)}) collective-permute-start(bf16[40,384]{1,0:T(8,128)(2,1)S(1)} %get-tuple-element.34), channel_id=1, source_target_pairs={{0,10},{2,12},{4,14},{6,0},{8,2},{10,4},{12,6},{14,8},{1,11},{3,13... | collective-permute-start | bytes 92168 | tf_op jit(solution)/shard_map/ppermute | solution.py:924
  59.0 33.4 %collective-permute-start.7 = (bf16[104,768]{1,0:T(8,128)(2,1)S(1)}, bf16[104,768]{1,0:T(8,128)(2,1)S(1)}, u32[]{:S(2)}, u32[]{:S(2)}) collective-permute-start(bf16[104,768]{1,0:T(8,128)(2,1)S(1)} %get-tuple-element.31), channel_id=1, source_target_pairs={{0,4},{2,6},{4,8},{6,10},{8,12},{10,14},{12,0},{14,2},{1,5},{3,7},... | collective-permute-start | bytes 479240 | tf_op jit(solution)/shard_map/ppermute | solution.py:924
  62.7 29.7 %collective-permute-start.8 = (bf16[104,768]{1,0:T(8,128)(2,1)S(1)}, bf16[104,768]{1,0:T(8,128)(2,1)S(1)}, u32[]{:S(2)}, u32[]{:S(2)}) collective-permute-start(bf16[104,768]{1,0:T(8,128)(2,1)S(1)} %get-tuple-element.32), channel_id=1, source_target_pairs={{0,12},{2,14},{4,0},{6,2},{8,4},{10,6},{12,8},{14,10},{1,13},{3,15... | collective-permute-start | bytes 479240 | tf_op jit(solution)/shard_map/ppermute | solution.py:924
  67.9 1.3 %collective-permute-start.13 = (bf16[16,1024]{1,0:T(8,128)(2,1)S(1)}, bf16[16,1024]{1,0:T(8,128)(2,1)S(1)}, u32[]{:S(2)}, u32[]{:S(2)}) collective-permute-start(bf16[16,1024]{1,0:T(8,128)(2,1)S(1)} %get-tuple-element.38), channel_id=1, source_target_pairs={{0,1},{1,0},{2,3},{3,2},{4,5},{5,4},{6,7},{7,6},{8,9},{9,8},{10,11... | collective-permute-start | bytes 98312 | tf_op jit(solution)/shard_map/ppermute | solution.py:980
  69.1 1.3 %collective-permute-start.4 = (bf16[29,1024]{1,0:T(8,128)(2,1)S(1)}, bf16[29,1024]{1,0:T(8,128)(2,1)S(1)}, u32[]{:S(2)}, u32[]{:S(2)}) collective-permute-start(bf16[29,1024]{1,0:T(8,128)(2,1)S(1)} %get-tuple-element.28.own), channel_id=1, source_target_pairs={{0,1},{1,0},{2,3},{3,2},{4,5},{5,4},{6,7},{7,6},{8,9},{9,8},{10,11... | collective-permute-start | bytes 178184 | tf_op jit(solution)/shard_map/ppermute | solution.py:1043
  70.4 22.0 %collective-permute-start.9 = (bf16[40,384]{1,0:T(8,128)(2,1)S(1)}, bf16[40,384]{1,0:T(8,128)(2,1)S(1)}, u32[]{:S(2)}, u32[]{:S(2)}) collective-permute-start(bf16[40,384]{1,0:T(8,128)(2,1)S(1)} %get-tuple-element.33), channel_id=1, source_target_pairs={{0,6},{2,8},{4,10},{6,12},{8,14},{10,0},{12,2},{14,4},{1,7},{3,9},... | collective-permute-start | bytes 92168 | tf_op jit(solution)/shard_map/ppermute | solution.py:924
  78.6 8.7 %copy-start = (bf16[256,768]{1,0:T(8,128)(2,1)S(1)}, bf16[256,768]{1,0:T(8,128)(2,1)}, u32[]{:S(2)}) copy-start(bf16[256,768]{1,0:T(8,128)(2,1)} %wqkv.1) | copy-start | bytes 1179652
  78.7 8.6 %copy-start.1 = (bf16[256,256]{1,0:T(8,128)(2,1)S(1)}, bf16[256,256]{1,0:T(8,128)(2,1)}, u32[]{:S(2)}) copy-start(bf16[256,256]{1,0:T(8,128)(2,1)} %wo.1) | copy-start | bytes 393220
  78.7 8.6 %copy-start.2 = (bf16[64,256]{1,0:T(8,128)(2,1)S(1)}, bf16[64,256]{1,0:T(8,128)(2,1)}, u32[]{:S(2)}) copy-start(bf16[64,256]{1,0:T(8,128)(2,1)} %we.1) | copy-start | bytes 98308
  78.7 8.6 %copy-start.3 = (bf16[256,64]{0,1:T(8,128)(2,1)S(1)}, bf16[256,64]{0,1:T(8,128)(2,1)}, u32[]{:S(2)}) copy-start(bf16[256,64]{0,1:T(8,128)(2,1)} %param.15) | copy-start | bytes 98308
  78.7 8.6 %copy-start.4 = (f32[256]{0:T(256)S(1)}, f32[256]{0:T(256)}, u32[]{:S(2)}) copy-start(f32[256]{0:T(256)} %param.14) | copy-start | bytes 3076
  78.7 8.6 %copy-start.5 = (f32[8]{0:T(128)S(1)}, f32[8]{0:T(128)}, u32[]{:S(2)}) copy-start(f32[8]{0:T(128)} %scale.1) | copy-start | bytes 100

commit v9 on v8

--- a/solution.py
+++ b/solution.py
@@ -1,3 +1,4 @@
+import copy
 import functools
 import math
 
@@ -224,17 +225,18 @@
         self.band = [
             None,
             (-4, up(self.rows[1] + 4, 120)),
-            (-8, up(self.rows[2] + 11, 16)),
+            (0, up(self.rows[2] + 3, 8)),
             (-3, up(self.rows[3] + 6, 8)),
-            (-3, up(self.rows[4] + 6, 8)),
+            (0, up(self.rows[4] + 3, 8)),
         ]
         self.low = [
             None,
             (-52, up(self.rows[1] + 97, 112)),
             (-24, up(self.rows[2] + 45, 88)),
             (-11, up(self.rows[3] + 20, 8)),
-            (-3, up(self.rows[4] + 6, 8)),
+            (0, up(self.rows[4] + 3, 8)),
         ]
+        self.skip = [None] + [self.band[level][0] - self.low[level][0] for level in (1, 2, 3, 4)]
         self.span = [None, (-2, self.cells[1] // 2 + 2)]
         for level in (2, 3, 4):
             self.span.append((-3, self.cells[level] // 2 + 3))
@@ -243,6 +245,16 @@
         )
 
 
+    def placed(self, lat):
+        here = copy.copy(self)
+        shift = jnp.where(lat == 0, 0, -3)
+        here.band, here.low = list(self.band), list(self.low)
+        for level in (2, 4):
+            for ranges in (here.band, here.low):
+                ranges[level] = (ranges[level][0] + shift, ranges[level][1])
+        return here
+
+
 STEP = 240
 SIDE = 8
 NEAR = 16
@@ -255,7 +267,7 @@
 def low_rows(geo, level, source, source_start, target):
     first, pairs = geo.span[level]
     rows = geo.low[level][1]
-    step = best_step(rows, 168)
+    step = best_step(rows, 336)
     left = first_half(step)
 
     def body(c, carry):
@@ -294,6 +306,7 @@
 
 def analysis_kernel(geo, lats, place, edge, gain, x, *refs):
     lat, parity = place[0], place[1] % 2
+    geo = geo.placed(lat)
     ll4, d2, d3, d4, send_e, send_o, p2, m2, p3, m3 = refs[:10]
     ext, la, g1, gh, gl, lo2, g2, lo3, g3, lo4, hi2, hi3, hi4, sems = refs[10:]
     rows = geo.rows[0]
@@ -377,20 +390,16 @@
 def deep_bands(geo, lats, lat, level, source, lo, hi, gain, bands):
     start, count = geo.band[level]
     in_start = geo.low[level - 1][0]
-    parts = 2 if level == 2 else 1
-    half = count // parts
-    for b in range(parts):
-        if parts == 1:
-            at, size = 0, source.shape[0]
-            vh, vl = two_terms(source[...])
-        else:
-            at = (2 * (start + half * b) - 3 - in_start) // 16 * 16
-            size = 2 * half + 16
-            vh, vl = source[0][at : at + size, :], source[1][at : at + size, :]
-        matrix = analysis_matrix(HIGH, start + half * b, half, in_start + at, size)
-        matrix = masked_rows(matrix, start + half * b, geo.rows[level], lat, lats)
-        hi[half * b : half * (b + 1), :] = dot3(matrix, vh, vl)
-    skip = start - geo.low[level][0]
+    if level == 2:
+        at, size = 32, 2 * count + 32
+        vh, vl = source[0][at : at + size, :], source[1][at : at + size, :]
+    else:
+        at, size = 0, source.shape[0]
+        vh, vl = two_terms(source[...])
+    matrix = analysis_matrix(HIGH, start, count, in_start + at, size)
+    matrix = masked_rows(matrix, start, geo.rows[level], lat, lats)
+    hi[...] = dot3(matrix, vh, vl)
+    skip = geo.skip[level]
     band_rows(geo, level, lo, skip, hi, geo.span[level - 1][0], gain, bands)
 
 
@@ -514,8 +523,9 @@
     fold = merged.shape[1] - around
     ring[:, 0:fold] = merged[:, 0:fold] + merged[:, around:]
     ring[:, fold:] = merged[:, fold:around]
-    skip = -geo.low[4][0]
-    tokens[...] = ring[skip : skip + geo.rows[4], :].astype(BF16)
+    count = geo.rows[4]
+    own = jnp.where(place[0] == 0, ring[0:count, :], ring[3 : 3 + count, :])
+    tokens[...] = own.astype(BF16)
 
 
 def latitude_bands(geo, lats, lat, ext, la, ha):
@@ -656,7 +666,7 @@
         ylow[target, used] = mxu(sh, vh) + mxu(sh, vl) + mxu(sl, vh)
 
     begin, pairs = geo.span[1]
-    most = 232
+    most = rows
 
     def chunk(i, carry):
         row = pl.multiple_of(i * most, 8)
@@ -674,7 +684,7 @@
     plan = {}
     for distance in (1, 2, 3):
         entries, row = [], 0
-        for level in (2, 3, 4):
+        for level in (3, 4, 2):
             count = geo.span[level][1] - distance * geo.cells[level] // 2
             if count > 0:
                 entries.append((level, count, row))
@@ -692,6 +702,7 @@
 
 def attention_kernel(geo, lats, blocks, place, ring, own, others, we, wqkv, scale, wo, gain, wb, out, around, listed, keys):
     lat, lon = place[0], place[1]
+    geo = geo.placed(lat)
     rows, width = out.shape
     cells = width // C
     total = ring.shape[1]
@@ -782,6 +793,7 @@
 
 def synthesis_kernel(geo, lats, place, coarse, e2, o2, from_m2, from_p2, from_m3, from_p3, *refs):
     lat, parity = place[0], place[1] % 2
+    geo = geo.placed(lat)
     part, d2, d3, d4, out, up3, up2, up1, ylow, yhigh, done, sems = refs
     bands = {2: d2, 3: d3, 4: d4}
     plan = exchange_plan(geo)

time: 100 us -> 94.4 us (0.944)
  Pallas kernels: 37.7 us -> 35.4 us
  starting transfers between devices: 25.3 us -> 23.1 us
  waiting for transfers between devices: 36.6 us -> 35.2 us
    pallas_call x10, Pallas kernels: 37.7 us -> 35.4 us  [call(): pl.pallas_call(kernel, out_shape=tuple(out_shape), in_specs=specs, out_sp...]
    ppermute x4, starting transfers between devices: 11 us -> 8.83 us  [shifted(): lax.ppermute(value, 'lon', [(i, (i + by) % lons) for i in range(lons)])]
    ppermute x3, waiting for transfers between devices: 32.8 us -> 31.5 us  [program(): other = lax.ppermute(merged, 'lon', [(i, i ^ size) for i in range(lons)])]
  transfers between devices with their start and end apart: 14 -> 14, of which waited for: 5 -> 5; matrix products, arithmetic and copies ran while one was open for 0% -> 0% of each run, Pallas kernels for 28% -> 27%
where the time goes in v9:
time: 94.4 us; the launch traced here: 94.2 us
  Pallas kernels  35.4 us (38%)
  waiting for transfers between devices  35.2 us (37%)
  starting transfers between devices  23.1 us (24%)
    pallas_call x10, Pallas kernels, call(): pl.pallas_call(kernel, out_shape=tuple(out_shape), in_specs=specs, out_sp...  35.4 us
    ppermute x3, waiting for transfers between devices, program(): other = lax.ppermute(merged, 'lon', [(i, i ^ size) for i in range(lons)])  31.5 us
    ppermute x4, starting transfers between devices, shifted(): lax.ppermute(value, 'lon', [(i, (i + by) % lons) for i in range(lons)])  8.83 us
    ppermute x3, starting transfers between devices, program(): other = lax.ppermute(merged, 'lon', [(i, i ^ size) for i in range(lons)])  5.39 us
    ppermute x1, starting transfers between devices, program(): side_o = lax.ppermute(side_o, 'lon', odd_pairs)  3.57 us
    ppermute x1, starting transfers between devices, program(): side_e = lax.ppermute(side_e, 'lon', even_pairs)  2.55 us
    ppermute x4, waiting for transfers between devices, shifted(): lax.ppermute(value, 'lon', [(i, (i + by) % lons) for i in range(lons)])  1.99 us
    ppermute x1, starting transfers between devices, program(): deep_o = lax.ppermute(deep_o, 'lon', odd_pairs)  1.89 us
  transfers between devices with their start and end apart: 14, of which 5 were waited for; matrix products, arithmetic and copies ran while one was open for 0% of the time, Pallas kernels for 27%

profile of v9, /device:TPU:0, one launch (start us, length us, event | category | flops | bytes accessed | tf_op | source)
XLA Modules:
  0.0 94.2 jit_solution(13887692615735896664)
XLA Ops:
  0.0 0.1 pad_add_fusion.place
  0.1 1.9 %shard_map.82 = (bf16[544,384]{1,0:T(8,128)(2,1)S(1)}, bf16[544,384]{1,0:T(8,128)(2,1)S(1)}, bf16[96,2048]{1,0:T(8,128)(2,1)S(1)}) custom-call(s32[2]{0:T(128)S(1)} %pad_add_fusion.place, bf16[464,2048]{1,0:T(8,128)(2,1)} %x.5), custom_call_target="tpu_custom_call" | custom-call | flops 1000000 | bytes 1048576 | tf_op jit(solution)/shard_map/pallas_call | solution.py:903
  2.0 0.6 collective-permute-start
  2.6 2.6 %collective-permute-start.11 = (bf16[544,384]{1,0:T(8,128)(2,1)S(1)}, bf16[544,384]{1,0:T(8,128)(2,1)S(1)}, u32[]{:S(2)}, u32[]{:S(2)}) collective-permute-start(bf16[544,384]{1,0:T(8,128)(2,1)S(1)} %get-tuple-element.35), channel_id=1, source_target_pairs={{0,2},{2,0},{4,6},{6,4},{8,10},{10,8},{12,14},{14,12},{1,3},{3,1},... | collective-permute-start | bytes 1253384 | tf_op jit(solution)/shard_map/ppermute | solution.py:951
  5.1 3.6 %collective-permute-start.12 = (bf16[544,384]{1,0:T(8,128)(2,1)S(1)}, bf16[544,384]{1,0:T(8,128)(2,1)S(1)}, u32[]{:S(2)}, u32[]{:S(2)}) collective-permute-start(bf16[544,384]{1,0:T(8,128)(2,1)S(1)} %get-tuple-element.36), channel_id=1, source_target_pairs={{0,14},{2,4},{4,2},{6,8},{8,6},{10,12},{12,10},{14,0},{1,15},{3,5}... | collective-permute-start | bytes 1253384 | tf_op jit(solution)/shard_map/ppermute | solution.py:952
  8.7 0.0 copy-done.6
  8.7 0.0 collective-permute-done.edge
  8.7 6.9 %shard_map.83 = (f32[32,512]{1,0:T(8,128)S(1)}, f32[3,120,896]{2,1,0:T(8,128)S(1)}, f32[3,64,640]{2,1,0:T(8,128)S(1)}, f32[3,32,512]{2,1,0:T(8,128)S(1)}, bf16[2...) custom-call(s32[2]{0:T(128)S(1)} %pad_add_fusion.place, ...), custom_call_target="tpu_custom_call" | custom-call | flops 20000000 | bytes 1048576 | tf_op jit(solution)/shard_map/pallas_call | solution.py:903
  15.6 0.1 collective-permute-start.5
  15.7 1.9 %collective-permute-start.6 = (bf16[216,1152]{1,0:T(8,128)(2,1)S(1)}, bf16[216,1152]{1,0:T(8,128)(2,1)S(1)}, u32[]{:S(2)}, u32[]{:S(2)}) collective-permute-start(bf16[216,1152]{1,0:T(8,128)(2,1)S(1)} %get-tuple-element.30), channel_id=1, source_target_pairs={{0,14},{2,4},{4,2},{6,8},{8,6},{10,12},{12,10},{14,0},{1,15},{3,5}... | collective-permute-start | bytes 1493000 | tf_op jit(solution)/shard_map/ppermute | solution.py:1058
  17.6 0.6 collective-permute-start.1
  18.2 28.9 %collective-permute-done.1.other = f32[32,512]{1,0:T(8,128)S(1)} collective-permute-done((f32[32,512]{1,0:T(8,128)S(1)}, f32[32,512]{1,0:T(8,128)S(1)}, u32[]{:S(2)}, u32[]{:S(2)}) %collective-permute-start.1) | collective-permute-done | bytes 65568 | tf_op jit(solution)/shard_map/ppermute | solution.py:1037
  47.0 0.6 shard_map.84.mine
  47.6 1.9 %collective-permute-start.2 = (f32[32,640]{1,0:T(8,128)S(1)}, f32[32,640]{1,0:T(8,128)S(1)}, u32[]{:S(2)}, u32[]{:S(2)}) collective-permute-start(f32[32,640]{1,0:T(8,128)S(1)} %shard_map.84.mine), channel_id=1, source_target_pairs={{0,4},{2,6},{4,0},{6,2},{8,12},{10,14},{12,8},{14,10},{1,5},{3,7},... | collective-permute-start | bytes 245768 | tf_op jit(solution)/shard_map/ppermute | solution.py:1037
  49.5 2.6 %collective-permute-done.2.other = f32[32,640]{1,0:T(8,128)S(1)} collective-permute-done((f32[32,640]{1,0:T(8,128)S(1)}, f32[32,640]{1,0:T(8,128)S(1)}, u32[]{:S(2)}, u32[]{:S(2)}) %collective-permute-start.2) | collective-permute-done | bytes 81952 | tf_op jit(solution)/shard_map/ppermute | solution.py:1037
  52.1 0.6 shard_map.85.mine
  52.7 2.9 %collective-permute-start.3 = (f32[32,896]{1,0:T(8,128)S(1)}, f32[32,896]{1,0:T(8,128)S(1)}, u32[]{:S(2)}, u32[]{:S(2)}) collective-permute-start(f32[32,896]{1,0:T(8,128)S(1)} %shard_map.85.mine), channel_id=1, source_target_pairs={{0,8},{2,10},{4,12},{6,14},{8,0},{10,2},{12,4},{14,6},{1,9},{3,11}... | collective-permute-start | bytes 344072 | tf_op jit(solution)/shard_map/ppermute | solution.py:1037
  55.6 0.0 collective-permute-done.11.side_e
  55.6 1.3 %collective-permute-start.10 = (bf16[32,384]{1,0:T(8,128)(2,1)S(1)}, bf16[32,384]{1,0:T(8,128)(2,1)S(1)}, u32[]{:S(2)}, u32[]{:S(2)}) collective-permute-start(bf16[32,384]{1,0:T(8,128)(2,1)S(1)} %get-tuple-element.34), channel_id=1, source_target_pairs={{0,10},{2,12},{4,14},{6,0},{8,2},{10,4},{12,6},{14,8},{1,11},{3,13... | collective-permute-start | bytes 73736 | tf_op jit(solution)/shard_map/ppermute | solution.py:936
  56.9 0.0 collective-permute-done.12.side_o
  56.9 1.6 %collective-permute-start.7 = (bf16[96,768]{1,0:T(8,128)(2,1)S(1)}, bf16[96,768]{1,0:T(8,128)(2,1)S(1)}, u32[]{:S(2)}, u32[]{:S(2)}) collective-permute-start(bf16[96,768]{1,0:T(8,128)(2,1)S(1)} %get-tuple-element.31), channel_id=1, source_target_pairs={{0,4},{2,6},{4,8},{6,10},{8,12},{10,14},{12,0},{14,2},{1,5},{3,7},... | collective-permute-start | bytes 442376 | tf_op jit(solution)/shard_map/ppermute | solution.py:936
  58.5 2.0 %collective-permute-done.10.from_p3 = bf16[32,384]{1,0:T(8,128)(2,1)S(1)} collective-permute-done((bf16[32,384]{1,0:T(8,128)(2,1)S(1)}, bf16[32,384]{1,0:T(8,128)(2,1)S(1)}, u32[]{:S(2)}, u32[]{:S(2)}) %collective-permute-start.10) | collective-permute-done | bytes 24608 | tf_op jit(solution)/shard_map/ppermute | solution.py:936
  60.4 3.7 %collective-permute-start.8 = (bf16[96,768]{1,0:T(8,128)(2,1)S(1)}, bf16[96,768]{1,0:T(8,128)(2,1)S(1)}, u32[]{:S(2)}, u32[]{:S(2)}) collective-permute-start(bf16[96,768]{1,0:T(8,128)(2,1)S(1)} %get-tuple-element.32), channel_id=1, source_target_pairs={{0,12},{2,14},{4,0},{6,2},{8,4},{10,6},{12,8},{14,10},{1,13},{3,15... | collective-permute-start | bytes 442376 | tf_op jit(solution)/shard_map/ppermute | solution.py:936
  64.1 0.7 shard_map.88
  64.8 0.0 collective-permute-done.3.other
  64.8 0.1 collective-permute-start.13
  64.9 0.6 shard_map.86
  65.5 0.6 collective-permute-done.13.corner
  66.1 0.2 collective-permute-start.4
  66.3 1.1 %collective-permute-done.4.others = bf16[29,1024]{1,0:T(8,128)(2,1)S(1)} collective-permute-done((bf16[29,1024]{1,0:T(8,128)(2,1)S(1)}, bf16[29,1024]{1,0:T(8,128)(2,1)S(1)}, u32[]{:S(2)}, u32[]{:S(2)}) %collective-permute-start.4) | collective-permute-done | bytes 59424 | tf_op jit(solution)/shard_map/ppermute | solution.py:1055
  67.3 2.3 %collective-permute-start.9 = (bf16[32,384]{1,0:T(8,128)(2,1)S(1)}, bf16[32,384]{1,0:T(8,128)(2,1)S(1)}, u32[]{:S(2)}, u32[]{:S(2)}) collective-permute-start(bf16[32,384]{1,0:T(8,128)(2,1)S(1)} %get-tuple-element.33), channel_id=1, source_target_pairs={{0,6},{2,8},{4,10},{6,12},{8,14},{10,0},{12,2},{14,4},{1,7},{3,9},... | collective-permute-start | bytes 73736 | tf_op jit(solution)/shard_map/ppermute | solution.py:936
  69.7 4.5 %shard_map.89 = (f32[3,240,1280]{2,1,0:T(8,128)S(1)}, f32[240,1024]{1,0:T(8,128)S(1)}, f32[240,1024]{1,0:T(8,128)S(1)}) custom-call(s32[2]{0:T(128)S(1)} %pad_add_fusion.place, bf16[96,2048]{1,0:T(8,128)(2,1)S(1)} %collective-permute-done.edge, f32[4,3,64]{2,1,0:T(4,128)S(1)} %copy.9.gain, bf16[464,2048]{1,0:T(8,128)(2,1)} %x.5), custom_call_target="tpu_custom_call" | custom-call | flops 20000000 | bytes 1048576 | tf_op jit(solution)/shard_map/pallas_call | solution.py:903
  74.1 0.0 copy-start
  74.2 0.0 copy-start.1
  74.2 0.0 copy-start.2
  74.2 0.0 copy-start.3
  74.2 0.0 copy-start.4
  74.2 0.0 copy-start.5
  74.2 7.5 %shard_map.90.refs_0_ = f32[464,2048]{1,0:T(8,128)S(1)} custom-call(s32[2]{0:T(128)S(1)} %pad_add_fusion.place, bf16[464,1024]{1,0:T(8,128)(2,1)S(1)} %get-tuple-element.37.beside, bf16[16,1024]{1,0:T(8,128)(2,1)S(1)} %collective-permute-done.13.corner, f32[4,3,64]{2,1,0:T(4,128)S(1)} %copy.9.gain, f32[3,240,1280]{2,1,0:T(8,128)S(1)} %get-tuple-element.39.inner, ...), custom_call_target="tpu_custom_call" | custom-call | flops 20000000 | bytes 1048576 | tf_op jit(solution)/shard_map/pallas_call | solution.py:903
  81.8 0.0 copy-done
  81.8 0.0 copy-done.1
  81.8 4.5 %shard_map.87.coarse = f32[32,512]{1,0:T(8,128)S(1)} custom-call(s32[2]{0:T(128)S(1)} %pad_add_fusion.place, f32[32,1024]{1,0:T(8,128)S(1)} %get-tuple-element.27.ring, bf16[29,1024]{1,0:T(8,128)(2,1)S(1)} %get-tuple-element.28.own, bf16[29,1024]{1,0:T(8,128)(2,1)S(1)} %collective-permute-done.4.others, bf16[64,256]{1,0:T(8,128)(2,1)S(1)} %copy-done.2, ...), custom_call_target="tpu_custom_call" | custom-call | flops 200000000 | bytes 1048576 | tf_op jit(solution)/shard_map/pallas_call | solution.py:903
  86.3 0.0 collective-permute-done.9.from_m3
  86.3 0.0 collective-permute-done.7.from_m2
  86.3 0.0 collective-permute-done.8.from_p2
  86.3 0.0 collective-permute-done.5.e2
  86.3 0.0 collective-permute-done.6.o2
  86.3 7.7 %shard_map.91 = bf16[464,2048]{1,0:T(8,128)(2,1)} custom-call(s32[2]{0:T(128)S(1)} %pad_add_fusion.place, f32[32,512]{1,0:T(8,128)S(1)} %shard_map.87.coarse, bf16[216,1152]{1,0:T(8,128)(2,1)S(1)} %collective-permute-done.5.e2, bf16[216,1152]{1,0:T(8,128)(2,1)S(1)} %collective-permute-done.6.o2, bf16[96,768]{1,0:T(8,128)(2,1)S(1)} %collective-permute-done.7.from_m2, ...), custom_call_target="tpu_custom_call" | custom-call | flops 20000000 | bytes 1048576 | tf_op jit(solution)/shard_map/pallas_call | solution.py:903
  (6 shorter events, 0.0 us)
Async XLA Ops:
  0.0 8.7 %copy-start.6 = (f32[4,3,64]{2,0,1:T(4,128)S(1)}, f32[4,3,64]{2,0,1:T(4,128)}, u32[]{:S(2)}) copy-start(f32[4,3,64]{2,0,1:T(4,128)} %param.9) | copy-start | bytes 9220
  2.0 6.7 %collective-permute-start = (bf16[96,2048]{1,0:T(8,128)(2,1)S(1)}, bf16[96,2048]{1,0:T(8,128)(2,1)S(1)}, u32[]{:S(2)}, u32[]{:S(2)}) collective-permute-start(bf16[96,2048]{1,0:T(8,128)(2,1)S(1)} %get-tuple-element.25), channel_id=1, source_target_pairs={{0,1},{1,0},{2,3},{3,2},{4,5},{5,4},{6,7},{7,6},{8,9},{9,8},{10,11... | collective-permute-start | bytes 1179656 | tf_op jit(solution)/shard_map/ppermute | solution.py:950
  2.6 53.0 %collective-permute-start.11 = (bf16[544,384]{1,0:T(8,128)(2,1)S(1)}, bf16[544,384]{1,0:T(8,128)(2,1)S(1)}, u32[]{:S(2)}, u32[]{:S(2)}) collective-permute-start(bf16[544,384]{1,0:T(8,128)(2,1)S(1)} %get-tuple-element.35), channel_id=1, source_target_pairs={{0,2},{2,0},{4,6},{6,4},{8,10},{10,8},{12,14},{14,12},{1,3},{3,1},... | collective-permute-start | bytes 1253384 | tf_op jit(solution)/shard_map/ppermute | solution.py:951
  5.1 51.8 %collective-permute-start.12 = (bf16[544,384]{1,0:T(8,128)(2,1)S(1)}, bf16[544,384]{1,0:T(8,128)(2,1)S(1)}, u32[]{:S(2)}, u32[]{:S(2)}) collective-permute-start(bf16[544,384]{1,0:T(8,128)(2,1)S(1)} %get-tuple-element.36), channel_id=1, source_target_pairs={{0,14},{2,4},{4,2},{6,8},{8,6},{10,12},{12,10},{14,0},{1,15},{3,5}... | collective-permute-start | bytes 1253384 | tf_op jit(solution)/shard_map/ppermute | solution.py:952
  15.6 70.7 %collective-permute-start.5 = (bf16[216,1152]{1,0:T(8,128)(2,1)S(1)}, bf16[216,1152]{1,0:T(8,128)(2,1)S(1)}, u32[]{:S(2)}, u32[]{:S(2)}) collective-permute-start(bf16[216,1152]{1,0:T(8,128)(2,1)S(1)} %get-tuple-element.29), channel_id=1, source_target_pairs={{0,2},{2,0},{4,6},{6,4},{8,10},{10,8},{12,14},{14,12},{1,3},{3,1},... | collective-permute-start | bytes 1493000 | tf_op jit(solution)/shard_map/ppermute | solution.py:1057
  15.7 70.6 %collective-permute-start.6 = (bf16[216,1152]{1,0:T(8,128)(2,1)S(1)}, bf16[216,1152]{1,0:T(8,128)(2,1)S(1)}, u32[]{:S(2)}, u32[]{:S(2)}) collective-permute-start(bf16[216,1152]{1,0:T(8,128)(2,1)S(1)} %get-tuple-element.30), channel_id=1, source_target_pairs={{0,14},{2,4},{4,2},{6,8},{8,6},{10,12},{12,10},{14,0},{1,15},{3,5}... | collective-permute-start | bytes 1493000 | tf_op jit(solution)/shard_map/ppermute | solution.py:1058
  17.6 29.5 %collective-permute-start.1 = (f32[32,512]{1,0:T(8,128)S(1)}, f32[32,512]{1,0:T(8,128)S(1)}, u32[]{:S(2)}, u32[]{:S(2)}) collective-permute-start(f32[32,512]{1,0:T(8,128)S(1)} %get-tuple-element.26.mine), channel_id=1, source_target_pairs={{0,2},{2,0},{4,6},{6,4},{8,10},{10,8},{12,14},{14,12},{1,3},{3,1},... | collective-permute-start | bytes 196616 | tf_op jit(solution)/shard_map/ppermute | solution.py:1037
  47.6 4.5 %collective-permute-start.2 = (f32[32,640]{1,0:T(8,128)S(1)}, f32[32,640]{1,0:T(8,128)S(1)}, u32[]{:S(2)}, u32[]{:S(2)}) collective-permute-start(f32[32,640]{1,0:T(8,128)S(1)} %shard_map.84.mine), channel_id=1, source_target_pairs={{0,4},{2,6},{4,0},{6,2},{8,12},{10,14},{12,8},{14,10},{1,5},{3,7},... | collective-permute-start | bytes 245768 | tf_op jit(solution)/shard_map/ppermute | solution.py:1037
  52.7 12.1 %collective-permute-start.3 = (f32[32,896]{1,0:T(8,128)S(1)}, f32[32,896]{1,0:T(8,128)S(1)}, u32[]{:S(2)}, u32[]{:S(2)}) collective-permute-start(f32[32,896]{1,0:T(8,128)S(1)} %shard_map.85.mine), channel_id=1, source_target_pairs={{0,8},{2,10},{4,12},{6,14},{8,0},{10,2},{12,4},{14,6},{1,9},{3,11}... | collective-permute-start | bytes 344072 | tf_op jit(solution)/shard_map/ppermute | solution.py:1037
  55.6 4.8 %collective-permute-start.10 = (bf16[32,384]{1,0:T(8,128)(2,1)S(1)}, bf16[32,384]{1,0:T(8,128)(2,1)S(1)}, u32[]{:S(2)}, u32[]{:S(2)}) collective-permute-start(bf16[32,384]{1,0:T(8,128)(2,1)S(1)} %get-tuple-element.34), channel_id=1, source_target_pairs={{0,10},{2,12},{4,14},{6,0},{8,2},{10,4},{12,6},{14,8},{1,11},{3,13... | collective-permute-start | bytes 73736 | tf_op jit(solution)/shard_map/ppermute | solution.py:936
  56.9 29.4 %collective-permute-start.7 = (bf16[96,768]{1,0:T(8,128)(2,1)S(1)}, bf16[96,768]{1,0:T(8,128)(2,1)S(1)}, u32[]{:S(2)}, u32[]{:S(2)}) collective-permute-start(bf16[96,768]{1,0:T(8,128)(2,1)S(1)} %get-tuple-element.31), channel_id=1, source_target_pairs={{0,4},{2,6},{4,8},{6,10},{8,12},{10,14},{12,0},{14,2},{1,5},{3,7},... | collective-permute-start | bytes 442376 | tf_op jit(solution)/shard_map/ppermute | solution.py:936
  60.4 25.9 %collective-permute-start.8 = (bf16[96,768]{1,0:T(8,128)(2,1)S(1)}, bf16[96,768]{1,0:T(8,128)(2,1)S(1)}, u32[]{:S(2)}, u32[]{:S(2)}) collective-permute-start(bf16[96,768]{1,0:T(8,128)(2,1)S(1)} %get-tuple-element.32), channel_id=1, source_target_pairs={{0,12},{2,14},{4,0},{6,2},{8,4},{10,6},{12,8},{14,10},{1,13},{3,15... | collective-permute-start | bytes 442376 | tf_op jit(solution)/shard_map/ppermute | solution.py:936
  64.8 1.3 %collective-permute-start.13 = (bf16[16,1024]{1,0:T(8,128)(2,1)S(1)}, bf16[16,1024]{1,0:T(8,128)(2,1)S(1)}, u32[]{:S(2)}, u32[]{:S(2)}) collective-permute-start(bf16[16,1024]{1,0:T(8,128)(2,1)S(1)} %get-tuple-element.38), channel_id=1, source_target_pairs={{0,1},{1,0},{2,3},{3,2},{4,5},{5,4},{6,7},{7,6},{8,9},{9,8},{10,11... | collective-permute-start | bytes 98312 | tf_op jit(solution)/shard_map/ppermute | solution.py:992
  66.1 1.3 %collective-permute-start.4 = (bf16[29,1024]{1,0:T(8,128)(2,1)S(1)}, bf16[29,1024]{1,0:T(8,128)(2,1)S(1)}, u32[]{:S(2)}, u32[]{:S(2)}) collective-permute-start(bf16[29,1024]{1,0:T(8,128)(2,1)S(1)} %get-tuple-element.28.own), channel_id=1, source_target_pairs={{0,1},{1,0},{2,3},{3,2},{4,5},{5,4},{6,7},{7,6},{8,9},{9,8},{10,11... | collective-permute-start | bytes 178184 | tf_op jit(solution)/shard_map/ppermute | solution.py:1055
  67.3 18.9 %collective-permute-start.9 = (bf16[32,384]{1,0:T(8,128)(2,1)S(1)}, bf16[32,384]{1,0:T(8,128)(2,1)S(1)}, u32[]{:S(2)}, u32[]{:S(2)}) collective-permute-start(bf16[32,384]{1,0:T(8,128)(2,1)S(1)} %get-tuple-element.33), channel_id=1, source_target_pairs={{0,6},{2,8},{4,10},{6,12},{8,14},{10,0},{12,2},{14,4},{1,7},{3,9},... | collective-permute-start | bytes 73736 | tf_op jit(solution)/shard_map/ppermute | solution.py:936
  74.1 7.6 %copy-start = (bf16[256,768]{1,0:T(8,128)(2,1)S(1)}, bf16[256,768]{1,0:T(8,128)(2,1)}, u32[]{:S(2)}) copy-start(bf16[256,768]{1,0:T(8,128)(2,1)} %wqkv.1) | copy-start | bytes 1179652
  74.2 7.6 %copy-start.1 = (bf16[256,256]{1,0:T(8,128)(2,1)S(1)}, bf16[256,256]{1,0:T(8,128)(2,1)}, u32[]{:S(2)}) copy-start(bf16[256,256]{1,0:T(8,128)(2,1)} %wo.1) | copy-start | bytes 393220
  74.2 7.6 %copy-start.2 = (bf16[64,256]{1,0:T(8,128)(2,1)S(1)}, bf16[64,256]{1,0:T(8,128)(2,1)}, u32[]{:S(2)}) copy-start(bf16[64,256]{1,0:T(8,128)(2,1)} %we.1) | copy-start | bytes 98308
  74.2 7.6 %copy-start.3 = (bf16[256,64]{0,1:T(8,128)(2,1)S(1)}, bf16[256,64]{0,1:T(8,128)(2,1)}, u32[]{:S(2)}) copy-start(bf16[256,64]{0,1:T(8,128)(2,1)} %param.15) | copy-start | bytes 98308
  74.2 7.6 %copy-start.4 = (f32[256]{0:T(256)S(1)}, f32[256]{0:T(256)}, u32[]{:S(2)}) copy-start(f32[256]{0:T(256)} %param.14) | copy-start | bytes 3076
  74.2 7.6 %copy-start.5 = (f32[8]{0:T(128)S(1)}, f32[8]{0:T(128)}, u32[]{:S(2)}) copy-start(f32[8]{0:T(128)} %scale.1) | copy-start | bytes 100
